TPU v7x, 32 devices: a whole 2x2x4 slice. The times are simulated.
32 devices in a mesh: dp: 2 (over y), ctx: 4 (over z), tp: 4 (over x, core).
Axes of the slice: x: 2, y: 2, z: 4, core: 2. Of those that a mesh axis runs over, the one named last changes fastest.
Arguments:
- layer_input: bfloat16 [2, 4096, 1024], P('dp', 'ctx'), may hold values from -6 to 6
- segments: int32 [2, 4096], P('dp', 'ctx'), may hold values from 0 to 16, as said below
- positions: int32 [2, 4096], P('dp', 'ctx'), may hold values from 0 to 4094, as said below
- w_q: bfloat16 [1024, 1024], P('dp', 'tp'), may hold values from -0.1875 to 0.1875
- w_k: bfloat16 [1024, 1024], P('dp', 'tp'), may hold values from -0.1875 to 0.1875
- w_v: bfloat16 [1024, 1024], P('dp', 'tp'), may hold values from -0.1875 to 0.1875
- w_o: bfloat16 [1024, 1024], P('tp', 'dp'), may hold values from -0.75 to 0.75
- w_in: bfloat16 [1024, 4096], P('dp', 'tp'), may hold values from -0.1875 to 0.1875
- w_out: bfloat16 [4096, 1024], P('tp', 'dp'), may hold values from -0.09375 to 0.09375
- ln1_gain: bfloat16 [1024], P('dp'), may hold values from 0.25 to 1.75
- ln1_bias: bfloat16 [1024], P('dp'), may hold values from -1 to 1
- ln2_gain: bfloat16 [1024], P('dp'), may hold values from 0.25 to 1.75
- ln2_bias: bfloat16 [1024], P('dp'), may hold values from -1 to 1
- cotangent: bfloat16 [2, 4096, 1024], P('dp', 'ctx'), may hold values from -6 to 6
Outputs:
- layer_output: float32 [2, 4096, 1024], P('dp', 'ctx')
- x_grad: float32 [2, 4096, 1024], P('dp', 'ctx')
- w_q_grad: float32 [1024, 1024], P('dp', 'tp')
- w_k_grad: float32 [1024, 1024], P('dp', 'tp')
- w_v_grad: float32 [1024, 1024], P('dp', 'tp')
- w_o_grad: float32 [1024, 1024], P('tp', 'dp')
- w_in_grad: float32 [1024, 4096], P('dp', 'tp')
- w_out_grad: float32 [4096, 1024], P('tp', 'dp')
- ln1_gain_grad: float32 [1024], P('dp')
- ln1_bias_grad: float32 [1024], P('dp')
- ln2_gain_grad: float32 [1024], P('dp')
- ln2_bias_grad: float32 [1024], P('dp')
Inputs may be any that keep to these rules, and one draw needn't show every extreme that they name: `segments`: along a sequence the document number never falls; it is 0 at the first slot and 16 at the last. `positions`: A slot's position is its offset from the first slot of its document.
All inputs are finite; a program needn't handle non-finite values.
Results may differ from a plain program's by a relative error of at most 0.023.
Values may be sent and summed in bfloat16 or wider, within the bound.
No kernel may reach another device: no remote copies, remote signals or barrier semaphores. Data moves between devices by JAX's collectives and lax.ppermute only.
A program may use at most 256 MiB of HBM per device.

v0:
```python
import jax
import jax.numpy as jnp
from jax import lax
from jax.sharding import PartitionSpec as P

D = 1024
H = 16


NEG_BIG = -1e30
SQRT_HALF = 0.7071067811865476
INV_SQRT_TAU = 0.3989422804014327


def rotate_heads(values, positions, head_size, sign):
    half = head_size // 2
    freq = 10000.0 ** (-jnp.arange(half, dtype=jnp.float32) * 2.0 / head_size)
    angles = positions.astype(jnp.float32)[..., None] * freq
    cosine = jnp.cos(angles)[..., None, :]
    sine = sign * jnp.sin(angles)[..., None, :]
    first = values[..., :half]
    second = values[..., half:]
    return jnp.concatenate(
        [first * cosine - second * sine, second * cosine + first * sine], axis=-1
    )


def norm_forward(values, gain, shift):
    centered = values - jnp.mean(values, axis=-1, keepdims=True)
    inverse = lax.rsqrt(jnp.mean(centered * centered, axis=-1, keepdims=True) + 1e-05)
    normed = centered * inverse
    return (normed * gain.astype(jnp.float32) + shift.astype(jnp.float32), normed, inverse)


def norm_backward(incoming, normed, inverse, gain):
    scaled = incoming * gain.astype(jnp.float32)
    inner = (
        scaled
        - jnp.mean(scaled, axis=-1, keepdims=True)
        - normed * jnp.mean(scaled * normed, axis=-1, keepdims=True)
    )
    return (inverse * inner, jnp.sum(incoming * normed, axis=0), jnp.sum(incoming, axis=0))


def body(
    layer_input,
    segments,
    positions,
    w_q,
    w_k,
    w_v,
    w_o,
    w_in,
    w_out,
    ln1_gain,
    ln1_bias,
    ln2_gain,
    ln2_bias,
    cotangent,
):
    seqs, piece_len, width = layer_input.shape
    head_size = D // H
    (
        query_weight,
        key_weight,
        value_weight,
        out_weight,
        in_weight,
        down_weight,
        gain_one,
        shift_one,
        gain_two,
        shift_two,
    ) = (
        lax.all_gather(w_q, "dp", axis=0, tiled=True),
        lax.all_gather(w_k, "dp", axis=0, tiled=True),
        lax.all_gather(w_v, "dp", axis=0, tiled=True),
        lax.all_gather(w_o, "dp", axis=1, tiled=True),
        lax.all_gather(w_in, "dp", axis=0, tiled=True),
        lax.all_gather(w_out, "dp", axis=1, tiled=True),
        lax.all_gather(ln1_gain, "dp", axis=0, tiled=True),
        lax.all_gather(ln1_bias, "dp", axis=0, tiled=True),
        lax.all_gather(ln2_gain, "dp", axis=0, tiled=True),
        lax.all_gather(ln2_bias, "dp", axis=0, tiled=True),
    )
    local_width = query_weight.shape[1]
    heads_here = local_width // head_size
    doc_whole = lax.all_gather(segments, "ctx", axis=1, tiled=True)
    full_len = doc_whole.shape[1]
    row_count = seqs * piece_len
    tokens = layer_input.reshape(row_count, width)
    scale = head_size ** (-0.5)
    doc_low = jnp.min(segments, axis=1)
    doc_high = jnp.max(segments, axis=1)
    share = row_count // lax.axis_size("tp")
    offset = lax.axis_index("tp") * share

    def reduce_heads(partial_sum):
        return lax.psum_scatter(
            partial_sum.astype(jnp.bfloat16), "tp", scatter_dimension=0, tiled=True
        ).astype(jnp.float32)

    def spread_rows(rows_low):
        return lax.all_gather(rows_low, "tp", axis=0, tiled=True)

    def own_rows(whole_rows):
        return lax.dynamic_slice_in_dim(whole_rows, offset, share, 0)

    def project(weight):
        return jnp.dot(tokens, weight, preferred_element_type=jnp.float32).reshape(
            seqs, piece_len, heads_here, head_size
        )

    queries = rotate_heads(project(query_weight), positions, head_size, 1.0).astype(jnp.bfloat16)
    keys = rotate_heads(project(key_weight), positions, head_size, 1.0).astype(jnp.bfloat16)
    values = project(value_weight).astype(jnp.bfloat16)

    def touches():
        meets = (doc_low <= jnp.max(doc_whole, axis=1)) & (jnp.min(doc_whole, axis=1) <= doc_high)
        return (jnp.any(meets), doc_whole)

    def masked_scores(key_piece, doc_keys):
        scores = (
            jnp.einsum("sqhd,skhd->shqk", queries, key_piece, preferred_element_type=jnp.float32)
            * scale
        )
        same = segments[:, None, :, None] == doc_keys[:, None, None, :]
        return jnp.where(same, scores, NEG_BIG)

    start_state = (
        jnp.full((seqs, heads_here, piece_len), NEG_BIG, jnp.float32),
        jnp.zeros((seqs, heads_here, piece_len), jnp.float32),
        jnp.zeros((seqs, piece_len, heads_here, head_size), jnp.float32),
    )
    key_piece = lax.all_gather(keys, "ctx", axis=1, tiled=True)
    value_piece = lax.all_gather(values, "ctx", axis=1, tiled=True)
    needed, doc_keys = touches()

    def forward_update(state):
        run_max, run_total, run_out = state
        scores = masked_scores(key_piece, doc_keys)
        new_max = jnp.maximum(run_max, jnp.max(scores, axis=-1))
        weights_now = jnp.exp(scores - new_max[..., None])
        factor = jnp.exp(run_max - new_max)
        new_total = jnp.sum(weights_now, axis=-1)
        added = jnp.einsum(
            "shqk,skhd->sqhd",
            weights_now.astype(jnp.bfloat16),
            value_piece,
            preferred_element_type=jnp.float32,
        )
        new_out = run_out * jnp.swapaxes(factor, 1, 2)[..., None] + added
        return (new_max, new_total, new_out)

    run_max, run_total, run_out = lax.cond(needed, forward_update, lambda state: state, start_state)
    attended = run_out / jnp.swapaxes(run_total, 1, 2)[..., None]
    log_total = run_max + jnp.log(run_total)
    attended_low = attended.astype(jnp.bfloat16).reshape(row_count, local_width)
    mixed = reduce_heads(jnp.dot(attended_low, out_weight, preferred_element_type=jnp.float32))
    token_rows = own_rows(tokens).astype(jnp.float32)
    hidden_one, normed_one, inverse_one = norm_forward(token_rows + mixed, gain_one, shift_one)
    hidden_low = spread_rows(hidden_one.astype(jnp.bfloat16))
    pre_act = jnp.dot(hidden_low, in_weight, preferred_element_type=jnp.float32)
    activated = jax.nn.gelu(pre_act, approximate=False).astype(jnp.bfloat16)
    branch_two = reduce_heads(jnp.dot(activated, down_weight, preferred_element_type=jnp.float32))
    output, normed_two, inverse_two = norm_forward(hidden_one + branch_two, gain_two, shift_two)
    out_grad = own_rows(cotangent.reshape(row_count, width)).astype(jnp.float32)
    second_grad, gain_two_grad, shift_two_grad = norm_backward(
        out_grad, normed_two, inverse_two, gain_two
    )
    second_low = spread_rows(second_grad.astype(jnp.bfloat16))
    down_grad = jnp.einsum("rf,rd->fd", activated, second_low, preferred_element_type=jnp.float32)
    act_grad = jnp.einsum("rd,fd->rf", second_low, down_weight, preferred_element_type=jnp.float32)
    slope = (
        0.5 * (1.0 + jax.scipy.special.erf(pre_act * SQRT_HALF))
        + pre_act * jnp.exp(-0.5 * pre_act * pre_act) * INV_SQRT_TAU
    )
    pre_grad = (act_grad * slope).astype(jnp.bfloat16)
    in_grad = jnp.einsum("rd,rf->df", hidden_low, pre_grad, preferred_element_type=jnp.float32)
    hidden_grad = second_grad + reduce_heads(
        jnp.einsum("rf,df->rd", pre_grad, in_weight, preferred_element_type=jnp.float32)
    )
    first_grad, gain_one_grad, shift_one_grad = norm_backward(
        hidden_grad, normed_one, inverse_one, gain_one
    )
    first_low = spread_rows(first_grad.astype(jnp.bfloat16))
    out_weight_grad = jnp.einsum(
        "rj,rd->jd", attended_low, first_low, preferred_element_type=jnp.float32
    )
    heads_grad = jnp.einsum("rd,jd->rj", first_low, out_weight, preferred_element_type=jnp.float32)
    heads_grad = heads_grad.astype(jnp.bfloat16).reshape(seqs, piece_len, heads_here, head_size)
    row_dot = jnp.swapaxes(jnp.sum(heads_grad.astype(jnp.float32) * attended, axis=-1), 1, 2)
    back_state = (
        jnp.zeros((seqs, piece_len, heads_here, head_size), jnp.float32),
        jnp.zeros((seqs, full_len, heads_here, head_size), jnp.float32),
        jnp.zeros((seqs, full_len, heads_here, head_size), jnp.float32),
    )
    backward_key_piece = lax.all_gather(keys, "ctx", axis=1, tiled=True)
    backward_value_piece = lax.all_gather(values, "ctx", axis=1, tiled=True)
    needed, backward_doc_keys = touches()

    def backward_update(state):
        scores = masked_scores(backward_key_piece, backward_doc_keys)
        probs = jnp.exp(scores - log_total[..., None])
        value_part = jnp.einsum(
            "shqk,sqhd->skhd",
            probs.astype(jnp.bfloat16),
            heads_grad,
            preferred_element_type=jnp.float32,
        )
        prob_grad = jnp.einsum(
            "sqhd,skhd->shqk", heads_grad, backward_value_piece, preferred_element_type=jnp.float32
        )
        score_grad = (probs * (prob_grad - row_dot[..., None])).astype(jnp.bfloat16)
        query_grad = (
            jnp.einsum(
                "shqk,skhd->sqhd",
                score_grad,
                backward_key_piece,
                preferred_element_type=jnp.float32,
            )
            * scale
        )
        key_part = (
            jnp.einsum("shqk,sqhd->skhd", score_grad, queries, preferred_element_type=jnp.float32)
            * scale
        )
        return (query_grad, key_part, value_part)

    query_grad, key_grad_all, value_grad_all = lax.cond(
        needed, backward_update, lambda state: state, back_state
    )
    key_grad, value_grad = (
        lax.psum_scatter(
            key_grad_all.astype(jnp.bfloat16), "ctx", scatter_dimension=1, tiled=True
        ).astype(jnp.float32),
        lax.psum_scatter(
            value_grad_all.astype(jnp.bfloat16), "ctx", scatter_dimension=1, tiled=True
        ).astype(jnp.float32),
    )
    query_low = (
        rotate_heads(query_grad, positions, head_size, -1.0)
        .astype(jnp.bfloat16)
        .reshape(row_count, local_width)
    )
    key_low = (
        rotate_heads(key_grad, positions, head_size, -1.0)
        .astype(jnp.bfloat16)
        .reshape(row_count, local_width)
    )
    value_low = value_grad.astype(jnp.bfloat16).reshape(row_count, local_width)
    query_weight_grad = jnp.einsum(
        "rd,rj->dj", tokens, query_low, preferred_element_type=jnp.float32
    )
    key_weight_grad = jnp.einsum("rd,rj->dj", tokens, key_low, preferred_element_type=jnp.float32)
    value_weight_grad = jnp.einsum(
        "rd,rj->dj", tokens, value_low, preferred_element_type=jnp.float32
    )
    input_part = jnp.einsum(
        "rj,dj->rd", query_low, query_weight, preferred_element_type=jnp.float32
    )
    input_part = input_part + jnp.einsum(
        "rj,dj->rd", key_low, key_weight, preferred_element_type=jnp.float32
    )
    input_part = input_part + jnp.einsum(
        "rj,dj->rd", value_low, value_weight, preferred_element_type=jnp.float32
    )
    input_grad = first_grad + reduce_heads(input_part)
    norm_terms = jnp.stack([gain_one_grad, shift_one_grad, gain_two_grad, shift_two_grad])[None]
    output, input_grad, norm_terms = (
        lax.all_gather(output.astype(jnp.bfloat16), "tp", axis=0, tiled=True).astype(output.dtype),
        lax.all_gather(input_grad.astype(jnp.bfloat16), "tp", axis=0, tiled=True).astype(
            input_grad.dtype
        ),
        lax.all_gather(norm_terms.astype(jnp.bfloat16), "tp", axis=0, tiled=True).astype(
            norm_terms.dtype
        ),
    )
    norm_terms = jnp.sum(norm_terms, axis=0)
    gain_one_grad, shift_one_grad, gain_two_grad, shift_two_grad = (
        norm_terms[0],
        norm_terms[1],
        norm_terms[2],
        norm_terms[3],
    )
    shares = (
        lax.psum_scatter(
            query_weight_grad.astype(jnp.bfloat16), "dp", scatter_dimension=0, tiled=True
        ).astype(jnp.float32),
        lax.psum_scatter(
            key_weight_grad.astype(jnp.bfloat16), "dp", scatter_dimension=0, tiled=True
        ).astype(jnp.float32),
        lax.psum_scatter(
            value_weight_grad.astype(jnp.bfloat16), "dp", scatter_dimension=0, tiled=True
        ).astype(jnp.float32),
        lax.psum_scatter(
            out_weight_grad.astype(jnp.bfloat16), "dp", scatter_dimension=1, tiled=True
        ).astype(jnp.float32),
        lax.psum_scatter(
            in_grad.astype(jnp.bfloat16), "dp", scatter_dimension=0, tiled=True
        ).astype(jnp.float32),
        lax.psum_scatter(
            down_grad.astype(jnp.bfloat16), "dp", scatter_dimension=1, tiled=True
        ).astype(jnp.float32),
        lax.psum_scatter(
            gain_one_grad.astype(jnp.bfloat16), "dp", scatter_dimension=0, tiled=True
        ).astype(jnp.float32),
        lax.psum_scatter(
            shift_one_grad.astype(jnp.bfloat16), "dp", scatter_dimension=0, tiled=True
        ).astype(jnp.float32),
        lax.psum_scatter(
            gain_two_grad.astype(jnp.bfloat16), "dp", scatter_dimension=0, tiled=True
        ).astype(jnp.float32),
        lax.psum_scatter(
            shift_two_grad.astype(jnp.bfloat16), "dp", scatter_dimension=0, tiled=True
        ).astype(jnp.float32),
    )
    totals = (
        lax.psum(shares[0].astype(jnp.bfloat16), "ctx").astype(jnp.float32),
        lax.psum(shares[1].astype(jnp.bfloat16), "ctx").astype(jnp.float32),
        lax.psum(shares[2].astype(jnp.bfloat16), "ctx").astype(jnp.float32),
        lax.psum(shares[3].astype(jnp.bfloat16), "ctx").astype(jnp.float32),
        lax.psum(shares[4].astype(jnp.bfloat16), "ctx").astype(jnp.float32),
        lax.psum(shares[5].astype(jnp.bfloat16), "ctx").astype(jnp.float32),
        lax.psum(shares[6].astype(jnp.bfloat16), "ctx").astype(jnp.float32),
        lax.psum(shares[7].astype(jnp.bfloat16), "ctx").astype(jnp.float32),
        lax.psum(shares[8].astype(jnp.bfloat16), "ctx").astype(jnp.float32),
        lax.psum(shares[9].astype(jnp.bfloat16), "ctx").astype(jnp.float32),
    )
    return (
        output.reshape(seqs, piece_len, width),
        input_grad.reshape(seqs, piece_len, width),
        totals[0],
        totals[1],
        totals[2],
        totals[3],
        totals[4],
        totals[5],
        totals[6],
        totals[7],
        totals[8],
        totals[9],
    )


def solution(mesh):
    return jax.shard_map(
        body,
        mesh=mesh,
        in_specs=(
            P("dp", "ctx", None),
            P("dp", "ctx"),
            P("dp", "ctx"),
            P("dp", "tp"),
            P("dp", "tp"),
            P("dp", "tp"),
            P("tp", "dp"),
            P("dp", "tp"),
            P("tp", "dp"),
            P("dp"),
            P("dp"),
            P("dp"),
            P("dp"),
            P("dp", "ctx", None),
        ),
        out_specs=(
            P("dp", "ctx", None),
            P("dp", "ctx", None),
            P("dp", "tp"),
            P("dp", "tp"),
            P("dp", "tp"),
            P("tp", "dp"),
            P("dp", "tp"),
            P("tp", "dp"),
            P("dp"),
            P("dp"),
            P("dp"),
            P("dp"),
        ),
        check_vma=False,
    )
```

profile of v0, /device:TPU:0, one launch (start us, length us, event | category | flops | bytes accessed | tf_op | source)
XLA Modules:
  0.0 972.7 jit_solution(8596426434265717203)
XLA Ops:
  8.1 10.4 %all_gather.63 = bf16[1024,256]{1,0:T(8,128)(2,1)S(1)} all-gather(bf16[512,256]{1,0:T(8,128)(2,1)} %param.23), channel_id=1, replica_groups=mesh['dp'=2,'ctx'=4,'tp'=4] {'dp'}, dimensions={0}, use_global_device_ids=true | all-gather | bytes 786432 | tf_op jit(solution)/shard_map/all_gather | solution.py:77
  21.9 8.1 all_gather.61
  30.3 7.3 all_gather.60
  45.1 13.8 %all_gather.59 = s32[1,4096]{1,0:T(1,128)S(1)} all-gather(s32[1,1024]{1,0:T(1,128)S(1)} %copy-done.25), channel_id=1, replica_groups=mesh['dp'=2,'ctx'=4,'tp'=4] {'ctx'}, dimensions={1}, use_global_device_ids=true | all-gather | bytes 20480 | tf_op jit(solution)/shard_map/all_gather | solution.py:88
  62.8 7.0 all_gather.65
  69.8 46.2 %all-gather.15.cloned.1.call-done = bf16[1,4096,4,64]{1,3,2,0:T(8,128)(2,1)} async-done(((bf16[1,1024,4,64]{1,3,2,0:T(8,128)(2,1)}), bf16[1,4096,4,64]{1,3,2,0:T(8,128)(2,1)}) %all-gather.15.cloned.1.call-update) | async-done | bytes 2097168 | tf_op jit(solution)/shard_map/all_gather | solution.py:135
  116.0 81.0 %conditional.2 = (f32[1,4,1024]{2,1,0:T(4,128)S(1)}, f32[1,4,1024]{2,1,0:T(4,128)}, f32[1,1024,4,64]{1,3,2,0:T(8,128)S(1)}, f32[1,4,1024]{2,1,0:T(4,128)S(1)}) conditional(s32[]{:T(128)} %convert_element_type.302, () %tuple.32, (s32[1,1024]{1,0:T(1,128)S(1)}, s32[1,4096]{1,0:T(1,128)S(1)}, bf16[1,1024,4,64]{1,3,2,0:T(8,128)(2,1)S(1)}, ...), branch_computations={%region_4.0_spmd, %region_5.8_spmd} | conditional | flops 4483981312 | bytes 232476736 | solution.py:155
  116.2 4.7 broadcast_compare_fusion
  120.9 25.9 %fusion = (f32[4,1024]{1,0:T(4,128)S(1)}, f32[4,1024,4096]{2,1,0:T(8,128)}) fusion(pred[1024,4096]{1,0:T(8,128)(4,1)} %broadcast_compare_fusion, bf16[1,4096,4,64]{1,3,2,0:T(8,128)(2,1)S(1)} %copy-done.2, bf16[1,1024,4,64]{1,3,2,0:T(8,128)(2,1)S(1)} %get-tuple-element.51), kind=kOutput, calls=%fused_computation.2 | convolution fusion | flops 2197811200 | bytes 73940992 | tf_op jit(solution)/shard_map/cond/branch_1_fun/sqhd,skhd->shqk/dot_general | solution.py:124
  146.8 23.3 %fusion.2 = f32[4,1024]{1,0:T(4,128)} fusion(f32[4,1024,4096]{2,1,0:T(8,128)} %get-tuple-element.155, f32[4,1024]{1,0:T(4,128)S(1)} %broadcast_maximum_fusion, pred[1024,4096]{1,0:T(8,128)(4,1)} %broadcast_compare_fusion), kind=kLoop, calls=%fused_computation.4 | loop fusion | flops 67104768 | bytes 71335936 | tf_op jit(solution)/shard_map/cond/branch_1_fun/reduce_sum | solution.py:145
  170.9 26.1 %fusion.14 = f32[1,1024,4,64]{1,3,2,0:T(8,128)S(1)} fusion(bf16[1,4096,4,64]{1,3,2,0:T(8,128)(2,1)} %get-tuple-element.53, f32[4,1024,4096]{2,1,0:T(8,128)} %get-tuple-element.155, f32[4,1024]{1,0:T(4,128)S(1)} %broadcast_maximum_fusion, pred[1024,4096]{1,0:T(8,128)(4,1)} %broadcast_compare_fusion, f32[1024,4]{0,1:T(4,128)S(1)} %get-tuple-element.144), kind=kOutput, calls=%fused_computation.12 | convolution fusion | flops 2214854656 | bytes 74481664 | tf_op jit(solution)/shard_map/cond/branch_1_fun/shqk,skhd->sqhd/dot_general | solution.py:146
  201.4 4.4 all-gather.1
  205.8 4.4 all-gather.2
  210.2 20.7 %reduce-scatter.13.cloned.1.call-done = bf16[256,1024]{1,0:T(8,128)(2,1)} async-done(((bf16[1024,1024]{1,0:T(8,128)(2,1)}), bf16[256,1024]{1,0:T(8,128)(2,1)}) %reduce-scatter.13.cloned.1.call-update) | async-done | bytes 524304 | tf_op jit(solution)/shard_map/reduce_scatter | solution.py:99
  236.8 22.2 %all-gather.17.cloned.1.call-done = bf16[1024,1024]{1,0:T(8,128)(2,1)} async-done(((bf16[256,1024]{1,0:T(8,128)(2,1)}), bf16[1024,1024]{1,0:T(8,128)(2,1)}) %all-gather.17.cloned.1.call-update) | async-done | bytes 2097168 | tf_op jit(solution)/shard_map/all_gather | solution.py:104
  259.1 14.3 %fusion.50 = (bf16[1024,1024]{1,0:T(8,128)(2,1)}, f32[1024,1024]{1,0:T(8,128)}) fusion(bf16[1024,1024]{1,0:T(8,128)(2,1)} %all-gather.17.cloned.1.call-done, bf16[1024,1024]{1,0:T(8,128)(2,1)} %all-gather.19.cloned.1.call-done), kind=kOutput, calls=%fused_computation.46 | convolution fusion | flops 2215641088 | bytes 10485760 | tf_op jit(solution)/shard_map/dot_general | solution.py:163
  273.4 20.1 %all-gather.21.cloned.1.call-done = bf16[1024,1024]{1,0:T(8,128)(2,1)} async-done(((bf16[1024,512]{1,0:T(8,128)(2,1)}), bf16[1024,1024]{1,0:T(8,128)(2,1)}) %all-gather.21.cloned.1.call-update) | async-done | bytes 2097168 | tf_op jit(solution)/shard_map/all_gather | solution.py:80
  293.5 5.9 convolution_convert_fusion.3
  299.5 4.4 all-gather.3
  303.9 4.4 all-gather.4
  308.3 22.5 %reduce-scatter.15.cloned.1.call-done = bf16[256,1024]{1,0:T(8,128)(2,1)} async-done(((bf16[1024,1024]{1,0:T(8,128)(2,1)}), bf16[256,1024]{1,0:T(8,128)(2,1)}) %reduce-scatter.15.cloned.1.call-update) | async-done | bytes 524304 | tf_op jit(solution)/shard_map/reduce_scatter | solution.py:99
  337.5 22.5 %all-gather.25.cloned.1.call-done = bf16[1024,1024]{1,0:T(8,128)(2,1)} async-done(((bf16[256,1024]{1,0:T(8,128)(2,1)}), bf16[1024,1024]{1,0:T(8,128)(2,1)}) %all-gather.25.cloned.1.call-update) | async-done | bytes 2097168 | tf_op jit(solution)/shard_map/all_gather | solution.py:104
  360.0 6.3 fusion.56
  371.5 31.3 %reduce-scatter.17.cloned.1.call-done = bf16[256,1024]{1,0:T(8,128)(2,1)} async-done(((bf16[1024,1024]{1,0:T(8,128)(2,1)}), bf16[256,1024]{1,0:T(8,128)(2,1)}) %reduce-scatter.17.cloned.1.call-update) | async-done | bytes 524304 | tf_op jit(solution)/shard_map/reduce_scatter | solution.py:99
  408.0 22.7 %all-gather.27.cloned.1.call-done = bf16[1024,1024]{1,0:T(8,128)(2,1)} async-done(((bf16[256,1024]{1,0:T(8,128)(2,1)}), bf16[1024,1024]{1,0:T(8,128)(2,1)}) %all-gather.27.cloned.1.call-update) | async-done | bytes 2097168 | tf_op jit(solution)/shard_map/all_gather | solution.py:104
  434.2 129.8 %conditional.3 = (bf16[1,4096,4,64]{1,3,2,0:T(8,128)(2,1)}, bf16[1,4096,4,64]{1,3,2,0:T(8,128)(2,1)}, f32[1,1024,4,32]{1,3,2,0:T(8,128)}, f32[1,1024,4,32]{1,3,2,0:T(8,128)S(1)}) conditional(s32[]{:T(128)} %convert_element_type.302, () %tuple.34, (s32[1,1024]{1,0:T(1,128)S(1)}, s32[1,4096]{1,0:T(1,128)S(1)}, ...), branch_computations={%region_20.21_spmd, %region_21.22_spmd} | conditional | flops 10911748096 | bytes 349294720 | solution.py:230
  434.3 4.7 broadcast_compare_fusion.1
  439.0 23.1 %fusion.34 = f32[4,1024,4096]{2,1,0:T(8,128)} fusion(bf16[1,4096,4,64]{1,3,2,0:T(8,128)(2,1)S(1)} %get-tuple-element.57, bf16[1,1024,4,64]{1,3,2,0:T(8,128)(2,1)S(1)} %get-tuple-element.56), kind=kOutput, calls=%fused_computation.31 | convolution fusion | flops 2147483648 | bytes 69730304 | tf_op jit(solution)/shard_map/cond/branch_1_fun/sqhd,skhd->shqk/dot_general | solution.py:124
  462.2 28.2 %fusion.28 = bf16[1,4096,4,64]{1,3,2,0:T(8,128)(2,1)} fusion(f32[4,1024,4096]{2,1,0:T(8,128)} %fusion.34, f32[4,1024]{1,0:T(4,128)S(1)} %add_bitcast_fusion, pred[1024,4096]{1,0:T(8,128)(4,1)} %broadcast_compare_fusion.1, bf16[1,1024,4,64]{1,3,2,0:T(8,128)(2,1)S(1)} %get-tuple-element.60), kind=kOutput, calls=%fused_computation.27 | convolution fusion | flops 2214592512 | bytes 73940992 | tf_op jit(solution)/shard_map/cond/branch_1_fun/shqk,sqhd->skhd/dot_general | solution.py:205
  490.3 41.9 %multiply_convert_fusion = bf16[4,1024,4096]{2,1,0:T(8,128)(2,1)} fusion(f32[4,1024,4096]{2,1,0:T(8,128)} %fusion.34, f32[4,1024]{1,0:T(4,128)S(1)} %bitcast.238, f32[4,1024]{1,0:T(4,128)S(1)} %add_bitcast_fusion, pred[1024,4096]{1,0:T(8,128)(4,1)} %broadcast_compare_fusion.1, bf16[1,4096,4,64]{1,3,2,0:T(8,128)(2,1)} %get-tuple-element.61, ...), kind=kOutput, calls=%fused_computation.19 | convolution fusion | flops 2248146944 | bytes 107511808 | tf_op jit(solution)/shard_map/cond/branch_1_fun/sqhd,skhd->shqk/dot_general | solution.py:211
  532.2 15.6 %fusion.39 = f32[1,1024,4,64]{1,3,2,0:T(8,128)S(1)} fusion(bf16[4,1024,4096]{2,1,0:T(8,128)(2,1)} %multiply_convert_fusion, bf16[1,4096,4,64]{1,3,2,0:T(8,128)(2,1)S(1)} %copy-done.4), kind=kOutput, calls=%fused_computation.34 | convolution fusion | flops 2147745792 | bytes 36700160 | tf_op jit(solution)/shard_map/cond/branch_1_fun/shqk,skhd->sqhd/dot_general | solution.py:216
  547.8 15.1 %fusion.27 = bf16[1,4096,4,64]{1,3,2,0:T(8,128)(2,1)} fusion(bf16[4,1024,4096]{2,1,0:T(8,128)(2,1)} %multiply_convert_fusion, bf16[1,1024,4,64]{1,3,2,0:T(8,128)(2,1)S(1)} %get-tuple-element.56), kind=kOutput, calls=%fused_computation.26 | convolution fusion | flops 2149580800 | bytes 36175872 | tf_op jit(solution)/shard_map/cond/branch_1_fun/shqk,sqhd->skhd/dot_general | solution.py:225
  565.6 5.3 convolution_convert_fusion.1
  571.0 6.0 convolution_convert_fusion
  580.4 27.4 %reduce-scatter.21.cloned.1.call-done = bf16[1,1024,4,64]{1,3,2,0:T(8,128)(2,1)} async-done(((bf16[1,4096,4,64]{1,3,2,0:T(8,128)(2,1)}), bf16[1,1024,4,64]{1,3,2,0:T(8,128)(2,1)}) %reduce-scatter.21.cloned.1.call-update) | async-done | bytes 524304 | tf_op jit(solution)/shard_map/reduce_scatter | solution.py:237
  610.4 43.1 %reduce-scatter.19.cloned.1.call-done = bf16[1,1024,4,64]{1,3,2,0:T(8,128)(2,1)} async-done(((bf16[1,4096,4,64]{1,3,2,0:T(8,128)(2,1)}), bf16[1,1024,4,64]{1,3,2,0:T(8,128)(2,1)}) %reduce-scatter.19.cloned.1.call-update) | async-done | bytes 524304 | tf_op jit(solution)/shard_map/reduce_scatter | solution.py:234
  667.2 20.3 %reduce-scatter.33.cloned.1.call-done = bf16[512,1024]{1,0:T(8,128)(2,1)} async-done(((bf16[1024,1024]{1,0:T(8,128)(2,1)}), bf16[512,1024]{1,0:T(8,128)(2,1)}) %reduce-scatter.33.cloned.1.call-update) | async-done | bytes 1048592 | tf_op jit(solution)/shard_map/reduce_scatter | solution.py:299
  687.5 34.2 %reduce-scatter.35.cloned.1.call-done = bf16[1024,512]{1,0:T(8,128)(2,1)} async-done(((bf16[1024,1024]{1,0:T(8,128)(2,1)}), bf16[1024,512]{1,0:T(8,128)(2,1)}) %reduce-scatter.35.cloned.1.call-update) | async-done | bytes 1048592 | tf_op jit(solution)/shard_map/reduce_scatter | solution.py:302
  721.7 16.8 %reduce-scatter.31.cloned.1.call-done = bf16[256,512]{1,0:T(8,128)(2,1)} async-done(((bf16[256,1024]{1,0:T(8,128)(2,1)}), bf16[256,512]{1,0:T(8,128)(2,1)}) %reduce-scatter.31.cloned.1.call-update) | async-done | bytes 262160 | tf_op jit(solution)/shard_map/reduce_scatter | solution.py:296
  738.5 17.5 %reduce-scatter.29.cloned.1.call-done = bf16[512,256]{0,1:T(8,128)(2,1)} async-done(((bf16[1024,256]{0,1:T(8,128)(2,1)}), bf16[512,256]{0,1:T(8,128)(2,1)}) %reduce-scatter.29.cloned.1.call-update) | async-done | bytes 262160 | tf_op jit(solution)/shard_map/reduce_scatter | solution.py:293
  756.0 17.3 %reduce-scatter.27.cloned.1.call-done = bf16[512,256]{0,1:T(8,128)(2,1)} async-done(((bf16[1024,256]{0,1:T(8,128)(2,1)}), bf16[512,256]{0,1:T(8,128)(2,1)}) %reduce-scatter.27.cloned.1.call-update) | async-done | bytes 262160 | tf_op jit(solution)/shard_map/reduce_scatter | solution.py:290
  773.3 17.5 %reduce-scatter.25.cloned.1.call-done = bf16[512,256]{0,1:T(8,128)(2,1)} async-done(((bf16[1024,256]{0,1:T(8,128)(2,1)}), bf16[512,256]{0,1:T(8,128)(2,1)}) %reduce-scatter.25.cloned.1.call-update) | async-done | bytes 262160 | tf_op jit(solution)/shard_map/reduce_scatter | solution.py:287
  790.9 34.1 %reduce-scatter.23.cloned.1.call-done = bf16[256,1024]{1,0:T(8,128)(2,1)} async-done(((bf16[1024,1024]{1,0:T(8,128)(2,1)}), bf16[256,1024]{1,0:T(8,128)(2,1)}) %reduce-scatter.23.cloned.1.call-update) | async-done | bytes 524304 | tf_op jit(solution)/shard_map/reduce_scatter | solution.py:99
  829.5 4.4 bitcast_convert_fusion.1
  833.9 5.3 all_gather.77
  839.3 5.0 all-reduce.6
  844.6 12.0 %all-reduce.4 = (bf16[512]{0:T(512)(128)(2,1)S(1)}, bf16[512]{0:T(512)(128)(2,1)S(1)}, bf16[512]{0:T(512)(128)(2,1)S(1)}, bf16[512]{0:T(512)(128)(2,1)S(1)}) all-reduce(bf16[512]{0:T(512)(128)(2,1)S(1)} %dynamic-slice.3, bf16[512]{0:T(512)(128)(2,1)S(1)} %dynamic-slice.5, ...), channel_id=1, replica_groups=mesh['dp'=2,'ctx'=4,'tp'=4] {'ctx'}, use_global_device_ids=true, to_apply=%region_43.44 | all-reduce | flops 2048 | bytes 8192 | tf_op jit(solution)/shard_map/psum | solution.py:325
  859.0 90.2 %all-reduce.9.cloned.1.call-done = (bf16[512,256]{0,1:T(8,128)(2,1)}, bf16[512,256]{0,1:T(8,128)(2,1)}, bf16[512,256]{0,1:T(8,128)(2,1)}, bf16[256,512]{1,0:T(8,...) async-done(((bf16[512,256]{0,1:T(8,128)(2,1)}, bf16[512,256]{0,1:T(8,128)(2,1)}, bf16[512,256]{0,1:T(8,128)(2,1)}, bf16[256,512]{1,0:T(8,128)(2,1)}, ...) | async-done | bytes 3145744 | tf_op jit(solution)/shard_map/psum | solution.py:319
  (208 shorter events, 88.6 us)
Async XLA Ops:
  8.0 13.9 %copy-start.29 = (s32[1,1024]{1,0:T(1,128)S(1)}, s32[1,1024]{1,0:T(1,128)}, u32[]{:S(2)}) copy-start(s32[1,1024]{1,0:T(1,128)} %param.20) | copy-start | bytes 12292
  8.0 13.9 %copy-start.22 = (bf16[512,256]{1,0:T(8,128)(2,1)S(1)}, bf16[512,256]{1,0:T(8,128)(2,1)}, u32[]{:S(2)}) copy-start(bf16[512,256]{1,0:T(8,128)(2,1)} %param.22) | copy-start | bytes 786436
  8.0 61.8 %all-gather.31.cloned.1.call-start = ((), (), s32[]{:S(2)}) async-start(), calls=%async_computation.32 | async-start | bytes 2621440 | tf_op jit(solution)/shard_map/all_gather | solution.py:136
  18.4 11.9 %copy-start.5 = (bf16[1024,256]{1,0:T(8,128)(2,1)}, bf16[1024,256]{1,0:T(8,128)(2,1)S(1)}, u32[]{:S(2)}) copy-start(bf16[1024,256]{1,0:T(8,128)(2,1)S(1)} %all_gather.63) | copy-start | bytes 1572868
  18.4 11.9 %copy-start.23 = (bf16[512,256]{1,0:T(8,128)(2,1)S(1)}, bf16[512,256]{1,0:T(8,128)(2,1)}, u32[]{:S(2)}) copy-start(bf16[512,256]{1,0:T(8,128)(2,1)} %param.21) | copy-start | bytes 786436
  21.9 94.1 %all-gather.15.cloned.1.call-start = ((), (), s32[]{:S(2)}) async-start(), calls=%async_computation.12 | async-start | bytes 2621440 | tf_op jit(solution)/shard_map/all_gather | solution.py:135
  30.1 13.7 %copy-start.7 = (bf16[1024,256]{1,0:T(8,128)(2,1)}, bf16[1024,256]{1,0:T(8,128)(2,1)S(1)}, u32[]{:S(2)}) copy-start(bf16[1024,256]{1,0:T(8,128)(2,1)S(1)} %all_gather.61) | copy-start | bytes 1572868
  37.6 6.2 copy-start.9
  43.8 19.0 %copy-start.24 = (bf16[256,512]{1,0:T(8,128)(2,1)S(1)}, bf16[256,512]{1,0:T(8,128)(2,1)}, u32[]{:S(2)}) copy-start(bf16[256,512]{1,0:T(8,128)(2,1)} %param.24) | copy-start | bytes 786436
  45.0 185.9 %reduce-scatter.13.cloned.1.call-start = ((), (), s32[]{:S(2)}) async-start(), calls=%async_computation.13 | async-start | bytes 2621440 | tf_op jit(solution)/shard_map/reduce_scatter | solution.py:99
  69.8 128.1 %copy-start.15 = (bf16[256,1024]{1,0:T(8,128)(2,1)}, bf16[256,1024]{1,0:T(8,128)(2,1)S(1)}, u32[]{:S(2)}) copy-start(bf16[256,1024]{1,0:T(8,128)(2,1)S(1)} %all_gather.65) | copy-start | bytes 1572868
  197.0 8.8 copy-start.31
  200.8 36.0 %all-gather.19.cloned.1.call-start = ((), (), s32[]{:S(2)}) async-start(), calls=%async_computation.15 | async-start | bytes 3145728 | tf_op jit(solution)/shard_map/all_gather | solution.py:79
  201.4 57.7 %all-gather.17.cloned.1.call-start = ((), (), s32[]{:S(2)}) async-start(), calls=%async_computation.14 | async-start | bytes 2621440 | tf_op jit(solution)/shard_map/all_gather | solution.py:104
  236.1 57.3 %all-gather.21.cloned.1.call-start = ((), (), s32[]{:S(2)}) async-start(), calls=%async_computation.16 | async-start | bytes 3145728 | tf_op jit(solution)/shard_map/all_gather | solution.py:80
  236.7 94.0 %reduce-scatter.15.cloned.1.call-start = ((), (), s32[]{:S(2)}) async-start(), calls=%async_computation.17 | async-start | bytes 2621440 | tf_op jit(solution)/shard_map/reduce_scatter | solution.py:99
  293.5 6.0 copy-start.32
  293.5 10.4 %copy-start.33 = (bf16[512]{0:T(512)(128)(2,1)S(1)}, bf16[512]{0:T(512)(128)(2,1)}, u32[]{:S(2)}) copy-start(bf16[512]{0:T(512)(128)(2,1)} %param.30) | copy-start | bytes 3076
  293.5 37.3 %copy-start = (bf16[256,1024]{1,0:T(8,128)(2,1)S(1)}, bf16[256,1024]{1,0:T(8,128)(2,1)}, u32[]{:S(2)}) copy-start(bf16[256,1024]{1,0:T(8,128)(2,1)} %reduce-scatter.13.cloned.1.call-done) | copy-start | bytes 1572868
  299.4 60.6 %all-gather.25.cloned.1.call-start = ((), (), s32[]{:S(2)}) async-start(), calls=%async_computation.19 | async-start | bytes 2621440 | tf_op jit(solution)/shard_map/all_gather | solution.py:104
  337.3 65.5 %reduce-scatter.17.cloned.1.call-start = ((), (), s32[]{:S(2)}) async-start(), calls=%async_computation.20 | async-start | bytes 2621440 | tf_op jit(solution)/shard_map/reduce_scatter | solution.py:99
  360.0 7.7 copy-start.35
  371.5 59.3 %all-gather.27.cloned.1.call-start = ((), (), s32[]{:S(2)}) async-start(), calls=%async_computation.21 | async-start | bytes 2621440 | tf_op jit(solution)/shard_map/all_gather | solution.py:104
  408.0 199.8 %reduce-scatter.21.cloned.1.call-start = ((), (), s32[]{:S(2)}) async-start(), calls=%async_computation.23 | async-start | bytes 2621440 | tf_op jit(solution)/shard_map/reduce_scatter | solution.py:237
  434.3 27.9 %copy-start.20 = (bf16[1,1024,4,64]{1,3,2,0:T(8,128)(2,1)}, bf16[1,1024,4,64]{1,3,2,0:T(8,128)(2,1)S(1)}, u32[]{:S(2)}) copy-start(bf16[1,1024,4,64]{1,3,2,0:T(8,128)(2,1)S(1)} %get-tuple-element.60) | copy-start | bytes 1572868 | tf_op jit(solution)/shard_map/cond
  490.3 41.9 %copy-start.4 = (bf16[1,4096,4,64]{1,3,2,0:T(8,128)(2,1)S(1)}, bf16[1,4096,4,64]{1,3,2,0:T(8,128)(2,1)}, u32[]{:S(2)}) copy-start(bf16[1,4096,4,64]{1,3,2,0:T(8,128)(2,1)} %copy-done.3) | copy-start | bytes 6291460 | tf_op jit(solution)/shard_map/cond
  564.0 89.5 %reduce-scatter.19.cloned.1.call-start = ((), (), s32[]{:S(2)}) async-start(), calls=%async_computation.22 | async-start | bytes 2621440 | tf_op jit(solution)/shard_map/reduce_scatter | solution.py:234
  564.8 122.7 %reduce-scatter.33.cloned.1.call-start = ((), (), s32[]{:S(2)}) async-start(), calls=%async_computation.30 | async-start | bytes 3145728 | tf_op jit(solution)/shard_map/reduce_scatter | solution.py:299
  570.9 6.1 copy-start.14
  570.9 150.8 %reduce-scatter.35.cloned.1.call-start = ((), (), s32[]{:S(2)}) async-start(), calls=%async_computation.31 | async-start | bytes 3145728 | tf_op jit(solution)/shard_map/reduce_scatter | solution.py:302
  577.0 30.9 %copy-start.11 = (bf16[1,1024,1024]{2,1,0:T(8,128)(2,1)S(1)}, bf16[1,1024,1024]{2,1,0:T(8,128)(2,1)}, u32[]{:S(2)}) copy-start(bf16[1,1024,1024]{2,1,0:T(8,128)(2,1)} %param.18) | copy-start | bytes 6291460
  577.0 77.7 %copy-start.17 = (f32[1024,32]{0,1:T(8,128)S(1)}, f32[1024,32]{0,1:T(8,128)}, u32[]{:S(2)}) copy-start(f32[1024,32]{0,1:T(8,128)} %copy-done.16) | copy-start | bytes 393220
  577.0 77.7 %copy-start.21 = (f32[1024,32]{0,1:T(8,128)S(1)}, f32[1024,32]{0,1:T(8,128)}, u32[]{:S(2)}) copy-start(f32[1024,32]{0,1:T(8,128)} %get-tuple-element.169) | copy-start | bytes 393220
  577.0 161.5 %reduce-scatter.31.cloned.1.call-start = ((), (), s32[]{:S(2)}) async-start(), calls=%async_computation.29 | async-start | bytes 786432 | tf_op jit(solution)/shard_map/reduce_scatter | solution.py:296
  580.3 175.6 %reduce-scatter.29.cloned.1.call-start = ((), (), s32[]{:S(2)}) async-start(), calls=%async_computation.28 | async-start | bytes 786432 | tf_op jit(solution)/shard_map/reduce_scatter | solution.py:293
  610.4 162.9 %reduce-scatter.27.cloned.1.call-start = ((), (), s32[]{:S(2)}) async-start(), calls=%async_computation.27 | async-start | bytes 786432 | tf_op jit(solution)/shard_map/reduce_scatter | solution.py:290
  656.2 6.5 copy-start.10
  659.3 131.5 %reduce-scatter.25.cloned.1.call-start = ((), (), s32[]{:S(2)}) async-start(), calls=%async_computation.26 | async-start | bytes 786432 | tf_op jit(solution)/shard_map/reduce_scatter | solution.py:287
  662.6 162.3 %reduce-scatter.23.cloned.1.call-start = ((), (), s32[]{:S(2)}) async-start(), calls=%async_computation.24 | async-start | bytes 2621440 | tf_op jit(solution)/shard_map/reduce_scatter | solution.py:99
  666.4 158.6 %copy-start.12 = (f32[256,1024]{1,0:T(8,128)S(1)}, f32[256,1024]{1,0:T(8,128)}, u32[]{:S(2)}) copy-start(f32[256,1024]{1,0:T(8,128)} %get-tuple-element.147) | copy-start | bytes 3145732
  666.4 161.8 %copy-start.36 = (u32[32]{0:T(128)S(1)}, u32[32]{0:T(128)}, u32[]{:S(2)}) copy-start(u32[32]{0:T(128)} %constant.140) | copy-start | bytes 388
  666.4 163.0 %copy-start.26 = (bf16[1024]{0:T(1024)(128)(2,1)S(1)}, bf16[1024]{0:T(1024)(128)(2,1)}, u32[]{:S(2)}) copy-start(bf16[1024]{0:T(1024)(128)(2,1)} %get-tuple-element.117) | copy-start | bytes 6148
  666.4 163.1 %all-gather.23.cloned.1.call-start = ((), (), s32[]{:S(2)}) async-start(), calls=%async_computation.18 | async-start | bytes 2621440 | tf_op jit(solution)/shard_map/all_gather | solution.py:271
  667.1 282.0 %all-reduce.9.cloned.1.call-start = ((), (), s32[]{:S(2)}) async-start(), calls=%async_computation.33 | async-start | bytes 6291456 | tf_op jit(solution)/shard_map/psum | solution.py:319
  790.8 170.3 %all-gather.29.cloned.1.call-start = ((), (), s32[]{:S(2)}) async-start(), calls=%async_computation.25 | async-start | bytes 2621440 | tf_op jit(solution)/shard_map/all_gather | solution.py:272
  827.0 6.9 copy-start.28
  827.0 6.9 copy-start.27
  949.1 10.3 %copy-start.18 = (bf16[1024,512]{1,0:T(8,128)(2,1)S(1)}, bf16[1024,512]{1,0:T(8,128)(2,1)}, u32[]{:S(2)}) copy-start(bf16[1024,512]{1,0:T(8,128)(2,1)} %get-tuple-element.139) | copy-start | bytes 3145732
  (12 other events, 36.9 us)
Sparse Core Ops, SparseCore 0:
  22.0 47.3 all-gather.30
  71.5 44.4 all-gather.14
  200.9 29.9 reduce-scatter.12
  337.4 22.5 all-gather.24
  408.1 22.5 all-gather.26
  564.1 43.6 reduce-scatter.20
  610.7 42.8 reduce-scatter.18
  656.4 31.0 reduce-scatter.32
  689.8 31.8 reduce-scatter.34
  723.8 14.6 reduce-scatter.30
  741.3 14.6 reduce-scatter.28
  758.6 14.6 reduce-scatter.26
  776.1 14.6 reduce-scatter.24
  793.8 31.1 reduce-scatter.22
  827.7 121.4 all-reduce.8
Sparse Core Ops, SparseCore 1:
  202.8 31.7 all-gather.18
  236.6 22.4 all-gather.16
  260.5 32.9 all-gather.20
  299.5 31.2 reduce-scatter.14
  371.5 31.2 reduce-scatter.16
  669.3 21.6 all-gather.22
  827.1 22.5 all-gather.28
where the time goes:
time: 978 us; the launch traced here: 973 us
  waiting for transfers between devices  529 us (54%)
  matrix products  246 us (25%)
  blocking collectives  86.4 us (9%)
  other arithmetic  78 us (8%)
  between operations  19.7 us (2%)
  local copies, waits for them, and re-layouts  12 us (1%)
    reduce_scatter x4, waiting for transfers between devices, reduce_heads(): lax.psum_scatter(partial_sum.astype(jnp.bfloat16), 'tp', scatter_dimensio...  109 us
    psum x1, waiting for transfers between devices, body(): lax.psum(shares[0].astype(jnp.bfloat16), 'ctx').astype(jnp.float32)  90.2 us
    all_gather x3, waiting for transfers between devices, spread_rows(): return lax.all_gather(rows_low, 'tp', axis=0, tiled=True)  67.4 us
    dot_general x2, matrix products, masked_scores(): jnp.einsum('sqhd,skhd->shqk', queries, key_piece, preferred_element_type=...  49 us
    all_gather x1, waiting for transfers between devices, body(): key_piece = lax.all_gather(keys, 'ctx', axis=1, tiled=True)  46.2 us
    reduce_scatter x1, waiting for transfers between devices, body(): lax.psum_scatter(key_grad_all.astype(jnp.bfloat16), 'ctx', scatter_dimens...  43.1 us
    dot_general x1, matrix products, backward_update(): jnp.einsum('sqhd,skhd->shqk', heads_grad, backward_value_piece, preferred...  41.9 us
    reduce_scatter x1, waiting for transfers between devices, body(): lax.psum_scatter(down_grad.astype(jnp.bfloat16), 'dp', scatter_dimension=...  34.2 us
  transfers between devices with their start and end apart: 22, of which 18 were waited for; matrix products, arithmetic and copies ran while one was open for 8% of the time, Pallas kernels for 0%

commit v1 on v0

v1 whole, which is shorter than its diff:
```python
import functools

import jax
import jax.numpy as jnp
from jax import lax
from jax.experimental import pallas as pl
from jax.experimental.pallas import tpu as pltpu
from jax.sharding import PartitionSpec as P

D = 1024
H = 16
HEAD = D // H
LANES = 128
DOCS = 17
NCH = 2

NEG_BIG = -1e30
SQRT_HALF = 0.7071067811865476
INV_SQRT_TAU = 0.3989422804014327
LOG2E = 1.4426950408889634
LN2 = 0.6931471805599453
F32 = jnp.float32
BF16 = jnp.bfloat16
NT = (((1,), (1,)), ((), ()))
VMEM_LIMIT = 60 * 1024 * 1024


def order(n):
    found, bit = [0], n >> 1
    while bit:
        found = found + [d | bit for d in found]
        bit >>= 1
    return found


def swap(value, axis, bit):
    n = lax.axis_size(axis)
    return lax.ppermute(value, axis, [(i, i ^ bit) for i in range(n)])


def gather(value, axis):
    parts, bit = [value], lax.axis_size(axis) >> 1
    while bit:
        parts = parts + [swap(p, axis, bit) for p in parts]
        bit >>= 1
    return parts


def part_of(value, dim, start, size):
    return lax.slice_in_dim(value, start, start + size, axis=dim)


def scatter(send, keep, axis, dim):
    n, bit = lax.axis_size(axis), 1
    while True:
        got = swap(send, axis, bit)
        bit <<= 1
        if bit >= n:
            return keep, got
        half = keep.shape[dim] // 2
        upper = part_of(keep, dim, half, half) + part_of(got, dim, half, half).astype(F32)
        keep = part_of(keep, dim, 0, half) + part_of(got, dim, 0, half).astype(F32)
        send = upper.astype(BF16)


def call(body, out_shape, *args, grid=None, in_specs=None, out_specs=None, scratch=(), flops=0, trans=0, name=None):
    size = sum(a.size * a.dtype.itemsize for a in args)
    outs = out_shape if isinstance(out_shape, (list, tuple)) else [out_shape]
    size += sum(o.size * o.dtype.itemsize for o in outs)
    extra = {}
    if grid is not None:
        extra["grid"] = grid
    if in_specs is not None:
        extra["in_specs"] = in_specs
    if out_specs is not None:
        extra["out_specs"] = out_specs
    return pl.pallas_call(
        body,
        out_shape=out_shape,
        scratch_shapes=list(scratch),
        compiler_params=pltpu.CompilerParams(vmem_limit_bytes=VMEM_LIMIT),
        cost_estimate=pl.CostEstimate(flops=int(flops), bytes_accessed=int(size), transcendentals=int(trans)),
        name=name,
        **extra,
    )(*args)


def shape(dims, dtype):
    return jax.ShapeDtypeStruct(dims, dtype)


SMEM = pl.BlockSpec(memory_space=pltpu.SMEM)
FULL = pl.BlockSpec(memory_space=pltpu.VMEM)


def whole_block(value):
    return pl.BlockSpec(value.shape, lambda i: (0,) * len(value.shape))


def arrange_body(ids, src, out, *, tp, dp, shares):
    rows, width = src.shape
    share, cols = rows // tp, width // dp
    piece = share // NCH
    for a in range(NCH):
        for j, d in enumerate(shares):
            for e, f in enumerate(order(dp)):
                row = pl.multiple_of((ids[2] ^ d) * share + a * piece, piece)
                col = pl.multiple_of((ids[0] ^ f) * cols, cols)
                at = (a * len(shares) + j) * piece
                out[at : at + piece, e * cols : (e + 1) * cols] = src[pl.ds(row, piece), pl.ds(col, cols)]


def arrange(ids, src, tp, dp, shares):
    rows = src.shape[0] // tp * len(shares)
    return call(
        functools.partial(arrange_body, tp=tp, dp=dp, shares=shares),
        shape((rows, src.shape[1]), src.dtype),
        ids,
        src,
        in_specs=[SMEM, FULL],
        name="arrange",
    )


def place_body(ids, *refs, tp, dp):
    *parts, out = refs
    rows, width = out.shape
    share, cols = rows // tp, width // dp
    piece = share // NCH
    for a in range(NCH):
        for j, d in enumerate(order(tp)):
            for e, f in enumerate(order(dp)):
                row = pl.multiple_of((ids[2] ^ d) * share + a * piece, piece)
                col = pl.multiple_of((ids[0] ^ f) * cols, cols)
                out[pl.ds(row, piece), pl.ds(col, cols)] = parts[a * tp + j][:, e * cols : (e + 1) * cols].astype(F32)


def place(ids, parts, tp, dp, rows):
    return call(
        functools.partial(place_body, tp=tp, dp=dp),
        shape((rows, parts[0].shape[1]), F32),
        ids,
        *parts,
        in_specs=[SMEM] + [FULL] * len(parts),
        name="place",
    )


def place_grad_body(ids, *refs, n, widths):
    parts, outs = refs[:n], refs[n:]
    rows = parts[0].shape[0]
    for part, d in zip(parts, order(n)):
        who = ids[1] ^ d
        at, bit, size = 0, 1, n * rows
        while bit < n:
            size //= 2
            at = at + ((who // bit) % 2) * size
            bit *= 2
        lane = 0
        for out, width in zip(outs, widths):
            out[pl.ds(pl.multiple_of(at, rows), rows), :] = part[:, lane : lane + width].astype(F32)
            lane += width


def sum_over_ctx(ids, value, widths):
    n, bit = lax.axis_size("ctx"), 1
    me = lax.axis_index("ctx")
    while bit < n:
        half = value.shape[0] // 2
        mine = (me // bit) % 2
        send = lax.dynamic_slice_in_dim(value, (1 - mine) * half, half, 0).astype(BF16)
        value = lax.dynamic_slice_in_dim(value, mine * half, half, 0) + swap(send, "ctx", bit).astype(F32)
        bit *= 2
    parts = gather(value.astype(BF16), "ctx")
    rows = parts[0].shape[0] * n
    return call(
        functools.partial(place_grad_body, n=n, widths=widths),
        [shape((rows, w), F32) for w in widths],
        ids,
        *parts,
        in_specs=[SMEM] + [FULL] * n,
        name="place_grad",
    )


def swap_halves(tile, lane):
    return jnp.where(lane % HEAD < HEAD // 2, pltpu.roll(tile, LANES - HEAD // 2, 1), pltpu.roll(tile, HEAD // 2, 1))


def turn(tile):
    return pltpu.roll(tile, HEAD, 1)


def pick(me, values, index):
    chosen = values[index]
    for i in range(1, len(values)):
        chosen = jnp.where(me == i, values[i ^ index], chosen)
    return chosen


def rows_dot(x, pieces):
    total, at = None, 0
    for w in pieces:
        size = w.shape[0]
        term = jnp.dot(x[:, at : at + size], w[...], preferred_element_type=F32)
        total = term if total is None else total + term
        at += size
    return total


def kv_body(ids, x, *refs, dp, n):
    wk, wv = refs[:dp], refs[dp : 2 * dp]
    cosine, sine = refs[2 * dp], refs[2 * dp + 1]
    outs = refs[2 * dp + 2 :]
    me = ids[1]
    step = 256
    lane = lax.broadcasted_iota(jnp.int32, (step, LANES), 1)
    for i in range(x.shape[0] // step):
        rows = slice(i * step, (i + 1) * step)
        tokens = x[rows, :]
        key, value = rows_dot(tokens, wk), rows_dot(tokens, wv)
        heads = []
        for t in range(n // 2):
            kt = key[:, t * LANES : (t + 1) * LANES]
            vt = value[:, t * LANES : (t + 1) * LANES]
            kt = kt * cosine[rows, :] + swap_halves(kt, lane) * sine[rows, :]
            heads.append(jnp.where(lane < HEAD, kt, turn(vt)))
            heads.append(jnp.where(lane < HEAD, turn(kt), vt))
        for e in range(n):
            outs[e][rows, :] = pick(me, heads, e).astype(BF16)


def q_body(ids, x, *refs, dp, n, half):
    wq = refs[:dp]
    cosine, sine = refs[dp], refs[dp + 1]
    outs = refs[dp + 2 :]
    me = ids[1]
    lane = lax.broadcasted_iota(jnp.int32, (half, LANES), 1)
    for a in range(NCH):
        sides = []
        for h in range(2):
            rows = slice((2 * a + h) * half, (2 * a + h + 1) * half)
            query = rows_dot(x[rows, :], wq)
            heads = []
            for t in range(n // 2):
                qt = query[:, t * LANES : (t + 1) * LANES]
                qt = qt * cosine[rows, :] + swap_halves(qt, lane) * sine[rows, :]
                qt = qt * (HEAD**-0.5 * LOG2E)
                other = turn(qt)
                heads.extend([qt, other] if h == 0 else [other, qt])
            sides.append(heads)
        packed = [jnp.where(lane < HEAD, lo, hi) for lo, hi in zip(*sides)]
        for e in range(n):
            outs[a * n + e][...] = pick(me, packed, e).astype(BF16)


def unpack_pairs(me, packed, n, h, lane):
    tiles = []
    for t in range(n // 2):
        lo, hi = pick(me, packed, 2 * t), pick(me, packed, 2 * t + 1)
        if h == 0:
            tiles.append(jnp.where(lane < HEAD, lo, turn(hi)))
        else:
            tiles.append(jnp.where(lane < HEAD, turn(lo), hi))
    return tiles


def out_proj_body(ids, *refs, dp, n):
    packed, wo = refs[:n], refs[n : n + dp]
    heads, send, keep = refs[n + dp :]
    half = packed[0].shape[0]
    lane = lax.broadcasted_iota(jnp.int32, (half, LANES), 1)
    pieces = [p[...].astype(F32) for p in packed]
    for h, target in ((1, send), (0, keep)):
        tiles = unpack_pairs(ids[1], pieces, n, h, lane)
        low = jnp.concatenate(tiles, axis=1).astype(BF16)
        heads[h * half : (h + 1) * half, :] = low
        at = 0
        for w in wo:
            cols = w.shape[1]
            target[:, at : at + cols] = jnp.dot(low, w[...], preferred_element_type=F32).astype(target.dtype)
            at += cols


def head_grad_body(ids, *refs, tp, dp, n):
    rows, wo = refs[:tp], refs[tp : tp + dp]
    whole, outs = refs[tp + dp], refs[tp + dp + 1 :]
    piece = rows[0].shape[0]
    for j in range(tp):
        whole[j * piece : (j + 1) * piece, :] = rows[j][...]
    half = tp * piece // 2
    lane = lax.broadcasted_iota(jnp.int32, (half, LANES), 1)
    sides = []
    for h in range(2):
        grad, at = None, 0
        for w in wo:
            cols = w.shape[1]
            term = lax.dot_general(
                whole[h * half : (h + 1) * half, at : at + cols], w[...], NT, preferred_element_type=F32
            )
            grad = term if grad is None else grad + term
            at += cols
        heads = []
        for t in range(n // 2):
            tile = grad[:, t * LANES : (t + 1) * LANES]
            heads.extend([tile, turn(tile)] if h == 0 else [turn(tile), tile])
        sides.append(heads)
    packed = [jnp.where(lane < HEAD, lo, hi) for lo, hi in zip(*sides)]
    for e in range(n):
        outs[e][...] = pick(ids[1], packed, e).astype(BF16)


BQ = 256
KC = 1024


def fill_keys(kv, marks, ka, va):
    size = kv[0].shape[0]
    lane = lax.broadcasted_iota(jnp.int32, (size, LANES), 1)
    ones = jnp.where(lane < 3, 1.0, 0.0).astype(BF16)
    for e, ref in enumerate(kv):
        rows = slice(e * size, (e + 1) * size)
        both = ref[...]
        ka[rows, :] = jnp.where(lane < HEAD, both, marks[rows, :])
        va[rows, :] = jnp.where(lane < HEAD, ones, both)


def query_marks(marks, row, lane):
    there = (lane >= HEAD) & (lane < HEAD + DOCS)
    bias = (marks[pl.ds(row, BQ), :].astype(F32) - 1.0) * -NEG_BIG
    return jnp.where(there, bias, 0.0)


def block_of(i, half, length, first):
    block, h = i // 2, i % 2
    blocks = half // BQ
    token = (block // blocks) * length + first + h * half + (block % blocks) * BQ
    return pl.multiple_of(block * BQ, BQ), h, pl.multiple_of(token, BQ)


def attend_body(*refs, n, first):
    queries, kv = refs[:n], refs[n : 2 * n]
    marks = refs[2 * n]
    outs, lse = refs[2 * n + 1 : 3 * n + 1], refs[3 * n + 1]
    qs, ka, va, os = refs[3 * n + 2 :]
    half, length = queries[0].shape[0], kv[0].shape[0]
    i = pl.program_id(0)

    @pl.when(i == 0)
    def _():
        fill_keys(kv, marks, ka, va)
        for e in range(n):
            qs[e * half : (e + 1) * half, :] = queries[e][...]

    at, h, token = block_of(i, half, length, first)
    lane = lax.broadcasted_iota(jnp.int32, (BQ, LANES), 1)
    q = qs[pl.ds(at, BQ), :].astype(F32)
    q = jnp.where(h == 1, turn(q), q)
    q = jnp.where(lane < HEAD, q, query_marks(marks, token, lane)).astype(BF16)
    scores, top = [], None
    for j in range(n * length // KC):
        s = lax.dot_general(q, ka[j * KC : (j + 1) * KC, :], NT, preferred_element_type=F32)
        scores.append(s)
        for t in range(KC // LANES):
            tile = s[:, t * LANES : (t + 1) * LANES]
            top = tile if top is None else jnp.maximum(top, tile)
    top = jnp.max(top, axis=1, keepdims=True)
    total = jnp.zeros((BQ, LANES), F32)
    for j, s in enumerate(scores):
        p = jnp.exp2(s - top).astype(BF16)
        total += jnp.dot(p, va[j * KC : (j + 1) * KC, :], preferred_element_type=F32)
    weight = total[:, :1]
    o = total / weight
    o = jnp.where(h == 0, turn(o), o)
    log = jnp.broadcast_to(top + jnp.log2(weight), (BQ, LANES))
    other = (lane < HEAD) & (h == 1)
    os[pl.ds(at, BQ), :] = jnp.where(other, os[pl.ds(at, BQ), :], o)
    lse[pl.ds(at, BQ), :] = jnp.where(other, lse[pl.ds(at, BQ), :], log)

    @pl.when(i == pl.num_programs(0) - 1)
    def _():
        for e in range(n):
            outs[e][...] = os[e * half : (e + 1) * half, :].astype(BF16)


def attend(queries, kv, marks, first):
    n, (half, _), length = len(kv), queries[0].shape, kv[0].shape[0]
    steps = n * 2 * half // BQ
    args = [*queries, *kv, marks]
    outs = [shape((half, LANES), BF16)] * n + [shape((n * half, LANES), F32)]
    out = call(
        functools.partial(attend_body, n=n, first=first),
        outs,
        *args,
        grid=(steps,),
        in_specs=[whole_block(a) for a in args],
        out_specs=[whole_block(o) for o in outs],
        scratch=[
            pltpu.VMEM((n * half, LANES), BF16),
            pltpu.VMEM((n * length, LANES), BF16),
            pltpu.VMEM((n * length, LANES), BF16),
            pltpu.VMEM((n * half, LANES), F32),
        ],
        flops=4 * steps * BQ * n * length * 256,
        trans=steps * BQ * n * length,
        name="attend",
    )
    return out[:n], out[n]


def split3(value):
    high = value.astype(BF16).astype(F32)
    rest = value - high
    middle = rest.astype(BF16).astype(F32)
    return high, middle, rest - middle


def attend_back_body(*refs, n, first, start, end):
    queries, grads, outs, kv = (refs[k * n : (k + 1) * n] for k in range(4))
    lse, marks = refs[4 * n], refs[4 * n + 1]
    at = 4 * n + 2
    before = None
    if not start:
        before, at = refs[at], at + 1
    dqs, at = refs[at : at + n], at + n
    if end:
        dkvs, at = refs[at : at + n], at + n
        qs, gs, os, ds_, ka, va, acc = refs[at:]
    else:
        acc, at = refs[at], at + 1
        qs, gs, os, ds_, ka, va = refs[at:]
    half, length = queries[0].shape[0], kv[0].shape[0]
    i = pl.program_id(0)

    @pl.when(i == 0)
    def _():
        fill_keys(kv, marks, ka, va)
        for e in range(n):
            rows = slice(e * half, (e + 1) * half)
            qs[rows, :] = queries[e][...]
            gs[rows, :] = grads[e][...]
            os[rows, :] = outs[e][...]
        acc[...] = jnp.zeros_like(acc) if start else before[...]

    row, h, token = block_of(i, half, length, first)
    lane = lax.broadcasted_iota(jnp.int32, (BQ, LANES), 1)
    here = pl.ds(row, BQ)
    q = qs[here, :].astype(F32)
    g = gs[here, :].astype(F32)
    o = os[here, :].astype(F32)
    log = lse[here, :]
    q = jnp.where(h == 1, turn(q), q)
    g = jnp.where(h == 0, turn(g), g)
    o = jnp.where(h == 0, turn(o), o)
    log = jnp.where(h == 1, turn(log), log)[:, :1]
    dot = jnp.sum(jnp.where(lane >= HEAD, g * o, 0.0), axis=1, keepdims=True)
    b0, b1, b2 = split3(-log)
    q_marks = query_marks(marks, token, lane)
    first_lane = HEAD + DOCS
    qa = jnp.where(lane == first_lane, b0, q_marks)
    qa = jnp.where(lane == first_lane + 1, b1, qa)
    qa = jnp.where(lane == first_lane + 2, b2, qa)
    qa = jnp.where(lane < HEAD, q, qa).astype(BF16)
    b0, b1, b2 = split3(-dot)
    ga = jnp.where(lane == 0, b0, jnp.where(lane == 1, b1, jnp.where(lane == 2, b2, 0.0)))
    ga = jnp.where(lane >= HEAD, g, ga).astype(BF16)
    q_t = q.T[:HEAD].astype(BF16)
    g_t = g.T[HEAD:].astype(BF16)
    total = jnp.zeros((BQ, LANES), F32)
    for j in range(n * length // KC):
        cols = slice(j * KC, (j + 1) * KC)
        s = lax.dot_general(qa, ka[cols, :], NT, preferred_element_type=F32)
        t = lax.dot_general(ga, va[cols, :], NT, preferred_element_type=F32)
        p = jnp.exp2(s)
        ds = (p * t).astype(BF16)
        p = p.astype(BF16)
        acc[HEAD:, cols] += jnp.dot(g_t, p, preferred_element_type=F32)
        acc[:HEAD, cols] += jnp.dot(q_t, ds, preferred_element_type=F32)
        total += jnp.dot(ds, ka[cols, :], preferred_element_type=F32)
    total = total * (HEAD**-0.5)
    total = jnp.where(h == 1, turn(total), total)
    other = (lane < HEAD) & (h == 1)
    ds_[here, :] = jnp.where(other, ds_[here, :], total)

    @pl.when(i == pl.num_programs(0) - 1)
    def _():
        for e in range(n):
            dqs[e][...] = ds_[e * half : (e + 1) * half, :].astype(BF16)
        if end:
            for e in range(n):
                cols = slice(e * length, (e + 1) * length)
                turned = acc[:, cols].T
                key_lane = lax.broadcasted_iota(jnp.int32, (length, LANES), 1)
                dkvs[e][...] = jnp.where(key_lane < HEAD, turned * LN2, turned).astype(BF16)


def attend_back(queries, grads, outs, kv, lse, marks, before, first, end):
    n, (half, _), length = len(kv), queries[0].shape, kv[0].shape[0]
    steps = n * 2 * half // BQ
    start = before is None
    args = [*queries, *grads, *outs, *kv, lse, marks] + ([] if start else [before])
    results = [shape((half, LANES), BF16)] * n
    results += [shape((length, LANES), BF16)] * n if end else [shape((LANES, n * length), F32)]
    out = call(
        functools.partial(attend_back_body, n=n, first=first, start=start, end=end),
        results,
        *args,
        grid=(steps,),
        in_specs=[whole_block(a) for a in args],
        out_specs=[whole_block(o) for o in results],
        scratch=[pltpu.VMEM((n * half, LANES), BF16)] * 3
        + [pltpu.VMEM((n * half, LANES), F32)]
        + [pltpu.VMEM((n * length, LANES), BF16)] * 2
        + ([pltpu.VMEM((LANES, n * length), F32)] if end else []),
        flops=10 * steps * BQ * n * length * 256,
        trans=steps * BQ * n * length,
        name="attend_back",
    )
    return out[:n], out[n:]


def input_grad_body(ids, *refs, dp, n, half):
    dqs, dkvs = refs[: NCH * n], refs[NCH * n : NCH * n + n]
    at = NCH * n + n
    ws = [refs[at + k * dp : at + (k + 1) * dp] for k in range(3)]
    at += 3 * dp
    cosine, sine = refs[at], refs[at + 1]
    whole = refs[at + 2]
    sends, keeps = refs[at + 3 : at + 3 + NCH], refs[at + 3 + NCH :]
    me = ids[1]
    lane = lax.broadcasted_iota(jnp.int32, (half, LANES), 1)
    for a in range(NCH):
        pieces = [dqs[a * n + e][...].astype(F32) for e in range(n)]
        for h, target in ((1, sends[a]), (0, keeps[a])):
            rows = slice((2 * a + h) * half, (2 * a + h + 1) * half)
            kv = [dkvs[e][rows, :].astype(F32) for e in range(n)]
            qt = unpack_pairs(me, pieces, n, h, lane)
            kt = unpack_pairs(me, kv, n, 0, lane)
            vt = unpack_pairs(me, kv, n, 1, lane)
            back = [x * cosine[rows, :] - swap_halves(x, lane) * sine[rows, :] for x in qt + kt]
            low = jnp.concatenate(back + vt, axis=1).astype(BF16)
            whole[rows, :] = low
            wide = low.shape[1] // 3
            col = 0
            for e in range(dp):
                total = None
                for k in range(3):
                    term = lax.dot_general(
                        low[:, k * wide : (k + 1) * wide], ws[k][e][...], NT, preferred_element_type=F32
                    )
                    total = term if total is None else total + term
                size = total.shape[1]
                target[:, col : col + size] = total.astype(target.dtype)
                col += size


FB = 256


def ffn_body(*refs, tp, dp):
    rows, w_in, w_out = refs[:tp], refs[tp : tp + dp], refs[tp + dp : tp + 2 * dp]
    whole, act, slope, send, keep, acc = refs[tp + 2 * dp :]
    piece = rows[0].shape[0]
    half = tp * piece // 2
    i = pl.program_id(0)

    @pl.when(i == 0)
    def _():
        for j in range(tp):
            whole[j * piece : (j + 1) * piece, :] = rows[j][...]
        acc[...] = jnp.zeros_like(acc)

    h = rows_dot(whole[...], w_in)
    phi = 0.5 * (1.0 + lax.erf(h * SQRT_HALF))
    low = (h * phi).astype(BF16)
    act[...] = low
    slope[...] = (phi + h * jnp.exp(-0.5 * h * h) * INV_SQRT_TAU).astype(BF16)
    at = 0
    for w in w_out:
        cols = w.shape[1]
        acc[:, at : at + cols] += jnp.dot(low, w[...], preferred_element_type=F32)
        at += cols

    @pl.when(i == pl.num_programs(0) - 1)
    def _():
        send[...] = acc[half:, :].astype(BF16)
        keep[...] = acc[:half, :]


def ffn_specs(rows, w_in, w_out):
    block = min(FB, w_in[0].shape[1])
    specs = [whole_block(r) for r in rows]
    specs += [pl.BlockSpec((w.shape[0], block), lambda i: (0, i)) for w in w_in]
    specs += [pl.BlockSpec((block, w.shape[1]), lambda i: (i, 0)) for w in w_out]
    return block, specs


def ffn(rows, w_in, w_out):
    tp, dp = len(rows), len(w_in)
    total, width, hidden = tp * rows[0].shape[0], rows[0].shape[1], w_in[0].shape[1]
    block, specs = ffn_specs(rows, w_in, w_out)
    outs = [
        shape((total, width), BF16),
        shape((total, hidden), BF16),
        shape((total, hidden), BF16),
        shape((total // 2, width), BF16),
        shape((total // 2, width), F32),
    ]
    wide = pl.BlockSpec((total, block), lambda i: (0, i))
    return call(
        functools.partial(ffn_body, tp=tp, dp=dp),
        outs,
        *rows,
        *w_in,
        *w_out,
        grid=(hidden // block,),
        in_specs=specs,
        out_specs=[whole_block(outs[0]), wide, wide, whole_block(outs[3]), whole_block(outs[4])],
        scratch=[pltpu.VMEM((total, width), F32)],
        flops=4 * total * width * hidden,
        trans=3 * total * hidden,
        name="ffn",
    )


def ffn_back_body(*refs, tp, dp):
    rows, w_in, w_out = refs[:tp], refs[tp : tp + dp], refs[tp + dp : tp + 2 * dp]
    slope, whole, pre, send, keep, acc = refs[tp + 2 * dp :]
    piece = rows[0].shape[0]
    half = tp * piece // 2
    i = pl.program_id(0)

    @pl.when(i == 0)
    def _():
        for j in range(tp):
            whole[j * piece : (j + 1) * piece, :] = rows[j][...]
        acc[...] = jnp.zeros_like(acc)

    grad, at = None, 0
    for w in w_out:
        cols = w.shape[1]
        term = lax.dot_general(whole[:, at : at + cols], w[...], NT, preferred_element_type=F32)
        grad = term if grad is None else grad + term
        at += cols
    low = (grad * slope[...].astype(F32)).astype(BF16)
    pre[...] = low
    at = 0
    for w in w_in:
        cols = w.shape[0]
        acc[:, at : at + cols] += lax.dot_general(low, w[...], NT, preferred_element_type=F32)
        at += cols

    @pl.when(i == pl.num_programs(0) - 1)
    def _():
        send[...] = acc[half:, :].astype(BF16)
        keep[...] = acc[:half, :]


def ffn_back(rows, w_in, w_out, slope):
    tp, dp = len(rows), len(w_in)
    total, width, hidden = tp * rows[0].shape[0], rows[0].shape[1], w_in[0].shape[1]
    block, specs = ffn_specs(rows, w_in, w_out)
    outs = [
        shape((total, width), BF16),
        shape((total, hidden), BF16),
        shape((total // 2, width), BF16),
        shape((total // 2, width), F32),
    ]
    wide = pl.BlockSpec((total, block), lambda i: (0, i))
    return call(
        functools.partial(ffn_back_body, tp=tp, dp=dp),
        outs,
        *rows,
        *w_in,
        *w_out,
        slope,
        grid=(hidden // block,),
        in_specs=specs + [wide],
        out_specs=[whole_block(outs[0]), wide, whole_block(outs[2]), whole_block(outs[3])],
        scratch=[pltpu.VMEM((total, width), F32)],
        flops=4 * total * width * hidden,
        name="ffn_back",
    )


def normed_of(value):
    centered = value - jnp.mean(value, axis=-1, keepdims=True)
    inverse = lax.rsqrt(jnp.mean(centered * centered, axis=-1, keepdims=True) + 1e-05)
    return centered * inverse, inverse


def norm_one_body(keep, got, tokens, gains, hidden, low, normed, inverse):
    z = keep[...] + got[...].astype(F32) + tokens[...].astype(F32)
    n, r = normed_of(z)
    out = n * gains[0:1, :] + gains[1:2, :]
    hidden[...] = out
    low[...] = out.astype(BF16)
    normed[...] = n
    inverse[...] = jnp.broadcast_to(r, inverse.shape)


def back_of(grad, normed, inverse, gain):
    scaled = grad * gain
    inner = (
        scaled
        - jnp.mean(scaled, axis=-1, keepdims=True)
        - normed * jnp.mean(scaled * normed, axis=-1, keepdims=True)
    )
    return inverse * inner


def norm_two_body(keep, got, hidden, gains, cotangent, out, second, low, terms):
    z = keep[...] + got[...].astype(F32) + hidden[...]
    n, r = normed_of(z)
    out[...] = (n * gains[2:3, :] + gains[3:4, :]).astype(BF16)
    grad = cotangent[...].astype(F32)
    result = back_of(grad, n, r, gains[2:3, :])
    second[...] = result
    low[...] = result.astype(BF16)
    terms[0:1, :] = jnp.sum(grad * n, axis=0, keepdims=True)
    terms[1:2, :] = jnp.sum(grad, axis=0, keepdims=True)


def norm_one_back_body(keep, got, second, normed, inverse, gains, first, low, terms):
    grad = keep[...] + got[...].astype(F32) + second[...]
    n = normed[...]
    result = back_of(grad, n, inverse[:, :1], gains[0:1, :])
    first[...] = result
    low[...] = result.astype(BF16)
    terms[0:1, :] = jnp.sum(grad * n, axis=0, keepdims=True)
    terms[1:2, :] = jnp.sum(grad, axis=0, keepdims=True)


def rotate_heads(values, angles, sign):
    half = HEAD // 2
    cosine = jnp.cos(angles)[:, None, :half]
    sine = sign * jnp.sin(angles)[:, None, :half]
    first, second = values[..., :half], values[..., half:]
    return jnp.concatenate([first * cosine - second * sine, second * cosine + first * sine], axis=-1)


def gathered_attention(tokens, weights, angles, docs):
    rows, width = tokens.shape[0], weights[0].shape[1]
    heads = width // HEAD
    scale = HEAD**-0.5

    def project(w):
        return jnp.dot(tokens, w, preferred_element_type=F32).reshape(rows, heads, HEAD)

    q = rotate_heads(project(weights[0]), angles, 1.0).astype(BF16)
    k = rotate_heads(project(weights[1]), angles, 1.0).astype(BF16)
    v = project(weights[2]).astype(BF16)
    keys = jnp.concatenate(gather(k, "ctx"))
    values = jnp.concatenate(gather(v, "ctx"))
    all_docs = jnp.concatenate(gather(docs, "ctx"))

    def masked():
        s = jnp.einsum("qhd,khd->hqk", q, keys, preferred_element_type=F32) * scale
        return jnp.where(docs[None, :, None] == all_docs[None, None, :], s, NEG_BIG)

    s = masked()
    top = jnp.max(s, axis=-1, keepdims=True)
    p = jnp.exp(s - top)
    total = jnp.sum(p, axis=-1)
    out = jnp.einsum("hqk,khd->qhd", p.astype(BF16), values, preferred_element_type=F32)
    out = out / total.T[..., None]
    log = top[..., 0] + jnp.log(total)

    def backward(grad):
        grad = grad.astype(BF16).reshape(rows, heads, HEAD)
        dot = jnp.sum(grad.astype(F32) * out, axis=-1).T
        p = jnp.exp(masked() - log[..., None])
        dv = jnp.einsum("hqk,qhd->khd", p.astype(BF16), grad, preferred_element_type=F32)
        dp = jnp.einsum("qhd,khd->hqk", grad, values, preferred_element_type=F32)
        ds = (p * (dp - dot[..., None])).astype(BF16)
        dq = jnp.einsum("hqk,khd->qhd", ds, keys, preferred_element_type=F32) * scale
        dk = jnp.einsum("hqk,qhd->khd", ds, q, preferred_element_type=F32) * scale

        def owned(value):
            half = value.shape[0] // 2
            keep, got = scatter(value[half:].astype(BF16), value[:half], "ctx", 0)
            return keep + got.astype(F32)

        dq = rotate_heads(dq, angles, -1.0)
        dk = rotate_heads(owned(dk), angles, -1.0)
        return jnp.concatenate([x.astype(BF16).reshape(rows, width) for x in (dq, dk, owned(dv))], axis=1)

    return out.astype(BF16).reshape(rows, width), backward


def body(
    layer_input,
    segments,
    positions,
    w_q,
    w_k,
    w_v,
    w_o,
    w_in,
    w_out,
    ln1_gain,
    ln1_bias,
    ln2_gain,
    ln2_bias,
    cotangent,
):
    seqs, length, width = layer_input.shape
    assert seqs == 1
    tp, dp, ctx = lax.axis_size("tp"), lax.axis_size("dp"), lax.axis_size("ctx")
    local_width = w_q.shape[1]
    heads = local_width // HEAD
    ids = jnp.stack([lax.axis_index("dp"), lax.axis_index("ctx"), lax.axis_index("tp")]).astype(jnp.int32)
    share = length // tp
    piece = share // NCH
    chunk = piece * tp
    half = chunk // 2
    spread = heads == ctx and heads % 2 == 0 and half % BQ == 0

    wk, wv, wq = gather(w_k, "dp"), gather(w_v, "dp"), gather(w_q, "dp")
    gains = jnp.concatenate(gather(jnp.stack([ln1_gain, ln1_bias, ln2_gain, ln2_bias]), "dp"), axis=1).astype(F32)
    wo, wi, wd = gather(w_o, "dp"), gather(w_in, "dp"), gather(w_out, "dp")

    x = arrange(ids, layer_input.reshape(length, width), tp, dp, order(tp))
    out_grad = arrange(ids, cotangent.reshape(length, width), tp, dp, [0])

    def arrange_tokens(value):
        table = value.reshape(tp, NCH, piece)
        picked = [lax.dynamic_index_in_dim(table, ids[2] ^ d, 0, keepdims=False) for d in order(tp)]
        return jnp.stack(picked, axis=1).reshape(length)

    docs = arrange_tokens(segments.reshape(length))
    places = arrange_tokens(positions.reshape(length)).astype(F32)
    freq = 10000.0 ** (-(jnp.arange(LANES, dtype=jnp.int32) % (HEAD // 2)).astype(F32) * 2.0 / HEAD)
    angles = places[:, None] * freq[None, :]

    if spread:
        side = jnp.where(jnp.arange(LANES) % HEAD < HEAD // 2, -1.0, 1.0)
        cosine, sine = jnp.cos(angles), jnp.sin(angles) * side[None, :]
        all_docs = jnp.concatenate([docs] + [swap(docs, "ctx", e) for e in range(1, ctx)])
        lane = jnp.arange(LANES)[None, :]
        in_docs = (lane >= HEAD) & (lane < HEAD + DOCS)
        marked = jnp.where(in_docs, lane - HEAD != all_docs[:, None], (lane >= HEAD + DOCS) & (lane < HEAD + DOCS + 3))
        marks = marked.astype(BF16)

        def exchange(parts):
            return [parts[0]] + [swap(parts[e], "ctx", e) for e in range(1, ctx)]

        kv = call(
            functools.partial(kv_body, dp=dp, n=heads),
            [shape((length, LANES), BF16)] * ctx,
            ids,
            x,
            *wk,
            *wv,
            cosine,
            sine,
            in_specs=[SMEM] + [FULL] * (3 + 2 * dp),
            flops=4 * length * width * local_width,
            name="project_kv",
        )
        kv = exchange(kv)
        qs = call(
            functools.partial(q_body, dp=dp, n=heads, half=half),
            [shape((half, LANES), BF16)] * (ctx * NCH),
            ids,
            x,
            *wq,
            cosine,
            sine,
            in_specs=[SMEM] + [FULL] * (3 + dp),
            flops=2 * length * width * local_width,
            name="project_q",
        )
        queries = [exchange(qs[a * ctx : (a + 1) * ctx]) for a in range(NCH)]
    else:
        attended, attend_backward = gathered_attention(
            x, [jnp.concatenate(w) for w in (wq, wk, wv)], angles, docs
        )

    outs, logs, attended_low = [], [], []
    normed_one, inverse_one, hidden_low, activated, slopes = [], [], [], [], []
    second_grad, second_low, norm_two_terms, out_parts = [], [], [], []
    pre_grad, first_grad, first_low, norm_one_terms, head_grads = [], [], [], [], []
    chunk_flops = 2 * chunk * width * local_width
    for a in range(NCH):
        if spread:
            o, log = attend(queries[a], kv, marks, a * chunk)
            outs.append(o)
            logs.append(log)
            low, send, keep = call(
                functools.partial(out_proj_body, dp=dp, n=heads),
                [shape((chunk, local_width), BF16), shape((half, width), BF16), shape((half, width), F32)],
                ids,
                *exchange(o),
                *wo,
                in_specs=[SMEM] + [FULL] * (ctx + dp),
                flops=chunk_flops,
                name="project_out",
            )
        else:
            low = attended[a * chunk : (a + 1) * chunk]
            mixed = jnp.concatenate([jnp.dot(low, w, preferred_element_type=F32) for w in wo], axis=1)
            send, keep = mixed[half:].astype(BF16), mixed[:half]
        attended_low.append(low)
        keep, got = scatter(send, keep, "tp", 0)
        hidden, low, normed, inverse = call(
            norm_one_body,
            [
                shape((piece, width), F32),
                shape((piece, width), BF16),
                shape((piece, width), F32),
                shape((piece, LANES), F32),
            ],
            keep,
            got,
            x[a * chunk : a * chunk + piece],
            gains,
            name="norm_one",
        )
        normed_one.append(normed)
        inverse_one.append(inverse)
        whole, act, slope, send, keep = ffn(gather(low, "tp"), wi, wd)
        hidden_low.append(whole)
        activated.append(act)
        slopes.append(slope)
        keep, got = scatter(send, keep, "tp", 0)
        out, second, low, terms = call(
            norm_two_body,
            [
                shape((piece, width), BF16),
                shape((piece, width), F32),
                shape((piece, width), BF16),
                shape((2, width), F32),
            ],
            keep,
            got,
            hidden,
            gains,
            out_grad[a * piece : (a + 1) * piece],
            name="norm_two",
        )
        out_parts.extend(gather(out, "tp"))
        norm_two_terms.append(terms)
        whole, pre, send, keep = ffn_back(gather(low, "tp"), wi, wd, slope)
        second_low.append(whole)
        pre_grad.append(pre)
        keep, got = scatter(send, keep, "tp", 0)
        first, low, terms = call(
            norm_one_back_body,
            [shape((piece, width), F32), shape((piece, width), BF16), shape((2, width), F32)],
            keep,
            got,
            second,
            normed,
            inverse,
            gains,
            name="norm_one_back",
        )
        first_grad.append(first)
        norm_one_terms.append(terms)
        rows = gather(low, "tp")
        if spread:
            whole, *grads = call(
                functools.partial(head_grad_body, tp=tp, dp=dp, n=heads),
                [shape((chunk, width), BF16)] + [shape((half, LANES), BF16)] * ctx,
                ids,
                *rows,
                *wo,
                in_specs=[SMEM] + [FULL] * (tp + dp),
                flops=chunk_flops,
                name="head_grad",
            )
            first_low.append(whole)
            head_grads.append(exchange(grads))
        else:
            whole = jnp.concatenate(rows)
            first_low.append(whole)
            head_grads.append(
                lax.dot_general(whole, jnp.concatenate(wo, axis=1), NT, preferred_element_type=F32)
            )

    def weight_grad(left, right, dim, widths):
        halves = []
        mid = width // 2
        for start in (mid, 0):
            total = None
            for l, r in zip(left, right):
                if dim == 0:
                    l = l[:, start : start + mid]
                else:
                    r = r[:, start : start + mid]
                term = lax.dot_general(l, r, (((0,), (0,)), ((), ())), preferred_element_type=F32)
                total = term if total is None else total + term
            halves.append(total)
        keep, got = scatter(halves[0].astype(BF16), halves[1], "dp", dim)
        return sum_over_ctx(ids, keep + got.astype(F32), widths)

    (w_out_grad,) = weight_grad(activated, second_low, 1, [width // dp])
    (w_in_grad,) = weight_grad(hidden_low, pre_grad, 0, [w_in.shape[1]])
    (w_o_grad,) = weight_grad(attended_low, first_low, 1, [width // dp])

    if spread:
        query_grads, carried = [], None
        for a in range(NCH):
            end = a == NCH - 1
            grads, rest = attend_back(
                queries[a], head_grads[a], outs[a], kv, logs[a], marks, carried, a * chunk, end
            )
            query_grads.extend(exchange(grads))
            if end:
                kv_grads = exchange(rest)
            else:
                (carried,) = rest
        whole, *parts = call(
            functools.partial(input_grad_body, dp=dp, n=heads, half=half),
            [shape((length, 3 * local_width), BF16)]
            + [shape((half, width), BF16)] * NCH
            + [shape((half, width), F32)] * NCH,
            ids,
            *query_grads,
            *kv_grads,
            *wq,
            *wk,
            *wv,
            cosine,
            sine,
            in_specs=[SMEM] + [FULL] * (NCH * ctx + ctx + 3 * dp + 2),
            flops=6 * length * width * local_width,
            name="input_grad",
        )
        sends, keeps = parts[:NCH], parts[NCH:]
    else:
        whole = attend_backward(jnp.concatenate(head_grads))
        weights = jnp.concatenate([jnp.concatenate(w) for w in (wq, wk, wv)], axis=1)
        total = lax.dot_general(whole, weights, NT, preferred_element_type=F32)
        sends = [total[a * chunk + half : (a + 1) * chunk].astype(BF16) for a in range(NCH)]
        keeps = [total[a * chunk : a * chunk + half] for a in range(NCH)]

    grad_parts = []
    for a in range(NCH):
        keep, got = scatter(sends[a], keeps[a], "tp", 0)
        grad_parts.extend(gather((first_grad[a] + keep + got.astype(F32)).astype(BF16), "tp"))
    w_q_grad, w_k_grad, w_v_grad = weight_grad([x], [whole], 0, [local_width] * 3)

    terms = jnp.concatenate([sum(norm_one_terms), sum(norm_two_terms)])
    for axis, n in (("tp", tp), ("ctx", ctx)):
        bit = 1
        while bit < n:
            terms = terms + swap(terms, axis, bit)
            bit *= 2
    bit = 1
    while bit < dp:
        mid = terms.shape[1] // 2
        terms = terms[:, :mid] + swap(terms[:, mid:], "dp", bit)
        bit *= 2

    output = place(ids, out_parts, tp, dp, length)
    input_grad = place(ids, grad_parts, tp, dp, length)
    return (
        output[None],
        input_grad[None],
        w_q_grad,
        w_k_grad,
        w_v_grad,
        w_o_grad,
        w_in_grad,
        w_out_grad,
        terms[0],
        terms[1],
        terms[2],
        terms[3],
    )


def solution(mesh):
    return jax.shard_map(
        body,
        mesh=mesh,
        in_specs=(
            P("dp", "ctx", None),
            P("dp", "ctx"),
            P("dp", "ctx"),
            P("dp", "tp"),
            P("dp", "tp"),
            P("dp", "tp"),
            P("tp", "dp"),
            P("dp", "tp"),
            P("tp", "dp"),
            P("dp"),
            P("dp"),
            P("dp"),
            P("dp"),
            P("dp", "ctx", None),
        ),
        out_specs=(
            P("dp", "ctx", None),
            P("dp", "ctx", None),
            P("dp", "tp"),
            P("dp", "tp"),
            P("dp", "tp"),
            P("tp", "dp"),
            P("dp", "tp"),
            P("tp", "dp"),
            P("dp"),
            P("dp"),
            P("dp"),
            P("dp"),
        ),
        check_vma=False,
    )
```

time: 978 us -> 556 us (0.57)
  waiting for transfers between devices: 529 us -> 175 us
  matrix products: 246 us -> 17.8 us
  Pallas kernels: 0 us -> 192 us
  starting transfers between devices: 1.55 us -> 108 us
  blocking collectives: 86.4 us -> 0 us
  other arithmetic: 78 us -> 24.3 us
  between operations: 19.7 us -> 2.74 us
  local copies, waits for them, and re-layouts: 12 us -> 26.7 us
    reduce_scatter x12 -> x0, waiting for transfers between devices: 303 us -> none  [the longest x4 109 us: reduce_heads(): lax.psum_scatter(partial_sum.astype(jnp.bfloat16), 'tp', scatter_dimensio...]
    dot_general x25 -> x14, matrix products: 246 us -> 17.8 us  [weight_grad(): lax.dot_general(l, r, (((0,), (0,)), ((), ())), preferred_element_type=F32)]
    pallas_call x0 -> x29, Pallas kernels: none -> 192 us  [call(): pl.pallas_call(body, out_shape=out_shape, scratch_shapes=list(scratch), c...]
    ppermute x0 -> x115, waiting for transfers between devices: none -> 175 us  [swap(): return lax.ppermute(value, axis, [(i, i ^ bit) for i in range(n)])]
    all_gather x9 -> x0, waiting for transfers between devices: 134 us -> none  [the longest x3 67.4 us: spread_rows(): return lax.all_gather(rows_low, 'tp', axis=0, tiled=True)]
    ppermute x0 -> x115, starting transfers between devices: none -> 108 us  [swap(): return lax.ppermute(value, axis, [(i, i ^ bit) for i in range(n)])]
    psum x1 -> x0, waiting for transfers between devices: 90.2 us -> none  [body(): lax.psum(shares[0].astype(jnp.bfloat16), 'ctx').astype(jnp.float32)]
    all_gather x10 -> x0, blocking collectives: 69.3 us -> none  [the longest x1 13.8 us: body(): doc_whole = lax.all_gather(segments, 'ctx', axis=1, tiled=True)]
  transfers between devices with their start and end apart: 22 -> 115, of which waited for: 18 -> 42; matrix products, arithmetic and copies ran while one was open for 8% -> 9% of each run, Pallas kernels for 0% -> 35%
where the time goes in v1:
time: 556 us; the launch traced here: 547 us
  Pallas kernels  192 us (35%)
  waiting for transfers between devices  175 us (31%)
  starting transfers between devices  108 us (19%)
  local copies, waits for them, and re-layouts  26.7 us (5%)
  other arithmetic  24.3 us (4%)
  matrix products  17.8 us (3%)
    pallas_call x29, Pallas kernels, call(): pl.pallas_call(body, out_shape=out_shape, scratch_shapes=list(scratch), c...  192 us
    ppermute x115, waiting for transfers between devices, swap(): return lax.ppermute(value, axis, [(i, i ^ bit) for i in range(n)])  175 us
    ppermute x115, starting transfers between devices, swap(): return lax.ppermute(value, axis, [(i, i ^ bit) for i in range(n)])  108 us
    unnamed x286, local copies, waits for them, and re-layouts  18.7 us
    dot_general x14, matrix products, weight_grad(): lax.dot_general(l, r, (((0,), (0,)), ((), ())), preferred_element_type=F32)  17.8 us
  transfers between devices with their start and end apart: 115, of which 42 were waited for; matrix products, arithmetic and copies ran while one was open for 9% of the time, Pallas kernels for 35%

profile of v1, /device:TPU:0, one launch (start us, length us, event | category | flops | bytes accessed | tf_op | source)
XLA Modules:
  0.0 546.7 jit_solution(3918003559910137896)
XLA Ops:
  2.2 4.1 collective-permute-start.10
  9.9 3.1 fusion.4
  15.2 3.1 arrange.2.x
  18.3 4.6 collective-permute-done.refs_1_.refs_13_
  23.6 3.9 project_q.1
  30.8 4.7 project_kv.1
  35.8 2.8 collective-permute-start.7
  45.2 17.9 %collective-permute-done.30.refs_2_ = bf16[256,128]{1,0:T(8,128)(2,1)S(1)} collective-permute-done((bf16[256,128]{1,0:T(8,128)(2,1)S(1)}, bf16[256,128]{1,0:T(8,128)(2,1)S(1)}, u32[]{:S(2)}, u32[]{:S(2)}) %collective-permute-start.30) | collective-permute-done | bytes 65568 | tf_op jit(solution)/shard_map/ppermute | solution.py:38
  65.5 16.4 %attend.3 = (bf16[256,128]{1,0:T(8,128)(2,1)}, bf16[256,128]{1,0:T(8,128)(2,1)}, bf16[256,128]{1,0:T(8,128)(2,1)}, bf16[256,128]{1,0:T(8,128)(2,1)}, f32[1024,128]{1,0:T(8,128)}) custom-call(bf16[256,128]{1,0:T(8,128)(2,1)} %get-tuple-element.130.refs_0_, bf16[256,128]{1,0:T(8,128)(2,1)} %copy-done.107, bf16[256,128]{1,0:T(8,128)(2,1)} %copy-done.108, ...), custom_call_target="tpu_custom_call" | custom-call | flops 8589934592 | bytes 3145728 | tf_op jit(solution)/shard_map/attend/pallas_call | solution.py:77
  81.9 2.9 collective-permute-start.33
  86.3 3.0 collective-permute-start.2
  91.8 2.7 project_out.3
  96.1 16.9 %attend.2 = (bf16[256,128]{1,0:T(8,128)(2,1)}, bf16[256,128]{1,0:T(8,128)(2,1)}, bf16[256,128]{1,0:T(8,128)(2,1)}, bf16[256,128]{1,0:T(8,128)(2,1)}, f32[1024,128]{1,0:T(8,128)}) custom-call(bf16[256,128]{1,0:T(8,128)(2,1)} %get-tuple-element.111.refs_0_, bf16[256,128]{1,0:T(8,128)(2,1)} %copy-done.110, bf16[256,128]{1,0:T(8,128)(2,1)} %copy-done.111, ...), custom_call_target="tpu_custom_call" | custom-call | flops 8589934592 | bytes 3145728 | tf_op jit(solution)/shard_map/attend/pallas_call | solution.py:77
  118.2 3.6 collective-permute-done.13.refs_2_
  122.5 2.7 project_out.2
  133.6 5.6 %collective-permute-done.36.got = bf16[128,1024]{1,0:T(8,128)(2,1)S(1)} collective-permute-done((bf16[128,1024]{1,0:T(8,128)(2,1)S(1)}, bf16[128,1024]{1,0:T(8,128)(2,1)S(1)}, u32[]{:S(2)}, u32[]{:S(2)}) %collective-permute-start.36) | collective-permute-done | bytes 262176 | tf_op jit(solution)/shard_map/ppermute | solution.py:38
  149.8 2.8 collective-permute-done.22.refs_5_
  154.7 19.5 %collective-permute-done.23.refs_7_ = bf16[1024,512]{1,0:T(8,128)(2,1)} collective-permute-done((bf16[1024,512]{1,0:T(8,128)(2,1)}, bf16[1024,512]{1,0:T(8,128)(2,1)}, u32[]{:S(2)}, u32[]{:S(2)}) %collective-permute-start.23) | collective-permute-done | bytes 1048608 | tf_op jit(solution)/shard_map/ppermute | solution.py:38
  175.7 9.1 %ffn.3 = (bf16[512,1024]{1,0:T(8,128)(2,1)}, bf16[512,1024]{1,0:T(8,128)(2,1)}, bf16[512,1024]{1,0:T(8,128)(2,1)}, bf16[256,1024]{1,0:T(8,128)(2,1)}, f32[256,1024]{1,0:T(8,128)}) custom-call(bf16[128,1024]{1,0:T(8,128)(2,1)} %get-tuple-element.140.refs_0_, bf16[128,1024]{1,0:T(8,128)(2,1)} %copy-done.102, bf16[128,1024]{1,0:T(8,128)(2,1)} %copy-done.104, ...), custom_call_target="tpu_custom_call" | custom-call | flops 2147483648 | bytes 9961472 | tf_op jit(solution)/shard_map/ffn/pallas_call | solution.py:77
  186.3 9.1 %ffn.2 = (bf16[512,1024]{1,0:T(8,128)(2,1)}, bf16[512,1024]{1,0:T(8,128)(2,1)}, bf16[512,1024]{1,0:T(8,128)(2,1)}, bf16[256,1024]{1,0:T(8,128)(2,1)}, f32[256,1024]{1,0:T(8,128)}) custom-call(bf16[128,1024]{1,0:T(8,128)(2,1)} %get-tuple-element.125.refs_0_, bf16[128,1024]{1,0:T(8,128)(2,1)} %copy-done.101, bf16[128,1024]{1,0:T(8,128)(2,1)} %copy-done.103, ...), custom_call_target="tpu_custom_call" | custom-call | flops 2147483648 | bytes 9961472 | tf_op jit(solution)/shard_map/ffn/pallas_call | solution.py:77
  204.2 4.3 collective-permute-done.41.got
  209.2 2.7 norm_two.3
  214.2 2.8 norm_two.2
  219.5 5.0 collective-permute-done.45.refs_1_
  226.1 8.9 %ffn_back.3 = (bf16[512,1024]{1,0:T(8,128)(2,1)}, bf16[512,1024]{1,0:T(8,128)(2,1)}, bf16[256,1024]{1,0:T(8,128)(2,1)}, f32[256,1024]{1,0:T(8,128)}) custom-call(bf16[128,1024]{1,0:T(8,128)(2,1)} %get-tuple-element.163.refs_0_, bf16[128,1024]{1,0:T(8,128)(2,1)} %copy-done.94, bf16[128,1024]{1,0:T(8,128)(2,1)} %copy-done.95, bf16[128,1024]{1,0:T(8,128)(2,1)} %copy-done.96, ...), custom_call_target="tpu_custom_call" | custom-call | flops 2147483648 | bytes 9961472 | tf_op jit(solution)/shard_map/ffn_back/pallas_call | solution.py:77
  235.6 9.1 %ffn_back.2 = (bf16[512,1024]{1,0:T(8,128)(2,1)}, bf16[512,1024]{1,0:T(8,128)(2,1)}, bf16[256,1024]{1,0:T(8,128)(2,1)}, f32[256,1024]{1,0:T(8,128)}) custom-call(bf16[128,1024]{1,0:T(8,128)(2,1)} %get-tuple-element.145.refs_0_, bf16[128,1024]{1,0:T(8,128)(2,1)} %copy-done.93, bf16[128,1024]{1,0:T(8,128)(2,1)} %collective-permute-done.46.refs_2_, ...), custom_call_target="tpu_custom_call" | custom-call | flops 2147483648 | bytes 9961472 | tf_op jit(solution)/shard_map/ffn_back/pallas_call | solution.py:77
  256.1 4.5 collective-permute-done.63.got
  261.3 2.7 norm_one_back.3
  266.1 2.7 norm_one_back.2
  288.3 11.1 %collective-permute-done.98 = bf16[512,1024]{1,0:T(8,128)(2,1)S(1)} collective-permute-done((bf16[512,1024]{1,0:T(8,128)(2,1)S(1)}, bf16[512,1024]{1,0:T(8,128)(2,1)S(1)}, u32[]{:S(2)}, u32[]{:S(2)}) %collective-permute-start.98) | collective-permute-done | bytes 1048608 | tf_op jit(solution)/shard_map/ppermute | solution.py:38
  304.9 2.7 head_grad.2
  317.5 9.7 %collective-permute-done.53.refs_5_ = bf16[256,128]{1,0:T(8,128)(2,1)S(1)} collective-permute-done((bf16[256,128]{1,0:T(8,128)(2,1)}, bf16[256,128]{1,0:T(8,128)(2,1)S(1)}, u32[]{:S(2)}, u32[]{:S(2)}) %collective-permute-start.53) | collective-permute-done | bytes 65568 | tf_op jit(solution)/shard_map/ppermute | solution.py:38
  332.1 28.8 %attend_back.2 = (bf16[256,128]{1,0:T(8,128)(2,1)}, bf16[256,128]{1,0:T(8,128)(2,1)}, bf16[256,128]{1,0:T(8,128)(2,1)}, bf16[256,128]{1,0:T(8,128)(2,1)}, f32[128,4096]{1,0:T(8,128)}) custom-call(bf16[256,128]{1,0:T(8,128)(2,1)} %get-tuple-element.111.refs_0_, bf16[256,128]{1,0:T(8,128)(2,1)} %copy-done.110, bf16[256,128]{1,0:T(8,128)(2,1)} %copy-done.111, ...), custom_call_target="tpu_custom_call" | custom-call | flops 21474836480 | bytes 5767168 | tf_op jit(solution)/shard_map/attend_back/pallas_call | solution.py:77
  362.8 29.8 %attend_back.3 = (bf16[256,128]{1,0:T(8,128)(2,1)}, bf16[256,128]{1,0:T(8,128)(2,1)}, bf16[256,128]{1,0:T(8,128)(2,1)}, bf16[256,128]{1,0:T(8,128)(2,1)}, bf16[1...) custom-call(bf16[256,128]{1,0:T(8,128)(2,1)} %get-tuple-element.130.refs, ...), custom_call_target="tpu_custom_call" | custom-call | flops 21474836480 | bytes 6815744 | tf_op jit(solution)/shard_map/attend_back/pallas_call | solution.py:77
  392.7 2.8 collective-permute-start.74
  406.8 8.3 %collective-permute-done.71.refs_6_ = bf16[256,128]{1,0:T(8,128)(2,1)S(1)} collective-permute-done((bf16[256,128]{1,0:T(8,128)(2,1)S(1)}, bf16[256,128]{1,0:T(8,128)(2,1)S(1)}, u32[]{:S(2)}, u32[]{:S(2)}) %collective-permute-start.71) | collective-permute-done | bytes 65568 | tf_op jit(solution)/shard_map/ppermute | solution.py:38
  429.2 2.9 collective-permute-start.100
  432.9 5.7 %input_grad.1 = (bf16[1024,768]{1,0:T(8,128)(2,1)}, bf16[256,1024]{1,0:T(8,128)(2,1)}, bf16[256,1024]{1,0:T(8,128)(2,1)}, f32[256,1024]{1,0:T(8,128)}, f32[256,1024]{1,0:T(8,128)}) custom-call(s32[3]{0:T(128)} %pad_add_fusion.2.ids, bf16[256,128]{1,0:T(8,128)(2,1)} %get-tuple-element.159.refs_0_, bf16[256,128]{1,0:T(8,128)(2,1)} %copy-done.123, ...), custom_call_target="tpu_custom_call" | custom-call | flops 1610612736 | bytes 8912908 | tf_op jit(solution)/shard_map/input_grad/pallas_call | solution.py:77
  441.7 2.9 collective-permute-start.94
  448.3 5.7 %collective-permute-done.94 = bf16[64,512]{1,0:T(8,128)(2,1)S(1)} collective-permute-done((bf16[64,512]{1,0:T(8,128)(2,1)S(1)}, bf16[64,512]{1,0:T(8,128)(2,1)S(1)}, u32[]{:S(2)}, u32[]{:S(2)}) %collective-permute-start.94) | collective-permute-done | bytes 65568 | tf_op jit(solution)/shard_map/ppermute | solution.py:38
  457.5 4.6 collective-permute-done.86
  465.1 4.5 collective-permute-done.82
  484.5 9.6 %collective-permute-done.107.refs_1_ = bf16[256,512]{1,0:T(8,128)(2,1)S(1)} collective-permute-done((bf16[256,512]{1,0:T(8,128)(2,1)S(1)}, bf16[256,512]{1,0:T(8,128)(2,1)S(1)}, u32[]{:S(2)}, u32[]{:S(2)}) %collective-permute-start.107) | collective-permute-done | bytes 262176 | tf_op jit(solution)/shard_map/ppermute | solution.py:38
  494.7 10.6 %collective-permute-done.101.refs_1_ = bf16[128,1024]{1,0:T(8,128)(2,1)S(1)} collective-permute-done((bf16[128,1024]{1,0:T(8,128)(2,1)S(1)}, bf16[128,1024]{1,0:T(8,128)(2,1)S(1)}, u32[]{:S(2)}, u32[]{:S(2)}) %collective-permute-start.101) | collective-permute-done | bytes 262176 | tf_op jit(solution)/shard_map/ppermute | solution.py:38
  506.0 3.8 place.2
  514.6 3.7 collective-permute-done.103.refs_3_
  520.8 8.5 %collective-permute-done.89.refs_1_ = bf16[128,768]{1,0:T(8,128)(2,1)S(1)} collective-permute-done((bf16[128,768]{1,0:T(8,128)(2,1)S(1)}, bf16[128,768]{1,0:T(8,128)(2,1)S(1)}, u32[]{:S(2)}, u32[]{:S(2)}) %collective-permute-start.89) | collective-permute-done | bytes 196640 | tf_op jit(solution)/shard_map/ppermute | solution.py:38
  538.6 3.8 place.3
  (567 shorter events, 203.2 us)
Async XLA Ops:
  7.9 21.5 %collective-permute-start.4 = (bf16[512,256]{1,0:T(8,128)(2,1)}, bf16[512,256]{1,0:T(8,128)(2,1)S(1)}, u32[]{:S(2)}, u32[]{:S(2)}) collective-permute-start(bf16[512,256]{1,0:T(8,128)(2,1)} %refs_14_.1), channel_id=1, source_target_pairs={{0,16},{16,0},{1,17},{17,1},{2,18},{18,2},{3,19},{19,3},{4,20},{20... | collective-permute-start | bytes 786440 | tf_op jit(solution)/shard_map/ppermute | solution.py:38
  13.0 16.4 %collective-permute-start.5 = (bf16[512,256]{1,0:T(8,128)(2,1)}, bf16[512,256]{1,0:T(8,128)(2,1)S(1)}, u32[]{:S(2)}, u32[]{:S(2)}) collective-permute-start(bf16[512,256]{1,0:T(8,128)(2,1)} %refs_16_.1), channel_id=1, source_target_pairs={{0,16},{16,0},{1,17},{17,1},{2,18},{18,2},{3,19},{19,3},{4,20},{20... | collective-permute-start | bytes 786440 | tf_op jit(solution)/shard_map/ppermute | solution.py:38
  35.5 29.1 %collective-permute-start.6 = (bf16[1024,128]{1,0:T(8,128)(2,1)}, bf16[1024,128]{1,0:T(8,128)(2,1)S(1)}, u32[]{:S(2)}, u32[]{:S(2)}) collective-permute-start(bf16[1024,128]{1,0:T(8,128)(2,1)} %get-tuple-element.116), channel_id=1, source_target_pairs={{0,4},{4,0},{8,12},{12,8},{1,5},{5,1},{9,13},{13,9},{2,6},{6,2},{1... | collective-permute-start | bytes 786440 | tf_op jit(solution)/shard_map/ppermute | solution.py:38
  35.8 28.8 %collective-permute-start.7 = (bf16[1024,128]{1,0:T(8,128)(2,1)}, bf16[1024,128]{1,0:T(8,128)(2,1)S(1)}, u32[]{:S(2)}, u32[]{:S(2)}) collective-permute-start(bf16[1024,128]{1,0:T(8,128)(2,1)} %get-tuple-element.117), channel_id=1, source_target_pairs={{0,8},{4,12},{8,0},{12,4},{1,9},{5,13},{9,1},{13,5},{2,10},{6,14},... | collective-permute-start | bytes 786440 | tf_op jit(solution)/shard_map/ppermute | solution.py:38
  38.6 26.1 %collective-permute-start.8 = (bf16[1024,128]{1,0:T(8,128)(2,1)}, bf16[1024,128]{1,0:T(8,128)(2,1)S(1)}, u32[]{:S(2)}, u32[]{:S(2)}) collective-permute-start(bf16[1024,128]{1,0:T(8,128)(2,1)} %get-tuple-element.118), channel_id=1, source_target_pairs={{0,12},{4,8},{8,4},{12,0},{1,13},{5,9},{9,5},{13,1},{2,14},{6,10},... | collective-permute-start | bytes 786440 | tf_op jit(solution)/shard_map/ppermute | solution.py:38
  39.9 23.1 %collective-permute-start.30 = (bf16[256,128]{1,0:T(8,128)(2,1)S(1)}, bf16[256,128]{1,0:T(8,128)(2,1)S(1)}, u32[]{:S(2)}, u32[]{:S(2)}) collective-permute-start(bf16[256,128]{1,0:T(8,128)(2,1)S(1)} %copy-done.135), channel_id=1, source_target_pairs={{0,8},{4,12},{8,0},{12,4},{1,9},{5,13},{9,1},{13,5},{2,10},{6,14},... | collective-permute-start | bytes 196616 | tf_op jit(solution)/shard_map/ppermute | solution.py:38
  40.7 23.9 %collective-permute-start.31 = (bf16[256,128]{1,0:T(8,128)(2,1)S(1)}, bf16[256,128]{1,0:T(8,128)(2,1)S(1)}, u32[]{:S(2)}, u32[]{:S(2)}) collective-permute-start(bf16[256,128]{1,0:T(8,128)(2,1)S(1)} %copy-done.134), channel_id=1, source_target_pairs={{0,12},{4,8},{8,4},{12,0},{1,13},{5,9},{9,5},{13,1},{2,14},{6,10},... | collective-permute-start | bytes 196616 | tf_op jit(solution)/shard_map/ppermute | solution.py:38
  63.1 23.2 %collective-permute-start.15 = (bf16[256,512]{1,0:T(8,128)(2,1)S(1)}, bf16[256,512]{1,0:T(8,128)(2,1)S(1)}, u32[]{:S(2)}, u32[]{:S(2)}) collective-permute-start(bf16[256,512]{1,0:T(8,128)(2,1)S(1)} %copy-done.37), channel_id=1, source_target_pairs={{0,16},{16,0},{1,17},{17,1},{2,18},{18,2},{3,19},{19,3},{4,20},{20... | collective-permute-start | bytes 786440 | tf_op jit(solution)/shard_map/ppermute | solution.py:38
  94.5 34.5 %collective-permute-start.35 = (bf16[256,1024]{1,0:T(8,128)(2,1)}, bf16[256,1024]{1,0:T(8,128)(2,1)S(1)}, u32[]{:S(2)}, u32[]{:S(2)}) collective-permute-start(bf16[256,1024]{1,0:T(8,128)(2,1)} %get-tuple-element.139), channel_id=1, source_target_pairs={{0,1},{1,0},{2,3},{3,2},{4,5},{5,4},{6,7},{7,6},{8,9},{9,8},{10,11... | collective-permute-start | bytes 1572872 | tf_op jit(solution)/shard_map/ppermute | solution.py:38
  126.2 26.3 %collective-permute-start.22 = (bf16[512,1024]{1,0:T(8,128)(2,1)}, bf16[512,1024]{1,0:T(8,128)(2,1)}, u32[]{:S(2)}, u32[]{:S(2)}) collective-permute-start(bf16[512,1024]{1,0:T(8,128)(2,1)} %refs_4_.14), channel_id=1, source_target_pairs={{0,16},{16,0},{1,17},{17,1},{2,18},{18,2},{3,19},{19,3},{4,20},{20... | collective-permute-start | bytes 3145736 | tf_op jit(solution)/shard_map/ppermute | solution.py:38
  127.3 47.0 %collective-permute-start.23 = (bf16[1024,512]{1,0:T(8,128)(2,1)}, bf16[1024,512]{1,0:T(8,128)(2,1)}, u32[]{:S(2)}, u32[]{:S(2)}) collective-permute-start(bf16[1024,512]{1,0:T(8,128)(2,1)} %refs_6_.7), channel_id=1, source_target_pairs={{0,16},{16,0},{1,17},{17,1},{2,18},{18,2},{3,19},{19,3},{4,20},{20... | collective-permute-start | bytes 3145736 | tf_op jit(solution)/shard_map/ppermute | solution.py:38
  148.9 25.4 %collective-permute-start.38 = (bf16[128,1024]{1,0:T(8,128)(2,1)}, bf16[128,1024]{1,0:T(8,128)(2,1)S(1)}, u32[]{:S(2)}, u32[]{:S(2)}) collective-permute-start(bf16[128,1024]{1,0:T(8,128)(2,1)} %get-tuple-element.140.refs_0_), channel_id=1, source_target_pairs={{0,1},{1,0},{2,3},{3,2},{4,5},{5,4},{6,7},{7,6},{8,9},{9,8},{10,11... | collective-permute-start | bytes 786440 | tf_op jit(solution)/shard_map/ppermute | solution.py:38
  149.8 24.5 %collective-permute-start.39 = (bf16[128,1024]{1,0:T(8,128)(2,1)S(1)}, bf16[128,1024]{1,0:T(8,128)(2,1)S(1)}, u32[]{:S(2)}, u32[]{:S(2)}) collective-permute-start(bf16[128,1024]{1,0:T(8,128)(2,1)S(1)} %collective-permute-done.37.refs_1_), channel_id=1, source_target_pairs={{0,1},{1,0},{2,3},{3,2},{4,5},{5,4},{6,7},{7,6},{8,9},{9,8},{10,11... | collective-permute-start | bytes 786440 | tf_op jit(solution)/shard_map/ppermute | solution.py:38
  152.6 32.4 %collective-permute-start.20 = (bf16[128,1024]{1,0:T(8,128)(2,1)}, bf16[128,1024]{1,0:T(8,128)(2,1)S(1)}, u32[]{:S(2)}, u32[]{:S(2)}) collective-permute-start(bf16[128,1024]{1,0:T(8,128)(2,1)} %get-tuple-element.125.refs_0_), channel_id=1, source_target_pairs={{0,1},{1,0},{2,3},{3,2},{4,5},{5,4},{6,7},{7,6},{8,9},{9,8},{10,11... | collective-permute-start | bytes 786440 | tf_op jit(solution)/shard_map/ppermute | solution.py:38
  154.7 30.2 %collective-permute-start.21 = (bf16[128,1024]{1,0:T(8,128)(2,1)S(1)}, bf16[128,1024]{1,0:T(8,128)(2,1)S(1)}, u32[]{:S(2)}, u32[]{:S(2)}) collective-permute-start(bf16[128,1024]{1,0:T(8,128)(2,1)S(1)} %collective-permute-done.19.refs_1_), channel_id=1, source_target_pairs={{0,1},{1,0},{2,3},{3,2},{4,5},{5,4},{6,7},{7,6},{8,9},{9,8},{10,11... | collective-permute-start | bytes 786440 | tf_op jit(solution)/shard_map/ppermute | solution.py:38
  219.0 16.5 %collective-permute-start.46 = (bf16[128,1024]{1,0:T(8,128)(2,1)}, bf16[128,1024]{1,0:T(8,128)(2,1)}, u32[]{:S(2)}, u32[]{:S(2)}) collective-permute-start(bf16[128,1024]{1,0:T(8,128)(2,1)} %get-tuple-element.145.refs_0_), channel_id=1, source_target_pairs={{0,1},{1,0},{2,3},{3,2},{4,5},{5,4},{6,7},{7,6},{8,9},{9,8},{10,11... | collective-permute-start | bytes 786440 | tf_op jit(solution)/shard_map/ppermute | solution.py:38
  248.6 36.8 %collective-permute-start.104 = (bf16[1024,512]{1,0:T(8,128)(2,1)}, bf16[1024,512]{1,0:T(8,128)(2,1)}, u32[]{:S(2)}, u32[]{:S(2)}) collective-permute-start(bf16[1024,512]{1,0:T(8,128)(2,1)} %add_convert_fusion), channel_id=1, source_target_pairs={{0,16},{16,0},{1,17},{17,1},{2,18},{18,2},{3,19},{19,3},{4,20},{20... | collective-permute-start | bytes 3145736 | tf_op jit(solution)/shard_map/ppermute | solution.py:38
  274.0 25.4 %collective-permute-start.98 = (bf16[512,1024]{1,0:T(8,128)(2,1)S(1)}, bf16[512,1024]{1,0:T(8,128)(2,1)S(1)}, u32[]{:S(2)}, u32[]{:S(2)}) collective-permute-start(bf16[512,1024]{1,0:T(8,128)(2,1)S(1)} %copy-done.36), channel_id=1, source_target_pairs={{0,16},{16,0},{1,17},{17,1},{2,18},{18,2},{3,19},{19,3},{4,20},{20... | collective-permute-start | bytes 3145736 | tf_op jit(solution)/shard_map/ppermute | solution.py:38
  281.6 18.9 %collective-permute-start.64 = (bf16[128,1024]{1,0:T(8,128)(2,1)S(1)}, bf16[128,1024]{1,0:T(8,128)(2,1)}, u32[]{:S(2)}, u32[]{:S(2)}) collective-permute-start(bf16[128,1024]{1,0:T(8,128)(2,1)S(1)} %copy-done.62), channel_id=1, source_target_pairs={{0,2},{1,3},{2,0},{3,1},{4,6},{5,7},{6,4},{7,5},{8,10},{9,11},{10,... | collective-permute-start | bytes 786440 | tf_op jit(solution)/shard_map/ppermute | solution.py:38
  283.2 25.7 %collective-permute-start.65 = (bf16[128,1024]{1,0:T(8,128)(2,1)S(1)}, bf16[128,1024]{1,0:T(8,128)(2,1)}, u32[]{:S(2)}, u32[]{:S(2)}) collective-permute-start(bf16[128,1024]{1,0:T(8,128)(2,1)S(1)} %copy-done.62), channel_id=1, source_target_pairs={{0,1},{1,0},{2,3},{3,2},{4,5},{5,4},{6,7},{7,6},{8,9},{9,8},{10,11... | collective-permute-start | bytes 786440 | tf_op jit(solution)/shard_map/ppermute | solution.py:38
  283.8 16.7 %collective-permute-start.50 = (bf16[128,1024]{1,0:T(8,128)(2,1)S(1)}, bf16[128,1024]{1,0:T(8,128)(2,1)S(1)}, u32[]{:S(2)}, u32[]{:S(2)}) collective-permute-start(bf16[128,1024]{1,0:T(8,128)(2,1)S(1)} %copy-done.63), channel_id=1, source_target_pairs={{0,2},{1,3},{2,0},{3,1},{4,6},{5,7},{6,4},{7,5},{8,10},{9,11},{10,... | collective-permute-start | bytes 786440 | tf_op jit(solution)/shard_map/ppermute | solution.py:38
  285.4 18.0 %collective-permute-start.51 = (bf16[128,1024]{1,0:T(8,128)(2,1)S(1)}, bf16[128,1024]{1,0:T(8,128)(2,1)S(1)}, u32[]{:S(2)}, u32[]{:S(2)}) collective-permute-start(bf16[128,1024]{1,0:T(8,128)(2,1)S(1)} %copy-done.63), channel_id=1, source_target_pairs={{0,1},{1,0},{2,3},{3,2},{4,5},{5,4},{6,7},{7,6},{8,9},{9,8},{10,11... | collective-permute-start | bytes 786440 | tf_op jit(solution)/shard_map/ppermute | solution.py:38
  299.3 96.1 %collective-permute-start.105 = (bf16[512,512]{1,0:T(8,128)(2,1)}, bf16[512,512]{1,0:T(8,128)(2,1)}, u32[]{:S(2)}, u32[]{:S(2)}) collective-permute-start(bf16[512,512]{1,0:T(8,128)(2,1)} %dynamic-slice_convert_fusion), channel_id=1, source_target_pairs={{0,4},{4,0},{8,12},{12,8},{1,5},{5,1},{9,13},{13,9},{2,6},{6,2},{1... | collective-permute-start | bytes 1572872 | tf_op jit(solution)/shard_map/ppermute | solution.py:38
  303.4 93.7 %collective-permute-start.99 = (bf16[256,1024]{1,0:T(8,128)(2,1)}, bf16[256,1024]{1,0:T(8,128)(2,1)}, u32[]{:S(2)}, u32[]{:S(2)}) collective-permute-start(bf16[256,1024]{1,0:T(8,128)(2,1)} %dynamic-slice_convert_fusion.1), channel_id=1, source_target_pairs={{0,4},{4,0},{8,12},{12,8},{1,5},{5,1},{9,13},{13,9},{2,6},{6,2},{1... | collective-permute-start | bytes 1572872 | tf_op jit(solution)/shard_map/ppermute | solution.py:38
  307.6 19.7 %collective-permute-start.53 = (bf16[256,128]{1,0:T(8,128)(2,1)}, bf16[256,128]{1,0:T(8,128)(2,1)S(1)}, u32[]{:S(2)}, u32[]{:S(2)}) collective-permute-start(bf16[256,128]{1,0:T(8,128)(2,1)} %get-tuple-element.155), channel_id=1, source_target_pairs={{0,4},{4,0},{8,12},{12,8},{1,5},{5,1},{9,13},{13,9},{2,6},{6,2},{1... | collective-permute-start | bytes 196616 | tf_op jit(solution)/shard_map/ppermute | solution.py:38
  308.9 19.2 %collective-permute-start.54 = (bf16[256,128]{1,0:T(8,128)(2,1)}, bf16[256,128]{1,0:T(8,128)(2,1)S(1)}, u32[]{:S(2)}, u32[]{:S(2)}) collective-permute-start(bf16[256,128]{1,0:T(8,128)(2,1)} %get-tuple-element.156), channel_id=1, source_target_pairs={{0,8},{4,12},{8,0},{12,4},{1,9},{5,13},{9,1},{13,5},{2,10},{6,14},... | collective-permute-start | bytes 196616 | tf_op jit(solution)/shard_map/ppermute | solution.py:38
  310.1 20.1 %collective-permute-start.55 = (bf16[256,128]{1,0:T(8,128)(2,1)}, bf16[256,128]{1,0:T(8,128)(2,1)}, u32[]{:S(2)}, u32[]{:S(2)}) collective-permute-start(bf16[256,128]{1,0:T(8,128)(2,1)} %get-tuple-element.157), channel_id=1, source_target_pairs={{0,12},{4,8},{8,4},{12,0},{1,13},{5,9},{9,5},{13,1},{2,14},{6,10},... | collective-permute-start | bytes 196616 | tf_op jit(solution)/shard_map/ppermute | solution.py:38
  327.3 33.6 %collective-permute-start.67 = (bf16[256,128]{1,0:T(8,128)(2,1)}, bf16[256,128]{1,0:T(8,128)(2,1)S(1)}, u32[]{:S(2)}, u32[]{:S(2)}) collective-permute-start(bf16[256,128]{1,0:T(8,128)(2,1)} %get-tuple-element.172), channel_id=1, source_target_pairs={{0,4},{4,0},{8,12},{12,8},{1,5},{5,1},{9,13},{13,9},{2,6},{6,2},{1... | collective-permute-start | bytes 196616 | tf_op jit(solution)/shard_map/ppermute | solution.py:38
  328.0 34.1 %collective-permute-start.68 = (bf16[256,128]{1,0:T(8,128)(2,1)S(1)}, bf16[256,128]{1,0:T(8,128)(2,1)S(1)}, u32[]{:S(2)}, u32[]{:S(2)}) collective-permute-start(bf16[256,128]{1,0:T(8,128)(2,1)S(1)} %copy-done.130), channel_id=1, source_target_pairs={{0,8},{4,12},{8,0},{12,4},{1,9},{5,13},{9,1},{13,5},{2,10},{6,14},... | collective-permute-start | bytes 196616 | tf_op jit(solution)/shard_map/ppermute | solution.py:38
  330.2 31.9 %collective-permute-start.69 = (bf16[256,128]{1,0:T(8,128)(2,1)S(1)}, bf16[256,128]{1,0:T(8,128)(2,1)S(1)}, u32[]{:S(2)}, u32[]{:S(2)}) collective-permute-start(bf16[256,128]{1,0:T(8,128)(2,1)S(1)} %copy-done.126), channel_id=1, source_target_pairs={{0,12},{4,8},{8,4},{12,0},{1,13},{5,9},{9,5},{13,1},{2,14},{6,10},... | collective-permute-start | bytes 196616 | tf_op jit(solution)/shard_map/ppermute | solution.py:38
  360.9 56.4 %collective-permute-start.92 = (bf16[256,512]{1,0:T(8,128)(2,1)}, bf16[256,512]{1,0:T(8,128)(2,1)}, u32[]{:S(2)}, u32[]{:S(2)}) collective-permute-start(bf16[256,512]{1,0:T(8,128)(2,1)} %fusion.1), channel_id=1, source_target_pairs={{0,16},{16,0},{1,17},{17,1},{2,18},{18,2},{3,19},{19,3},{4,20},{20... | collective-permute-start | bytes 786440 | tf_op jit(solution)/shard_map/ppermute | solution.py:38
  392.6 36.6 %collective-permute-start.73 = (bf16[1024,128]{1,0:T(8,128)(2,1)}, bf16[1024,128]{1,0:T(8,128)(2,1)S(1)}, u32[]{:S(2)}, u32[]{:S(2)}) collective-permute-start(bf16[1024,128]{1,0:T(8,128)(2,1)} %get-tuple-element.182), channel_id=1, source_target_pairs={{0,4},{4,0},{8,12},{12,8},{1,5},{5,1},{9,13},{13,9},{2,6},{6,2},{1... | collective-permute-start | bytes 786440 | tf_op jit(solution)/shard_map/ppermute | solution.py:38
  392.7 39.5 %collective-permute-start.74 = (bf16[1024,128]{1,0:T(8,128)(2,1)}, bf16[1024,128]{1,0:T(8,128)(2,1)S(1)}, u32[]{:S(2)}, u32[]{:S(2)}) collective-permute-start(bf16[1024,128]{1,0:T(8,128)(2,1)} %get-tuple-element.183), channel_id=1, source_target_pairs={{0,8},{4,12},{8,0},{12,4},{1,9},{5,13},{9,1},{13,5},{2,10},{6,14},... | collective-permute-start | bytes 786440 | tf_op jit(solution)/shard_map/ppermute | solution.py:38
  397.1 18.0 %collective-permute-start.71 = (bf16[256,128]{1,0:T(8,128)(2,1)S(1)}, bf16[256,128]{1,0:T(8,128)(2,1)S(1)}, u32[]{:S(2)}, u32[]{:S(2)}) collective-permute-start(bf16[256,128]{1,0:T(8,128)(2,1)S(1)} %copy-done.131), channel_id=1, source_target_pairs={{0,8},{4,12},{8,0},{12,4},{1,9},{5,13},{9,1},{13,5},{2,10},{6,14},... | collective-permute-start | bytes 196616 | tf_op jit(solution)/shard_map/ppermute | solution.py:38
  405.0 27.1 %collective-permute-start.75 = (bf16[1024,128]{1,0:T(8,128)(2,1)S(1)}, bf16[1024,128]{1,0:T(8,128)(2,1)S(1)}, u32[]{:S(2)}, u32[]{:S(2)}) collective-permute-start(bf16[1024,128]{1,0:T(8,128)(2,1)S(1)} %copy-done.97), channel_id=1, source_target_pairs={{0,12},{4,8},{8,4},{12,0},{1,13},{5,9},{9,5},{13,1},{2,14},{6,10},... | collective-permute-start | bytes 786440 | tf_op jit(solution)/shard_map/ppermute | solution.py:38
  427.2 37.3 %collective-permute-start.42 = (bf16[128,1024]{1,0:T(8,128)(2,1)}, bf16[128,1024]{1,0:T(8,128)(2,1)S(1)}, u32[]{:S(2)}, u32[]{:S(2)}) collective-permute-start(bf16[128,1024]{1,0:T(8,128)(2,1)} %get-tuple-element.144.refs_4_), channel_id=1, source_target_pairs={{0,2},{1,3},{2,0},{3,1},{4,6},{5,7},{6,4},{7,5},{8,10},{9,11},{10,... | collective-permute-start | bytes 786440 | tf_op jit(solution)/shard_map/ppermute | solution.py:38
  429.2 24.9 %collective-permute-start.106 = (bf16[256,512]{1,0:T(8,128)(2,1)}, bf16[256,512]{1,0:T(8,128)(2,1)}, u32[]{:S(2)}, u32[]{:S(2)}) collective-permute-start(bf16[256,512]{1,0:T(8,128)(2,1)} %dynamic-slice_convert_fusion.3), channel_id=1, source_target_pairs={{0,8},{4,12},{8,0},{12,4},{1,9},{5,13},{9,1},{13,5},{2,10},{6,14},... | collective-permute-start | bytes 786440 | tf_op jit(solution)/shard_map/ppermute | solution.py:38
  429.2 26.5 %collective-permute-start.100 = (bf16[128,1024]{1,0:T(8,128)(2,1)}, bf16[128,1024]{1,0:T(8,128)(2,1)}, u32[]{:S(2)}, u32[]{:S(2)}) collective-permute-start(bf16[128,1024]{1,0:T(8,128)(2,1)} %dynamic-slice_convert_fusion.4), channel_id=1, source_target_pairs={{0,8},{4,12},{8,0},{12,4},{1,9},{5,13},{9,1},{13,5},{2,10},{6,14},... | collective-permute-start | bytes 786440 | tf_op jit(solution)/shard_map/ppermute | solution.py:38
  477.1 17.0 %collective-permute-start.107 = (bf16[256,512]{1,0:T(8,128)(2,1)S(1)}, bf16[256,512]{1,0:T(8,128)(2,1)S(1)}, u32[]{:S(2)}, u32[]{:S(2)}) collective-permute-start(bf16[256,512]{1,0:T(8,128)(2,1)S(1)} %add_convert_fusion.2.refs_0_), channel_id=1, source_target_pairs={{0,8},{4,12},{8,0},{12,4},{1,9},{5,13},{9,1},{13,5},{2,10},{6,14},... | collective-permute-start | bytes 786440 | tf_op jit(solution)/shard_map/ppermute | solution.py:38
  479.7 25.7 %collective-permute-start.101 = (bf16[128,1024]{1,0:T(8,128)(2,1)S(1)}, bf16[128,1024]{1,0:T(8,128)(2,1)S(1)}, u32[]{:S(2)}, u32[]{:S(2)}) collective-permute-start(bf16[128,1024]{1,0:T(8,128)(2,1)S(1)} %add_convert_fusion.3.refs_0_), channel_id=1, source_target_pairs={{0,8},{4,12},{8,0},{12,4},{1,9},{5,13},{9,1},{13,5},{2,10},{6,14},... | collective-permute-start | bytes 786440 | tf_op jit(solution)/shard_map/ppermute | solution.py:38
  481.9 24.1 %collective-permute-start.102 = (bf16[128,1024]{1,0:T(8,128)(2,1)S(1)}, bf16[128,1024]{1,0:T(8,128)(2,1)S(1)}, u32[]{:S(2)}, u32[]{:S(2)}) collective-permute-start(bf16[128,1024]{1,0:T(8,128)(2,1)S(1)} %add_convert_fusion.3.refs_0_), channel_id=1, source_target_pairs={{0,4},{4,0},{8,12},{12,8},{1,5},{5,1},{9,13},{13,9},{2,6},{6,2},{1... | collective-permute-start | bytes 786440 | tf_op jit(solution)/shard_map/ppermute | solution.py:38
  482.2 29.3 %collective-permute-start.88 = (bf16[128,768]{1,0:T(8,128)(2,1)}, bf16[128,768]{1,0:T(8,128)(2,1)S(1)}, u32[]{:S(2)}, u32[]{:S(2)}) collective-permute-start(bf16[128,768]{1,0:T(8,128)(2,1)} %dynamic-slice_convert_fusion.5), channel_id=1, source_target_pairs={{0,8},{4,12},{8,0},{12,4},{1,9},{5,13},{9,1},{13,5},{2,10},{6,14},... | collective-permute-start | bytes 589832 | tf_op jit(solution)/shard_map/ppermute | solution.py:38
  494.1 19.9 %collective-permute-start.109 = (bf16[256,512]{1,0:T(8,128)(2,1)S(1)}, bf16[256,512]{1,0:T(8,128)(2,1)}, u32[]{:S(2)}, u32[]{:S(2)}) collective-permute-start(bf16[256,512]{1,0:T(8,128)(2,1)S(1)} %collective-permute-done.107.refs_1_), channel_id=1, source_target_pairs={{0,4},{4,0},{8,12},{12,8},{1,5},{5,1},{9,13},{13,9},{2,6},{6,2},{1... | collective-permute-start | bytes 786440 | tf_op jit(solution)/shard_map/ppermute | solution.py:38
  494.1 19.9 %collective-permute-start.83 = (bf16[128,1024]{1,0:T(8,128)(2,1)S(1)}, bf16[128,1024]{1,0:T(8,128)(2,1)S(1)}, u32[]{:S(2)}, u32[]{:S(2)}) collective-permute-start(bf16[128,1024]{1,0:T(8,128)(2,1)S(1)} %add_convert_fusion.4.refs_4_), channel_id=1, source_target_pairs={{0,2},{1,3},{2,0},{3,1},{4,6},{5,7},{6,4},{7,5},{8,10},{9,11},{10,... | collective-permute-start | bytes 786440 | tf_op jit(solution)/shard_map/ppermute | solution.py:38
  514.0 23.1 %collective-permute-start.79 = (bf16[128,1024]{1,0:T(8,128)(2,1)S(1)}, bf16[128,1024]{1,0:T(8,128)(2,1)S(1)}, u32[]{:S(2)}, u32[]{:S(2)}) collective-permute-start(bf16[128,1024]{1,0:T(8,128)(2,1)S(1)} %add_convert_fusion.6.refs_0_), channel_id=1, source_target_pairs={{0,1},{1,0},{2,3},{3,2},{4,5},{5,4},{6,7},{7,6},{8,9},{9,8},{10,11... | collective-permute-start | bytes 786440 | tf_op jit(solution)/shard_map/ppermute | solution.py:38
  514.0 23.1 %collective-permute-start.85 = (bf16[128,1024]{1,0:T(8,128)(2,1)S(1)}, bf16[128,1024]{1,0:T(8,128)(2,1)S(1)}, u32[]{:S(2)}, u32[]{:S(2)}) collective-permute-start(bf16[128,1024]{1,0:T(8,128)(2,1)S(1)} %collective-permute-done.83.refs_5_), channel_id=1, source_target_pairs={{0,1},{1,0},{2,3},{3,2},{4,5},{5,4},{6,7},{7,6},{8,9},{9,8},{10,11... | collective-permute-start | bytes 786440 | tf_op jit(solution)/shard_map/ppermute | solution.py:38
  514.5 22.6 %collective-permute-start.80 = (bf16[128,1024]{1,0:T(8,128)(2,1)S(1)}, bf16[128,1024]{1,0:T(8,128)(2,1)S(1)}, u32[]{:S(2)}, u32[]{:S(2)}) collective-permute-start(bf16[128,1024]{1,0:T(8,128)(2,1)S(1)} %collective-permute-done.78.refs_1_), channel_id=1, source_target_pairs={{0,1},{1,0},{2,3},{3,2},{4,5},{5,4},{6,7},{7,6},{8,9},{9,8},{10,11... | collective-permute-start | bytes 786440 | tf_op jit(solution)/shard_map/ppermute | solution.py:38
  520.2 22.2 %collective-permute-start.90 = (bf16[128,768]{1,0:T(8,128)(2,1)S(1)}, bf16[128,768]{1,0:T(8,128)(2,1)S(1)}, u32[]{:S(2)}, u32[]{:S(2)}) collective-permute-start(bf16[128,768]{1,0:T(8,128)(2,1)S(1)} %add_convert_fusion.14.refs_0_), channel_id=1, source_target_pairs={{0,4},{4,0},{8,12},{12,8},{1,5},{5,1},{9,13},{13,9},{2,6},{6,2},{1... | collective-permute-start | bytes 589832 | tf_op jit(solution)/shard_map/ppermute | solution.py:38
  (210 other events, 1956.3 us)

commit v2 on v1

v2 whole, which is shorter than its diff:
```python
import functools

import jax
import jax.numpy as jnp
from jax import lax
from jax.experimental import pallas as pl
from jax.experimental.pallas import tpu as pltpu
from jax.sharding import PartitionSpec as P

D = 1024
H = 16
HEAD = D // H
LANES = 128
DOCS = 17

NEG_BIG = -1e30
SQRT_HALF = 0.7071067811865476
INV_SQRT_TAU = 0.3989422804014327
LOG2E = 1.4426950408889634
LN2 = 0.6931471805599453
F32 = jnp.float32
BF16 = jnp.bfloat16
NT = (((1,), (1,)), ((), ()))
VMEM_LIMIT = 60 * 1024 * 1024


def order(n):
    found, bit = [0], n >> 1
    while bit:
        found = found + [d | bit for d in found]
        bit >>= 1
    return found


def swap(value, axis, bit):
    n = lax.axis_size(axis)
    return lax.ppermute(value, axis, [(i, i ^ bit) for i in range(n)])


def gather(value, axis):
    parts, bit = [value], lax.axis_size(axis) >> 1
    while bit:
        parts = parts + [swap(p, axis, bit) for p in parts]
        bit >>= 1
    return parts


def gather_weight(value):
    tp, dp = lax.axis_size("tp"), lax.axis_size("dp")
    parts = {(0, 0): value}

    def double(axis, bit):
        for d, f in list(parts):
            key = (d | bit, f) if axis == "tp" else (d, f | bit)
            parts[key] = swap(parts[d, f], axis, bit)

    bit = tp >> 1
    while bit > 1:
        double("tp", bit)
        bit >>= 1
    bit = dp >> 1
    while bit:
        double("dp", bit)
        bit >>= 1
    if tp > 1:
        double("tp", 1)
    return [parts[d, f] for d in order(tp) for f in order(dp)]


def after(value, *others):
    return lax.optimization_barrier((value, *others))[0]


LINE = []


def in_line(value):
    return after(value, LINE[-1]) if LINE else value


def step(function, *args):
    result = function(in_line(args[0]), *args[1:])
    LINE[:] = [result[0] if isinstance(result, (list, tuple)) else result]
    return result


def part_of(value, dim, start, size):
    return lax.slice_in_dim(value, start, start + size, axis=dim)


def split_sum(got, keep, dim):
    half = keep.shape[dim] // 2
    upper = part_of(keep, dim, half, half) + part_of(got, dim, half, half).astype(F32)
    return upper.astype(BF16), part_of(keep, dim, 0, half) + part_of(got, dim, 0, half).astype(F32)


def scatter(send, keep, axis, dim, got=None):
    n, bit = lax.axis_size(axis), 1
    while True:
        got = swap(send, axis, bit) if got is None else got
        bit <<= 1
        if bit >= n:
            return keep, got
        send, keep = step(functools.partial(split_sum, dim=dim), got, keep)
        got = None


def call(body, out_shape, *args, grid=None, in_specs=None, out_specs=None, scratch=(), flops=0, trans=0, name=None):
    size = sum(a.size * a.dtype.itemsize for a in args)
    outs = out_shape if isinstance(out_shape, (list, tuple)) else [out_shape]
    size += sum(o.size * o.dtype.itemsize for o in outs)
    extra = {}
    if grid is not None:
        extra["grid"] = grid
    if in_specs is not None:
        extra["in_specs"] = in_specs
    if out_specs is not None:
        extra["out_specs"] = out_specs
    args = list(args)
    first = 1 if args[0].shape == (3,) else 0
    args[first] = in_line(args[first])
    result = pl.pallas_call(
        body,
        out_shape=out_shape,
        scratch_shapes=list(scratch),
        compiler_params=pltpu.CompilerParams(vmem_limit_bytes=VMEM_LIMIT),
        cost_estimate=pl.CostEstimate(flops=int(flops), bytes_accessed=int(size), transcendentals=int(trans)),
        name=name,
        **extra,
    )(*args)
    LINE[:] = [result[0] if isinstance(result, (list, tuple)) else result]
    return result


def shape(dims, dtype):
    return jax.ShapeDtypeStruct(dims, dtype)


SMEM = pl.BlockSpec(memory_space=pltpu.SMEM)
FULL = pl.BlockSpec(memory_space=pltpu.VMEM)


def whole_block(value):
    return pl.BlockSpec(value.shape, lambda i: (0,) * len(value.shape))


def arrange_body(ids, src, out, *, tp, dp, shares):
    rows, width = src.shape
    share, cols = rows // tp, width // dp
    for j, d in enumerate(shares):
        for e, f in enumerate(order(dp)):
            row = pl.multiple_of((ids[2] ^ d) * share, share)
            col = pl.multiple_of((ids[0] ^ f) * cols, cols)
            out[j * share : (j + 1) * share, e * cols : (e + 1) * cols] = src[pl.ds(row, share), pl.ds(col, cols)]


def arrange(ids, src, tp, dp, shares):
    rows = src.shape[0] // tp * len(shares)
    return call(
        functools.partial(arrange_body, tp=tp, dp=dp, shares=shares),
        shape((rows, src.shape[1]), src.dtype),
        ids,
        src,
        in_specs=[SMEM, FULL],
        name="arrange",
    )


def place_body(ids, *refs, tp, dp, first):
    *parts, out = refs
    rows, width = out.shape
    share, cols = rows // tp, width // dp
    for j, d in enumerate(order(tp)):
        for e, f in enumerate(order(dp)):
            row = pl.multiple_of((ids[2] ^ d) * share, share)
            col = pl.multiple_of((ids[0] ^ f) * cols, cols)
            block = parts[j][first : first + share, e * cols : (e + 1) * cols]
            out[pl.ds(row, share), pl.ds(col, cols)] = block.astype(F32)


def place(ids, parts, tp, dp, rows, first=0):
    return call(
        functools.partial(place_body, tp=tp, dp=dp, first=first),
        shape((rows, parts[0].shape[1]), F32),
        ids,
        *parts,
        in_specs=[SMEM] + [FULL] * len(parts),
        name="place",
    )


def split_body(ids, got, keep, *outs):
    n, rows = len(outs), outs[0].shape[0]
    for e in range(n):
        at = pl.multiple_of((ids[1] ^ e) * rows, rows)
        total = keep[pl.ds(at, rows), :] + got[pl.ds(at, rows), :].astype(F32)
        outs[e][...] = total.astype(outs[e].dtype)


def merge_body(own, *refs):
    *others, out = refs
    total = own[...]
    for other in others:
        total = total + other[...].astype(F32)
    out[...] = total.astype(BF16)


def place_columns_body(ids, *refs, n, widths):
    parts, outs = refs[:n], refs[n:]
    rows = parts[0].shape[0]
    for e, part in enumerate(parts):
        at = pl.multiple_of((ids[1] ^ e) * rows, rows)
        lane = 0
        for out, width in zip(outs, widths):
            out[pl.ds(at, rows), :] = part[:, lane : lane + width].astype(F32)
            lane += width


def place_rows_body(ids, *refs, n):
    parts, (first, second, terms, whole) = refs[:n], refs[n:]
    rows = parts[0].shape[0]
    for e, part in enumerate(parts):
        at = pl.multiple_of((ids[1] ^ e) * rows, rows)
        whole[pl.ds(at, rows), :] = part[...].astype(F32)
    hidden, middle = first.shape[1], second.shape[0]
    first[...] = whole[:hidden, :].T
    second[...] = whole[hidden : hidden + middle, :]
    terms[...] = whole[hidden + middle : hidden + middle + 8, :]


class GradSum:
    def __init__(self, ids, dim, product):
        self.ids, self.dim, self.product = ids, dim, product

    def begin(self, width):
        mid = width // 2
        send = step(lambda *a: self.product(mid, mid, *a).astype(BF16), *self.operands)
        self.got = swap(send, "dp", 1)
        self.keep = step(lambda *a: self.product(0, mid, *a), *self.operands)

    def over_dp(self):
        keep, got = scatter(None, self.keep, "dp", self.dim, self.got)
        n = lax.axis_size("ctx")
        rows, cols = keep.shape
        block = rows // n
        self.own, *sends = call(
            split_body,
            [shape((block, cols), F32)] + [shape((block, cols), BF16)] * (n - 1),
            self.ids,
            got,
            keep,
            in_specs=[SMEM, FULL, FULL],
            name="split",
        )
        self.parts = [swap(sends[e - 1], "ctx", e) for e in range(1, n)]

    def over_ctx(self):
        own = call(merge_body, shape(self.own.shape, BF16), self.own, *self.parts, name="merge")
        self.parts = [own] + [swap(own, "ctx", e) for e in range(1, lax.axis_size("ctx"))]

    def columns(self, widths):
        n = len(self.parts)
        rows = self.parts[0].shape[0] * n
        return call(
            functools.partial(place_columns_body, n=n, widths=widths),
            [shape((rows, w), F32) for w in widths],
            self.ids,
            *self.parts,
            in_specs=[SMEM] + [FULL] * n,
            name="place_columns",
        )

    def rows(self, hidden, middle):
        n = len(self.parts)
        rows, cols = self.parts[0].shape
        return call(
            functools.partial(place_rows_body, n=n),
            [shape((cols, hidden), F32), shape((middle, cols), F32), shape((8, cols), F32)],
            self.ids,
            *self.parts,
            in_specs=[SMEM] + [FULL] * n,
            scratch=[pltpu.VMEM((n * rows, cols), F32)],
            name="place_rows",
        )


def over_rows(left, right):
    return lax.dot_general(left, right, (((0,), (0,)), ((), ())), preferred_element_type=F32)


def sum_over_rows(left, right, start, size):
    total = None
    for l, r in zip(left, right):
        term = over_rows(l, r[: l.shape[0], start : start + size])
        total = term if total is None else total + term
    return total


def swap_halves(tile, lane):
    return jnp.where(lane % HEAD < HEAD // 2, pltpu.roll(tile, LANES - HEAD // 2, 1), pltpu.roll(tile, HEAD // 2, 1))


def turn(tile):
    return pltpu.roll(tile, HEAD, 1)


def pick(me, values, index):
    chosen = values[index]
    for i in range(1, len(values)):
        chosen = jnp.where(me == i, values[i ^ index], chosen)
    return chosen


def rows_dot(x, pieces, start, size):
    total, at = None, 0
    for w in pieces:
        depth = w.shape[0]
        term = jnp.dot(x[:, at : at + depth], w[:, start : start + size], preferred_element_type=F32)
        total = term if total is None else total + term
        at += depth
    return total


def kv_body(ids, x, *refs, dp, n):
    ws = refs[:dp]
    cosine, sine = refs[dp], refs[dp + 1]
    outs = refs[dp + 2 :]
    me = ids[1]
    step = 256
    width = n * HEAD
    lane = lax.broadcasted_iota(jnp.int32, (step, LANES), 1)
    for i in range(x.shape[0] // step):
        rows = slice(i * step, (i + 1) * step)
        tokens = x[rows, :]
        both = rows_dot(tokens, ws, width, 2 * width)
        heads = []
        for t in range(n // 2):
            kt = both[:, t * LANES : (t + 1) * LANES]
            vt = both[:, width + t * LANES : width + (t + 1) * LANES]
            kt = kt * cosine[rows, :] + swap_halves(kt, lane) * sine[rows, :]
            heads.append(jnp.where(lane < HEAD, kt, turn(vt)))
            heads.append(jnp.where(lane < HEAD, turn(kt), vt))
        for e in range(n):
            outs[e][rows, :] = pick(me, heads, e).astype(BF16)


def q_body(ids, x, *refs, dp, n):
    ws = refs[:dp]
    cosine, sine = refs[dp], refs[dp + 1]
    outs = refs[dp + 2 :]
    me = ids[1]
    step = 256
    half = outs[0].shape[0]
    lane = lax.broadcasted_iota(jnp.int32, (step, LANES), 1)
    for i in range(half // step):
        sides = []
        for h in range(2):
            rows = slice(h * half + i * step, h * half + (i + 1) * step)
            query = rows_dot(x[rows, :], ws, 0, n * HEAD)
            heads = []
            for t in range(n // 2):
                qt = query[:, t * LANES : (t + 1) * LANES]
                qt = qt * cosine[rows, :] + swap_halves(qt, lane) * sine[rows, :]
                qt = qt * (HEAD**-0.5 * LOG2E)
                other = turn(qt)
                heads.extend([qt, other] if h == 0 else [other, qt])
            sides.append(heads)
        packed = [jnp.where(lane < HEAD, lo, hi) for lo, hi in zip(*sides)]
        for e in range(n):
            outs[e][i * step : (i + 1) * step, :] = pick(me, packed, e).astype(BF16)


def unpack_pairs(me, packed, n, h, lane):
    tiles = []
    for t in range(n // 2):
        lo, hi = pick(me, packed, 2 * t), pick(me, packed, 2 * t + 1)
        if h == 0:
            tiles.append(jnp.where(lane < HEAD, lo, turn(hi)))
        else:
            tiles.append(jnp.where(lane < HEAD, turn(lo), hi))
    return tiles


def unpack_body(ids, *refs, n):
    packed, outs = refs[:n], refs[n:]
    half, share = packed[0].shape[0], outs[0].shape[0]
    lane = lax.broadcasted_iota(jnp.int32, (share, LANES), 1)
    for i in range(half // share):
        pieces = [p[i * share : (i + 1) * share, :].astype(F32) for p in packed]
        for h in range(2):
            tiles = unpack_pairs(ids[1], pieces, n, h, lane)
            out = outs[h * (half // share) + i]
            for t, tile in enumerate(tiles):
                out[:, t * LANES : (t + 1) * LANES] = tile.astype(BF16)


def pack_body(ids, *refs, tp, n):
    parts, outs = refs[:tp], refs[tp:]
    half, share = outs[0].shape[0], parts[0].shape[0]
    lane = lax.broadcasted_iota(jnp.int32, (share, LANES), 1)
    for i in range(half // share):
        sides = []
        for h in range(2):
            grad = parts[h * (half // share) + i]
            heads = []
            for t in range(n // 2):
                tile = grad[:, t * LANES : (t + 1) * LANES].astype(F32)
                heads.extend([tile, turn(tile)] if h == 0 else [turn(tile), tile])
            sides.append(heads)
        packed = [jnp.where(lane < HEAD, lo, hi) for lo, hi in zip(*sides)]
        for e in range(n):
            outs[e][i * share : (i + 1) * share, :] = pick(ids[1], packed, e).astype(BF16)


BQ = 256
KC = 1024


def fill_keys(kv, marks, ka, va):
    size = kv[0].shape[0]
    lane = lax.broadcasted_iota(jnp.int32, (size, LANES), 1)
    ones = jnp.where(lane < 3, 1.0, 0.0).astype(BF16)
    for e, ref in enumerate(kv):
        rows = slice(e * size, (e + 1) * size)
        both = ref[...]
        ka[rows, :] = jnp.where(lane < HEAD, both, marks[rows, :])
        va[rows, :] = jnp.where(lane < HEAD, ones, both)


def query_marks(marks, row, lane):
    there = (lane >= HEAD) & (lane < HEAD + DOCS)
    bias = (marks[pl.ds(row, BQ), :].astype(F32) - 1.0) * -NEG_BIG
    return jnp.where(there, bias, 0.0)


def block_of(i, half, length, first):
    block, h = i // 2, i % 2
    blocks = half // BQ
    token = (first + block // blocks) * length + h * half + (block % blocks) * BQ
    return pl.multiple_of(block * BQ, BQ), h, pl.multiple_of(token, BQ)


def attend_body(*refs, m, n, first):
    queries, kv = refs[:m], refs[m : m + n]
    marks = refs[m + n]
    outs, lse = refs[m + n + 1 : 2 * m + n + 1], refs[2 * m + n + 1]
    qs, ka, va, os = refs[2 * m + n + 2 :]
    half, length = queries[0].shape[0], kv[0].shape[0]
    i = pl.program_id(0)

    @pl.when(i == 0)
    def _():
        fill_keys(kv, marks, ka, va)
        for e in range(m):
            qs[e * half : (e + 1) * half, :] = queries[e][...]

    at, h, token = block_of(i, half, length, first)
    lane = lax.broadcasted_iota(jnp.int32, (BQ, LANES), 1)
    q = qs[pl.ds(at, BQ), :].astype(F32)
    q = jnp.where(h == 1, turn(q), q)
    q = jnp.where(lane < HEAD, q, query_marks(marks, token, lane)).astype(BF16)
    scores, top = [], None
    for j in range(n * length // KC):
        s = lax.dot_general(q, ka[j * KC : (j + 1) * KC, :], NT, preferred_element_type=F32)
        scores.append(s)
        for t in range(KC // LANES):
            tile = s[:, t * LANES : (t + 1) * LANES]
            top = tile if top is None else jnp.maximum(top, tile)
    top = jnp.max(top, axis=1, keepdims=True)
    total = jnp.zeros((BQ, LANES), F32)
    for j, s in enumerate(scores):
        p = jnp.exp2(s - top).astype(BF16)
        total += jnp.dot(p, va[j * KC : (j + 1) * KC, :], preferred_element_type=F32)
    weight = total[:, :1]
    o = total / weight
    o = jnp.where(h == 0, turn(o), o)
    log = jnp.broadcast_to(top + jnp.log2(weight), (BQ, LANES))
    other = (lane < HEAD) & (h == 1)
    os[pl.ds(at, BQ), :] = jnp.where(other, os[pl.ds(at, BQ), :], o)
    lse[pl.ds(at, BQ), :] = jnp.where(other, lse[pl.ds(at, BQ), :], log)

    @pl.when(i == pl.num_programs(0) - 1)
    def _():
        for e in range(m):
            outs[e][...] = os[e * half : (e + 1) * half, :].astype(BF16)


def attend(queries, kv, marks, first):
    m, n, (half, _), length = len(queries), len(kv), queries[0].shape, kv[0].shape[0]
    steps = m * 2 * half // BQ
    args = [*queries, *kv, marks]
    outs = [shape((half, LANES), BF16)] * m + [shape((m * half, LANES), F32)]
    out = call(
        functools.partial(attend_body, m=m, n=n, first=first),
        outs,
        *args,
        grid=(steps,),
        in_specs=[whole_block(a) for a in args],
        out_specs=[whole_block(o) for o in outs],
        scratch=[
            pltpu.VMEM((m * half, LANES), BF16),
            pltpu.VMEM((n * length, LANES), BF16),
            pltpu.VMEM((n * length, LANES), BF16),
            pltpu.VMEM((m * half, LANES), F32),
        ],
        flops=4 * steps * BQ * n * length * 256,
        trans=steps * BQ * n * length,
        name="attend",
    )
    return out[:m], out[m]


def split3(value):
    high = value.astype(BF16).astype(F32)
    rest = value - high
    middle = rest.astype(BF16).astype(F32)
    return high, middle, rest - middle


def attend_back_body(*refs, m, n, first, start, end):
    queries, grads, outs = (refs[k * m : (k + 1) * m] for k in range(3))
    kv, lse, marks = refs[3 * m : 3 * m + n], refs[3 * m + n], refs[3 * m + n + 1]
    at = 3 * m + n + 2
    before = None
    if not start:
        before, at = refs[at], at + 1
    if end:
        earlier, at = refs[at : at + n - m], at + n - m
        results, at = refs[at : at + n], at + n
        qs, gs, os, ds_, ka, va, acc = refs[at:]
    else:
        dqs, at = refs[at : at + m], at + m
        acc, at = refs[at], at + 1
        qs, gs, os, ds_, ka, va = refs[at:]
    half, length = queries[0].shape[0], kv[0].shape[0]
    i = pl.program_id(0)

    @pl.when(i == 0)
    def _():
        fill_keys(kv, marks, ka, va)
        for e in range(m):
            rows = slice(e * half, (e + 1) * half)
            qs[rows, :] = queries[e][...]
            gs[rows, :] = grads[e][...]
            os[rows, :] = outs[e][...]
        acc[...] = jnp.zeros_like(acc) if start else before[...]

    row, h, token = block_of(i, half, length, first)
    lane = lax.broadcasted_iota(jnp.int32, (BQ, LANES), 1)
    here = pl.ds(row, BQ)
    q = qs[here, :].astype(F32)
    g = gs[here, :].astype(F32)
    o = os[here, :].astype(F32)
    log = lse[here, :]
    q = jnp.where(h == 1, turn(q), q)
    g = jnp.where(h == 0, turn(g), g)
    o = jnp.where(h == 0, turn(o), o)
    log = jnp.where(h == 1, turn(log), log)[:, :1]
    dot = jnp.sum(jnp.where(lane >= HEAD, g * o, 0.0), axis=1, keepdims=True)
    b0, b1, b2 = split3(-log)
    q_marks = query_marks(marks, token, lane)
    first_lane = HEAD + DOCS
    qa = jnp.where(lane == first_lane, b0, q_marks)
    qa = jnp.where(lane == first_lane + 1, b1, qa)
    qa = jnp.where(lane == first_lane + 2, b2, qa)
    qa = jnp.where(lane < HEAD, q, qa).astype(BF16)
    b0, b1, b2 = split3(-dot)
    ga = jnp.where(lane == 0, b0, jnp.where(lane == 1, b1, jnp.where(lane == 2, b2, 0.0)))
    ga = jnp.where(lane >= HEAD, g, ga).astype(BF16)
    q_t = q.T[:HEAD].astype(BF16)
    g_t = g.T[HEAD:].astype(BF16)
    total = jnp.zeros((BQ, LANES), F32)
    for j in range(n * length // KC):
        cols = slice(j * KC, (j + 1) * KC)
        s = lax.dot_general(qa, ka[cols, :], NT, preferred_element_type=F32)
        t = lax.dot_general(ga, va[cols, :], NT, preferred_element_type=F32)
        p = jnp.exp2(s)
        ds = (p * t).astype(BF16)
        p = p.astype(BF16)
        acc[HEAD:, cols] += jnp.dot(g_t, p, preferred_element_type=F32)
        acc[:HEAD, cols] += jnp.dot(q_t, ds, preferred_element_type=F32)
        total += jnp.dot(ds, ka[cols, :], preferred_element_type=F32)
    total = total * (HEAD**-0.5)
    total = jnp.where(h == 1, turn(total), total)
    other = (lane < HEAD) & (h == 1)
    ds_[here, :] = jnp.where(other, ds_[here, :], total)

    @pl.when(i == pl.num_programs(0) - 1)
    def _():
        if not end:
            for e in range(m):
                dqs[e][...] = ds_[e * half : (e + 1) * half, :].astype(BF16)
        else:
            for e in range(n):
                if e < n - m:
                    results[e][:half, :] = earlier[e][...]
                else:
                    at = (e - n + m) * half
                    results[e][:half, :] = ds_[at : at + half, :].astype(BF16)
                cols = slice(e * length, (e + 1) * length)
                turned = acc[:, cols].T
                key_lane = lax.broadcasted_iota(jnp.int32, (length, LANES), 1)
                results[e][half:, :] = jnp.where(key_lane < HEAD, turned * LN2, turned).astype(BF16)


def attend_back(queries, grads, outs, kv, lse, marks, before, earlier, first, end):
    m, n, (half, _), length = len(queries), len(kv), queries[0].shape, kv[0].shape[0]
    steps = m * 2 * half // BQ
    start = before is None
    args = [*queries, *grads, *outs, *kv, lse, marks] + ([] if start else [before]) + (list(earlier) if end else [])
    if end:
        results = [shape((half + length, LANES), BF16)] * n
    else:
        results = [shape((half, LANES), BF16)] * m + [shape((LANES, n * length), F32)]
    out = call(
        functools.partial(attend_back_body, m=m, n=n, first=first, start=start, end=end),
        results,
        *args,
        grid=(steps,),
        in_specs=[whole_block(a) for a in args],
        out_specs=[whole_block(o) for o in results],
        scratch=[pltpu.VMEM((m * half, LANES), BF16)] * 3
        + [pltpu.VMEM((m * half, LANES), F32)]
        + [pltpu.VMEM((n * length, LANES), BF16)] * 2
        + ([pltpu.VMEM((LANES, n * length), F32)] if end else []),
        flops=10 * steps * BQ * n * length * 256,
        trans=steps * BQ * n * length,
        name="attend_back",
    )
    return out if end else (out[:m], out[m])


def input_grad_body(ids, *refs, dp, n):
    pieces, ws = refs[:n], refs[n : n + dp]
    cosine, sine, whole, send, keep = refs[n + dp :]
    me = ids[1]
    half = send.shape[0]
    step = 256
    lane = lax.broadcasted_iota(jnp.int32, (step, LANES), 1)
    for h, target in ((1, send), (0, keep)):
        for i in range(half // step):
            rows = slice(h * half + i * step, h * half + (i + 1) * step)
            there = slice(i * step, (i + 1) * step)
            dq = [p[there, :].astype(F32) for p in pieces]
            kv = [p[half + rows.start : half + rows.stop, :].astype(F32) for p in pieces]
            qt = unpack_pairs(me, dq, n, h, lane)
            kt = unpack_pairs(me, kv, n, 0, lane)
            vt = unpack_pairs(me, kv, n, 1, lane)
            back = [x * cosine[rows, :] - swap_halves(x, lane) * sine[rows, :] for x in qt + kt]
            low = jnp.concatenate(back + vt, axis=1).astype(BF16)
            whole[rows, :] = low
            col = 0
            for w in ws:
                size = w.shape[0]
                total = lax.dot_general(low, w[...], NT, preferred_element_type=F32)
                target[there, col : col + size] = total.astype(target.dtype)
                col += size


def normed_of(value):
    centered = value - jnp.mean(value, axis=-1, keepdims=True)
    inverse = lax.rsqrt(jnp.mean(centered * centered, axis=-1, keepdims=True) + 1e-05)
    return centered * inverse, inverse


def back_of(grad, normed, inverse, gain):
    scaled = grad * gain
    inner = (
        scaled
        - jnp.mean(scaled, axis=-1, keepdims=True)
        - normed * jnp.mean(scaled * normed, axis=-1, keepdims=True)
    )
    return inverse * inner


RB = 64
CB = 512


def spans(total, size):
    size = min(size, total)
    return [slice(i, i + size) for i in range(0, total, size)]


class Copies:
    def __init__(self, sems):
        self.sems, self.count, self.groups = sems, 0, {}

    def start(self, group, src, dst):
        copy = pltpu.make_async_copy(src, dst, self.sems.at[self.count])
        copy.start()
        self.count += 1
        self.groups.setdefault(group, []).append(copy)

    def wait(self, group):
        for copy in self.groups[group]:
            copy.wait()


def weight_copies(copies, wod, wi, tp, dp, heads, gains, wi_all, wd_all, x=None, tokens=None):
    hidden = wi[0].shape[1]
    cols = wi[0].shape[0]
    lw = wod[0].shape[0] - hidden - 16

    def small():
        for f in range(dp):
            src = wod[f].at[pl.ds(hidden + lw, 16), :]
            copies.start("small", src, gains.at[:, pl.ds(f * cols, cols)])
        for d in range(tp):
            for f in range(dp):
                src = wod[d * dp + f].at[pl.ds(hidden, lw), :]
                copies.start("small", src, heads.at[pl.ds(d * lw, lw), pl.ds(f * cols, cols)])
        if x is not None:
            copies.start("small", x.at[pl.ds(0, tokens.shape[0]), :], tokens)

    def large():
        for d in range(tp):
            for f in range(dp):
                copies.start(d, wi[d * dp + f], wi_all.at[d, pl.ds(f * cols, cols), :])
                src = wod[d * dp + f].at[pl.ds(0, hidden), :]
                copies.start(d, src, wd_all.at[d, :, pl.ds(f * cols, cols)])

    return small, large


def forward_body(*refs, tp, dp):
    received, cotangent, x = refs[:tp], refs[tp], refs[tp + 1]
    at = tp + 2
    wod, wi = refs[at : at + tp * dp], refs[at + tp * dp : at + 2 * tp * dp]
    at += 2 * tp * dp
    lows, out_low, slope, normed, inverse, second, terms = refs[at : at + 7]
    act = refs[at + 7 : at + 7 + tp]
    heads, gains, wi_all, wd_all, tokens, attended, acc, sems = refs[at + 7 + tp :]
    share, width = tokens.shape
    hidden = wi[0].shape[1]
    lw = received[0].shape[1]
    copies = Copies(sems)
    small, large = weight_copies(copies, wod, wi, tp, dp, heads, gains, wi_all, wd_all, x, tokens)
    small()
    large()
    for j in range(tp):
        attended[:, j * lw : (j + 1) * lw] = received[j][...]
    copies.wait("small")
    for c in spans(width, CB):
        mixed = jnp.dot(attended[...], heads[:, c], preferred_element_type=F32)
        acc[:, c] = mixed + tokens[:, c].astype(F32)
    gain = gains[...].astype(F32)
    for b in spans(share, RB):
        n, r = normed_of(acc[b, :])
        out = n * gain[0:1, :] + gain[1:2, :]
        acc[b, :] = out
        lows[b, :] = out.astype(BF16)
        normed[b, :] = n
        inverse[b, :] = jnp.broadcast_to(r, (r.shape[0], LANES))
    for d in range(tp):
        copies.wait(d)
        for c in spans(hidden, CB):
            h = jnp.dot(lows[:share, :], wi_all[d, :, c], preferred_element_type=F32)
            phi = 0.5 * (1.0 + lax.erf(h * SQRT_HALF))
            act[d][:, c] = (h * phi).astype(BF16)
            there = slice(d * hidden + c.start, d * hidden + c.stop)
            slope[:, there] = (phi + h * jnp.exp(-0.5 * h * h) * INV_SQRT_TAU).astype(BF16)
        for c in spans(width, CB):
            acc[:, c] += jnp.dot(act[d][...], wd_all[d, :, c], preferred_element_type=F32)
    sums = [jnp.zeros((1, width), F32)] * 2
    for b in spans(share, RB):
        n, r = normed_of(acc[b, :])
        out_low[b, :] = (n * gain[2:3, :] + gain[3:4, :]).astype(BF16)
        grad = cotangent[b, :].astype(F32)
        result = back_of(grad, n, r, gain[2:3, :])
        second[b, :] = result
        lows[share + b.start : share + b.stop, :] = result.astype(BF16)
        sums = [sums[0] + jnp.sum(grad * n, axis=0, keepdims=True), sums[1] + jnp.sum(grad, axis=0, keepdims=True)]
    terms[0:1, :], terms[1:2, :] = sums


def middle_scratch(tp, dp, lw, hidden, width, share):
    return [
        pltpu.VMEM((tp * lw, width), BF16),
        pltpu.VMEM((16, width), BF16),
        pltpu.VMEM((tp, width, hidden), BF16),
        pltpu.VMEM((tp, hidden, width), BF16),
    ]


ANY = pl.BlockSpec(memory_space=pl.ANY)


def forward(received, cotangent, x, wod, wi, tp, dp):
    (share, lw), (cols, hidden) = received[0].shape, wi[0].shape
    width = cols * dp
    outs = [
        shape((2 * share, width), BF16),
        shape((share, width), BF16),
        shape((share, tp * hidden), BF16),
        shape((share, width), F32),
        shape((share, LANES), F32),
        shape((share, width), F32),
        shape((2, width), F32),
    ]
    out = call(
        functools.partial(forward_body, tp=tp, dp=dp),
        outs + [shape((share, hidden), BF16)] * tp,
        *received,
        cotangent,
        x,
        *wod,
        *wi,
        in_specs=[FULL] * (tp + 1) + [ANY] * (1 + 2 * tp * dp),
        scratch=middle_scratch(tp, dp, lw, hidden, width, share)
        + [
            pltpu.VMEM((share, width), BF16),
            pltpu.VMEM((share, tp * lw), BF16),
            pltpu.VMEM((share, width), F32),
            pltpu.SemaphoreType.DMA((dp + tp * dp * 3 + 1,)),
        ],
        flops=2 * share * width * (tp * lw + 2 * tp * hidden),
        trans=3 * share * tp * hidden,
        name="forward",
    )
    return out[:7], out[7:]


def backward_body(*refs, tp, dp):
    lows, out_low, slope, normed, inverse, second, terms = refs[:7]
    wod, wi = refs[7 : 7 + tp * dp], refs[7 + tp * dp : 7 + 2 * tp * dp]
    at = 7 + 2 * tp * dp
    rows, first = refs[at], refs[at + 1]
    pre, grads = refs[at + 2 : at + 2 + tp], refs[at + 2 + tp : at + 2 + 2 * tp]
    heads, gains, wi_all, wd_all, acc, edge, sems = refs[at + 2 + 2 * tp :]
    share, width = out_low.shape
    hidden, lw = pre[0].shape[1], grads[0].shape[1]
    copies = Copies(sems)
    small, large = weight_copies(copies, wod, wi, tp, dp, heads, gains, wi_all, wd_all)
    large()
    small()
    acc[...] = second[...]
    for d in range(tp):
        copies.wait(d)
        for c in spans(hidden, CB):
            grad = lax.dot_general(lows[share:, :], wd_all[d, c, :], NT, preferred_element_type=F32)
            there = slice(d * hidden + c.start, d * hidden + c.stop)
            pre[d][:, c] = (grad * slope[:, there].astype(F32)).astype(BF16)
        for c in spans(width, CB):
            acc[:, c] += lax.dot_general(pre[d][...], wi_all[d, c, :], NT, preferred_element_type=F32)
    copies.wait("small")
    gain = gains[...].astype(F32)
    sums = [jnp.zeros((1, width), F32)] * 2
    for b in spans(share, RB):
        grad, n = acc[b, :], normed[b, :]
        result = back_of(grad, n, inverse[b, :1], gain[0:1, :])
        first[b, :] = result
        rows[b, :] = result.astype(BF16)
        sums = [sums[0] + jnp.sum(grad * n, axis=0, keepdims=True), sums[1] + jnp.sum(grad, axis=0, keepdims=True)]
    for j in range(tp):
        part = lax.dot_general(rows[:share, :], heads[j * lw : (j + 1) * lw, :], NT, preferred_element_type=F32)
        grads[j][...] = part.astype(BF16)
    rows[share : 2 * share, :] = out_low[...]
    edge[...] = jnp.zeros_like(edge)
    edge[0:1, :], edge[1:2, :] = sums
    edge[2:4, :] = terms[...]
    rows[2 * share :, :] = edge[...].astype(BF16)


def backward(forwarded, wod, wi, tp, dp, lw):
    cols, hidden = wi[0].shape
    share, width = forwarded[1].shape
    out = call(
        functools.partial(backward_body, tp=tp, dp=dp),
        [shape((2 * share + 16, width), BF16), shape((share, width), F32)]
        + [shape((share, hidden), BF16)] * tp
        + [shape((share, lw), BF16)] * tp,
        *forwarded,
        *wod,
        *wi,
        in_specs=[FULL] * 7 + [ANY] * (2 * tp * dp),
        scratch=middle_scratch(tp, dp, lw, hidden, width, share)
        + [
            pltpu.VMEM((share, width), F32),
            pltpu.VMEM((16, width), F32),
            pltpu.SemaphoreType.DMA((dp + tp * dp * 3,)),
        ],
        flops=2 * share * width * (tp * lw + 2 * tp * hidden),
        name="backward",
    )
    return out[0], out[1], out[2 : 2 + tp], out[2 + tp :]


def rotate_heads(values, angles, sign):
    half = HEAD // 2
    cosine = jnp.cos(angles)[:, None, :half]
    sine = sign * jnp.sin(angles)[:, None, :half]
    first, second = values[..., :half], values[..., half:]
    return jnp.concatenate([first * cosine - second * sine, second * cosine + first * sine], axis=-1)


def gathered_attention(tokens, weights, angles, docs):
    rows, width = tokens.shape[0], weights[0].shape[1]
    heads = width // HEAD
    scale = HEAD**-0.5

    def project(w):
        return jnp.dot(tokens, w, preferred_element_type=F32).reshape(rows, heads, HEAD)

    q = rotate_heads(project(weights[0]), angles, 1.0).astype(BF16)
    k = rotate_heads(project(weights[1]), angles, 1.0).astype(BF16)
    v = project(weights[2]).astype(BF16)
    keys = jnp.concatenate(gather(k, "ctx"))
    values = jnp.concatenate(gather(v, "ctx"))
    all_docs = jnp.concatenate(gather(docs, "ctx"))

    def masked():
        s = jnp.einsum("qhd,khd->hqk", q, keys, preferred_element_type=F32) * scale
        return jnp.where(docs[None, :, None] == all_docs[None, None, :], s, NEG_BIG)

    s = masked()
    top = jnp.max(s, axis=-1, keepdims=True)
    p = jnp.exp(s - top)
    total = jnp.sum(p, axis=-1)
    out = jnp.einsum("hqk,khd->qhd", p.astype(BF16), values, preferred_element_type=F32)
    out = out / total.T[..., None]
    log = top[..., 0] + jnp.log(total)

    def backward(grad):
        grad = grad.astype(BF16).reshape(rows, heads, HEAD)
        dot = jnp.sum(grad.astype(F32) * out, axis=-1).T
        p = jnp.exp(masked() - log[..., None])
        dv = jnp.einsum("hqk,qhd->khd", p.astype(BF16), grad, preferred_element_type=F32)
        dp = jnp.einsum("qhd,khd->hqk", grad, values, preferred_element_type=F32)
        ds = (p * (dp - dot[..., None])).astype(BF16)
        dq = jnp.einsum("hqk,khd->qhd", ds, keys, preferred_element_type=F32) * scale
        dk = jnp.einsum("hqk,qhd->khd", ds, q, preferred_element_type=F32) * scale

        def owned(value):
            half = value.shape[0] // 2
            keep, got = scatter(value[half:].astype(BF16), value[:half], "ctx", 0)
            return keep + got.astype(F32)

        dq = rotate_heads(dq, angles, -1.0)
        dk = rotate_heads(owned(dk), angles, -1.0)
        return jnp.concatenate([x.astype(BF16).reshape(rows, width) for x in (dq, dk, owned(dv))], axis=1)

    return out.astype(BF16).reshape(rows, width), backward


def body(
    layer_input,
    segments,
    positions,
    w_q,
    w_k,
    w_v,
    w_o,
    w_in,
    w_out,
    ln1_gain,
    ln1_bias,
    ln2_gain,
    ln2_bias,
    cotangent,
):
    LINE.clear()
    seqs, length, width = layer_input.shape
    assert seqs == 1
    tp, dp, ctx = lax.axis_size("tp"), lax.axis_size("dp"), lax.axis_size("ctx")
    lw, hidden = w_q.shape[1], w_in.shape[1]
    heads = lw // HEAD
    ids = jnp.stack([lax.axis_index("dp"), lax.axis_index("ctx"), lax.axis_index("tp")]).astype(jnp.int32)
    share = length // tp
    half = length // 2
    spread = heads == ctx and heads % 2 == 0 and half % BQ == 0 and tp % 2 == 0

    def exchange(parts, first=0):
        return [p if first + k == 0 else swap(p, "ctx", first + k) for k, p in enumerate(parts)]

    def exchange_tp(parts):
        return [p if d == 0 else swap(p, "tp", d) for d, p in zip(order(tp), parts)]

    def arrange_tokens(value):
        table = value.reshape(tp, share)
        picked = [lax.dynamic_index_in_dim(table, ids[2] ^ d, 0, keepdims=False) for d in order(tp)]
        return jnp.stack(picked).reshape(length)

    w_qkv = gather(jnp.concatenate([w_q, w_k, w_v], axis=1), "dp")
    vectors = jnp.stack([ln1_gain, ln1_bias, ln2_gain, ln2_bias])
    tall = jnp.concatenate([w_out, w_o, jnp.pad(vectors, ((0, 12), (0, 0)))])

    docs = arrange_tokens(segments.reshape(length))
    places = arrange_tokens(positions.reshape(length)).astype(F32)
    freq = 10000.0 ** (-(jnp.arange(LANES, dtype=jnp.int32) % (HEAD // 2)).astype(F32) * 2.0 / HEAD)
    angles = places[:, None] * freq[None, :]
    x = arrange(ids, layer_input.reshape(length, width), tp, dp, order(tp))

    if spread:
        side = jnp.where(jnp.arange(LANES) % HEAD < HEAD // 2, -1.0, 1.0)
        cosine, sine = step(lambda t: (jnp.cos(t), jnp.sin(t) * side[None, :]), angles)
        all_docs = jnp.concatenate([docs] + [swap(docs, "ctx", e) for e in range(1, ctx)])
        lane = jnp.arange(LANES)[None, :]
        in_docs = (lane >= HEAD) & (lane < HEAD + DOCS)
        folded = (lane >= HEAD + DOCS) & (lane < HEAD + DOCS + 3)

        kv = call(
            functools.partial(kv_body, dp=dp, n=heads),
            [shape((length, LANES), BF16)] * ctx,
            ids,
            x,
            *w_qkv,
            cosine,
            sine,
            in_specs=[SMEM] + [FULL] * (3 + dp),
            flops=4 * length * width * lw,
            name="project_kv",
        )
        wi, wod = gather_weight(after(w_in, kv[0])), gather_weight(after(tall, kv[0]))
        kv = exchange(kv)
        queries = call(
            functools.partial(q_body, dp=dp, n=heads),
            [shape((half, LANES), BF16)] * ctx,
            ids,
            x,
            *w_qkv,
            cosine,
            sine,
            in_specs=[SMEM] + [FULL] * (3 + dp),
            flops=2 * length * width * lw,
            name="project_q",
        )
        queries = exchange(queries)
        marks = step(lambda d: jnp.where(in_docs, lane - HEAD != d[:, None], folded).astype(BF16), all_docs)
        out_grad = arrange(ids, cotangent.reshape(length, width), tp, dp, [0])
        middle = ctx // 2
        groups = ((0, middle), (middle, ctx))
        outs, logs, mixed = [], [], []
        for lo, hi in groups:
            o, log = attend(queries[lo:hi], kv, marks, lo)
            outs.append(o)
            logs.append(log)
            mixed.extend(exchange(o, lo))
        attended = call(
            functools.partial(unpack_body, n=heads),
            [shape((share, lw), BF16)] * tp,
            ids,
            *mixed,
            in_specs=[SMEM] + [FULL] * ctx,
            name="unpack",
        )
    else:
        wi, wod = gather_weight(w_in), gather_weight(tall)
        out_grad = arrange(ids, cotangent.reshape(length, width), tp, dp, [0])
        joined = jnp.concatenate(w_qkv)
        mixed, attend_backward = gathered_attention(
            x, [joined[:, k * lw : (k + 1) * lw] for k in range(3)], angles, docs
        )
        attended = [mixed[j * share : (j + 1) * share] for j in range(tp)]

    received = exchange_tp(attended)
    forwarded, act = forward(received, out_grad, x, wod, wi, tp, dp)
    lows = gather(forwarded[0], "tp")
    act = exchange_tp(act)
    rows, first_grad, pre, grads = backward(forwarded, wod, wi, tp, dp, lw)
    grads = exchange_tp(grads)

    out_sum = GradSum(ids, 1, lambda start, size, *a: sum_over_rows(a[:tp], a[tp:], start, size))
    out_sum.operands = [*act, *[p[share:] for p in lows]]
    rows = gather(after(rows, grads[-1]), "tp")
    pre = exchange_tp([after(p, grads[-1]) for p in pre])

    filler = -(hidden + lw + 8) % (16 * ctx) + 8

    def product(start, size, *a):
        into = sum_over_rows(a[:tp], a[tp : 2 * tp], start, size)
        back = sum_over_rows(a[2 * tp : 3 * tp], a[3 * tp :], start, size)
        terms = sum(p[2 * share : 2 * share + 8, start : start + size].astype(F32) for p in a[3 * tp :])
        return jnp.concatenate([into, back, jnp.pad(terms, ((0, filler - 8), (0, 0)))])

    in_sum = GradSum(ids, 1, product)
    in_sum.operands = [*pre, *lows, *attended, *rows]

    if spread:
        out_sum.begin(width)
        packed = call(
            functools.partial(pack_body, tp=tp, n=heads),
            [shape((half, LANES), BF16)] * ctx,
            ids,
            *grads,
            in_specs=[SMEM] + [FULL] * tp,
            name="pack",
        )
        packed = exchange(packed)
        query_grads, carried = attend_back(
            queries[:middle], packed[:middle], outs[0], kv, logs[0], marks, None, None, 0, False
        )
        out_sum.over_dp()
        in_sum.begin(width)
        pieces = attend_back(
            queries[middle:], packed[middle:], outs[1], kv, logs[1], marks, carried, query_grads, middle, True
        )
        pieces = exchange(pieces)
        out_sum.over_ctx()
        in_sum.over_dp()
        output = place(ids, rows, tp, dp, length, share)
        whole, send, keep = call(
            functools.partial(input_grad_body, dp=dp, n=heads),
            [shape((length, 3 * lw), BF16), shape((half, width), BF16), shape((half, width), F32)],
            ids,
            *pieces,
            *w_qkv,
            cosine,
            sine,
            in_specs=[SMEM] + [FULL] * (ctx + dp + 2),
            flops=6 * length * width * lw,
            name="input_grad",
        )
    else:
        out_sum.begin(width)
        out_sum.over_dp()
        in_sum.begin(width)
        out_sum.over_ctx()
        in_sum.over_dp()
        output = place(ids, rows, tp, dp, length, share)
        whole = attend_backward(jnp.concatenate(grads))
        total = lax.dot_general(whole, joined, NT, preferred_element_type=F32)
        send, keep = total[half:].astype(BF16), total[:half]

    got = swap(send, "tp", 1)
    qkv_sum = GradSum(ids, 0, lambda start, size, l, r: over_rows(l[:, start : start + size], r))
    qkv_sum.operands = [x, whole]
    qkv_sum.begin(width)
    keep, got = scatter(None, keep, "tp", 0, got)
    in_sum.over_ctx()
    (w_out_grad,) = out_sum.columns([width // dp])
    low = step(lambda l, k, f: (f + k + l.astype(F32)).astype(BF16), got, keep, first_grad)
    low = gather(low, "tp")
    qkv_sum.over_dp()
    w_in_grad, w_o_grad, terms = in_sum.rows(hidden, lw)
    input_grad = place(ids, low, tp, dp, length)
    qkv_sum.over_ctx()
    w_q_grad, w_k_grad, w_v_grad = qkv_sum.columns([lw] * 3)
    return (
        output[None],
        input_grad[None],
        w_q_grad,
        w_k_grad,
        w_v_grad,
        w_o_grad,
        w_in_grad,
        w_out_grad,
        terms[0],
        terms[1],
        terms[2],
        terms[3],
    )


def solution(mesh):
    return jax.shard_map(
        body,
        mesh=mesh,
        in_specs=(
            P("dp", "ctx", None),
            P("dp", "ctx"),
            P("dp", "ctx"),
            P("dp", "tp"),
            P("dp", "tp"),
            P("dp", "tp"),
            P("tp", "dp"),
            P("dp", "tp"),
            P("tp", "dp"),
            P("dp"),
            P("dp"),
            P("dp"),
            P("dp"),
            P("dp", "ctx", None),
        ),
        out_specs=(
            P("dp", "ctx", None),
            P("dp", "ctx", None),
            P("dp", "tp"),
            P("dp", "tp"),
            P("dp", "tp"),
            P("tp", "dp"),
            P("dp", "tp"),
            P("tp", "dp"),
            P("dp"),
            P("dp"),
            P("dp"),
            P("dp"),
        ),
        check_vma=False,
    )
```

time: 556 us -> 654 us (1.18)
  waiting for transfers between devices: 175 us -> 285 us
  matrix products: 17.8 us -> 39.2 us
  Pallas kernels: 192 us -> 176 us
  other arithmetic: 24.3 us -> 16.2 us
    ppermute x115 -> x77, waiting for transfers between devices: 175 us -> 285 us  [swap(): return lax.ppermute(value, axis, [(i, i ^ bit) for i in range(n)])]
    dot_general x14 -> x26, matrix products: 17.8 us -> 39.2 us  [over_rows(): lax.dot_general(left, right, (((0,), (0,)), ((), ())), preferred_element_...]
    pallas_call x29 -> x24, Pallas kernels: 192 us -> 176 us  [call(): pl.pallas_call(body, out_shape=out_shape, scratch_shapes=list(scratch), c...]
    convert_element_type x17 -> x3, other arithmetic: 12.5 us -> 5.16 us  [the longest x1 2.71 us: body(): jnp.where(in_docs, lane - HEAD != d[:, None], folded).astype(BF16)]
    add x13 -> x1, other arithmetic: 8.08 us -> 0.83 us  [product(): sum((p[2 * share:2 * share + 8, start:start + size].astype(F32) for p in...]
    ppermute x115 -> x77, starting transfers between devices: 108 us -> 105 us  [swap(): return lax.ppermute(value, axis, [(i, i ^ bit) for i in range(n)])]
    unnamed x286 -> x179, local copies, waits for them, and re-layouts: 18.7 us -> 18.1 us
  transfers between devices with their start and end apart: 115 -> 77, of which waited for: 42 -> 26; matrix products, arithmetic and copies ran while one was open for 9% -> 9% of each run, Pallas kernels for 35% -> 22%
where the time goes in v2:
time: 654 us; the launch traced here: 646 us
  waiting for transfers between devices  285 us (44%)
  Pallas kernels  176 us (27%)
  starting transfers between devices  105 us (16%)
  matrix products  39.2 us (6%)
  local copies, waits for them, and re-layouts  22.4 us (3%)
  other arithmetic  16.2 us (2%)
    ppermute x77, waiting for transfers between devices, swap(): return lax.ppermute(value, axis, [(i, i ^ bit) for i in range(n)])  285 us
    pallas_call x24, Pallas kernels, call(): pl.pallas_call(body, out_shape=out_shape, scratch_shapes=list(scratch), c...  176 us
    ppermute x77, starting transfers between devices, swap(): return lax.ppermute(value, axis, [(i, i ^ bit) for i in range(n)])  105 us
    dot_general x26, matrix products, over_rows(): lax.dot_general(left, right, (((0,), (0,)), ((), ())), preferred_element_...  39.2 us
    unnamed x179, local copies, waits for them, and re-layouts  18.1 us
  transfers between devices with their start and end apart: 77, of which 26 were waited for; matrix products, arithmetic and copies ran while one was open for 9% of the time, Pallas kernels for 22%

profile of v2, /device:TPU:0, one launch (start us, length us, event | category | flops | bytes accessed | tf_op | source)
XLA Modules:
  0.0 646.1 jit_solution(11058230478588173047)
XLA Ops:
  4.0 3.1 collective-permute-start.1
  18.0 3.1 arrange.2.x.refs_5_
  25.0 6.4 collective-permute-done.refs_1_.refs_5_
  32.3 4.9 project_kv.1
  37.2 4.4 project_q.1
  57.8 13.0 %collective-permute-done.6.refs_4_.refs_8_ = bf16[1024,128]{1,0:T(8,128)(2,1)S(1)} collective-permute-done((bf16[1024,128]{1,0:T(8,128)(2,1)}, bf16[1024,128]{1,0:T(8,128)(2,1)S(1)}, u32[]{:S(2)}, u32[]{:S(2)}) %collective-permute-start.6) | collective-permute-done | bytes 262176 | tf_op jit(solution)/shard_map/ppermute | solution.py:37
  73.0 16.2 %attend.2 = (bf16[512,128]{1,0:T(8,128)(2,1)}, bf16[512,128]{1,0:T(8,128)(2,1)}, f32[1024,128]{1,0:T(8,128)}) custom-call(bf16[512,128]{1,0:T(8,128)(2,1)} %get-tuple-element.174.refs_0_, bf16[512,128]{1,0:T(8,128)(2,1)} %copy-done.82, bf16[1024,128]{1,0:T(8,128)(2,1)} %get-tuple-element.125.refs_2_.refs_6_, bf16[1024,128]{1,0:T(8,128)(2,1)} %copy-done.72, ...), custom_call_target="tpu_custom_call" | custom-call | flops 8589934592 | bytes 3145728 | tf_op jit(solution)/shard_map/attend/pallas_call | solution.py:122
  90.5 16.6 %attend.3 = (bf16[512,128]{1,0:T(8,128)(2,1)}, bf16[512,128]{1,0:T(8,128)(2,1)}, f32[1024,128]{1,0:T(8,128)}) custom-call(bf16[512,128]{1,0:T(8,128)(2,1)} %copy-done.80, bf16[512,128]{1,0:T(8,128)(2,1)} %copy-done.81, bf16[1024,128]{1,0:T(8,128)(2,1)} %get-tuple-element.125.refs_2_.refs_6_, bf16[1024,128]{1,0:T(8,128)(2,1)} %copy-done.72, ...), custom_call_target="tpu_custom_call" | custom-call | flops 8589934592 | bytes 3145728 | tf_op jit(solution)/shard_map/attend/pallas_call | solution.py:122
  107.2 6.2 collective-permute-start.11
  114.0 3.9 collective-permute-done.11.refs_2_
  125.4 4.0 collective-permute-done.13.refs_1_
  132.2 4.5 collective-permute-done.15.refs_3_
  140.5 28.3 %collective-permute-done.16.refs_7_.refs_8_ = bf16[1296,512]{1,0:T(8,128)(2,1)S(1)} collective-permute-done((bf16[1296,512]{1,0:T(8,128)(2,1)S(1)}, bf16[1296,512]{1,0:T(8,128)(2,1)S(1)}, u32[]{:S(2)}, u32[]{:S(2)}) %collective-permute-start.16) | collective-permute-done | bytes 1327136 | tf_op jit(solution)/shard_map/ppermute | solution.py:37
  169.2 27.9 %collective-permute-done.18.refs_9_.refs_10_ = bf16[1296,512]{1,0:T(8,128)(2,1)S(1)} collective-permute-done((bf16[1296,512]{1,0:T(8,128)(2,1)S(1)}, bf16[1296,512]{1,0:T(8,128)(2,1)S(1)}, u32[]{:S(2)}, u32[]{:S(2)}) %collective-permute-start.18) | collective-permute-done | bytes 1327136 | tf_op jit(solution)/shard_map/ppermute | solution.py:37
  197.2 21.9 %collective-permute-done.25.refs_17_.refs_18_ = bf16[512,1024]{1,0:T(8,128)(2,1)S(1)} collective-permute-done((bf16[512,1024]{1,0:T(8,128)(2,1)}, bf16[512,1024]{1,0:T(8,128)(2,1)S(1)}, u32[]{:S(2)}, u32[]{:S(2)}) %collective-permute-start.25) | collective-permute-done | bytes 1048608 | tf_op jit(solution)/shard_map/ppermute | solution.py:37
  224.6 13.7 %forward.1 = (bf16[512,1024]{1,0:T(8,128)(2,1)}, bf16[256,1024]{1,0:T(8,128)(2,1)}, bf16[256,4096]{1,0:T(8,128)(2,1)}, f32[256,1024]{1,0:T(8,128)}, f32[256,128]...) custom-call(bf16[256,256]{1,0:T(8,128)(2,1)} %get-tuple-element.144., ...), custom_call_target="tpu_custom_call" | custom-call | flops 4831838208 | bytes 30154752 | tf_op jit(solution)/shard_map/forward/pallas_call | solution.py:122
  240.4 12.7 %backward.1 = (bf16[528,1024]{1,0:T(8,128)(2,1)}, f32[256,1024]{1,0:T(8,128)}, bf16[256,1024]{1,0:T(8,128)(2,1)}, bf16[256,1024]{1,0:T(8,128)(2,1)}, bf16[256,10...) custom-call(bf16[512,1024]{1,0:T(8,128)(2,1)} %get-tuple-element.151, ...), custom_call_target="tpu_custom_call" | custom-call | flops 4831838208 | bytes 29663232 | tf_op jit(solution)/shard_map/backward/pallas_call | solution.py:122
  254.8 22.2 %collective-permute-done.30.refs_3_ = bf16[256,256]{1,0:T(8,128)(2,1)S(1)} collective-permute-done((bf16[256,256]{1,0:T(8,128)(2,1)}, bf16[256,256]{1,0:T(8,128)(2,1)S(1)}, u32[]{:S(2)}, u32[]{:S(2)}) %collective-permute-start.30) | collective-permute-done | bytes 131104 | tf_op jit(solution)/shard_map/ppermute | solution.py:37
  285.4 43.2 %collective-permute-done.41 = bf16[256,1024]{1,0:T(8,128)(2,1)S(1)} collective-permute-done((bf16[256,1024]{1,0:T(8,128)(2,1)S(1)}, bf16[256,1024]{1,0:T(8,128)(2,1)S(1)}, u32[]{:S(2)}, u32[]{:S(2)}) %collective-permute-start.41) | collective-permute-done | bytes 524320 | tf_op jit(solution)/shard_map/ppermute | solution.py:37
  328.6 2.8 fusion.28
  356.9 2.9 fusion.24
  359.8 2.9 fusion.13
  363.3 28.6 %attend_back.2 = (bf16[512,128]{1,0:T(8,128)(2,1)}, bf16[512,128]{1,0:T(8,128)(2,1)}, f32[128,4096]{1,0:T(8,128)}) custom-call(bf16[512,128]{1,0:T(8,128)(2,1)} %get-tuple-element.174.refs_0_, bf16[512,128]{1,0:T(8,128)(2,1)} %copy-done.82, bf16[512,128]{1,0:T(8,128)(2,1)} %get-tuple-element.173.refs_2_, bf16[512,128]{1,0:T(8,128)(2,1)} %copy-done.85, ...), custom_call_target="tpu_custom_call" | custom-call | flops 21474836480 | bytes 5767168 | tf_op jit(solution)/shard_map/attend_back/pallas_call | solution.py:122
  396.2 3.1 split.3
  399.4 3.5 add_convert_fusion
  409.5 29.7 %attend_back.3 = (bf16[1536,128]{1,0:T(8,128)(2,1)}, bf16[1536,128]{1,0:T(8,128)(2,1)}, bf16[1536,128]{1,0:T(8,128)(2,1)}, bf16[1536,128]{1,0:T(8,128)(2,1)}) custom-call(bf16[512,128]{1,0:T(8,128)(2,1)} %copy-done.80, bf16[512,128]{1,0:T(8,128)(2,1)} %copy-done.81, bf16[512,128]{1,0:T(8,128)(2,1)} %collective-permute-done.48.refs_2_, ...), custom_call_target="tpu_custom_call" | custom-call | flops 21474836480 | bytes 7340032 | tf_op jit(solution)/shard_map/attend_back/pallas_call | solution.py:122
  439.4 2.8 collective-permute-start.54
  446.0 26.5 %collective-permute-done.52.refs_2_ = bf16[256,512]{1,0:T(8,128)(2,1)S(1)} collective-permute-done((bf16[256,512]{1,0:T(8,128)(2,1)S(1)}, bf16[256,512]{1,0:T(8,128)(2,1)S(1)}, u32[]{:S(2)}, u32[]{:S(2)}) %collective-permute-start.52) | collective-permute-done | bytes 262176 | tf_op jit(solution)/shard_map/ppermute | solution.py:37
  475.3 3.6 split.4
  479.0 4.5 place.2
  485.1 5.8 input_grad.1
  491.0 3.5 convolution_convert_fusion
  494.5 15.0 %collective-permute-start.58 = (bf16[336,512]{1,0:T(8,128)(2,1)S(1)}, bf16[336,512]{1,0:T(8,128)(2,1)S(1)}, u32[]{:S(2)}, u32[]{:S(2)}) collective-permute-start(bf16[336,512]{1,0:T(8,128)(2,1)S(1)} %copy-done.71), channel_id=1, source_target_pairs={{0,4},{4,0},{8,12},{12,8},{1,5},{5,1},{9,13},{13,9},{2,6},{6,2},{1... | collective-permute-start | bytes 1032200 | tf_op jit(solution)/shard_map/ppermute | solution.py:37
  516.7 8.5 %collective-permute-done.58.refs_0_ = bf16[336,512]{1,0:T(8,128)(2,1)S(1)} collective-permute-done((bf16[336,512]{1,0:T(8,128)(2,1)S(1)}, bf16[336,512]{1,0:T(8,128)(2,1)S(1)}, u32[]{:S(2)}, u32[]{:S(2)}) %collective-permute-start.58) | collective-permute-done | bytes 344096 | tf_op jit(solution)/shard_map/ppermute | solution.py:37
  525.2 10.9 %collective-permute-done.59.refs_1_ = bf16[336,512]{1,0:T(8,128)(2,1)S(1)} collective-permute-done((bf16[336,512]{1,0:T(8,128)(2,1)S(1)}, bf16[336,512]{1,0:T(8,128)(2,1)S(1)}, u32[]{:S(2)}, u32[]{:S(2)}) %collective-permute-start.59) | collective-permute-done | bytes 344096 | tf_op jit(solution)/shard_map/ppermute | solution.py:37
  542.2 18.2 %collective-permute-done.62.refs_2_ = bf16[256,512]{1,0:T(8,128)(2,1)} collective-permute-done((bf16[256,512]{1,0:T(8,128)(2,1)S(1)}, bf16[256,512]{1,0:T(8,128)(2,1)}, u32[]{:S(2)}, u32[]{:S(2)}) %collective-permute-start.62) | collective-permute-done | bytes 262176 | tf_op jit(solution)/shard_map/ppermute | solution.py:37
  566.1 5.4 collective-permute-start.65
  573.8 4.1 collective-permute-done.68.refs_1_
  577.9 3.0 split.5
  580.9 4.0 collective-permute-done.65.refs_1_
  587.1 11.1 %collective-permute-done.66.refs_2_ = bf16[336,512]{1,0:T(8,128)(2,1)S(1)} collective-permute-done((bf16[336,512]{1,0:T(8,128)(2,1)S(1)}, bf16[336,512]{1,0:T(8,128)(2,1)S(1)}, u32[]{:S(2)}, u32[]{:S(2)}) %collective-permute-start.66) | collective-permute-done | bytes 344096 | tf_op jit(solution)/shard_map/ppermute | solution.py:37
  598.3 3.0 collective-permute-start.73
  601.3 3.5 place_rows.1
  606.5 3.8 place.3
  610.3 7.8 %collective-permute-done.72.refs_1_ = bf16[128,768]{1,0:T(8,128)(2,1)S(1)} collective-permute-done((bf16[128,768]{1,0:T(8,128)(2,1)}, bf16[128,768]{1,0:T(8,128)(2,1)S(1)}, u32[]{:S(2)}, u32[]{:S(2)}) %collective-permute-start.72) | collective-permute-done | bytes 196640 | tf_op jit(solution)/shard_map/ppermute | solution.py:37
  621.4 6.8 %collective-permute-start.74 = (bf16[128,768]{1,0:T(8,128)(2,1)}, bf16[128,768]{1,0:T(8,128)(2,1)S(1)}, u32[]{:S(2)}, u32[]{:S(2)}) collective-permute-start(bf16[128,768]{1,0:T(8,128)(2,1)} %merge.5.refs_0_), channel_id=1, source_target_pairs={{0,4},{4,0},{8,12},{12,8},{1,5},{5,1},{9,13},{13,9},{2,6},{6,2},{1... | collective-permute-start | bytes 589832 | tf_op jit(solution)/shard_map/ppermute | solution.py:37
  631.2 4.4 collective-permute-done.74.refs_1_
  635.6 6.3 collective-permute-done.75.refs_2_
  (363 shorter events, 151.7 us)
Async XLA Ops:
  43.6 27.1 %collective-permute-start.6 = (bf16[1024,128]{1,0:T(8,128)(2,1)}, bf16[1024,128]{1,0:T(8,128)(2,1)S(1)}, u32[]{:S(2)}, u32[]{:S(2)}) collective-permute-start(bf16[1024,128]{1,0:T(8,128)(2,1)} %get-tuple-element.133), channel_id=1, source_target_pairs={{0,8},{4,12},{8,0},{12,4},{1,9},{5,13},{9,1},{13,5},{2,10},{6,14},... | collective-permute-start | bytes 786440 | tf_op jit(solution)/shard_map/ppermute | solution.py:37
  45.8 26.5 %collective-permute-start.7 = (bf16[1024,128]{1,0:T(8,128)(2,1)S(1)}, bf16[1024,128]{1,0:T(8,128)(2,1)S(1)}, u32[]{:S(2)}, u32[]{:S(2)}) collective-permute-start(bf16[1024,128]{1,0:T(8,128)(2,1)S(1)} %copy-done.78), channel_id=1, source_target_pairs={{0,12},{4,8},{8,4},{12,0},{1,13},{5,9},{9,5},{13,1},{2,14},{6,10},... | collective-permute-start | bytes 786440 | tf_op jit(solution)/shard_map/ppermute | solution.py:37
  52.3 36.9 %collective-permute-start.8 = (bf16[512,128]{1,0:T(8,128)(2,1)}, bf16[512,128]{1,0:T(8,128)(2,1)S(1)}, u32[]{:S(2)}, u32[]{:S(2)}) collective-permute-start(bf16[512,128]{1,0:T(8,128)(2,1)} %get-tuple-element.136), channel_id=1, source_target_pairs={{0,8},{4,12},{8,0},{12,4},{1,9},{5,13},{9,1},{13,5},{2,10},{6,14},... | collective-permute-start | bytes 393224 | tf_op jit(solution)/shard_map/ppermute | solution.py:37
  54.3 34.9 %collective-permute-start.9 = (bf16[512,128]{1,0:T(8,128)(2,1)}, bf16[512,128]{1,0:T(8,128)(2,1)S(1)}, u32[]{:S(2)}, u32[]{:S(2)}) collective-permute-start(bf16[512,128]{1,0:T(8,128)(2,1)} %get-tuple-element.138), channel_id=1, source_target_pairs={{0,12},{4,8},{8,4},{12,0},{1,13},{5,9},{9,5},{13,1},{2,14},{6,10},... | collective-permute-start | bytes 393224 | tf_op jit(solution)/shard_map/ppermute | solution.py:37
  56.7 81.7 %collective-permute-start.17 = (bf16[1296,512]{1,0:T(8,128)(2,1)S(1)}, bf16[1296,512]{1,0:T(8,128)(2,1)S(1)}, u32[]{:S(2)}, u32[]{:S(2)}) collective-permute-start(bf16[1296,512]{1,0:T(8,128)(2,1)S(1)} %pad_maximum_fusion.refs_6_.refs_7_), channel_id=1, source_target_pairs={{0,2},{1,3},{2,0},{3,1},{4,6},{5,7},{6,4},{7,5},{8,10},{9,11},{10,... | collective-permute-start | bytes 3981320 | tf_op jit(solution)/shard_map/ppermute | solution.py:37
  70.8 67.5 %collective-permute-start.24 = (bf16[512,1024]{1,0:T(8,128)(2,1)}, bf16[512,1024]{1,0:T(8,128)(2,1)}, u32[]{:S(2)}, u32[]{:S(2)}) collective-permute-start(bf16[512,1024]{1,0:T(8,128)(2,1)} %refs_15_), channel_id=1, source_target_pairs={{0,2},{1,3},{2,0},{3,1},{4,6},{5,7},{6,4},{7,5},{8,10},{9,11},{10,... | collective-permute-start | bytes 3145736 | tf_op jit(solution)/shard_map/ppermute | solution.py:37
  136.7 32.0 %collective-permute-start.16 = (bf16[1296,512]{1,0:T(8,128)(2,1)S(1)}, bf16[1296,512]{1,0:T(8,128)(2,1)S(1)}, u32[]{:S(2)}, u32[]{:S(2)}) collective-permute-start(bf16[1296,512]{1,0:T(8,128)(2,1)S(1)} %pad_maximum_fusion.refs_6_.refs_7_), channel_id=1, source_target_pairs={{0,16},{16,0},{1,17},{17,1},{2,18},{18,2},{3,19},{19,3},{4,20},{20... | collective-permute-start | bytes 3981320 | tf_op jit(solution)/shard_map/ppermute | solution.py:37
  138.3 30.5 %collective-permute-start.19 = (bf16[1296,512]{1,0:T(8,128)(2,1)S(1)}, bf16[1296,512]{1,0:T(8,128)(2,1)S(1)}, u32[]{:S(2)}, u32[]{:S(2)}) collective-permute-start(bf16[1296,512]{1,0:T(8,128)(2,1)S(1)} %pad_maximum_fusion.refs_6_.refs_7_), channel_id=1, source_target_pairs={{0,1},{1,0},{2,3},{3,2},{4,5},{5,4},{6,7},{7,6},{8,9},{9,8},{10,11... | collective-permute-start | bytes 3981320 | tf_op jit(solution)/shard_map/ppermute | solution.py:37
  138.4 58.7 %collective-permute-start.18 = (bf16[1296,512]{1,0:T(8,128)(2,1)S(1)}, bf16[1296,512]{1,0:T(8,128)(2,1)S(1)}, u32[]{:S(2)}, u32[]{:S(2)}) collective-permute-start(bf16[1296,512]{1,0:T(8,128)(2,1)S(1)} %collective-permute-done.17.refs_8_.refs_9_), channel_id=1, source_target_pairs={{0,16},{16,0},{1,17},{17,1},{2,18},{18,2},{3,19},{19,3},{4,20},{20... | collective-permute-start | bytes 3981320 | tf_op jit(solution)/shard_map/ppermute | solution.py:37
  138.9 80.2 %collective-permute-start.25 = (bf16[512,1024]{1,0:T(8,128)(2,1)}, bf16[512,1024]{1,0:T(8,128)(2,1)S(1)}, u32[]{:S(2)}, u32[]{:S(2)}) collective-permute-start(bf16[512,1024]{1,0:T(8,128)(2,1)} %collective-permute-done.24.refs_16_.refs_17_), channel_id=1, source_target_pairs={{0,16},{16,0},{1,17},{17,1},{2,18},{18,2},{3,19},{19,3},{4,20},{20... | collective-permute-start | bytes 3145736 | tf_op jit(solution)/shard_map/ppermute | solution.py:37
  140.5 78.7 %collective-permute-start.27 = (bf16[512,1024]{1,0:T(8,128)(2,1)}, bf16[512,1024]{1,0:T(8,128)(2,1)S(1)}, u32[]{:S(2)}, u32[]{:S(2)}) collective-permute-start(bf16[512,1024]{1,0:T(8,128)(2,1)} %collective-permute-done.23.refs_15_.refs_16_), channel_id=1, source_target_pairs={{0,1},{1,0},{2,3},{3,2},{4,5},{5,4},{6,7},{7,6},{8,9},{9,8},{10,11... | collective-permute-start | bytes 3145736 | tf_op jit(solution)/shard_map/ppermute | solution.py:37
  168.7 53.3 %collective-permute-start.20 = (bf16[1296,512]{1,0:T(8,128)(2,1)S(1)}, bf16[1296,512]{1,0:T(8,128)(2,1)S(1)}, u32[]{:S(2)}, u32[]{:S(2)}) collective-permute-start(bf16[1296,512]{1,0:T(8,128)(2,1)S(1)} %collective-permute-done.16.refs_7_.refs_8_), channel_id=1, source_target_pairs={{0,1},{1,0},{2,3},{3,2},{4,5},{5,4},{6,7},{7,6},{8,9},{9,8},{10,11... | collective-permute-start | bytes 3981320 | tf_op jit(solution)/shard_map/ppermute | solution.py:37
  168.7 53.3 %collective-permute-start.21 = (bf16[1296,512]{1,0:T(8,128)(2,1)S(1)}, bf16[1296,512]{1,0:T(8,128)(2,1)S(1)}, u32[]{:S(2)}, u32[]{:S(2)}) collective-permute-start(bf16[1296,512]{1,0:T(8,128)(2,1)S(1)} %collective-permute-done.17.refs_8_.refs_9_), channel_id=1, source_target_pairs={{0,1},{1,0},{2,3},{3,2},{4,5},{5,4},{6,7},{7,6},{8,9},{9,8},{10,11... | collective-permute-start | bytes 3981320 | tf_op jit(solution)/shard_map/ppermute | solution.py:37
  197.2 27.4 %collective-permute-start.22 = (bf16[1296,512]{1,0:T(8,128)(2,1)S(1)}, bf16[1296,512]{1,0:T(8,128)(2,1)}, u32[]{:S(2)}, u32[]{:S(2)}) collective-permute-start(bf16[1296,512]{1,0:T(8,128)(2,1)S(1)} %collective-permute-done.18.refs_9_.refs_10_), channel_id=1, source_target_pairs={{0,1},{1,0},{2,3},{3,2},{4,5},{5,4},{6,7},{7,6},{8,9},{9,8},{10,11... | collective-permute-start | bytes 3981320 | tf_op jit(solution)/shard_map/ppermute | solution.py:37
  238.3 41.0 %collective-permute-start.32 = (bf16[512,1024]{1,0:T(8,128)(2,1)}, bf16[512,1024]{1,0:T(8,128)(2,1)}, u32[]{:S(2)}, u32[]{:S(2)}) collective-permute-start(bf16[512,1024]{1,0:T(8,128)(2,1)} %get-tuple-element.151.refs_0_), channel_id=1, source_target_pairs={{0,2},{1,3},{2,0},{3,1},{4,6},{5,7},{6,4},{7,5},{8,10},{9,11},{10,... | collective-permute-start | bytes 3145736 | tf_op jit(solution)/shard_map/ppermute | solution.py:37
  239.9 44.0 %collective-permute-start.34 = (bf16[512,1024]{1,0:T(8,128)(2,1)}, bf16[512,1024]{1,0:T(8,128)(2,1)S(1)}, u32[]{:S(2)}, u32[]{:S(2)}) collective-permute-start(bf16[512,1024]{1,0:T(8,128)(2,1)} %get-tuple-element.151.refs_0_), channel_id=1, source_target_pairs={{0,1},{1,0},{2,3},{3,2},{4,5},{5,4},{6,7},{7,6},{8,9},{9,8},{10,11... | collective-permute-start | bytes 3145736 | tf_op jit(solution)/shard_map/ppermute | solution.py:37
  239.9 38.9 %collective-permute-start.31 = (bf16[256,1024]{1,0:T(8,128)(2,1)}, bf16[256,1024]{1,0:T(8,128)(2,1)S(1)}, u32[]{:S(2)}, u32[]{:S(2)}) collective-permute-start(bf16[256,1024]{1,0:T(8,128)(2,1)} %get-tuple-element.165), channel_id=1, source_target_pairs={{0,2},{1,3},{2,0},{3,1},{4,6},{5,7},{6,4},{7,5},{8,10},{9,11},{10,... | collective-permute-start | bytes 1572872 | tf_op jit(solution)/shard_map/ppermute | solution.py:37
  253.1 23.9 %collective-permute-start.30 = (bf16[256,256]{1,0:T(8,128)(2,1)}, bf16[256,256]{1,0:T(8,128)(2,1)S(1)}, u32[]{:S(2)}, u32[]{:S(2)}) collective-permute-start(bf16[256,256]{1,0:T(8,128)(2,1)} %get-tuple-element.159), channel_id=1, source_target_pairs={{0,3},{1,2},{2,1},{3,0},{4,7},{5,6},{6,5},{7,4},{8,11},{9,10},{10,... | collective-permute-start | bytes 393224 | tf_op jit(solution)/shard_map/ppermute | solution.py:37
  254.5 29.3 %collective-permute-start.33 = (bf16[256,1024]{1,0:T(8,128)(2,1)S(1)}, bf16[256,1024]{1,0:T(8,128)(2,1)S(1)}, u32[]{:S(2)}, u32[]{:S(2)}) collective-permute-start(bf16[256,1024]{1,0:T(8,128)(2,1)S(1)} %copy-done.64), channel_id=1, source_target_pairs={{0,1},{1,0},{2,3},{3,2},{4,5},{5,4},{6,7},{7,6},{8,9},{9,8},{10,11... | collective-permute-start | bytes 1572872 | tf_op jit(solution)/shard_map/ppermute | solution.py:37
  277.0 66.1 %collective-permute-start.35 = (bf16[256,1024]{1,0:T(8,128)(2,1)}, bf16[256,1024]{1,0:T(8,128)(2,1)S(1)}, u32[]{:S(2)}, u32[]{:S(2)}) collective-permute-start(bf16[256,1024]{1,0:T(8,128)(2,1)} %get-tuple-element.167), channel_id=1, source_target_pairs={{0,3},{1,2},{2,1},{3,0},{4,7},{5,6},{6,5},{7,4},{8,11},{9,10},{10,... | collective-permute-start | bytes 1572872 | tf_op jit(solution)/shard_map/ppermute | solution.py:37
  278.7 70.2 %collective-permute-start.38 = (bf16[256,256]{1,0:T(8,128)(2,1)}, bf16[256,256]{1,0:T(8,128)(2,1)S(1)}, u32[]{:S(2)}, u32[]{:S(2)}) collective-permute-start(bf16[256,256]{1,0:T(8,128)(2,1)} %get-tuple-element.171), channel_id=1, source_target_pairs={{0,2},{1,3},{2,0},{3,1},{4,6},{5,7},{6,4},{7,5},{8,10},{9,11},{10,... | collective-permute-start | bytes 393224 | tf_op jit(solution)/shard_map/ppermute | solution.py:37
  279.3 57.8 %collective-permute-start.44 = (bf16[528,1024]{1,0:T(8,128)(2,1)}, bf16[528,1024]{1,0:T(8,128)(2,1)}, u32[]{:S(2)}, u32[]{:S(2)}) collective-permute-start(bf16[528,1024]{1,0:T(8,128)(2,1)} %get-tuple-element.201.refs_0_), channel_id=1, source_target_pairs={{0,2},{1,3},{2,0},{3,1},{4,6},{5,7},{6,4},{7,5},{8,10},{9,11},{10,... | collective-permute-start | bytes 3244040 | tf_op jit(solution)/shard_map/ppermute | solution.py:37
  283.8 55.6 %collective-permute-start.45 = (bf16[528,1024]{1,0:T(8,128)(2,1)S(1)}, bf16[528,1024]{1,0:T(8,128)(2,1)S(1)}, u32[]{:S(2)}, u32[]{:S(2)}) collective-permute-start(bf16[528,1024]{1,0:T(8,128)(2,1)S(1)} %copy-done.17), channel_id=1, source_target_pairs={{0,1},{1,0},{2,3},{3,2},{4,5},{5,4},{6,7},{7,6},{8,9},{9,8},{10,11... | collective-permute-start | bytes 3244040 | tf_op jit(solution)/shard_map/ppermute | solution.py:37
  283.9 44.8 %collective-permute-start.41 = (bf16[256,1024]{1,0:T(8,128)(2,1)S(1)}, bf16[256,1024]{1,0:T(8,128)(2,1)S(1)}, u32[]{:S(2)}, u32[]{:S(2)}) collective-permute-start(bf16[256,1024]{1,0:T(8,128)(2,1)S(1)} %copy-done.65), channel_id=1, source_target_pairs={{0,2},{1,3},{2,0},{3,1},{4,6},{5,7},{6,4},{7,5},{8,10},{9,11},{10,... | collective-permute-start | bytes 1572872 | tf_op jit(solution)/shard_map/ppermute | solution.py:37
  343.0 48.9 %collective-permute-start.46 = (bf16[528,1024]{1,0:T(8,128)(2,1)}, bf16[528,1024]{1,0:T(8,128)(2,1)}, u32[]{:S(2)}, u32[]{:S(2)}) collective-permute-start(bf16[528,1024]{1,0:T(8,128)(2,1)} %collective-permute-done.44.refs_1_), channel_id=1, source_target_pairs={{0,1},{1,0},{2,3},{3,2},{4,5},{5,4},{6,7},{7,6},{8,9},{9,8},{10,11... | collective-permute-start | bytes 3244040 | tf_op jit(solution)/shard_map/ppermute | solution.py:37
  345.0 51.2 %collective-permute-start.37 = (bf16[1024,512]{1,0:T(8,128)(2,1)}, bf16[1024,512]{1,0:T(8,128)(2,1)}, u32[]{:S(2)}, u32[]{:S(2)}) collective-permute-start(bf16[1024,512]{1,0:T(8,128)(2,1)} %add_convert_fusion.1), channel_id=1, source_target_pairs={{0,16},{16,0},{1,17},{17,1},{2,18},{18,2},{3,19},{19,3},{4,20},{20... | collective-permute-start | bytes 3145736 | tf_op jit(solution)/shard_map/ppermute | solution.py:37
  353.0 56.4 %collective-permute-start.48 = (bf16[512,128]{1,0:T(8,128)(2,1)}, bf16[512,128]{1,0:T(8,128)(2,1)}, u32[]{:S(2)}, u32[]{:S(2)}) collective-permute-start(bf16[512,128]{1,0:T(8,128)(2,1)} %get-tuple-element.189), channel_id=1, source_target_pairs={{0,8},{4,12},{8,0},{12,4},{1,9},{5,13},{9,1},{13,5},{2,10},{6,14},... | collective-permute-start | bytes 393224 | tf_op jit(solution)/shard_map/ppermute | solution.py:37
  354.6 54.9 %collective-permute-start.49 = (bf16[512,128]{1,0:T(8,128)(2,1)}, bf16[512,128]{1,0:T(8,128)(2,1)}, u32[]{:S(2)}, u32[]{:S(2)}) collective-permute-start(bf16[512,128]{1,0:T(8,128)(2,1)} %get-tuple-element.190), channel_id=1, source_target_pairs={{0,12},{4,8},{8,4},{12,0},{1,13},{5,9},{9,5},{13,1},{2,14},{6,10},... | collective-permute-start | bytes 393224 | tf_op jit(solution)/shard_map/ppermute | solution.py:37
  404.0 71.3 %collective-permute-start.47 = (bf16[1344,512]{1,0:T(8,128)(2,1)}, bf16[1344,512]{1,0:T(8,128)(2,1)}, u32[]{:S(2)}, u32[]{:S(2)}) collective-permute-start(bf16[1344,512]{1,0:T(8,128)(2,1)} %fusion.1), channel_id=1, source_target_pairs={{0,16},{16,0},{1,17},{17,1},{2,18},{18,2},{3,19},{19,3},{4,20},{20... | collective-permute-start | bytes 4128776 | tf_op jit(solution)/shard_map/ppermute | solution.py:37
  407.3 34.8 %collective-permute-start.50 = (bf16[256,512]{1,0:T(8,128)(2,1)S(1)}, bf16[256,512]{1,0:T(8,128)(2,1)S(1)}, u32[]{:S(2)}, u32[]{:S(2)}) collective-permute-start(bf16[256,512]{1,0:T(8,128)(2,1)S(1)} %copy-done.77), channel_id=1, source_target_pairs={{0,4},{4,0},{8,12},{12,8},{1,5},{5,1},{9,13},{13,9},{2,6},{6,2},{1... | collective-permute-start | bytes 786440 | tf_op jit(solution)/shard_map/ppermute | solution.py:37
  407.4 36.3 %collective-permute-start.51 = (bf16[256,512]{1,0:T(8,128)(2,1)S(1)}, bf16[256,512]{1,0:T(8,128)(2,1)S(1)}, u32[]{:S(2)}, u32[]{:S(2)}) collective-permute-start(bf16[256,512]{1,0:T(8,128)(2,1)S(1)} %copy-done.76), channel_id=1, source_target_pairs={{0,8},{4,12},{8,0},{12,4},{1,9},{5,13},{9,1},{13,5},{2,10},{6,14},... | collective-permute-start | bytes 786440 | tf_op jit(solution)/shard_map/ppermute | solution.py:37
  439.2 44.3 %collective-permute-start.53 = (bf16[1536,128]{1,0:T(8,128)(2,1)}, bf16[1536,128]{1,0:T(8,128)(2,1)S(1)}, u32[]{:S(2)}, u32[]{:S(2)}) collective-permute-start(bf16[1536,128]{1,0:T(8,128)(2,1)} %get-tuple-element.204), channel_id=1, source_target_pairs={{0,4},{4,0},{8,12},{12,8},{1,5},{5,1},{9,13},{13,9},{2,6},{6,2},{1... | collective-permute-start | bytes 1179656 | tf_op jit(solution)/shard_map/ppermute | solution.py:37
  439.4 44.1 %collective-permute-start.54 = (bf16[1536,128]{1,0:T(8,128)(2,1)}, bf16[1536,128]{1,0:T(8,128)(2,1)S(1)}, u32[]{:S(2)}, u32[]{:S(2)}) collective-permute-start(bf16[1536,128]{1,0:T(8,128)(2,1)} %get-tuple-element.205), channel_id=1, source_target_pairs={{0,8},{4,12},{8,0},{12,4},{1,9},{5,13},{9,1},{13,5},{2,10},{6,14},... | collective-permute-start | bytes 1179656 | tf_op jit(solution)/shard_map/ppermute | solution.py:37
  442.2 41.4 %collective-permute-start.55 = (bf16[1536,128]{1,0:T(8,128)(2,1)}, bf16[1536,128]{1,0:T(8,128)(2,1)S(1)}, u32[]{:S(2)}, u32[]{:S(2)}) collective-permute-start(bf16[1536,128]{1,0:T(8,128)(2,1)} %get-tuple-element.206), channel_id=1, source_target_pairs={{0,12},{4,8},{8,4},{12,0},{1,13},{5,9},{9,5},{13,1},{2,14},{6,10},... | collective-permute-start | bytes 1179656 | tf_op jit(solution)/shard_map/ppermute | solution.py:37
  443.7 28.8 %collective-permute-start.52 = (bf16[256,512]{1,0:T(8,128)(2,1)S(1)}, bf16[256,512]{1,0:T(8,128)(2,1)S(1)}, u32[]{:S(2)}, u32[]{:S(2)}) collective-permute-start(bf16[256,512]{1,0:T(8,128)(2,1)S(1)} %copy-done.75), channel_id=1, source_target_pairs={{0,12},{4,8},{8,4},{12,0},{1,13},{5,9},{9,5},{13,1},{2,14},{6,10},... | collective-permute-start | bytes 786440 | tf_op jit(solution)/shard_map/ppermute | solution.py:37
  494.5 30.7 %collective-permute-start.58 = (bf16[336,512]{1,0:T(8,128)(2,1)S(1)}, bf16[336,512]{1,0:T(8,128)(2,1)S(1)}, u32[]{:S(2)}, u32[]{:S(2)}) collective-permute-start(bf16[336,512]{1,0:T(8,128)(2,1)S(1)} %copy-done.71), channel_id=1, source_target_pairs={{0,4},{4,0},{8,12},{12,8},{1,5},{5,1},{9,13},{13,9},{2,6},{6,2},{1... | collective-permute-start | bytes 1032200 | tf_op jit(solution)/shard_map/ppermute | solution.py:37
  509.4 26.7 %collective-permute-start.59 = (bf16[336,512]{1,0:T(8,128)(2,1)S(1)}, bf16[336,512]{1,0:T(8,128)(2,1)S(1)}, u32[]{:S(2)}, u32[]{:S(2)}) collective-permute-start(bf16[336,512]{1,0:T(8,128)(2,1)S(1)} %copy-done.70), channel_id=1, source_target_pairs={{0,8},{4,12},{8,0},{12,4},{1,9},{5,13},{9,1},{13,5},{2,10},{6,14},... | collective-permute-start | bytes 1032200 | tf_op jit(solution)/shard_map/ppermute | solution.py:37
  513.5 49.6 %collective-permute-start.57 = (bf16[256,1024]{1,0:T(8,128)(2,1)}, bf16[256,1024]{1,0:T(8,128)(2,1)S(1)}, u32[]{:S(2)}, u32[]{:S(2)}) collective-permute-start(bf16[256,1024]{1,0:T(8,128)(2,1)} %add_convert_fusion.3), channel_id=1, source_target_pairs={{0,2},{1,3},{2,0},{3,1},{4,6},{5,7},{6,4},{7,5},{8,10},{9,11},{10,... | collective-permute-start | bytes 1572872 | tf_op jit(solution)/shard_map/ppermute | solution.py:37
  514.0 24.3 %collective-permute-start.60 = (bf16[336,512]{1,0:T(8,128)(2,1)S(1)}, bf16[336,512]{1,0:T(8,128)(2,1)S(1)}, u32[]{:S(2)}, u32[]{:S(2)}) collective-permute-start(bf16[336,512]{1,0:T(8,128)(2,1)S(1)} %copy-done.69), channel_id=1, source_target_pairs={{0,12},{4,8},{8,4},{12,0},{1,13},{5,9},{9,5},{13,1},{2,14},{6,10},... | collective-permute-start | bytes 1032200 | tf_op jit(solution)/shard_map/ppermute | solution.py:37
  515.7 26.5 %collective-permute-start.61 = (bf16[256,512]{1,0:T(8,128)(2,1)S(1)}, bf16[256,512]{1,0:T(8,128)(2,1)}, u32[]{:S(2)}, u32[]{:S(2)}) collective-permute-start(bf16[256,512]{1,0:T(8,128)(2,1)S(1)} %copy-done.30), channel_id=1, source_target_pairs={{0,4},{4,0},{8,12},{12,8},{1,5},{5,1},{9,13},{13,9},{2,6},{6,2},{1... | collective-permute-start | bytes 786440 | tf_op jit(solution)/shard_map/ppermute | solution.py:37
  525.2 35.3 %collective-permute-start.62 = (bf16[256,512]{1,0:T(8,128)(2,1)S(1)}, bf16[256,512]{1,0:T(8,128)(2,1)}, u32[]{:S(2)}, u32[]{:S(2)}) collective-permute-start(bf16[256,512]{1,0:T(8,128)(2,1)S(1)} %copy-done.30), channel_id=1, source_target_pairs={{0,8},{4,12},{8,0},{12,4},{1,9},{5,13},{9,1},{13,5},{2,10},{6,14},... | collective-permute-start | bytes 786440 | tf_op jit(solution)/shard_map/ppermute | solution.py:37
  536.1 24.3 %collective-permute-start.63 = (bf16[256,512]{1,0:T(8,128)(2,1)S(1)}, bf16[256,512]{1,0:T(8,128)(2,1)}, u32[]{:S(2)}, u32[]{:S(2)}) collective-permute-start(bf16[256,512]{1,0:T(8,128)(2,1)S(1)} %copy-done.30), channel_id=1, source_target_pairs={{0,12},{4,8},{8,4},{12,0},{1,13},{5,9},{9,5},{13,1},{2,14},{6,10},... | collective-permute-start | bytes 786440 | tf_op jit(solution)/shard_map/ppermute | solution.py:37
  539.1 34.7 %collective-permute-start.64 = (bf16[512,768]{1,0:T(8,128)(2,1)}, bf16[512,768]{1,0:T(8,128)(2,1)}, u32[]{:S(2)}, u32[]{:S(2)}) collective-permute-start(bf16[512,768]{1,0:T(8,128)(2,1)} %convolution_convert_fusion), channel_id=1, source_target_pairs={{0,16},{16,0},{1,17},{17,1},{2,18},{18,2},{3,19},{19,3},{4,20},{20... | collective-permute-start | bytes 2359304 | tf_op jit(solution)/shard_map/ppermute | solution.py:37
  571.5 26.8 %collective-permute-start.66 = (bf16[336,512]{1,0:T(8,128)(2,1)S(1)}, bf16[336,512]{1,0:T(8,128)(2,1)S(1)}, u32[]{:S(2)}, u32[]{:S(2)}) collective-permute-start(bf16[336,512]{1,0:T(8,128)(2,1)S(1)} %copy-done.25), channel_id=1, source_target_pairs={{0,8},{4,12},{8,0},{12,4},{1,9},{5,13},{9,1},{13,5},{2,10},{6,14},... | collective-permute-start | bytes 1032200 | tf_op jit(solution)/shard_map/ppermute | solution.py:37
  572.3 26.0 %collective-permute-start.67 = (bf16[336,512]{1,0:T(8,128)(2,1)S(1)}, bf16[336,512]{1,0:T(8,128)(2,1)S(1)}, u32[]{:S(2)}, u32[]{:S(2)}) collective-permute-start(bf16[336,512]{1,0:T(8,128)(2,1)S(1)} %copy-done.25), channel_id=1, source_target_pairs={{0,12},{4,8},{8,4},{12,0},{1,13},{5,9},{9,5},{13,1},{2,14},{6,10},... | collective-permute-start | bytes 1032200 | tf_op jit(solution)/shard_map/ppermute | solution.py:37
  573.8 31.0 %collective-permute-start.69 = (bf16[256,1024]{1,0:T(8,128)(2,1)S(1)}, bf16[256,1024]{1,0:T(8,128)(2,1)S(1)}, u32[]{:S(2)}, u32[]{:S(2)}) collective-permute-start(bf16[256,1024]{1,0:T(8,128)(2,1)S(1)} %add_convert_fusion.2.refs_0_), channel_id=1, source_target_pairs={{0,1},{1,0},{2,3},{3,2},{4,5},{5,4},{6,7},{7,6},{8,9},{9,8},{10,11... | collective-permute-start | bytes 1572872 | tf_op jit(solution)/shard_map/ppermute | solution.py:37
  577.9 27.0 %collective-permute-start.70 = (bf16[256,1024]{1,0:T(8,128)(2,1)S(1)}, bf16[256,1024]{1,0:T(8,128)(2,1)S(1)}, u32[]{:S(2)}, u32[]{:S(2)}) collective-permute-start(bf16[256,1024]{1,0:T(8,128)(2,1)S(1)} %collective-permute-done.68.refs_1_), channel_id=1, source_target_pairs={{0,1},{1,0},{2,3},{3,2},{4,5},{5,4},{6,7},{7,6},{8,9},{9,8},{10,11... | collective-permute-start | bytes 1572872 | tf_op jit(solution)/shard_map/ppermute | solution.py:37
  584.9 25.4 %collective-permute-start.71 = (bf16[128,768]{1,0:T(8,128)(2,1)}, bf16[128,768]{1,0:T(8,128)(2,1)S(1)}, u32[]{:S(2)}, u32[]{:S(2)}) collective-permute-start(bf16[128,768]{1,0:T(8,128)(2,1)} %get-tuple-element.225), channel_id=1, source_target_pairs={{0,4},{4,0},{8,12},{12,8},{1,5},{5,1},{9,13},{13,9},{2,6},{6,2},{1... | collective-permute-start | bytes 589832 | tf_op jit(solution)/shard_map/ppermute | solution.py:37
  (116 other events, 1460.1 us)

commit v3 on v2

--- a/solution.py
+++ b/solution.py
@@ -45,26 +45,16 @@
     return parts
 
 
-def gather_weight(value):
-    tp, dp = lax.axis_size("tp"), lax.axis_size("dp")
-    parts = {(0, 0): value}
-
-    def double(axis, bit):
-        for d, f in list(parts):
-            key = (d | bit, f) if axis == "tp" else (d, f | bit)
-            parts[key] = swap(parts[d, f], axis, bit)
-
-    bit = tp >> 1
+def chips(value):
+    parts, bit = [value], lax.axis_size("tp") >> 1
     while bit > 1:
-        double("tp", bit)
+        parts = parts + [swap(p, "tp", bit) for p in parts]
         bit >>= 1
-    bit = dp >> 1
-    while bit:
-        double("dp", bit)
-        bit >>= 1
-    if tp > 1:
-        double("tp", 1)
-    return [parts[d, f] for d in order(tp) for f in order(dp)]
+    return parts
+
+
+def cores(parts):
+    return parts + [swap(p, "tp", 1) for p in parts]
 
 
 def after(value, *others):
@@ -76,6 +66,10 @@
 
 def in_line(value):
     return after(value, LINE[-1]) if LINE else value
+
+
+def due(*values):
+    LINE[:] = [after(LINE[-1], *jax.tree.leaves(values))]
 
 
 def step(function, *args):
@@ -106,9 +100,6 @@
 
 
 def call(body, out_shape, *args, grid=None, in_specs=None, out_specs=None, scratch=(), flops=0, trans=0, name=None):
-    size = sum(a.size * a.dtype.itemsize for a in args)
-    outs = out_shape if isinstance(out_shape, (list, tuple)) else [out_shape]
-    size += sum(o.size * o.dtype.itemsize for o in outs)
     extra = {}
     if grid is not None:
         extra["grid"] = grid
@@ -124,7 +115,7 @@
         out_shape=out_shape,
         scratch_shapes=list(scratch),
         compiler_params=pltpu.CompilerParams(vmem_limit_bytes=VMEM_LIMIT),
-        cost_estimate=pl.CostEstimate(flops=int(flops), bytes_accessed=int(size), transcendentals=int(trans)),
+        cost_estimate=pl.CostEstimate(flops=int(flops), bytes_accessed=1 << 24, transcendentals=int(trans)),
         name=name,
         **extra,
     )(*args)
@@ -189,27 +180,106 @@
     )
 
 
-def split_body(ids, got, keep, *outs):
-    n, rows = len(outs), outs[0].shape[0]
-    for e in range(n):
-        at = pl.multiple_of((ids[1] ^ e) * rows, rows)
-        total = keep[pl.ds(at, rows), :] + got[pl.ds(at, rows), :].astype(F32)
-        outs[e][...] = total.astype(outs[e].dtype)
-
-
-def merge_body(own, *refs):
-    *others, out = refs
-    total = own[...]
-    for other in others:
-        total = total + other[...].astype(F32)
-    out[...] = total.astype(BF16)
+def halve_body(ids, got, keep, send, left, *, bit):
+    rows = send.shape[0]
+    mine = (ids[1] // bit) % 2
+    at = pl.multiple_of((1 - mine) * rows, rows)
+    send[...] = (keep[pl.ds(at, rows), :] + got[pl.ds(at, rows), :].astype(F32)).astype(BF16)
+    at = pl.multiple_of(mine * rows, rows)
+    left[...] = keep[pl.ds(at, rows), :] + got[pl.ds(at, rows), :].astype(F32)
+
+
+def merge_body(got, keep, out):
+    out[...] = (keep[...] + got[...].astype(F32)).astype(BF16)
+
+
+def row_of(who, n, rows):
+    at, bit, size = 0, 1, n * rows
+    while bit < n:
+        size //= 2
+        at = at + ((who // bit) % 2) * size
+        bit *= 2
+    return pl.multiple_of(at, rows)
+
+
+def product_body(*refs, tp):
+    left, right = refs[:tp], refs[tp : 2 * tp]
+    send, keep, tall, wide = refs[2 * tp :]
+    share = left[0].shape[0]
+    for j in range(tp):
+        tall[j * share : (j + 1) * share, :] = left[j][...]
+        wide[j * share : (j + 1) * share, :] = right[j][...]
+    mid = send.shape[1]
+    for c in spans(tall.shape[1], CB):
+        total = over_rows(tall[:, c], wide[...])
+        keep[c, :] = total[:, :mid]
+        send[c, :] = total[:, mid:].astype(BF16)
+
+
+def products_body(*refs, tp):
+    pre, hidden, attended, rows = (refs[k * tp : (k + 1) * tp] for k in range(4))
+    send, keep, tall, wide, thin, broad = refs[4 * tp :]
+    share = pre[0].shape[0]
+    mid = send.shape[1]
+    terms = None
+    for j in range(tp):
+        there = slice(j * share, (j + 1) * share)
+        tall[there, :] = pre[j][...]
+        wide[there, :] = hidden[j][...]
+        thin[there, :] = attended[j][...]
+        broad[there, :] = rows[j][:share, :]
+        term = rows[j][share:, :].astype(F32)
+        terms = term if terms is None else terms + term
+    at = 0
+    for left, right in ((tall, wide), (thin, broad)):
+        for c in spans(left.shape[1], CB):
+            total = over_rows(left[:, c], right[...])
+            size = total.shape[0]
+            keep[at : at + size, :] = total[:, :mid]
+            send[at : at + size, :] = total[:, mid:].astype(BF16)
+            at += size
+    keep[at : at + 16, :] = terms[:, :mid]
+    send[at : at + 16, :] = terms[:, mid:].astype(BF16)
+    at += 16
+    if at < send.shape[0]:
+        keep[at:, :] = jnp.zeros((send.shape[0] - at, mid), F32)
+        send[at:, :] = jnp.zeros((send.shape[0] - at, mid), BF16)
+
+
+def product(left, right):
+    tp, (share, m), n = len(left), left[0].shape, right[0].shape[1]
+    return call(
+        functools.partial(product_body, tp=tp),
+        [shape((m, n // 2), BF16), shape((m, n // 2), F32)],
+        *left,
+        *right,
+        scratch=[pltpu.VMEM((tp * share, m), BF16), pltpu.VMEM((tp * share, n), BF16)],
+        flops=2 * tp * share * m * n,
+        name="product",
+    )
+
+
+def products(pre, hidden, attended, rows, ctx):
+    tp, (share, m), n, lw = len(pre), pre[0].shape, hidden[0].shape[1], attended[0].shape[1]
+    total = -(-(m + lw + 16) // (16 * ctx)) * 16 * ctx
+    return call(
+        functools.partial(products_body, tp=tp),
+        [shape((total, n // 2), BF16), shape((total, n // 2), F32)],
+        *pre,
+        *hidden,
+        *attended,
+        *rows,
+        scratch=[pltpu.VMEM((tp * share, w), BF16) for w in (m, n, lw, n)],
+        flops=2 * tp * share * (m + lw) * n,
+        name="products",
+    )
 
 
 def place_columns_body(ids, *refs, n, widths):
     parts, outs = refs[:n], refs[n:]
     rows = parts[0].shape[0]
-    for e, part in enumerate(parts):
-        at = pl.multiple_of((ids[1] ^ e) * rows, rows)
+    for e, part in zip(order(n), parts):
+        at = row_of(ids[1] ^ e, n, rows)
         lane = 0
         for out, width in zip(outs, widths):
             out[pl.ds(at, rows), :] = part[:, lane : lane + width].astype(F32)
@@ -219,8 +289,8 @@
 def place_rows_body(ids, *refs, n):
     parts, (first, second, terms, whole) = refs[:n], refs[n:]
     rows = parts[0].shape[0]
-    for e, part in enumerate(parts):
-        at = pl.multiple_of((ids[1] ^ e) * rows, rows)
+    for e, part in zip(order(n), parts):
+        at = row_of(ids[1] ^ e, n, rows)
         whole[pl.ds(at, rows), :] = part[...].astype(F32)
     hidden, middle = first.shape[1], second.shape[0]
     first[...] = whole[:hidden, :].T
@@ -229,34 +299,31 @@
 
 
 class GradSum:
-    def __init__(self, ids, dim, product):
-        self.ids, self.dim, self.product = ids, dim, product
-
-    def begin(self, width):
-        mid = width // 2
-        send = step(lambda *a: self.product(mid, mid, *a).astype(BF16), *self.operands)
+    def __init__(self, ids, dim, send, keep):
+        self.ids, self.dim, self.keep = ids, dim, keep
         self.got = swap(send, "dp", 1)
-        self.keep = step(lambda *a: self.product(0, mid, *a), *self.operands)
-
-    def over_dp(self):
-        keep, got = scatter(None, self.keep, "dp", self.dim, self.got)
+        self.bit = 0
+
+    def next(self):
         n = lax.axis_size("ctx")
-        rows, cols = keep.shape
-        block = rows // n
-        self.own, *sends = call(
-            split_body,
-            [shape((block, cols), F32)] + [shape((block, cols), BF16)] * (n - 1),
-            self.ids,
-            got,
-            keep,
-            in_specs=[SMEM, FULL, FULL],
-            name="split",
-        )
-        self.parts = [swap(sends[e - 1], "ctx", e) for e in range(1, n)]
-
-    def over_ctx(self):
-        own = call(merge_body, shape(self.own.shape, BF16), self.own, *self.parts, name="merge")
-        self.parts = [own] + [swap(own, "ctx", e) for e in range(1, lax.axis_size("ctx"))]
+        if self.bit == 0:
+            self.keep, self.got = scatter(None, self.keep, "dp", self.dim, self.got)
+        self.bit = max(1, 2 * self.bit)
+        rows, cols = self.keep.shape
+        if self.bit < n:
+            send, self.keep = call(
+                functools.partial(halve_body, bit=self.bit),
+                [shape((rows // 2, cols), BF16), shape((rows // 2, cols), F32)],
+                self.ids,
+                self.got,
+                self.keep,
+                in_specs=[SMEM, FULL, FULL],
+                name="halve",
+            )
+            self.got = swap(send, "ctx", self.bit)
+        else:
+            own = call(merge_body, shape((rows, cols), BF16), self.got, self.keep, name="merge")
+            self.parts = gather(own, "ctx")
 
     def columns(self, widths):
         n = len(self.parts)
@@ -288,14 +355,6 @@
     return lax.dot_general(left, right, (((0,), (0,)), ((), ())), preferred_element_type=F32)
 
 
-def sum_over_rows(left, right, start, size):
-    total = None
-    for l, r in zip(left, right):
-        term = over_rows(l, r[: l.shape[0], start : start + size])
-        total = term if total is None else total + term
-    return total
-
-
 def swap_halves(tile, lane):
     return jnp.where(lane % HEAD < HEAD // 2, pltpu.roll(tile, LANES - HEAD // 2, 1), pltpu.roll(tile, HEAD // 2, 1))
 
@@ -321,53 +380,38 @@
     return total
 
 
-def kv_body(ids, x, *refs, dp, n):
+def project_body(ids, x, *refs, dp, n):
     ws = refs[:dp]
     cosine, sine = refs[dp], refs[dp + 1]
     outs = refs[dp + 2 :]
     me = ids[1]
     step = 256
+    length = x.shape[0]
+    half = length // 2
     width = n * HEAD
-    lane = lax.broadcasted_iota(jnp.int32, (step, LANES), 1)
-    for i in range(x.shape[0] // step):
-        rows = slice(i * step, (i + 1) * step)
-        tokens = x[rows, :]
-        both = rows_dot(tokens, ws, width, 2 * width)
-        heads = []
-        for t in range(n // 2):
-            kt = both[:, t * LANES : (t + 1) * LANES]
-            vt = both[:, width + t * LANES : width + (t + 1) * LANES]
-            kt = kt * cosine[rows, :] + swap_halves(kt, lane) * sine[rows, :]
-            heads.append(jnp.where(lane < HEAD, kt, turn(vt)))
-            heads.append(jnp.where(lane < HEAD, turn(kt), vt))
-        for e in range(n):
-            outs[e][rows, :] = pick(me, heads, e).astype(BF16)
-
-
-def q_body(ids, x, *refs, dp, n):
-    ws = refs[:dp]
-    cosine, sine = refs[dp], refs[dp + 1]
-    outs = refs[dp + 2 :]
-    me = ids[1]
-    step = 256
-    half = outs[0].shape[0]
     lane = lax.broadcasted_iota(jnp.int32, (step, LANES), 1)
     for i in range(half // step):
         sides = []
         for h in range(2):
             rows = slice(h * half + i * step, h * half + (i + 1) * step)
-            query = rows_dot(x[rows, :], ws, 0, n * HEAD)
-            heads = []
+            total = rows_dot(x[rows, :], ws, 0, 3 * width)
+            tiles = [total[:, t * LANES : (t + 1) * LANES] for t in range(3 * n // 2)]
+            tiles = [
+                tile * cosine[rows, :] + swap_halves(tile, lane) * sine[rows, :] if t < n else tile
+                for t, tile in enumerate(tiles)
+            ]
+            heads, pairs = [], []
             for t in range(n // 2):
-                qt = query[:, t * LANES : (t + 1) * LANES]
-                qt = qt * cosine[rows, :] + swap_halves(qt, lane) * sine[rows, :]
-                qt = qt * (HEAD**-0.5 * LOG2E)
-                other = turn(qt)
-                heads.extend([qt, other] if h == 0 else [other, qt])
+                qt, kt, vt = tiles[t] * (HEAD**-0.5 * LOG2E), tiles[n // 2 + t], tiles[n + t]
+                pairs.append(jnp.where(lane < HEAD, kt, turn(vt)))
+                pairs.append(jnp.where(lane < HEAD, turn(kt), vt))
+                heads.extend([qt, turn(qt)] if h == 0 else [turn(qt), qt])
             sides.append(heads)
+            for e in range(n):
+                outs[e][rows, :] = pick(me, pairs, e).astype(BF16)
         packed = [jnp.where(lane < HEAD, lo, hi) for lo, hi in zip(*sides)]
         for e in range(n):
-            outs[e][i * step : (i + 1) * step, :] = pick(me, packed, e).astype(BF16)
+            outs[e][length + i * step : length + (i + 1) * step, :] = pick(me, packed, e).astype(BF16)
 
 
 def unpack_pairs(me, packed, n, h, lane):
@@ -417,12 +461,12 @@
 
 
 def fill_keys(kv, marks, ka, va):
-    size = kv[0].shape[0]
+    size = kv[0].shape[0] // 3 * 2
     lane = lax.broadcasted_iota(jnp.int32, (size, LANES), 1)
     ones = jnp.where(lane < 3, 1.0, 0.0).astype(BF16)
     for e, ref in enumerate(kv):
         rows = slice(e * size, (e + 1) * size)
-        both = ref[...]
+        both = ref[:size, :]
         ka[rows, :] = jnp.where(lane < HEAD, both, marks[rows, :])
         va[rows, :] = jnp.where(lane < HEAD, ones, both)
 
@@ -441,18 +485,18 @@
 
 
 def attend_body(*refs, m, n, first):
-    queries, kv = refs[:m], refs[m : m + n]
-    marks = refs[m + n]
-    outs, lse = refs[m + n + 1 : 2 * m + n + 1], refs[2 * m + n + 1]
-    qs, ka, va, os = refs[2 * m + n + 2 :]
-    half, length = queries[0].shape[0], kv[0].shape[0]
+    kv, marks = refs[:n], refs[n]
+    outs, lse = refs[n + 1 : n + 1 + m], refs[n + 1 + m]
+    qs, ka, va, os = refs[n + 2 + m :]
+    half = kv[0].shape[0] // 3
+    length = 2 * half
     i = pl.program_id(0)
 
     @pl.when(i == 0)
     def _():
         fill_keys(kv, marks, ka, va)
         for e in range(m):
-            qs[e * half : (e + 1) * half, :] = queries[e][...]
+            qs[e * half : (e + 1) * half, :] = kv[first + e][length:, :]
 
     at, h, token = block_of(i, half, length, first)
     lane = lax.broadcasted_iota(jnp.int32, (BQ, LANES), 1)
@@ -485,10 +529,11 @@
             outs[e][...] = os[e * half : (e + 1) * half, :].astype(BF16)
 
 
-def attend(queries, kv, marks, first):
-    m, n, (half, _), length = len(queries), len(kv), queries[0].shape, kv[0].shape[0]
+def attend(kv, marks, first, m):
+    n, half = len(kv), kv[0].shape[0] // 3
+    length = 2 * half
     steps = m * 2 * half // BQ
-    args = [*queries, *kv, marks]
+    args = [*kv, marks]
     outs = [shape((half, LANES), BF16)] * m + [shape((m * half, LANES), F32)]
     out = call(
         functools.partial(attend_body, m=m, n=n, first=first),
@@ -518,9 +563,9 @@
 
 
 def attend_back_body(*refs, m, n, first, start, end):
-    queries, grads, outs = (refs[k * m : (k + 1) * m] for k in range(3))
-    kv, lse, marks = refs[3 * m : 3 * m + n], refs[3 * m + n], refs[3 * m + n + 1]
-    at = 3 * m + n + 2
+    grads, outs = (refs[k * m : (k + 1) * m] for k in range(2))
+    kv, lse, marks = refs[2 * m : 2 * m + n], refs[2 * m + n], refs[2 * m + n + 1]
+    at = 2 * m + n + 2
     before = None
     if not start:
         before, at = refs[at], at + 1
@@ -532,7 +577,8 @@
         dqs, at = refs[at : at + m], at + m
         acc, at = refs[at], at + 1
         qs, gs, os, ds_, ka, va = refs[at:]
-    half, length = queries[0].shape[0], kv[0].shape[0]
+    half = kv[0].shape[0] // 3
+    length = 2 * half
     i = pl.program_id(0)
 
     @pl.when(i == 0)
@@ -540,7 +586,7 @@
         fill_keys(kv, marks, ka, va)
         for e in range(m):
             rows = slice(e * half, (e + 1) * half)
-            qs[rows, :] = queries[e][...]
+            qs[rows, :] = kv[first + e][length:, :]
             gs[rows, :] = grads[e][...]
             os[rows, :] = outs[e][...]
         acc[...] = jnp.zeros_like(acc) if start else before[...]
@@ -603,11 +649,12 @@
                 results[e][half:, :] = jnp.where(key_lane < HEAD, turned * LN2, turned).astype(BF16)
 
 
-def attend_back(queries, grads, outs, kv, lse, marks, before, earlier, first, end):
-    m, n, (half, _), length = len(queries), len(kv), queries[0].shape, kv[0].shape[0]
+def attend_back(grads, outs, kv, lse, marks, before, earlier, first, end):
+    m, n, half = len(grads), len(kv), kv[0].shape[0] // 3
+    length = 2 * half
     steps = m * 2 * half // BQ
     start = before is None
-    args = [*queries, *grads, *outs, *kv, lse, marks] + ([] if start else [before]) + (list(earlier) if end else [])
+    args = [*grads, *outs, *kv, lse, marks] + ([] if start else [before]) + (list(earlier) if end else [])
     if end:
         results = [shape((half + length, LANES), BF16)] * n
     else:
@@ -728,9 +775,9 @@
     at = tp + 2
     wod, wi = refs[at : at + tp * dp], refs[at + tp * dp : at + 2 * tp * dp]
     at += 2 * tp * dp
-    lows, out_low, slope, normed, inverse, second, terms = refs[at : at + 7]
-    act = refs[at + 7 : at + 7 + tp]
-    heads, gains, wi_all, wd_all, tokens, attended, acc, sems = refs[at + 7 + tp :]
+    second_low, out_low, slope, normed, inverse, second, terms, lows = refs[at : at + 8]
+    act = refs[at + 8 : at + 8 + tp]
+    heads, gains, wi_all, wd_all, tokens, attended, acc, sems = refs[at + 8 + tp :]
     share, width = tokens.shape
     hidden = wi[0].shape[1]
     lw = received[0].shape[1]
@@ -755,7 +802,7 @@
     for d in range(tp):
         copies.wait(d)
         for c in spans(hidden, CB):
-            h = jnp.dot(lows[:share, :], wi_all[d, :, c], preferred_element_type=F32)
+            h = jnp.dot(lows[...], wi_all[d, :, c], preferred_element_type=F32)
             phi = 0.5 * (1.0 + lax.erf(h * SQRT_HALF))
             act[d][:, c] = (h * phi).astype(BF16)
             there = slice(d * hidden + c.start, d * hidden + c.stop)
@@ -769,7 +816,7 @@
         grad = cotangent[b, :].astype(F32)
         result = back_of(grad, n, r, gain[2:3, :])
         second[b, :] = result
-        lows[share + b.start : share + b.stop, :] = result.astype(BF16)
+        second_low[b, :] = result.astype(BF16)
         sums = [sums[0] + jnp.sum(grad * n, axis=0, keepdims=True), sums[1] + jnp.sum(grad, axis=0, keepdims=True)]
     terms[0:1, :], terms[1:2, :] = sums
 
@@ -790,13 +837,14 @@
     (share, lw), (cols, hidden) = received[0].shape, wi[0].shape
     width = cols * dp
     outs = [
-        shape((2 * share, width), BF16),
+        shape((share, width), BF16),
         shape((share, width), BF16),
         shape((share, tp * hidden), BF16),
         shape((share, width), F32),
         shape((share, LANES), F32),
         shape((share, width), F32),
         shape((2, width), F32),
+        shape((share, width), BF16),
     ]
     out = call(
         functools.partial(forward_body, tp=tp, dp=dp),
@@ -818,17 +866,17 @@
         trans=3 * share * tp * hidden,
         name="forward",
     )
-    return out[:7], out[7:]
+    return out[:7], out[7], out[8:]
 
 
 def backward_body(*refs, tp, dp):
-    lows, out_low, slope, normed, inverse, second, terms = refs[:7]
-    wod, wi = refs[7 : 7 + tp * dp], refs[7 + tp * dp : 7 + 2 * tp * dp]
-    at = 7 + 2 * tp * dp
+    second_low, slope, normed, inverse, second, terms = refs[:6]
+    wod, wi = refs[6 : 6 + tp * dp], refs[6 + tp * dp : 6 + 2 * tp * dp]
+    at = 6 + 2 * tp * dp
     rows, first = refs[at], refs[at + 1]
     pre, grads = refs[at + 2 : at + 2 + tp], refs[at + 2 + tp : at + 2 + 2 * tp]
     heads, gains, wi_all, wd_all, acc, edge, sems = refs[at + 2 + 2 * tp :]
-    share, width = out_low.shape
+    share, width = second_low.shape
     hidden, lw = pre[0].shape[1], grads[0].shape[1]
     copies = Copies(sems)
     small, large = weight_copies(copies, wod, wi, tp, dp, heads, gains, wi_all, wd_all)
@@ -838,7 +886,7 @@
     for d in range(tp):
         copies.wait(d)
         for c in spans(hidden, CB):
-            grad = lax.dot_general(lows[share:, :], wd_all[d, c, :], NT, preferred_element_type=F32)
+            grad = lax.dot_general(second_low[...], wd_all[d, c, :], NT, preferred_element_type=F32)
             there = slice(d * hidden + c.start, d * hidden + c.stop)
             pre[d][:, c] = (grad * slope[:, there].astype(F32)).astype(BF16)
         for c in spans(width, CB):
@@ -855,25 +903,24 @@
     for j in range(tp):
         part = lax.dot_general(rows[:share, :], heads[j * lw : (j + 1) * lw, :], NT, preferred_element_type=F32)
         grads[j][...] = part.astype(BF16)
-    rows[share : 2 * share, :] = out_low[...]
     edge[...] = jnp.zeros_like(edge)
     edge[0:1, :], edge[1:2, :] = sums
     edge[2:4, :] = terms[...]
-    rows[2 * share :, :] = edge[...].astype(BF16)
+    rows[share:, :] = edge[...].astype(BF16)
 
 
 def backward(forwarded, wod, wi, tp, dp, lw):
     cols, hidden = wi[0].shape
-    share, width = forwarded[1].shape
+    share, width = forwarded[0].shape
     out = call(
         functools.partial(backward_body, tp=tp, dp=dp),
-        [shape((2 * share + 16, width), BF16), shape((share, width), F32)]
+        [shape((share + 16, width), BF16), shape((share, width), F32)]
         + [shape((share, hidden), BF16)] * tp
         + [shape((share, lw), BF16)] * tp,
         *forwarded,
         *wod,
         *wi,
-        in_specs=[FULL] * 7 + [ANY] * (2 * tp * dp),
+        in_specs=[FULL] * 6 + [ANY] * (2 * tp * dp),
         scratch=middle_scratch(tp, dp, lw, hidden, width, share)
         + [
             pltpu.VMEM((share, width), F32),
@@ -976,15 +1023,17 @@
     def exchange_tp(parts):
         return [p if d == 0 else swap(p, "tp", d) for d, p in zip(order(tp), parts)]
 
+    def over_dp(parts):
+        return [gather(p, "dp") for p in parts]
+
     def arrange_tokens(value):
         table = value.reshape(tp, share)
         picked = [lax.dynamic_index_in_dim(table, ids[2] ^ d, 0, keepdims=False) for d in order(tp)]
         return jnp.stack(picked).reshape(length)
 
-    w_qkv = gather(jnp.concatenate([w_q, w_k, w_v], axis=1), "dp")
+    w_qkv = gather(step(lambda *w: jnp.concatenate(w, axis=1), w_q, w_k, w_v), "dp")
     vectors = jnp.stack([ln1_gain, ln1_bias, ln2_gain, ln2_bias])
-    tall = jnp.concatenate([w_out, w_o, jnp.pad(vectors, ((0, 12), (0, 0)))])
-
+    tall = chips(jnp.concatenate([w_out, w_o, jnp.pad(vectors, ((0, 12), (0, 0)))]))
     docs = arrange_tokens(segments.reshape(length))
     places = arrange_tokens(positions.reshape(length)).astype(F32)
     freq = 10000.0 ** (-(jnp.arange(LANES, dtype=jnp.int32) % (HEAD // 2)).astype(F32) * 2.0 / HEAD)
@@ -992,50 +1041,47 @@
     x = arrange(ids, layer_input.reshape(length, width), tp, dp, order(tp))
 
     if spread:
+        all_docs = jnp.concatenate([docs] + [swap(docs, "ctx", e) for e in range(1, ctx)])
         side = jnp.where(jnp.arange(LANES) % HEAD < HEAD // 2, -1.0, 1.0)
         cosine, sine = step(lambda t: (jnp.cos(t), jnp.sin(t) * side[None, :]), angles)
-        all_docs = jnp.concatenate([docs] + [swap(docs, "ctx", e) for e in range(1, ctx)])
         lane = jnp.arange(LANES)[None, :]
         in_docs = (lane >= HEAD) & (lane < HEAD + DOCS)
         folded = (lane >= HEAD + DOCS) & (lane < HEAD + DOCS + 3)
-
+        marks = step(lambda d: jnp.where(in_docs, lane - HEAD != d[:, None], folded).astype(BF16), all_docs)
+        due(w_qkv)
+        wi = gather(in_line(w_in), "dp")
         kv = call(
-            functools.partial(kv_body, dp=dp, n=heads),
-            [shape((length, LANES), BF16)] * ctx,
+            functools.partial(project_body, dp=dp, n=heads),
+            [shape((length + half, LANES), BF16)] * ctx,
             ids,
             x,
             *w_qkv,
             cosine,
             sine,
             in_specs=[SMEM] + [FULL] * (3 + dp),
-            flops=4 * length * width * lw,
-            name="project_kv",
+            flops=6 * length * width * lw,
+            name="project",
         )
-        wi, wod = gather_weight(after(w_in, kv[0])), gather_weight(after(tall, kv[0]))
         kv = exchange(kv)
-        queries = call(
-            functools.partial(q_body, dp=dp, n=heads),
-            [shape((half, LANES), BF16)] * ctx,
-            ids,
-            x,
-            *w_qkv,
-            cosine,
-            sine,
-            in_specs=[SMEM] + [FULL] * (3 + dp),
-            flops=2 * length * width * lw,
-            name="project_q",
-        )
-        queries = exchange(queries)
-        marks = step(lambda d: jnp.where(in_docs, lane - HEAD != d[:, None], folded).astype(BF16), all_docs)
         out_grad = arrange(ids, cotangent.reshape(length, width), tp, dp, [0])
+        due(tall, wi)
+        out_grad = step(lambda v: v, out_grad)
+        tall = over_dp([in_line(p) for p in tall])
+        wi = [chips(in_line(p)) for p in wi]
+        due(kv)
         middle = ctx // 2
-        groups = ((0, middle), (middle, ctx))
-        outs, logs, mixed = [], [], []
-        for lo, hi in groups:
-            o, log = attend(queries[lo:hi], kv, marks, lo)
-            outs.append(o)
-            logs.append(log)
-            mixed.extend(exchange(o, lo))
+        o, log = attend(kv, marks, 0, middle)
+        outs, logs = [o], [log]
+        mixed = exchange(o)
+        due(wi, tall[: max(1, tp // 4)])
+        wi = [list(p) for p in zip(*wi)]
+        first_cores = [[swap(in_line(p), "tp", 1) for p in wi[k]] for k in range(len(wi))]
+        o, log = attend(kv, marks, middle, ctx - middle)
+        outs.append(o)
+        logs.append(log)
+        mixed.extend(exchange(o, middle))
+        due(mixed, first_cores)
+        wi = [q for p in wi + first_cores for q in p]
         attended = call(
             functools.partial(unpack_body, n=heads),
             [shape((share, lw), BF16)] * tp,
@@ -1044,8 +1090,11 @@
             in_specs=[SMEM] + [FULL] * ctx,
             name="unpack",
         )
+        tall = [in_line(q) for p in tall for q in p]
     else:
-        wi, wod = gather_weight(w_in), gather_weight(tall)
+        wi = [list(p) for p in zip(*[chips(p) for p in gather(w_in, "dp")])]
+        wi = cores([q for p in wi for q in p])
+        tall = [q for p in over_dp(tall) for q in p]
         out_grad = arrange(ids, cotangent.reshape(length, width), tp, dp, [0])
         joined = jnp.concatenate(w_qkv)
         mixed, attend_backward = gathered_attention(
@@ -1054,30 +1103,18 @@
         attended = [mixed[j * share : (j + 1) * share] for j in range(tp)]
 
     received = exchange_tp(attended)
-    forwarded, act = forward(received, out_grad, x, wod, wi, tp, dp)
-    lows = gather(forwarded[0], "tp")
-    act = exchange_tp(act)
-    rows, first_grad, pre, grads = backward(forwarded, wod, wi, tp, dp, lw)
-    grads = exchange_tp(grads)
-
-    out_sum = GradSum(ids, 1, lambda start, size, *a: sum_over_rows(a[:tp], a[tp:], start, size))
-    out_sum.operands = [*act, *[p[share:] for p in lows]]
-    rows = gather(after(rows, grads[-1]), "tp")
-    pre = exchange_tp([after(p, grads[-1]) for p in pre])
-
-    filler = -(hidden + lw + 8) % (16 * ctx) + 8
-
-    def product(start, size, *a):
-        into = sum_over_rows(a[:tp], a[tp : 2 * tp], start, size)
-        back = sum_over_rows(a[2 * tp : 3 * tp], a[3 * tp :], start, size)
-        terms = sum(p[2 * share : 2 * share + 8, start : start + size].astype(F32) for p in a[3 * tp :])
-        return jnp.concatenate([into, back, jnp.pad(terms, ((0, filler - 8), (0, 0)))])
-
-    in_sum = GradSum(ids, 1, product)
-    in_sum.operands = [*pre, *lows, *attended, *rows]
+    tall = cores(tall)
+    forwarded, hidden_low, act = forward(received, out_grad, x, tall, wi, tp, dp)
+    second_low, out_low, *forwarded = forwarded
+    act = list(act)
+    for j, d in enumerate(order(tp)):
+        if d in (1, tp // 2):
+            act[j] = swap(act[j], "tp", d)
+    rows, first_grad, pre, grads = backward([second_low, *forwarded], tall, wi, tp, dp, lw)
+    due([act[j] for j, d in enumerate(order(tp)) if d in (1, tp // 2)])
+    grads = exchange_tp([in_line(g) for g in grads])
 
     if spread:
-        out_sum.begin(width)
         packed = call(
             functools.partial(pack_body, tp=tp, n=heads),
             [shape((half, LANES), BF16)] * ctx,
@@ -1087,18 +1124,40 @@
             name="pack",
         )
         packed = exchange(packed)
+        due(packed[:middle])
+
+    second_low = chips(in_line(second_low))
+    for j, d in enumerate(order(tp)):
+        if d not in (0, 1, tp // 2):
+            act[j] = swap(in_line(act[j]), "tp", d)
+    hidden_low = chips(in_line(hidden_low))
+    if spread:
         query_grads, carried = attend_back(
-            queries[:middle], packed[:middle], outs[0], kv, logs[0], marks, None, None, 0, False
+            packed[:middle], outs[0], kv, logs[0], marks, None, None, 0, False
         )
-        out_sum.over_dp()
-        in_sum.begin(width)
+        due(packed, second_low, act)
+    second_low = cores(second_low)
+    out_sum = GradSum(ids, 1, *product(act, second_low))
+    rows = chips(in_line(rows))
+    pre = list(pre)
+    for j, d in enumerate(order(tp)):
+        if d > 1:
+            pre[j] = swap(in_line(pre[j]), "tp", d)
+    if spread:
+        due(hidden_low)
         pieces = attend_back(
-            queries[middle:], packed[middle:], outs[1], kv, logs[1], marks, carried, query_grads, middle, True
+            packed[middle:], outs[1], kv, logs[1], marks, carried, query_grads, middle, True
         )
+        due(rows, pre, out_sum.got)
         pieces = exchange(pieces)
-        out_sum.over_ctx()
-        in_sum.over_dp()
-        output = place(ids, rows, tp, dp, length, share)
+    hidden_low = cores(hidden_low)
+    rows = cores(rows)
+    pre[order(tp).index(1)] = swap(pre[order(tp).index(1)], "tp", 1)
+    in_sum = GradSum(ids, 1, *products(pre, hidden_low, attended, rows, ctx))
+    out_low = chips(in_line(out_low))
+    out_sum.next()
+    if spread:
+        due(pieces)
         whole, send, keep = call(
             functools.partial(input_grad_body, dp=dp, n=heads),
             [shape((length, 3 * lw), BF16), shape((half, width), BF16), shape((half, width), F32)],
@@ -1112,29 +1171,28 @@
             name="input_grad",
         )
     else:
-        out_sum.begin(width)
-        out_sum.over_dp()
-        in_sum.begin(width)
-        out_sum.over_ctx()
-        in_sum.over_dp()
-        output = place(ids, rows, tp, dp, length, share)
         whole = attend_backward(jnp.concatenate(grads))
         total = lax.dot_general(whole, joined, NT, preferred_element_type=F32)
         send, keep = total[half:].astype(BF16), total[:half]
-
     got = swap(send, "tp", 1)
-    qkv_sum = GradSum(ids, 0, lambda start, size, l, r: over_rows(l[:, start : start + size], r))
-    qkv_sum.operands = [x, whole]
-    qkv_sum.begin(width)
+    mid = width // 2
+    send = step(lambda l, r: over_rows(l[:, mid:], r).astype(BF16), x, whole)
+    qkv_sum = GradSum(ids, 0, send, step(lambda l, r: over_rows(l[:, :mid], r), x, whole))
     keep, got = scatter(None, keep, "tp", 0, got)
-    in_sum.over_ctx()
+    in_sum.next()
+    out_sum.next()
+    output = place(ids, cores(out_low), tp, dp, length)
+    low = step(lambda l, k, f: (f + k + l.astype(F32)).astype(BF16), got, keep, first_grad)
+    low = chips(low)
+    qkv_sum.next()
+    in_sum.next()
+    out_sum.next()
+    qkv_sum.next()
+    in_sum.next()
+    input_grad = place(ids, cores(low), tp, dp, length)
+    qkv_sum.next()
     (w_out_grad,) = out_sum.columns([width // dp])
-    low = step(lambda l, k, f: (f + k + l.astype(F32)).astype(BF16), got, keep, first_grad)
-    low = gather(low, "tp")
-    qkv_sum.over_dp()
     w_in_grad, w_o_grad, terms = in_sum.rows(hidden, lw)
-    input_grad = place(ids, low, tp, dp, length)
-    qkv_sum.over_ctx()
     w_q_grad, w_k_grad, w_v_grad = qkv_sum.columns([lw] * 3)
     return (
         output[None],

time: 654 us -> 525 us (0.80)
  waiting for transfers between devices: 285 us -> 192 us
  matrix products: 39.2 us -> 5.49 us
  starting transfers between devices: 105 us -> 89.2 us
  Pallas kernels: 176 us -> 191 us
    ppermute x77, waiting for transfers between devices: 285 us -> 192 us  [swap(): return lax.ppermute(value, axis, [(i, i ^ bit) for i in range(n)])]
    dot_general x26 -> x2, matrix products: 39.2 us -> 5.49 us  [over_rows(): lax.dot_general(left, right, (((0,), (0,)), ((), ())), preferred_element_...]
    ppermute x77, starting transfers between devices: 105 us -> 89.2 us  [swap(): return lax.ppermute(value, axis, [(i, i ^ bit) for i in range(n)])]
    pallas_call x24 -> x28, Pallas kernels: 176 us -> 191 us  [call(): pl.pallas_call(body, out_shape=out_shape, scratch_shapes=list(scratch), c...]
    unnamed x179 -> x131, local copies, waits for them, and re-layouts: 18.1 us -> 17.9 us
  transfers between devices with their start and end apart: 77 -> 77, of which waited for: 26 -> 24; matrix products, arithmetic and copies ran while one was open for 9% -> 5% of each run, Pallas kernels for 22% -> 33%
where the time goes in v3:
time: 525 us; the launch traced here: 516 us
  waiting for transfers between devices  192 us (37%)
  Pallas kernels  191 us (36%)
  starting transfers between devices  89.2 us (17%)
  local copies, waits for them, and re-layouts  23.1 us (4%)
  other arithmetic  13.5 us (3%)
  matrix products  5.49 us (1%)
    ppermute x77, waiting for transfers between devices, swap(): return lax.ppermute(value, axis, [(i, i ^ bit) for i in range(n)])  192 us
    pallas_call x28, Pallas kernels, call(): pl.pallas_call(body, out_shape=out_shape, scratch_shapes=list(scratch), c...  191 us
    ppermute x77, starting transfers between devices, swap(): return lax.ppermute(value, axis, [(i, i ^ bit) for i in range(n)])  89.2 us
    unnamed x131, local copies, waits for them, and re-layouts  17.9 us
  transfers between devices with their start and end apart: 77, of which 24 were waited for; matrix products, arithmetic and copies ran while one was open for 5% of the time, Pallas kernels for 33%

profile of v3, /device:TPU:0, one launch (start us, length us, event | category | flops | bytes accessed | tf_op | source)
XLA Modules:
  0.0 516.4 jit_solution(5090609250100505184)
XLA Ops:
  4.0 5.1 collective-permute-start.2
  20.6 3.1 arrange.2.x.refs_5_
  23.7 2.7 sine_multiply_fusion
  26.4 2.7 select_convert_fusion.refs_4_.refs_9_
  33.1 5.9 %project.1 = (bf16[1536,128]{1,0:T(8,128)(2,1)}, bf16[1536,128]{1,0:T(8,128)(2,1)}, bf16[1536,128]{1,0:T(8,128)(2,1)}, bf16[1536,128]{1,0:T(8,128)(2,1)}) custom-call(s32[3]{0:T(128)} %pad_add_fusion.1.ids, bf16[1024,1024]{1,0:T(8,128)(2,1)} %arrange.2.x.refs_5_, bf16[512,768]{1,0:T(8,128)(2,1)} %copy-done.40, ...), custom_call_target="tpu_custom_call" | custom-call | flops 1610612736 | bytes 16777216 | tf_op jit(solution)/shard_map/project/pallas_call | solution.py:113
  43.3 2.6 collective-permute-start.5
  46.0 12.0 %collective-permute-done.9.refs_15_ = bf16[512,1024]{1,0:T(8,128)(2,1)} collective-permute-done((bf16[512,1024]{1,0:T(8,128)(2,1)}, bf16[512,1024]{1,0:T(8,128)(2,1)}, u32[]{:S(2)}, u32[]{:S(2)}) %collective-permute-start.9) | collective-permute-done | bytes 1048608 | tf_op jit(solution)/shard_map/ppermute | solution.py:37
  57.9 3.5 collective-permute-start.6
  63.4 9.4 %collective-permute-done.5.refs_2_.refs_6_ = bf16[1536,128]{1,0:T(8,128)(2,1)S(1)} collective-permute-done((bf16[1536,128]{1,0:T(8,128)(2,1)}, bf16[1536,128]{1,0:T(8,128)(2,1)S(1)}, u32[]{:S(2)}, u32[]{:S(2)}) %collective-permute-start.5) | collective-permute-done | bytes 393248 | tf_op jit(solution)/shard_map/ppermute | solution.py:37
  74.7 16.2 %attend.2 = (bf16[512,128]{1,0:T(8,128)(2,1)}, bf16[512,128]{1,0:T(8,128)(2,1)}, f32[1024,128]{1,0:T(8,128)}) custom-call(bf16[1536,128]{1,0:T(8,128)(2,1)} %get-tuple-element.157.refs_0_.refs_4_, bf16[1536,128]{1,0:T(8,128)(2,1)} %copy-done.53, bf16[1536,128]{1,0:T(8,128)(2,1)} %copy-done.54, bf16[1536,128]{1,0:T(8,128)(2,1)} %copy-done.55, ...), custom_call_target="tpu_custom_call" | custom-call | flops 8589934592 | bytes 16777216 | tf_op jit(solution)/shard_map/attend/pallas_call | solution.py:113
  90.9 5.0 collective-permute-start.7
  95.9 7.5 %collective-permute-done.10.refs_17_ = bf16[512,1024]{1,0:T(8,128)(2,1)} collective-permute-done((bf16[512,1024]{1,0:T(8,128)(2,1)}, bf16[512,1024]{1,0:T(8,128)(2,1)}, u32[]{:S(2)}, u32[]{:S(2)}) %collective-permute-start.10) | collective-permute-done | bytes 1048608 | tf_op jit(solution)/shard_map/ppermute | solution.py:37
  103.9 16.4 %attend.3 = (bf16[512,128]{1,0:T(8,128)(2,1)}, bf16[512,128]{1,0:T(8,128)(2,1)}, f32[1024,128]{1,0:T(8,128)}) custom-call(bf16[1536,128]{1,0:T(8,128)(2,1)} %get-tuple-element.157.refs_0_.refs_4_, bf16[1536,128]{1,0:T(8,128)(2,1)} %copy-done.53, bf16[1536,128]{1,0:T(8,128)(2,1)} %copy-done.54, bf16[1536,128]{1,0:T(8,128)(2,1)} %copy-done.55, ...), custom_call_target="tpu_custom_call" | custom-call | flops 8589934592 | bytes 16777216 | tf_op jit(solution)/shard_map/attend/pallas_call | solution.py:113
  120.4 9.2 %collective-permute-done.12.refs_2_ = bf16[512,128]{1,0:T(8,128)(2,1)S(1)} collective-permute-done((bf16[512,128]{1,0:T(8,128)(2,1)}, bf16[512,128]{1,0:T(8,128)(2,1)S(1)}, u32[]{:S(2)}, u32[]{:S(2)}) %collective-permute-start.12) | collective-permute-done | bytes 131104 | tf_op jit(solution)/shard_map/ppermute | solution.py:37
  131.2 5.9 %collective-permute-done.13.refs_3_ = bf16[512,128]{1,0:T(8,128)(2,1)S(1)} collective-permute-done((bf16[512,128]{1,0:T(8,128)(2,1)}, bf16[512,128]{1,0:T(8,128)(2,1)S(1)}, u32[]{:S(2)}, u32[]{:S(2)}) %collective-permute-start.13) | collective-permute-done | bytes 131104 | tf_op jit(solution)/shard_map/ppermute | solution.py:37
  141.4 3.7 collective-permute-done.14.refs_1_
  146.8 4.3 collective-permute-done.16.refs_3_
  152.1 7.5 %collective-permute-done.26.refs_21_ = bf16[512,1024]{1,0:T(8,128)(2,1)S(1)} collective-permute-done((bf16[512,1024]{1,0:T(8,128)(2,1)}, bf16[512,1024]{1,0:T(8,128)(2,1)S(1)}, u32[]{:S(2)}, u32[]{:S(2)}) %collective-permute-start.26) | collective-permute-done | bytes 1048608 | tf_op jit(solution)/shard_map/ppermute | solution.py:37
  162.6 13.7 %forward.1 = (bf16[256,1024]{1,0:T(8,128)(2,1)}, bf16[256,1024]{1,0:T(8,128)(2,1)}, bf16[256,4096]{1,0:T(8,128)(2,1)}, f32[256,1024]{1,0:T(8,128)}, f32[256,128]...) custom-call(bf16[256,256]{1,0:T(8,128)(2,1)} %get-tuple-element.161., ...), custom_call_target="tpu_custom_call" | custom-call | flops 4831838208 | bytes 16777216 | tf_op jit(solution)/shard_map/forward/pallas_call | solution.py:113
  177.0 12.5 %backward.1 = (bf16[272,1024]{1,0:T(8,128)(2,1)}, f32[256,1024]{1,0:T(8,128)}, bf16[256,1024]{1,0:T(8,128)(2,1)}, bf16[256,1024]{1,0:T(8,128)(2,1)}, bf16[256,10...) custom-call(bf16[256,1024]{1,0:T(8,128)(2,1)} %get-tuple-element.203, ...), custom_call_target="tpu_custom_call" | custom-call | flops 4831838208 | bytes 16777216 | tf_op jit(solution)/shard_map/backward/pallas_call | solution.py:113
  192.8 4.4 collective-permute-done.29.refs_1_
  205.5 3.5 collective-permute-done.32.refs_1_
  210.3 28.6 %attend_back.2 = (bf16[512,128]{1,0:T(8,128)(2,1)}, bf16[512,128]{1,0:T(8,128)(2,1)}, f32[128,4096]{1,0:T(8,128)}) custom-call(bf16[512,128]{1,0:T(8,128)(2,1)} %get-tuple-element.220.refs_0_, bf16[512,128]{1,0:T(8,128)(2,1)} %copy-done.61, bf16[512,128]{1,0:T(8,128)(2,1)} %get-tuple-element.156.refs_0_.refs_2_, ...), custom_call_target="tpu_custom_call" | custom-call | flops 21474836480 | bytes 16777216 | tf_op jit(solution)/shard_map/attend_back/pallas_call | solution.py:113
  240.5 29.7 %attend_back.3 = (bf16[1536,128]{1,0:T(8,128)(2,1)}, bf16[1536,128]{1,0:T(8,128)(2,1)}, bf16[1536,128]{1,0:T(8,128)(2,1)}, bf16[1536,128]{1,0:T(8,128)(2,1)}) custom-call(bf16[512,128]{1,0:T(8,128)(2,1)} %copy-done.59, bf16[512,128]{1,0:T(8,128)(2,1)} %copy-done.60, bf16[512,128]{1,0:T(8,128)(2,1)} %get-tuple-element.158.refs_2_, ...), custom_call_target="tpu_custom_call" | custom-call | flops 21474836480 | bytes 16777216 | tf_op jit(solution)/shard_map/attend_back/pallas_call | solution.py:113
  271.9 5.7 %product.1 = (bf16[1024,512]{1,0:T(8,128)(2,1)}, f32[1024,512]{1,0:T(8,128)}) custom-call(bf16[256,1024]{1,0:T(8,128)(2,1)} %get-tuple-element.184.refs_0_, bf16[256,1024]{1,0:T(8,128)(2,1)} %copy-done.46, bf16[256,1024]{1,0:T(8,128)(2,1)} %copy-done.48, bf16[256,1024]{1,0:T(8,128)(2,1)} %copy-done.51, bf16[256,1024]{1,0:T(8,128)(2,1)} %get-tuple-element.203.refs_0_.refs_4_, ...), custom_call_target="tpu_custom_call" | custom-call | flops 2147483648 | bytes 16777216 | tf_op jit(solution)/shard_map/product/pallas_call | solution.py:113
  284.0 25.7 %collective-permute-done.52.refs_2_ = bf16[1536,128]{1,0:T(8,128)(2,1)} collective-permute-done((bf16[1536,128]{1,0:T(8,128)(2,1)}, bf16[1536,128]{1,0:T(8,128)(2,1)}, u32[]{:S(2)}, u32[]{:S(2)}) %collective-permute-start.52) | collective-permute-done | bytes 393248 | tf_op jit(solution)/shard_map/ppermute | solution.py:37
  312.4 5.8 %input_grad.1 = (bf16[1024,768]{1,0:T(8,128)(2,1)}, bf16[512,1024]{1,0:T(8,128)(2,1)}, f32[512,1024]{1,0:T(8,128)}) custom-call(s32[3]{0:T(128)} %pad_add_fusion.1.ids, bf16[1536,128]{1,0:T(8,128)(2,1)} %get-tuple-element.225.refs_0_, bf16[1536,128]{1,0:T(8,128)(2,1)} %copy-done.56, bf16[1536,128]{1,0:T(8,128)(2,1)} %collective-permute-done.52.refs_2_, ...), custom_call_target="tpu_custom_call" | custom-call | flops 1610612736 | bytes 16777216 | tf_op jit(solution)/shard_map/input_grad/pallas_call | solution.py:113
  318.5 6.9 %collective-permute-done.37.refs_1_ = bf16[256,1024]{1,0:T(8,128)(2,1)} collective-permute-done((bf16[256,1024]{1,0:T(8,128)(2,1)}, bf16[256,1024]{1,0:T(8,128)(2,1)}, u32[]{:S(2)}, u32[]{:S(2)}) %collective-permute-start.37) | collective-permute-done | bytes 524320 | tf_op jit(solution)/shard_map/ppermute | solution.py:37
  327.0 8.6 %collective-permute-done.39.refs_3_ = bf16[256,1024]{1,0:T(8,128)(2,1)} collective-permute-done((bf16[256,1024]{1,0:T(8,128)(2,1)}, bf16[256,1024]{1,0:T(8,128)(2,1)}, u32[]{:S(2)}, u32[]{:S(2)}) %collective-permute-start.39) | collective-permute-done | bytes 524320 | tf_op jit(solution)/shard_map/ppermute | solution.py:37
  336.4 7.8 %products.1 = (bf16[1344,512]{1,0:T(8,128)(2,1)}, f32[1344,512]{1,0:T(8,128)}) custom-call(bf16[256,1024]{1,0:T(8,128)(2,1)} %get-tuple-element.182.refs_0_, bf16[256,1024]{1,0:T(8,128)(2,1)} %collective-permute-done.37.refs_1_, bf16[256,1024]{1,0:T(8,128)(2,1)} %copy-done.45, bf16[256,1024]{1,0:T(8,128)(2,1)} %collective-permute-done.39.refs_3_, ...), custom_call_target="tpu_custom_call" | custom-call | flops 2684354560 | bytes 16777216 | tf_op jit(solution)/shard_map/products/pallas_call | solution.py:113
  347.1 3.3 convolution_convert_fusion
  352.7 3.4 halve.6
  356.0 6.8 %collective-permute-start.47 = (bf16[512,512]{1,0:T(8,128)(2,1)}, bf16[512,512]{1,0:T(8,128)(2,1)}, u32[]{:S(2)}, u32[]{:S(2)}) collective-permute-start(bf16[512,512]{1,0:T(8,128)(2,1)} %get-tuple-element.216), channel_id=1, source_target_pairs={{0,4},{4,0},{8,12},{12,8},{1,5},{5,1},{9,13},{13,9},{2,6},{6,2},{1... | collective-permute-start | bytes 1572872 | tf_op jit(solution)/shard_map/ppermute | solution.py:37
  365.6 13.6 %collective-permute-done.48.got = bf16[1344,512]{1,0:T(8,128)(2,1)S(1)} collective-permute-done((bf16[1344,512]{1,0:T(8,128)(2,1)}, bf16[1344,512]{1,0:T(8,128)(2,1)S(1)}, u32[]{:S(2)}, u32[]{:S(2)}) %collective-permute-start.48) | collective-permute-done | bytes 1376288 | tf_op jit(solution)/shard_map/ppermute | solution.py:37
  380.8 3.7 halve.7
  384.5 6.1 %collective-permute-start.59 = (bf16[672,512]{1,0:T(8,128)(2,1)}, bf16[672,512]{1,0:T(8,128)(2,1)}, u32[]{:S(2)}, u32[]{:S(2)}) collective-permute-start(bf16[672,512]{1,0:T(8,128)(2,1)} %get-tuple-element.237), channel_id=1, source_target_pairs={{0,4},{4,0},{8,12},{12,8},{1,5},{5,1},{9,13},{13,9},{2,6},{6,2},{1... | collective-permute-start | bytes 2064392 | tf_op jit(solution)/shard_map/ppermute | solution.py:37
  393.7 3.8 place.2
  400.4 2.8 halve.9
  403.2 3.5 collective-permute-start.62
  412.8 24.0 %collective-permute-done.63.got = bf16[256,512]{1,0:T(8,128)(2,1)S(1)} collective-permute-done((bf16[256,512]{1,0:T(8,128)(2,1)S(1)}, bf16[256,512]{1,0:T(8,128)(2,1)S(1)}, u32[]{:S(2)}, u32[]{:S(2)}) %collective-permute-start.63) | collective-permute-done | bytes 262176 | tf_op jit(solution)/shard_map/ppermute | solution.py:37
  445.1 2.9 collective-permute-start.68
  450.3 19.5 %collective-permute-done.71.refs_1_ = bf16[336,512]{1,0:T(8,128)(2,1)S(1)} collective-permute-done((bf16[336,512]{1,0:T(8,128)(2,1)}, bf16[336,512]{1,0:T(8,128)(2,1)S(1)}, u32[]{:S(2)}, u32[]{:S(2)}) %collective-permute-start.71) | collective-permute-done | bytes 344096 | tf_op jit(solution)/shard_map/ppermute | solution.py:37
  469.8 5.7 %collective-permute-done.68.refs_1_ = bf16[256,512]{1,0:T(8,128)(2,1)S(1)} collective-permute-done((bf16[256,512]{1,0:T(8,128)(2,1)S(1)}, bf16[256,512]{1,0:T(8,128)(2,1)S(1)}, u32[]{:S(2)}, u32[]{:S(2)}) %collective-permute-start.68) | collective-permute-done | bytes 262176 | tf_op jit(solution)/shard_map/ppermute | solution.py:37
  477.6 3.8 place.3
  485.8 11.1 %collective-permute-done.69.refs_2_ = bf16[256,512]{1,0:T(8,128)(2,1)S(1)} collective-permute-done((bf16[256,512]{1,0:T(8,128)(2,1)S(1)}, bf16[256,512]{1,0:T(8,128)(2,1)S(1)}, u32[]{:S(2)}, u32[]{:S(2)}) %collective-permute-start.69) | collective-permute-done | bytes 262176 | tf_op jit(solution)/shard_map/ppermute | solution.py:37
  496.8 5.6 %collective-permute-done.70.refs_3_ = bf16[256,512]{1,0:T(8,128)(2,1)S(1)} collective-permute-done((bf16[256,512]{1,0:T(8,128)(2,1)S(1)}, bf16[256,512]{1,0:T(8,128)(2,1)S(1)}, u32[]{:S(2)}, u32[]{:S(2)}) %collective-permute-start.70) | collective-permute-done | bytes 262176 | tf_op jit(solution)/shard_map/ppermute | solution.py:37
  503.2 2.7 place_columns.2
  507.3 3.5 place_rows.1
  (292 shorter events, 113.6 us)
Async XLA Ops:
  4.0 22.4 %collective-permute-start.2 = (s32[1024]{0:T(1024)S(1)}, s32[1024]{0:T(1024)S(1)}, u32[]{:S(2)}, u32[]{:S(2)}) collective-permute-start(s32[1024]{0:T(1024)S(1)} %bitcast.24), channel_id=1, source_target_pairs={{0,12},{4,8},{8,4},{12,0},{1,13},{5,9},{9,5},{13,1},{2,14},{6,10},... | collective-permute-start | bytes 12296 | tf_op jit(solution)/shard_map/ppermute | solution.py:37
  18.2 44.7 %collective-permute-start.17 = (bf16[1296,512]{1,0:T(8,128)(2,1)S(1)}, bf16[1296,512]{1,0:T(8,128)(2,1)S(1)}, u32[]{:S(2)}, u32[]{:S(2)}) collective-permute-start(bf16[1296,512]{1,0:T(8,128)(2,1)S(1)} %pad_maximum_fusion.refs_6_), channel_id=1, source_target_pairs={{0,2},{1,3},{2,0},{3,1},{4,6},{5,7},{6,4},{7,5},{8,10},{9,11},{10,... | collective-permute-start | bytes 3981320 | tf_op jit(solution)/shard_map/ppermute | solution.py:37
  31.6 26.3 %collective-permute-start.9 = (bf16[512,1024]{1,0:T(8,128)(2,1)}, bf16[512,1024]{1,0:T(8,128)(2,1)}, u32[]{:S(2)}, u32[]{:S(2)}) collective-permute-start(bf16[512,1024]{1,0:T(8,128)(2,1)} %refs_14_.1), channel_id=1, source_target_pairs={{0,16},{16,0},{1,17},{17,1},{2,18},{18,2},{3,19},{19,3},{4,20},{20... | collective-permute-start | bytes 3145736 | tf_op jit(solution)/shard_map/ppermute | solution.py:37
  39.0 22.4 %collective-permute-start.4 = (bf16[1536,128]{1,0:T(8,128)(2,1)}, bf16[1536,128]{1,0:T(8,128)(2,1)S(1)}, u32[]{:S(2)}, u32[]{:S(2)}) collective-permute-start(bf16[1536,128]{1,0:T(8,128)(2,1)} %get-tuple-element.146), channel_id=1, source_target_pairs={{0,4},{4,0},{8,12},{12,8},{1,5},{5,1},{9,13},{13,9},{2,6},{6,2},{1... | collective-permute-start | bytes 1179656 | tf_op jit(solution)/shard_map/ppermute | solution.py:37
  42.8 53.1 %collective-permute-start.11 = (bf16[1296,512]{1,0:T(8,128)(2,1)S(1)}, bf16[1296,512]{1,0:T(8,128)(2,1)}, u32[]{:S(2)}, u32[]{:S(2)}) collective-permute-start(bf16[1296,512]{1,0:T(8,128)(2,1)S(1)} %pad_maximum_fusion.refs_6_), channel_id=1, source_target_pairs={{0,16},{16,0},{1,17},{17,1},{2,18},{18,2},{3,19},{19,3},{4,20},{20... | collective-permute-start | bytes 3981320 | tf_op jit(solution)/shard_map/ppermute | solution.py:37
  43.3 29.5 %collective-permute-start.5 = (bf16[1536,128]{1,0:T(8,128)(2,1)}, bf16[1536,128]{1,0:T(8,128)(2,1)S(1)}, u32[]{:S(2)}, u32[]{:S(2)}) collective-permute-start(bf16[1536,128]{1,0:T(8,128)(2,1)} %get-tuple-element.147), channel_id=1, source_target_pairs={{0,8},{4,12},{8,0},{12,4},{1,9},{5,13},{9,1},{13,5},{2,10},{6,14},... | collective-permute-start | bytes 1179656 | tf_op jit(solution)/shard_map/ppermute | solution.py:37
  61.4 34.5 %collective-permute-start.8 = (bf16[512,1024]{1,0:T(8,128)(2,1)}, bf16[512,1024]{1,0:T(8,128)(2,1)}, u32[]{:S(2)}, u32[]{:S(2)}) collective-permute-start(bf16[512,1024]{1,0:T(8,128)(2,1)} %refs_14_.1), channel_id=1, source_target_pairs={{0,2},{1,3},{2,0},{3,1},{4,6},{5,7},{6,4},{7,5},{8,10},{9,11},{10,... | collective-permute-start | bytes 3145736 | tf_op jit(solution)/shard_map/ppermute | solution.py:37
  62.9 40.5 %collective-permute-start.10 = (bf16[512,1024]{1,0:T(8,128)(2,1)}, bf16[512,1024]{1,0:T(8,128)(2,1)}, u32[]{:S(2)}, u32[]{:S(2)}) collective-permute-start(bf16[512,1024]{1,0:T(8,128)(2,1)} %collective-permute-done.9.refs_15_), channel_id=1, source_target_pairs={{0,2},{1,3},{2,0},{3,1},{4,6},{5,7},{6,4},{7,5},{8,10},{9,11},{10,... | collective-permute-start | bytes 3145736 | tf_op jit(solution)/shard_map/ppermute | solution.py:37
  72.8 68.6 %collective-permute-start.18 = (bf16[1296,512]{1,0:T(8,128)(2,1)S(1)}, bf16[1296,512]{1,0:T(8,128)(2,1)}, u32[]{:S(2)}, u32[]{:S(2)}) collective-permute-start(bf16[1296,512]{1,0:T(8,128)(2,1)S(1)} %collective-permute-done.17.refs_8_), channel_id=1, source_target_pairs={{0,16},{16,0},{1,17},{17,1},{2,18},{18,2},{3,19},{19,3},{4,20},{20... | collective-permute-start | bytes 3981320 | tf_op jit(solution)/shard_map/ppermute | solution.py:37
  90.9 29.4 %collective-permute-start.7 = (bf16[512,128]{1,0:T(8,128)(2,1)}, bf16[512,128]{1,0:T(8,128)(2,1)S(1)}, u32[]{:S(2)}, u32[]{:S(2)}) collective-permute-start(bf16[512,128]{1,0:T(8,128)(2,1)} %get-tuple-element.150.refs_3_), channel_id=1, source_target_pairs={{0,4},{4,0},{8,12},{12,8},{1,5},{5,1},{9,13},{13,9},{2,6},{6,2},{1... | collective-permute-start | bytes 393224 | tf_op jit(solution)/shard_map/ppermute | solution.py:37
  103.4 47.7 %collective-permute-start.23 = (bf16[512,1024]{1,0:T(8,128)(2,1)}, bf16[512,1024]{1,0:T(8,128)(2,1)}, u32[]{:S(2)}, u32[]{:S(2)}) collective-permute-start(bf16[512,1024]{1,0:T(8,128)(2,1)} %refs_14_.1), channel_id=1, source_target_pairs={{0,1},{1,0},{2,3},{3,2},{4,5},{5,4},{6,7},{7,6},{8,9},{9,8},{10,11... | collective-permute-start | bytes 3145736 | tf_op jit(solution)/shard_map/ppermute | solution.py:37
  103.4 48.1 %collective-permute-start.24 = (bf16[512,1024]{1,0:T(8,128)(2,1)}, bf16[512,1024]{1,0:T(8,128)(2,1)}, u32[]{:S(2)}, u32[]{:S(2)}) collective-permute-start(bf16[512,1024]{1,0:T(8,128)(2,1)} %collective-permute-done.9.refs_15_), channel_id=1, source_target_pairs={{0,1},{1,0},{2,3},{3,2},{4,5},{5,4},{6,7},{7,6},{8,9},{9,8},{10,11... | collective-permute-start | bytes 3145736 | tf_op jit(solution)/shard_map/ppermute | solution.py:37
  103.9 47.7 %collective-permute-start.25 = (bf16[512,1024]{1,0:T(8,128)(2,1)}, bf16[512,1024]{1,0:T(8,128)(2,1)}, u32[]{:S(2)}, u32[]{:S(2)}) collective-permute-start(bf16[512,1024]{1,0:T(8,128)(2,1)} %collective-permute-done.8.refs_16_), channel_id=1, source_target_pairs={{0,1},{1,0},{2,3},{3,2},{4,5},{5,4},{6,7},{7,6},{8,9},{9,8},{10,11... | collective-permute-start | bytes 3145736 | tf_op jit(solution)/shard_map/ppermute | solution.py:37
  200.8 78.8 %collective-permute-start.38 = (bf16[256,1024]{1,0:T(8,128)(2,1)}, bf16[256,1024]{1,0:T(8,128)(2,1)S(1)}, u32[]{:S(2)}, u32[]{:S(2)}) collective-permute-start(bf16[256,1024]{1,0:T(8,128)(2,1)} %get-tuple-element.206), channel_id=1, source_target_pairs={{0,1},{1,0},{2,3},{3,2},{4,5},{5,4},{6,7},{7,6},{8,9},{9,8},{10,11... | collective-permute-start | bytes 1572872 | tf_op jit(solution)/shard_map/ppermute | solution.py:37
  201.4 37.5 %collective-permute-start.49 = (bf16[512,128]{1,0:T(8,128)(2,1)}, bf16[512,128]{1,0:T(8,128)(2,1)S(1)}, u32[]{:S(2)}, u32[]{:S(2)}) collective-permute-start(bf16[512,128]{1,0:T(8,128)(2,1)} %get-tuple-element.217), channel_id=1, source_target_pairs={{0,8},{4,12},{8,0},{12,4},{1,9},{5,13},{9,1},{13,5},{2,10},{6,14},... | collective-permute-start | bytes 393224 | tf_op jit(solution)/shard_map/ppermute | solution.py:37
  202.9 36.9 %collective-permute-start.50 = (bf16[512,128]{1,0:T(8,128)(2,1)}, bf16[512,128]{1,0:T(8,128)(2,1)S(1)}, u32[]{:S(2)}, u32[]{:S(2)}) collective-permute-start(bf16[512,128]{1,0:T(8,128)(2,1)} %get-tuple-element.218), channel_id=1, source_target_pairs={{0,12},{4,8},{8,4},{12,0},{1,13},{5,9},{9,5},{13,1},{2,14},{6,10},... | collective-permute-start | bytes 393224 | tf_op jit(solution)/shard_map/ppermute | solution.py:37
  208.9 61.4 %collective-permute-start.35 = (bf16[256,1024]{1,0:T(8,128)(2,1)S(1)}, bf16[256,1024]{1,0:T(8,128)(2,1)}, u32[]{:S(2)}, u32[]{:S(2)}) collective-permute-start(bf16[256,1024]{1,0:T(8,128)(2,1)S(1)} %copy-done.13), channel_id=1, source_target_pairs={{0,1},{1,0},{2,3},{3,2},{4,5},{5,4},{6,7},{7,6},{8,9},{9,8},{10,11... | collective-permute-start | bytes 1572872 | tf_op jit(solution)/shard_map/ppermute | solution.py:37
  208.9 30.5 %collective-permute-start.34 = (bf16[256,1024]{1,0:T(8,128)(2,1)S(1)}, bf16[256,1024]{1,0:T(8,128)(2,1)}, u32[]{:S(2)}, u32[]{:S(2)}) collective-permute-start(bf16[256,1024]{1,0:T(8,128)(2,1)S(1)} %copy-done.13), channel_id=1, source_target_pairs={{0,2},{1,3},{2,0},{3,1},{4,6},{5,7},{6,4},{7,5},{8,10},{9,11},{10,... | collective-permute-start | bytes 1572872 | tf_op jit(solution)/shard_map/ppermute | solution.py:37
  238.9 31.4 %collective-permute-start.33 = (bf16[256,1024]{1,0:T(8,128)(2,1)S(1)}, bf16[256,1024]{1,0:T(8,128)(2,1)S(1)}, u32[]{:S(2)}, u32[]{:S(2)}) collective-permute-start(bf16[256,1024]{1,0:T(8,128)(2,1)S(1)} %copy-done.47), channel_id=1, source_target_pairs={{0,3},{1,2},{2,1},{3,0},{4,7},{5,6},{6,5},{7,4},{8,11},{9,10},{10,... | collective-permute-start | bytes 1572872 | tf_op jit(solution)/shard_map/ppermute | solution.py:37
  239.5 30.8 %collective-permute-start.36 = (bf16[256,1024]{1,0:T(8,128)(2,1)}, bf16[256,1024]{1,0:T(8,128)(2,1)S(1)}, u32[]{:S(2)}, u32[]{:S(2)}) collective-permute-start(bf16[256,1024]{1,0:T(8,128)(2,1)} %collective-permute-done.34.refs_5_), channel_id=1, source_target_pairs={{0,1},{1,0},{2,3},{3,2},{4,5},{5,4},{6,7},{7,6},{8,9},{9,8},{10,11... | collective-permute-start | bytes 1572872 | tf_op jit(solution)/shard_map/ppermute | solution.py:37
  277.5 32.2 %collective-permute-start.43 = (bf16[272,1024]{1,0:T(8,128)(2,1)S(1)}, bf16[272,1024]{1,0:T(8,128)(2,1)S(1)}, u32[]{:S(2)}, u32[]{:S(2)}) collective-permute-start(bf16[272,1024]{1,0:T(8,128)(2,1)S(1)} %copy-done.41), channel_id=1, source_target_pairs={{0,2},{1,3},{2,0},{3,1},{4,6},{5,7},{6,4},{7,5},{8,10},{9,11},{10,... | collective-permute-start | bytes 1671176 | tf_op jit(solution)/shard_map/ppermute | solution.py:37
  278.9 31.4 %collective-permute-start.40 = (bf16[256,1024]{1,0:T(8,128)(2,1)S(1)}, bf16[256,1024]{1,0:T(8,128)(2,1)S(1)}, u32[]{:S(2)}, u32[]{:S(2)}) collective-permute-start(bf16[256,1024]{1,0:T(8,128)(2,1)S(1)} %copy-done.44), channel_id=1, source_target_pairs={{0,2},{1,3},{2,0},{3,1},{4,6},{5,7},{6,4},{7,5},{8,10},{9,11},{10,... | collective-permute-start | bytes 1572872 | tf_op jit(solution)/shard_map/ppermute | solution.py:37
  279.6 32.1 %collective-permute-start.41 = (bf16[256,1024]{1,0:T(8,128)(2,1)S(1)}, bf16[256,1024]{1,0:T(8,128)(2,1)S(1)}, u32[]{:S(2)}, u32[]{:S(2)}) collective-permute-start(bf16[256,1024]{1,0:T(8,128)(2,1)S(1)} %copy-done.44), channel_id=1, source_target_pairs={{0,1},{1,0},{2,3},{3,2},{4,5},{5,4},{6,7},{7,6},{8,9},{9,8},{10,11... | collective-permute-start | bytes 1572872 | tf_op jit(solution)/shard_map/ppermute | solution.py:37
  279.6 30.1 %collective-permute-start.52 = (bf16[1536,128]{1,0:T(8,128)(2,1)}, bf16[1536,128]{1,0:T(8,128)(2,1)}, u32[]{:S(2)}, u32[]{:S(2)}) collective-permute-start(bf16[1536,128]{1,0:T(8,128)(2,1)} %get-tuple-element.227), channel_id=1, source_target_pairs={{0,8},{4,12},{8,0},{12,4},{1,9},{5,13},{9,1},{13,5},{2,10},{6,14},... | collective-permute-start | bytes 1179656 | tf_op jit(solution)/shard_map/ppermute | solution.py:37
  281.7 28.7 %collective-permute-start.53 = (bf16[1536,128]{1,0:T(8,128)(2,1)}, bf16[1536,128]{1,0:T(8,128)(2,1)S(1)}, u32[]{:S(2)}, u32[]{:S(2)}) collective-permute-start(bf16[1536,128]{1,0:T(8,128)(2,1)} %get-tuple-element.228), channel_id=1, source_target_pairs={{0,12},{4,8},{8,4},{12,0},{1,13},{5,9},{9,5},{13,1},{2,14},{6,10},... | collective-permute-start | bytes 1179656 | tf_op jit(solution)/shard_map/ppermute | solution.py:37
  309.7 25.9 %collective-permute-start.44 = (bf16[272,1024]{1,0:T(8,128)(2,1)S(1)}, bf16[272,1024]{1,0:T(8,128)(2,1)S(1)}, u32[]{:S(2)}, u32[]{:S(2)}) collective-permute-start(bf16[272,1024]{1,0:T(8,128)(2,1)S(1)} %copy-done.41), channel_id=1, source_target_pairs={{0,1},{1,0},{2,3},{3,2},{4,5},{5,4},{6,7},{7,6},{8,9},{9,8},{10,11... | collective-permute-start | bytes 1671176 | tf_op jit(solution)/shard_map/ppermute | solution.py:37
  309.7 25.9 %collective-permute-start.45 = (bf16[272,1024]{1,0:T(8,128)(2,1)S(1)}, bf16[272,1024]{1,0:T(8,128)(2,1)}, u32[]{:S(2)}, u32[]{:S(2)}) collective-permute-start(bf16[272,1024]{1,0:T(8,128)(2,1)S(1)} %collective-permute-done.43.refs_13_), channel_id=1, source_target_pairs={{0,1},{1,0},{2,3},{3,2},{4,5},{5,4},{6,7},{7,6},{8,9},{9,8},{10,11... | collective-permute-start | bytes 1671176 | tf_op jit(solution)/shard_map/ppermute | solution.py:37
  311.7 23.9 %collective-permute-start.39 = (bf16[256,1024]{1,0:T(8,128)(2,1)}, bf16[256,1024]{1,0:T(8,128)(2,1)}, u32[]{:S(2)}, u32[]{:S(2)}) collective-permute-start(bf16[256,1024]{1,0:T(8,128)(2,1)} %get-tuple-element.208), channel_id=1, source_target_pairs={{0,3},{1,2},{2,1},{3,0},{4,7},{5,6},{6,5},{7,4},{8,11},{9,10},{10,... | collective-permute-start | bytes 1572872 | tf_op jit(solution)/shard_map/ppermute | solution.py:37
  318.3 34.2 %collective-permute-start.54 = (bf16[512,1024]{1,0:T(8,128)(2,1)}, bf16[512,1024]{1,0:T(8,128)(2,1)}, u32[]{:S(2)}, u32[]{:S(2)}) collective-permute-start(bf16[512,1024]{1,0:T(8,128)(2,1)} %get-tuple-element.230), channel_id=1, source_target_pairs={{0,1},{1,0},{2,3},{3,2},{4,5},{5,4},{6,7},{7,6},{8,9},{9,8},{10,11... | collective-permute-start | bytes 3145736 | tf_op jit(solution)/shard_map/ppermute | solution.py:37
  325.4 27.2 %collective-permute-start.46 = (bf16[1024,512]{1,0:T(8,128)(2,1)}, bf16[1024,512]{1,0:T(8,128)(2,1)}, u32[]{:S(2)}, u32[]{:S(2)}) collective-permute-start(bf16[1024,512]{1,0:T(8,128)(2,1)} %get-tuple-element.204), channel_id=1, source_target_pairs={{0,16},{16,0},{1,17},{17,1},{2,18},{18,2},{3,19},{19,3},{4,20},{20... | collective-permute-start | bytes 3145736 | tf_op jit(solution)/shard_map/ppermute | solution.py:37
  344.2 35.0 %collective-permute-start.48 = (bf16[1344,512]{1,0:T(8,128)(2,1)}, bf16[1344,512]{1,0:T(8,128)(2,1)S(1)}, u32[]{:S(2)}, u32[]{:S(2)}) collective-permute-start(bf16[1344,512]{1,0:T(8,128)(2,1)} %get-tuple-element.212), channel_id=1, source_target_pairs={{0,16},{16,0},{1,17},{17,1},{2,18},{18,2},{3,19},{19,3},{4,20},{20... | collective-permute-start | bytes 4128776 | tf_op jit(solution)/shard_map/ppermute | solution.py:37
  352.6 40.3 %collective-permute-start.56 = (bf16[256,1024]{1,0:T(8,128)(2,1)}, bf16[256,1024]{1,0:T(8,128)(2,1)S(1)}, u32[]{:S(2)}, u32[]{:S(2)}) collective-permute-start(bf16[256,1024]{1,0:T(8,128)(2,1)} %get-tuple-element.241.refs_0_), channel_id=1, source_target_pairs={{0,1},{1,0},{2,3},{3,2},{4,5},{5,4},{6,7},{7,6},{8,9},{9,8},{10,11... | collective-permute-start | bytes 1572872 | tf_op jit(solution)/shard_map/ppermute | solution.py:37
  356.0 28.4 %collective-permute-start.47 = (bf16[512,512]{1,0:T(8,128)(2,1)}, bf16[512,512]{1,0:T(8,128)(2,1)}, u32[]{:S(2)}, u32[]{:S(2)}) collective-permute-start(bf16[512,512]{1,0:T(8,128)(2,1)} %get-tuple-element.216), channel_id=1, source_target_pairs={{0,4},{4,0},{8,12},{12,8},{1,5},{5,1},{9,13},{13,9},{2,6},{6,2},{1... | collective-permute-start | bytes 1572872 | tf_op jit(solution)/shard_map/ppermute | solution.py:37
  362.9 30.1 %collective-permute-start.57 = (bf16[256,1024]{1,0:T(8,128)(2,1)}, bf16[256,1024]{1,0:T(8,128)(2,1)}, u32[]{:S(2)}, u32[]{:S(2)}) collective-permute-start(bf16[256,1024]{1,0:T(8,128)(2,1)} %collective-permute-done.55.refs_1_), channel_id=1, source_target_pairs={{0,1},{1,0},{2,3},{3,2},{4,5},{5,4},{6,7},{7,6},{8,9},{9,8},{10,11... | collective-permute-start | bytes 1572872 | tf_op jit(solution)/shard_map/ppermute | solution.py:37
  364.8 32.7 %collective-permute-start.58 = (bf16[256,1024]{1,0:T(8,128)(2,1)}, bf16[256,1024]{1,0:T(8,128)(2,1)}, u32[]{:S(2)}, u32[]{:S(2)}) collective-permute-start(bf16[256,1024]{1,0:T(8,128)(2,1)} %add_convert_fusion.1), channel_id=1, source_target_pairs={{0,2},{1,3},{2,0},{3,1},{4,6},{5,7},{6,4},{7,5},{8,10},{9,11},{10,... | collective-permute-start | bytes 1572872 | tf_op jit(solution)/shard_map/ppermute | solution.py:37
  384.5 22.3 %collective-permute-start.59 = (bf16[672,512]{1,0:T(8,128)(2,1)}, bf16[672,512]{1,0:T(8,128)(2,1)}, u32[]{:S(2)}, u32[]{:S(2)}) collective-permute-start(bf16[672,512]{1,0:T(8,128)(2,1)} %get-tuple-element.237), channel_id=1, source_target_pairs={{0,4},{4,0},{8,12},{12,8},{1,5},{5,1},{9,13},{13,9},{2,6},{6,2},{1... | collective-permute-start | bytes 2064392 | tf_op jit(solution)/shard_map/ppermute | solution.py:37
  403.2 36.2 %collective-permute-start.62 = (bf16[256,768]{1,0:T(8,128)(2,1)}, bf16[256,768]{1,0:T(8,128)(2,1)S(1)}, u32[]{:S(2)}, u32[]{:S(2)}) collective-permute-start(bf16[256,768]{1,0:T(8,128)(2,1)} %get-tuple-element.245), channel_id=1, source_target_pairs={{0,4},{4,0},{8,12},{12,8},{1,5},{5,1},{9,13},{13,9},{2,6},{6,2},{1... | collective-permute-start | bytes 1179656 | tf_op jit(solution)/shard_map/ppermute | solution.py:37
  409.4 32.9 %collective-permute-start.61 = (bf16[336,512]{1,0:T(8,128)(2,1)}, bf16[336,512]{1,0:T(8,128)(2,1)S(1)}, u32[]{:S(2)}, u32[]{:S(2)}) collective-permute-start(bf16[336,512]{1,0:T(8,128)(2,1)} %get-tuple-element.248), channel_id=1, source_target_pairs={{0,8},{4,12},{8,0},{12,4},{1,9},{5,13},{9,1},{13,5},{2,10},{6,14},... | collective-permute-start | bytes 1032200 | tf_op jit(solution)/shard_map/ppermute | solution.py:37
  410.0 26.9 %collective-permute-start.63 = (bf16[256,512]{1,0:T(8,128)(2,1)S(1)}, bf16[256,512]{1,0:T(8,128)(2,1)S(1)}, u32[]{:S(2)}, u32[]{:S(2)}) collective-permute-start(bf16[256,512]{1,0:T(8,128)(2,1)S(1)} %copy-done.58), channel_id=1, source_target_pairs={{0,8},{4,12},{8,0},{12,4},{1,9},{5,13},{9,1},{13,5},{2,10},{6,14},... | collective-permute-start | bytes 786440 | tf_op jit(solution)/shard_map/ppermute | solution.py:37
  412.3 35.7 %collective-permute-start.65 = (bf16[256,1024]{1,0:T(8,128)(2,1)S(1)}, bf16[256,1024]{1,0:T(8,128)(2,1)S(1)}, u32[]{:S(2)}, u32[]{:S(2)}) collective-permute-start(bf16[256,1024]{1,0:T(8,128)(2,1)S(1)} %add_convert_fusion.refs_0_), channel_id=1, source_target_pairs={{0,1},{1,0},{2,3},{3,2},{4,5},{5,4},{6,7},{7,6},{8,9},{9,8},{10,11... | collective-permute-start | bytes 1572872 | tf_op jit(solution)/shard_map/ppermute | solution.py:37
  412.3 63.2 %collective-permute-start.66 = (bf16[256,1024]{1,0:T(8,128)(2,1)S(1)}, bf16[256,1024]{1,0:T(8,128)(2,1)S(1)}, u32[]{:S(2)}, u32[]{:S(2)}) collective-permute-start(bf16[256,1024]{1,0:T(8,128)(2,1)S(1)} %collective-permute-done.64.refs_1_), channel_id=1, source_target_pairs={{0,1},{1,0},{2,3},{3,2},{4,5},{5,4},{6,7},{7,6},{8,9},{9,8},{10,11... | collective-permute-start | bytes 1572872 | tf_op jit(solution)/shard_map/ppermute | solution.py:37
  445.1 24.7 %collective-permute-start.71 = (bf16[336,512]{1,0:T(8,128)(2,1)}, bf16[336,512]{1,0:T(8,128)(2,1)S(1)}, u32[]{:S(2)}, u32[]{:S(2)}) collective-permute-start(bf16[336,512]{1,0:T(8,128)(2,1)} %merge.4.refs_0_), channel_id=1, source_target_pairs={{0,8},{4,12},{8,0},{12,4},{1,9},{5,13},{9,1},{13,5},{2,10},{6,14},... | collective-permute-start | bytes 1032200 | tf_op jit(solution)/shard_map/ppermute | solution.py:37
  445.1 30.4 %collective-permute-start.68 = (bf16[256,512]{1,0:T(8,128)(2,1)S(1)}, bf16[256,512]{1,0:T(8,128)(2,1)S(1)}, u32[]{:S(2)}, u32[]{:S(2)}) collective-permute-start(bf16[256,512]{1,0:T(8,128)(2,1)S(1)} %copy-done.12), channel_id=1, source_target_pairs={{0,8},{4,12},{8,0},{12,4},{1,9},{5,13},{9,1},{13,5},{2,10},{6,14},... | collective-permute-start | bytes 786440 | tf_op jit(solution)/shard_map/ppermute | solution.py:37
  448.0 33.4 %collective-permute-start.67 = (bf16[128,768]{1,0:T(8,128)(2,1)}, bf16[128,768]{1,0:T(8,128)(2,1)S(1)}, u32[]{:S(2)}, u32[]{:S(2)}) collective-permute-start(bf16[128,768]{1,0:T(8,128)(2,1)} %get-tuple-element.253), channel_id=1, source_target_pairs={{0,8},{4,12},{8,0},{12,4},{1,9},{5,13},{9,1},{13,5},{2,10},{6,14},... | collective-permute-start | bytes 589832 | tf_op jit(solution)/shard_map/ppermute | solution.py:37
  448.0 57.8 %collective-permute-start.72 = (bf16[336,512]{1,0:T(8,128)(2,1)}, bf16[336,512]{1,0:T(8,128)(2,1)S(1)}, u32[]{:S(2)}, u32[]{:S(2)}) collective-permute-start(bf16[336,512]{1,0:T(8,128)(2,1)} %merge.4.refs_0_), channel_id=1, source_target_pairs={{0,4},{4,0},{8,12},{12,8},{1,5},{5,1},{9,13},{13,9},{2,6},{6,2},{1... | collective-permute-start | bytes 1032200 | tf_op jit(solution)/shard_map/ppermute | solution.py:37
  469.8 36.1 %collective-permute-start.73 = (bf16[336,512]{1,0:T(8,128)(2,1)S(1)}, bf16[336,512]{1,0:T(8,128)(2,1)S(1)}, u32[]{:S(2)}, u32[]{:S(2)}) collective-permute-start(bf16[336,512]{1,0:T(8,128)(2,1)S(1)} %collective-permute-done.71.refs_1_), channel_id=1, source_target_pairs={{0,4},{4,0},{8,12},{12,8},{1,5},{5,1},{9,13},{13,9},{2,6},{6,2},{1... | collective-permute-start | bytes 1032200 | tf_op jit(solution)/shard_map/ppermute | solution.py:37
  475.5 26.9 %collective-permute-start.70 = (bf16[256,512]{1,0:T(8,128)(2,1)S(1)}, bf16[256,512]{1,0:T(8,128)(2,1)S(1)}, u32[]{:S(2)}, u32[]{:S(2)}) collective-permute-start(bf16[256,512]{1,0:T(8,128)(2,1)S(1)} %collective-permute-done.68.refs_1_), channel_id=1, source_target_pairs={{0,4},{4,0},{8,12},{12,8},{1,5},{5,1},{9,13},{13,9},{2,6},{6,2},{1... | collective-permute-start | bytes 786440 | tf_op jit(solution)/shard_map/ppermute | solution.py:37
  483.9 22.0 %collective-permute-start.74 = (bf16[128,768]{1,0:T(8,128)(2,1)}, bf16[128,768]{1,0:T(8,128)(2,1)S(1)}, u32[]{:S(2)}, u32[]{:S(2)}) collective-permute-start(bf16[128,768]{1,0:T(8,128)(2,1)} %merge.5.refs_0_), channel_id=1, source_target_pairs={{0,8},{4,12},{8,0},{12,4},{1,9},{5,13},{9,1},{13,5},{2,10},{6,14},... | collective-permute-start | bytes 589832 | tf_op jit(solution)/shard_map/ppermute | solution.py:37
  (92 other events, 1175.2 us)

commit v4 on v3

--- a/solution.py
+++ b/solution.py
@@ -65,11 +65,11 @@
 
 
 def in_line(value):
-    return after(value, LINE[-1]) if LINE else value
+    return after(value, *LINE) if LINE else value
 
 
 def due(*values):
-    LINE[:] = [after(LINE[-1], *jax.tree.leaves(values))]
+    LINE.extend(jax.tree.leaves(values))
 
 
 def step(function, *args):
@@ -115,7 +115,7 @@
         out_shape=out_shape,
         scratch_shapes=list(scratch),
         compiler_params=pltpu.CompilerParams(vmem_limit_bytes=VMEM_LIMIT),
-        cost_estimate=pl.CostEstimate(flops=int(flops), bytes_accessed=1 << 24, transcendentals=int(trans)),
+        cost_estimate=pl.CostEstimate(flops=1, bytes_accessed=1, transcendentals=0),
         name=name,
         **extra,
     )(*args)
@@ -304,26 +304,34 @@
         self.got = swap(send, "dp", 1)
         self.bit = 0
 
-    def next(self):
-        n = lax.axis_size("ctx")
+    def halve(self):
         if self.bit == 0:
             self.keep, self.got = scatter(None, self.keep, "dp", self.dim, self.got)
         self.bit = max(1, 2 * self.bit)
         rows, cols = self.keep.shape
-        if self.bit < n:
-            send, self.keep = call(
-                functools.partial(halve_body, bit=self.bit),
-                [shape((rows // 2, cols), BF16), shape((rows // 2, cols), F32)],
-                self.ids,
-                self.got,
-                self.keep,
-                in_specs=[SMEM, FULL, FULL],
-                name="halve",
-            )
-            self.got = swap(send, "ctx", self.bit)
-        else:
-            own = call(merge_body, shape((rows, cols), BF16), self.got, self.keep, name="merge")
-            self.parts = gather(own, "ctx")
+        send, self.keep = call(
+            functools.partial(halve_body, bit=self.bit),
+            [shape((rows // 2, cols), BF16), shape((rows // 2, cols), F32)],
+            self.ids,
+            self.got,
+            self.keep,
+            in_specs=[SMEM, FULL, FULL],
+            name="halve",
+        )
+        self.got = swap(send, "ctx", self.bit)
+
+    def merge(self):
+        while 2 * self.bit < lax.axis_size("ctx"):
+            self.halve()
+        self.parts = [call(merge_body, shape(self.keep.shape, BF16), self.got, self.keep, name="merge")]
+        bit = self.bit
+        while bit > 1:
+            self.parts = self.parts + [swap(p, "ctx", bit) for p in self.parts]
+            bit >>= 1
+
+    def last(self):
+        due(self.parts)
+        self.parts = self.parts + [swap(p, "ctx", 1) for p in [in_line(p) for p in self.parts]]
 
     def columns(self, widths):
         n = len(self.parts)
@@ -1031,24 +1039,31 @@
         picked = [lax.dynamic_index_in_dim(table, ids[2] ^ d, 0, keepdims=False) for d in order(tp)]
         return jnp.stack(picked).reshape(length)
 
+    def lined(parts):
+        return [in_line(p) for p in parts]
+
     w_qkv = gather(step(lambda *w: jnp.concatenate(w, axis=1), w_q, w_k, w_v), "dp")
     vectors = jnp.stack([ln1_gain, ln1_bias, ln2_gain, ln2_bias])
-    tall = chips(jnp.concatenate([w_out, w_o, jnp.pad(vectors, ((0, 12), (0, 0)))]))
-    docs = arrange_tokens(segments.reshape(length))
-    places = arrange_tokens(positions.reshape(length)).astype(F32)
+    tall = chips(step(lambda *w: jnp.concatenate(w), w_out, w_o, jnp.pad(vectors, ((0, 12), (0, 0)))))
+    x = arrange(ids, layer_input.reshape(length, width), tp, dp, order(tp))
+    docs = arrange_tokens(in_line(segments).reshape(length))
+    places = arrange_tokens(in_line(positions).reshape(length)).astype(F32)
     freq = 10000.0 ** (-(jnp.arange(LANES, dtype=jnp.int32) % (HEAD // 2)).astype(F32) * 2.0 / HEAD)
     angles = places[:, None] * freq[None, :]
-    x = arrange(ids, layer_input.reshape(length, width), tp, dp, order(tp))
+    middle = ctx // 2
+    near = [j for j, d in enumerate(order(tp)) if d in (1, tp // 2)]
+    far = [j for j, d in enumerate(order(tp)) if d not in (0, 1, tp // 2)]
 
     if spread:
         all_docs = jnp.concatenate([docs] + [swap(docs, "ctx", e) for e in range(1, ctx)])
         side = jnp.where(jnp.arange(LANES) % HEAD < HEAD // 2, -1.0, 1.0)
         cosine, sine = step(lambda t: (jnp.cos(t), jnp.sin(t) * side[None, :]), angles)
+        out_grad = arrange(ids, cotangent.reshape(length, width), tp, dp, [0])
         lane = jnp.arange(LANES)[None, :]
         in_docs = (lane >= HEAD) & (lane < HEAD + DOCS)
         folded = (lane >= HEAD + DOCS) & (lane < HEAD + DOCS + 3)
-        marks = step(lambda d: jnp.where(in_docs, lane - HEAD != d[:, None], folded).astype(BF16), all_docs)
         due(w_qkv)
+        wi_far = chips(in_line(w_in))
         wi = gather(in_line(w_in), "dp")
         kv = call(
             functools.partial(project_body, dp=dp, n=heads),
@@ -1063,25 +1078,26 @@
             name="project",
         )
         kv = exchange(kv)
-        out_grad = arrange(ids, cotangent.reshape(length, width), tp, dp, [0])
-        due(tall, wi)
-        out_grad = step(lambda v: v, out_grad)
-        tall = over_dp([in_line(p) for p in tall])
-        wi = [chips(in_line(p)) for p in wi]
-        due(kv)
-        middle = ctx // 2
+        marks = step(lambda d: jnp.where(in_docs, lane - HEAD != d[:, None], folded).astype(BF16), all_docs)
+        due(tall, kv, wi_far)
+        tall_cores = [[swap(in_line(p), "tp", 1)] for p in tall]
+        tall_own = gather(in_line(tall[0]), "dp")
+        wi = [[p, *chips(in_line(p))[1:]] for p in wi[1:]]
         o, log = attend(kv, marks, 0, middle)
         outs, logs = [o], [log]
         mixed = exchange(o)
-        due(wi, tall[: max(1, tp // 4)])
-        wi = [list(p) for p in zip(*wi)]
-        first_cores = [[swap(in_line(p), "tp", 1) for p in wi[k]] for k in range(len(wi))]
+        due(wi, tall_cores)
+        wi = [q for p in zip(wi_far, *wi) for q in p]
+        tall = [tall_own] + over_dp(lined(tall[1:]))
+        few = len(wi) // 2
+        wi_cores = [swap(p, "tp", 1) for p in lined(wi[:few])]
         o, log = attend(kv, marks, middle, ctx - middle)
         outs.append(o)
         logs.append(log)
-        mixed.extend(exchange(o, middle))
-        due(mixed, first_cores)
-        wi = [q for p in wi + first_cores for q in p]
+        due(wi_cores, tall[0])
+        mixed.extend(exchange(lined(o), middle))
+        wi = wi + wi_cores + [swap(p, "tp", 1) for p in lined(wi[few:])]
+        due(mixed, wi)
         attended = call(
             functools.partial(unpack_body, n=heads),
             [shape((share, lw), BF16)] * tp,
@@ -1090,11 +1106,13 @@
             in_specs=[SMEM] + [FULL] * ctx,
             name="unpack",
         )
-        tall = [in_line(q) for p in tall for q in p]
+        due(tall)
+        tall_cores = [c + [swap(in_line(q), "tp", 1) for q in p[1:]] for c, p in zip(tall_cores, tall)]
+        tall = [q for p in tall + tall_cores for q in p]
     else:
         wi = [list(p) for p in zip(*[chips(p) for p in gather(w_in, "dp")])]
         wi = cores([q for p in wi for q in p])
-        tall = [q for p in over_dp(tall) for q in p]
+        tall = cores([q for p in over_dp(tall) for q in p])
         out_grad = arrange(ids, cotangent.reshape(length, width), tp, dp, [0])
         joined = jnp.concatenate(w_qkv)
         mixed, attend_backward = gathered_attention(
@@ -1103,16 +1121,14 @@
         attended = [mixed[j * share : (j + 1) * share] for j in range(tp)]
 
     received = exchange_tp(attended)
-    tall = cores(tall)
     forwarded, hidden_low, act = forward(received, out_grad, x, tall, wi, tp, dp)
     second_low, out_low, *forwarded = forwarded
     act = list(act)
-    for j, d in enumerate(order(tp)):
-        if d in (1, tp // 2):
-            act[j] = swap(act[j], "tp", d)
+    for j in near:
+        act[j] = swap(act[j], "tp", order(tp)[j])
     rows, first_grad, pre, grads = backward([second_low, *forwarded], tall, wi, tp, dp, lw)
-    due([act[j] for j, d in enumerate(order(tp)) if d in (1, tp // 2)])
-    grads = exchange_tp([in_line(g) for g in grads])
+    due([act[j] for j in near])
+    grads = exchange_tp(lined(grads))
 
     if spread:
         packed = call(
@@ -1125,39 +1141,42 @@
         )
         packed = exchange(packed)
         due(packed[:middle])
-
+    else:
+        due(grads)
     second_low = chips(in_line(second_low))
-    for j, d in enumerate(order(tp)):
-        if d not in (0, 1, tp // 2):
-            act[j] = swap(in_line(act[j]), "tp", d)
+    for j in far:
+        act[j] = swap(in_line(act[j]), "tp", order(tp)[j])
     hidden_low = chips(in_line(hidden_low))
     if spread:
         query_grads, carried = attend_back(
             packed[:middle], outs[0], kv, logs[0], marks, None, None, 0, False
         )
-        due(packed, second_low, act)
-    second_low = cores(second_low)
-    out_sum = GradSum(ids, 1, *product(act, second_low))
+        due(packed)
+    due(second_low, act, hidden_low)
+    second_low = second_low + [swap(p, "tp", 1) for p in lined(second_low)]
+    hidden_low = hidden_low + [swap(p, "tp", 1) for p in lined(hidden_low)]
     rows = chips(in_line(rows))
+    due(second_low)
+    left = product(act, second_low)
     pre = list(pre)
-    for j, d in enumerate(order(tp)):
-        if d > 1:
-            pre[j] = swap(in_line(pre[j]), "tp", d)
+    for j in far + near:
+        pre[j] = swap(in_line(pre[j]), "tp", order(tp)[j])
+    due(hidden_low)
+    out_sum = GradSum(ids, 1, *left)
     if spread:
-        due(hidden_low)
         pieces = attend_back(
             packed[middle:], outs[1], kv, logs[1], marks, carried, query_grads, middle, True
         )
-        due(rows, pre, out_sum.got)
-        pieces = exchange(pieces)
-    hidden_low = cores(hidden_low)
-    rows = cores(rows)
-    pre[order(tp).index(1)] = swap(pre[order(tp).index(1)], "tp", 1)
-    in_sum = GradSum(ids, 1, *products(pre, hidden_low, attended, rows, ctx))
-    out_low = chips(in_line(out_low))
-    out_sum.next()
+    due(rows, pre, out_sum.got)
+    rows = rows + [swap(p, "tp", 1) for p in lined(rows)]
+    if spread:
+        pieces = exchange(lined(pieces))
+    out_sum.halve()
+    left = products(pre, hidden_low, attended, rows, ctx)
+    in_sum = GradSum(ids, 1, *left)
     if spread:
         due(pieces)
+        out_sum.halve()
         whole, send, keep = call(
             functools.partial(input_grad_body, dp=dp, n=heads),
             [shape((length, 3 * lw), BF16), shape((half, width), BF16), shape((half, width), F32)],
@@ -1171,27 +1190,32 @@
             name="input_grad",
         )
     else:
+        out_sum.halve()
         whole = attend_backward(jnp.concatenate(grads))
         total = lax.dot_general(whole, joined, NT, preferred_element_type=F32)
         send, keep = total[half:].astype(BF16), total[:half]
     got = swap(send, "tp", 1)
     mid = width // 2
     send = step(lambda l, r: over_rows(l[:, mid:], r).astype(BF16), x, whole)
-    qkv_sum = GradSum(ids, 0, send, step(lambda l, r: over_rows(l[:, :mid], r), x, whole))
+    qkv_send = in_line(send)
+    in_sum.halve()
+    qkv_sum = GradSum(ids, 0, qkv_send, step(lambda l, r: over_rows(l[:, :mid], r), x, whole))
+    out_sum.merge()
     keep, got = scatter(None, keep, "tp", 0, got)
-    in_sum.next()
-    out_sum.next()
-    output = place(ids, cores(out_low), tp, dp, length)
+    out_low = chips(in_line(out_low))
+    in_sum.halve()
+    qkv_sum.halve()
+    out_sum.last()
     low = step(lambda l, k, f: (f + k + l.astype(F32)).astype(BF16), got, keep, first_grad)
     low = chips(low)
-    qkv_sum.next()
-    in_sum.next()
-    out_sum.next()
-    qkv_sum.next()
-    in_sum.next()
+    qkv_sum.halve()
+    in_sum.merge()
+    output = place(ids, cores(out_low), tp, dp, length)
+    qkv_sum.merge()
+    in_sum.last()
+    (w_out_grad,) = out_sum.columns([width // dp])
+    qkv_sum.last()
     input_grad = place(ids, cores(low), tp, dp, length)
-    qkv_sum.next()
-    (w_out_grad,) = out_sum.columns([width // dp])
     w_in_grad, w_o_grad, terms = in_sum.rows(hidden, lw)
     w_q_grad, w_k_grad, w_v_grad = qkv_sum.columns([lw] * 3)
     return (

time: 525 us -> 490 us (0.933)
  waiting for transfers between devices: 192 us -> 167 us
  starting transfers between devices: 89.2 us -> 80.1 us
    ppermute x77, waiting for transfers between devices: 192 us -> 167 us  [swap(): return lax.ppermute(value, axis, [(i, i ^ bit) for i in range(n)])]
    ppermute x77, starting transfers between devices: 89.2 us -> 80.1 us  [swap(): return lax.ppermute(value, axis, [(i, i ^ bit) for i in range(n)])]
    unnamed x131 -> x140, local copies, waits for them, and re-layouts: 17.9 us -> 17.4 us
  transfers between devices with their start and end apart: 77 -> 77, of which waited for: 24 -> 26; matrix products, arithmetic and copies ran while one was open for 5% -> 5% of each run, Pallas kernels for 33% -> 34%
where the time goes in v4:
time: 490 us; the launch traced here: 482 us
  Pallas kernels  191 us (39%)
  waiting for transfers between devices  167 us (34%)
  starting transfers between devices  80.1 us (16%)
  local copies, waits for them, and re-layouts  23.1 us (5%)
  other arithmetic  11.7 us (2%)
  matrix products  6.92 us (1%)
    pallas_call x28, Pallas kernels, call(): pl.pallas_call(body, out_shape=out_shape, scratch_shapes=list(scratch), c...  191 us
    ppermute x77, waiting for transfers between devices, swap(): return lax.ppermute(value, axis, [(i, i ^ bit) for i in range(n)])  167 us
    ppermute x77, starting transfers between devices, swap(): return lax.ppermute(value, axis, [(i, i ^ bit) for i in range(n)])  80.1 us
    unnamed x140, local copies, waits for them, and re-layouts  17.4 us
  transfers between devices with their start and end apart: 77, of which 26 were waited for; matrix products, arithmetic and copies ran while one was open for 5% of the time, Pallas kernels for 34%

profile of v4, /device:TPU:0, one launch (start us, length us, event | category | flops | bytes accessed | tf_op | source)
XLA Modules:
  0.0 481.6 jit_solution(14123040397802017708)
XLA Ops:
  3.7 3.1 collective-permute-start
  12.7 3.1 arrange.2.x.refs_5_
  18.0 2.7 sine_multiply_fusion
  20.7 2.4 arrange.3.refs_4_
  24.4 5.9 %project.1 = (bf16[1536,128]{1,0:T(8,128)(2,1)}, bf16[1536,128]{1,0:T(8,128)(2,1)}, bf16[1536,128]{1,0:T(8,128)(2,1)}, bf16[1536,128]{1,0:T(8,128)(2,1)}) custom-call(s32[3]{0:T(128)} %pad_add_fusion.1.ids, bf16[1024,1024]{1,0:T(8,128)(2,1)} %arrange.2.x.refs_5_, bf16[512,768]{1,0:T(8,128)(2,1)} %copy-done.8, ...), custom_call_target="tpu_custom_call" | custom-call | flops 1 | bytes 1 | tf_op jit(solution)/shard_map/project/pallas_call | solution.py:113
  32.1 2.5 collective-permute-start.3
  36.6 6.3 %collective-permute-done.3 = s32[1024]{0:T(1024)S(1)} collective-permute-done((s32[1024]{0:T(1024)S(1)}, s32[1024]{0:T(1024)S(1)}, u32[]{:S(2)}, u32[]{:S(2)}) %collective-permute-start.3) | collective-permute-done | bytes 4128 | tf_op jit(solution)/shard_map/ppermute | solution.py:37
  47.5 2.7 select_convert_fusion.refs_4_.refs_9_
  50.2 20.8 %collective-permute-done.6.refs_2_.refs_6_ = bf16[1536,128]{1,0:T(8,128)(2,1)S(1)} collective-permute-done((bf16[1536,128]{1,0:T(8,128)(2,1)}, bf16[1536,128]{1,0:T(8,128)(2,1)S(1)}, u32[]{:S(2)}, u32[]{:S(2)}) %collective-permute-start.6) | collective-permute-done | bytes 393248 | tf_op jit(solution)/shard_map/ppermute | solution.py:37
  74.2 16.2 %attend.2 = (bf16[512,128]{1,0:T(8,128)(2,1)}, bf16[512,128]{1,0:T(8,128)(2,1)}, f32[1024,128]{1,0:T(8,128)}) custom-call(bf16[1536,128]{1,0:T(8,128)(2,1)} %get-tuple-element.181.refs_0_.refs_4_, bf16[1536,128]{1,0:T(8,128)(2,1)} %copy-done.2, bf16[1536,128]{1,0:T(8,128)(2,1)} %copy-done.3, bf16[1536,128]{1,0:T(8,128)(2,1)} %copy-done.4, ...), custom_call_target="tpu_custom_call" | custom-call | flops 1 | bytes 1 | tf_op jit(solution)/shard_map/attend/pallas_call | solution.py:113
  90.4 7.1 %collective-permute-done.10.refs_17_ = bf16[512,1024]{1,0:T(8,128)(2,1)} collective-permute-done((bf16[512,1024]{1,0:T(8,128)(2,1)}, bf16[512,1024]{1,0:T(8,128)(2,1)}, u32[]{:S(2)}, u32[]{:S(2)}) %collective-permute-start.10) | collective-permute-done | bytes 1048608 | tf_op jit(solution)/shard_map/ppermute | solution.py:37
  98.5 16.4 %attend.3 = (bf16[512,128]{1,0:T(8,128)(2,1)}, bf16[512,128]{1,0:T(8,128)(2,1)}, f32[1024,128]{1,0:T(8,128)}) custom-call(bf16[1536,128]{1,0:T(8,128)(2,1)} %get-tuple-element.181.refs_0_.refs_4_, bf16[1536,128]{1,0:T(8,128)(2,1)} %copy-done.2, bf16[1536,128]{1,0:T(8,128)(2,1)} %copy-done.3, bf16[1536,128]{1,0:T(8,128)(2,1)} %copy-done.4, ...), custom_call_target="tpu_custom_call" | custom-call | flops 1 | bytes 1 | tf_op jit(solution)/shard_map/attend/pallas_call | solution.py:113
  115.5 8.9 %collective-permute-start.16 = (bf16[512,128]{1,0:T(8,128)(2,1)S(1)}, bf16[512,128]{1,0:T(8,128)(2,1)S(1)}, u32[]{:S(2)}, u32[]{:S(2)}) collective-permute-start(bf16[512,128]{1,0:T(8,128)(2,1)S(1)} %copy-done.56), channel_id=1, source_target_pairs={{0,4},{4,0},{8,12},{12,8},{1,5},{5,1},{9,13},{13,9},{2,6},{6,2},{1... | collective-permute-start | bytes 393224 | tf_op jit(solution)/shard_map/ppermute | solution.py:37
  125.3 4.4 collective-permute-done.16.refs_1_
  131.3 4.1 collective-permute-done.17.refs_2_
  142.4 4.4 collective-permute-done.22.refs_1_
  150.5 13.7 %forward.1 = (bf16[256,1024]{1,0:T(8,128)(2,1)}, bf16[256,1024]{1,0:T(8,128)(2,1)}, bf16[256,4096]{1,0:T(8,128)(2,1)}, f32[256,1024]{1,0:T(8,128)}, f32[256,128]...) custom-call(bf16[256,256]{1,0:T(8,128)(2,1)} %get-tuple-element.194., ...), custom_call_target="tpu_custom_call" | custom-call | flops 1 | bytes 1 | tf_op jit(solution)/shard_map/forward/pallas_call | solution.py:113
  166.2 12.5 %backward.1 = (bf16[272,1024]{1,0:T(8,128)(2,1)}, f32[256,1024]{1,0:T(8,128)}, bf16[256,1024]{1,0:T(8,128)(2,1)}, bf16[256,1024]{1,0:T(8,128)(2,1)}, bf16[256,10...) custom-call(bf16[256,1024]{1,0:T(8,128)(2,1)} %get-tuple-element.233, ...), custom_call_target="tpu_custom_call" | custom-call | flops 1 | bytes 1 | tf_op jit(solution)/shard_map/backward/pallas_call | solution.py:113
  181.0 4.2 collective-permute-done.29.refs_1_
  191.9 4.5 collective-permute-done.33.refs_1_
  203.3 28.5 %attend_back.2 = (bf16[512,128]{1,0:T(8,128)(2,1)}, bf16[512,128]{1,0:T(8,128)(2,1)}, f32[128,4096]{1,0:T(8,128)}) custom-call(bf16[512,128]{1,0:T(8,128)(2,1)} %get-tuple-element.224.refs_0_, bf16[512,128]{1,0:T(8,128)(2,1)} %copy-done.59, bf16[512,128]{1,0:T(8,128)(2,1)} %get-tuple-element.191.refs_0_.refs_2_, ...), custom_call_target="tpu_custom_call" | custom-call | flops 1 | bytes 1 | tf_op jit(solution)/shard_map/attend_back/pallas_call | solution.py:113
  236.3 5.6 %product.1 = (bf16[1024,512]{1,0:T(8,128)(2,1)}, f32[1024,512]{1,0:T(8,128)}) custom-call(bf16[256,1024]{1,0:T(8,128)(2,1)} %get-tuple-element.235.refs_0_, bf16[256,1024]{1,0:T(8,128)(2,1)} %copy-done.33, bf16[256,1024]{1,0:T(8,128)(2,1)} %copy-done.34, bf16[256,1024]{1,0:T(8,128)(2,1)} %copy-done.38, bf16[256,1024]{1,0:T(8,128)(2,1)} %get-tuple-element.233.refs_0_.refs_4_, ...), custom_call_target="tpu_custom_call" | custom-call | flops 1 | bytes 1 | tf_op jit(solution)/shard_map/product/pallas_call | solution.py:113
  246.8 29.7 %attend_back.3 = (bf16[1536,128]{1,0:T(8,128)(2,1)}, bf16[1536,128]{1,0:T(8,128)(2,1)}, bf16[1536,128]{1,0:T(8,128)(2,1)}, bf16[1536,128]{1,0:T(8,128)(2,1)}) custom-call(bf16[512,128]{1,0:T(8,128)(2,1)} %copy-done.57, bf16[512,128]{1,0:T(8,128)(2,1)} %copy-done.58, bf16[512,128]{1,0:T(8,128)(2,1)} %get-tuple-element.186.refs_2_, ...), custom_call_target="tpu_custom_call" | custom-call | flops 1 | bytes 1 | tf_op jit(solution)/shard_map/attend_back/pallas_call | solution.py:113
  276.6 2.6 collective-permute-done.45.refs_3_
  281.0 3.2 halve.6
  285.8 7.8 %products.1 = (bf16[1344,512]{1,0:T(8,128)(2,1)}, f32[1344,512]{1,0:T(8,128)}) custom-call(bf16[256,1024]{1,0:T(8,128)(2,1)} %get-tuple-element.256.refs_0_, bf16[256,1024]{1,0:T(8,128)(2,1)} %collective-permute-done.43.refs_1_, bf16[256,1024]{1,0:T(8,128)(2,1)} %copy-done.35, bf16[256,1024]{1,0:T(8,128)(2,1)} %copy-done.36, ...), custom_call_target="tpu_custom_call" | custom-call | flops 1 | bytes 1 | tf_op jit(solution)/shard_map/products/pallas_call | solution.py:113
  296.2 2.5 collective-permute-start.51
  300.0 25.3 %collective-permute-done.50.refs_1_ = bf16[1536,128]{1,0:T(8,128)(2,1)S(1)} collective-permute-done((bf16[1536,128]{1,0:T(8,128)(2,1)}, bf16[1536,128]{1,0:T(8,128)(2,1)S(1)}, u32[]{:S(2)}, u32[]{:S(2)}) %collective-permute-start.50) | collective-permute-done | bytes 393248 | tf_op jit(solution)/shard_map/ppermute | solution.py:37
  325.3 10.4 %collective-permute-done.52.refs_3_ = bf16[1536,128]{1,0:T(8,128)(2,1)S(1)} collective-permute-done((bf16[1536,128]{1,0:T(8,128)(2,1)}, bf16[1536,128]{1,0:T(8,128)(2,1)S(1)}, u32[]{:S(2)}, u32[]{:S(2)}) %collective-permute-start.52) | collective-permute-done | bytes 393248 | tf_op jit(solution)/shard_map/ppermute | solution.py:37
  338.9 6.0 %input_grad.1 = (bf16[1024,768]{1,0:T(8,128)(2,1)}, bf16[512,1024]{1,0:T(8,128)(2,1)}, f32[512,1024]{1,0:T(8,128)}) custom-call(s32[3]{0:T(128)} %pad_add_fusion.1.ids, bf16[1536,128]{1,0:T(8,128)(2,1)} %get-tuple-element.269.refs_0_, bf16[1536,128]{1,0:T(8,128)(2,1)} %copy-done.41, bf16[1536,128]{1,0:T(8,128)(2,1)} %copy-done.42, ...), custom_call_target="tpu_custom_call" | custom-call | flops 1 | bytes 1 | tf_op jit(solution)/shard_map/input_grad/pallas_call | solution.py:113
  344.9 3.3 convolution_convert_fusion
  350.8 3.8 halve.8
  356.4 3.6 fusion.keep
  367.3 12.0 %collective-permute-done.62.refs_1_ = bf16[256,1024]{1,0:T(8,128)(2,1)} collective-permute-done((bf16[256,1024]{1,0:T(8,128)(2,1)}, bf16[256,1024]{1,0:T(8,128)(2,1)}, u32[]{:S(2)}, u32[]{:S(2)}) %collective-permute-start.62) | collective-permute-done | bytes 524320 | tf_op jit(solution)/shard_map/ppermute | solution.py:37
  380.2 2.8 halve.9
  383.0 2.8 halve.10
  385.9 3.3 collective-permute-done.60
  393.2 8.1 %collective-permute-done.59.got = bf16[256,768]{1,0:T(8,128)(2,1)} collective-permute-done((bf16[256,768]{1,0:T(8,128)(2,1)}, bf16[256,768]{1,0:T(8,128)(2,1)}, u32[]{:S(2)}, u32[]{:S(2)}) %collective-permute-start.59) | collective-permute-done | bytes 393248 | tf_op jit(solution)/shard_map/ppermute | solution.py:37
  403.4 6.1 %collective-permute-done.57.got = bf16[336,512]{1,0:T(8,128)(2,1)S(1)} collective-permute-done((bf16[336,512]{1,0:T(8,128)(2,1)}, bf16[336,512]{1,0:T(8,128)(2,1)S(1)}, u32[]{:S(2)}, u32[]{:S(2)}) %collective-permute-start.57) | collective-permute-done | bytes 344096 | tf_op jit(solution)/shard_map/ppermute | solution.py:37
  412.2 2.9 collective-permute-start.65
  415.7 20.4 %collective-permute-done.65.got = bf16[128,768]{1,0:T(8,128)(2,1)S(1)} collective-permute-done((bf16[128,768]{1,0:T(8,128)(2,1)}, bf16[128,768]{1,0:T(8,128)(2,1)S(1)}, u32[]{:S(2)}, u32[]{:S(2)}) %collective-permute-start.65) | collective-permute-done | bytes 196640 | tf_op jit(solution)/shard_map/ppermute | solution.py:37
  436.1 3.9 place.2
  446.4 2.7 place_columns.2
  449.1 13.7 %collective-permute-done.69.refs_1_ = bf16[128,768]{1,0:T(8,128)(2,1)S(1)} collective-permute-done((bf16[128,768]{1,0:T(8,128)(2,1)}, bf16[128,768]{1,0:T(8,128)(2,1)S(1)}, u32[]{:S(2)}, u32[]{:S(2)}) %collective-permute-start.69) | collective-permute-done | bytes 196640 | tf_op jit(solution)/shard_map/ppermute | solution.py:37
  462.8 2.9 collective-permute-start.75
  467.2 3.8 place.3
  472.5 3.5 place_rows.1
  478.9 2.5 place_columns.3
  (302 shorter events, 110.3 us)
Async XLA Ops:
  3.7 20.7 %collective-permute-start = (bf16[512,768]{1,0:T(8,128)(2,1)S(1)}, bf16[512,768]{1,0:T(8,128)(2,1)}, u32[]{:S(2)}, u32[]{:S(2)}) collective-permute-start(bf16[512,768]{1,0:T(8,128)(2,1)S(1)} %constant_dynamic-update-slice_fusion.refs_0_.refs_4_), channel_id=1, source_target_pairs={{0,16},{16,0},{1,17},{17,1},{2,18},{18,2},{3,19},{19,3},{4,20},{20... | collective-permute-start | bytes 2359304 | tf_op jit(solution)/shard_map/ppermute | solution.py:37
  10.5 60.5 %collective-permute-start.4 = (bf16[1296,512]{1,0:T(8,128)(2,1)S(1)}, bf16[1296,512]{1,0:T(8,128)(2,1)S(1)}, u32[]{:S(2)}, u32[]{:S(2)}) collective-permute-start(bf16[1296,512]{1,0:T(8,128)(2,1)S(1)} %pad_maximum_fusion.refs_6_), channel_id=1, source_target_pairs={{0,2},{1,3},{2,0},{3,1},{4,6},{5,7},{6,4},{7,5},{8,10},{9,11},{10,... | collective-permute-start | bytes 3981320 | tf_op jit(solution)/shard_map/ppermute | solution.py:37
  30.3 15.7 %collective-permute-start.5 = (bf16[1536,128]{1,0:T(8,128)(2,1)}, bf16[1536,128]{1,0:T(8,128)(2,1)S(1)}, u32[]{:S(2)}, u32[]{:S(2)}) collective-permute-start(bf16[1536,128]{1,0:T(8,128)(2,1)} %get-tuple-element.172), channel_id=1, source_target_pairs={{0,4},{4,0},{8,12},{12,8},{1,5},{5,1},{9,13},{13,9},{2,6},{6,2},{1... | collective-permute-start | bytes 1179656 | tf_op jit(solution)/shard_map/ppermute | solution.py:37
  42.9 28.2 %collective-permute-start.8 = (bf16[512,1024]{1,0:T(8,128)(2,1)}, bf16[512,1024]{1,0:T(8,128)(2,1)S(1)}, u32[]{:S(2)}, u32[]{:S(2)}) collective-permute-start(bf16[512,1024]{1,0:T(8,128)(2,1)} %refs_14_.1), channel_id=1, source_target_pairs={{0,2},{1,3},{2,0},{3,1},{4,6},{5,7},{6,4},{7,5},{8,10},{9,11},{10,... | collective-permute-start | bytes 3145736 | tf_op jit(solution)/shard_map/ppermute | solution.py:37
  44.4 27.3 %collective-permute-start.9 = (bf16[512,1024]{1,0:T(8,128)(2,1)}, bf16[512,1024]{1,0:T(8,128)(2,1)}, u32[]{:S(2)}, u32[]{:S(2)}) collective-permute-start(bf16[512,1024]{1,0:T(8,128)(2,1)} %refs_14_.1), channel_id=1, source_target_pairs={{0,16},{16,0},{1,17},{17,1},{2,18},{18,2},{3,19},{19,3},{4,20},{20... | collective-permute-start | bytes 3145736 | tf_op jit(solution)/shard_map/ppermute | solution.py:37
  46.0 25.1 %collective-permute-start.6 = (bf16[1536,128]{1,0:T(8,128)(2,1)}, bf16[1536,128]{1,0:T(8,128)(2,1)S(1)}, u32[]{:S(2)}, u32[]{:S(2)}) collective-permute-start(bf16[1536,128]{1,0:T(8,128)(2,1)} %get-tuple-element.173), channel_id=1, source_target_pairs={{0,8},{4,12},{8,0},{12,4},{1,9},{5,13},{9,1},{13,5},{2,10},{6,14},... | collective-permute-start | bytes 1179656 | tf_op jit(solution)/shard_map/ppermute | solution.py:37
  46.0 25.0 %collective-permute-start.7 = (bf16[1536,128]{1,0:T(8,128)(2,1)}, bf16[1536,128]{1,0:T(8,128)(2,1)S(1)}, u32[]{:S(2)}, u32[]{:S(2)}) collective-permute-start(bf16[1536,128]{1,0:T(8,128)(2,1)} %get-tuple-element.174), channel_id=1, source_target_pairs={{0,12},{4,8},{8,4},{12,0},{1,13},{5,9},{9,5},{13,1},{2,14},{6,10},... | collective-permute-start | bytes 1179656 | tf_op jit(solution)/shard_map/ppermute | solution.py:37
  71.1 26.4 %collective-permute-start.11 = (bf16[1296,512]{1,0:T(8,128)(2,1)S(1)}, bf16[1296,512]{1,0:T(8,128)(2,1)}, u32[]{:S(2)}, u32[]{:S(2)}) collective-permute-start(bf16[1296,512]{1,0:T(8,128)(2,1)S(1)} %pad_maximum_fusion.refs_6_), channel_id=1, source_target_pairs={{0,1},{1,0},{2,3},{3,2},{4,5},{5,4},{6,7},{7,6},{8,9},{9,8},{10,11... | collective-permute-start | bytes 3981320 | tf_op jit(solution)/shard_map/ppermute | solution.py:37
  71.2 26.3 %collective-permute-start.12 = (bf16[1296,512]{1,0:T(8,128)(2,1)S(1)}, bf16[1296,512]{1,0:T(8,128)(2,1)}, u32[]{:S(2)}, u32[]{:S(2)}) collective-permute-start(bf16[1296,512]{1,0:T(8,128)(2,1)S(1)} %collective-permute-done.4.refs_8_), channel_id=1, source_target_pairs={{0,1},{1,0},{2,3},{3,2},{4,5},{5,4},{6,7},{7,6},{8,9},{9,8},{10,11... | collective-permute-start | bytes 3981320 | tf_op jit(solution)/shard_map/ppermute | solution.py:37
  72.2 25.3 %collective-permute-start.10 = (bf16[512,1024]{1,0:T(8,128)(2,1)}, bf16[512,1024]{1,0:T(8,128)(2,1)}, u32[]{:S(2)}, u32[]{:S(2)}) collective-permute-start(bf16[512,1024]{1,0:T(8,128)(2,1)} %collective-permute-done.9.refs_15_), channel_id=1, source_target_pairs={{0,2},{1,3},{2,0},{3,1},{4,6},{5,7},{6,4},{7,5},{8,10},{9,11},{10,... | collective-permute-start | bytes 3145736 | tf_op jit(solution)/shard_map/ppermute | solution.py:37
  73.6 41.2 %collective-permute-start.15 = (bf16[1296,512]{1,0:T(8,128)(2,1)S(1)}, bf16[1296,512]{1,0:T(8,128)(2,1)}, u32[]{:S(2)}, u32[]{:S(2)}) collective-permute-start(bf16[1296,512]{1,0:T(8,128)(2,1)S(1)} %pad_maximum_fusion.refs_6_), channel_id=1, source_target_pairs={{0,16},{16,0},{1,17},{17,1},{2,18},{18,2},{3,19},{19,3},{4,20},{20... | collective-permute-start | bytes 3981320 | tf_op jit(solution)/shard_map/ppermute | solution.py:37
  97.5 17.4 %collective-permute-start.13 = (bf16[512,1024]{1,0:T(8,128)(2,1)}, bf16[512,1024]{1,0:T(8,128)(2,1)}, u32[]{:S(2)}, u32[]{:S(2)}) collective-permute-start(bf16[512,1024]{1,0:T(8,128)(2,1)} %refs_14_.1), channel_id=1, source_target_pairs={{0,1},{1,0},{2,3},{3,2},{4,5},{5,4},{6,7},{7,6},{8,9},{9,8},{10,11... | collective-permute-start | bytes 3145736 | tf_op jit(solution)/shard_map/ppermute | solution.py:37
  97.5 17.4 %collective-permute-start.14 = (bf16[512,1024]{1,0:T(8,128)(2,1)}, bf16[512,1024]{1,0:T(8,128)(2,1)}, u32[]{:S(2)}, u32[]{:S(2)}) collective-permute-start(bf16[512,1024]{1,0:T(8,128)(2,1)} %collective-permute-done.9.refs_15_), channel_id=1, source_target_pairs={{0,1},{1,0},{2,3},{3,2},{4,5},{5,4},{6,7},{7,6},{8,9},{9,8},{10,11... | collective-permute-start | bytes 3145736 | tf_op jit(solution)/shard_map/ppermute | solution.py:37
  98.0 41.6 %collective-permute-start.21 = (bf16[1296,512]{1,0:T(8,128)(2,1)S(1)}, bf16[1296,512]{1,0:T(8,128)(2,1)}, u32[]{:S(2)}, u32[]{:S(2)}) collective-permute-start(bf16[1296,512]{1,0:T(8,128)(2,1)S(1)} %collective-permute-done.4.refs_8_), channel_id=1, source_target_pairs={{0,16},{16,0},{1,17},{17,1},{2,18},{18,2},{3,19},{19,3},{4,20},{20... | collective-permute-start | bytes 3981320 | tf_op jit(solution)/shard_map/ppermute | solution.py:37
  114.9 21.9 %collective-permute-start.19 = (bf16[512,1024]{1,0:T(8,128)(2,1)S(1)}, bf16[512,1024]{1,0:T(8,128)(2,1)S(1)}, u32[]{:S(2)}, u32[]{:S(2)}) collective-permute-start(bf16[512,1024]{1,0:T(8,128)(2,1)S(1)} %copy-done.10), channel_id=1, source_target_pairs={{0,1},{1,0},{2,3},{3,2},{4,5},{5,4},{6,7},{7,6},{8,9},{9,8},{10,11... | collective-permute-start | bytes 3145736 | tf_op jit(solution)/shard_map/ppermute | solution.py:37
  115.0 21.9 %collective-permute-start.20 = (bf16[512,1024]{1,0:T(8,128)(2,1)}, bf16[512,1024]{1,0:T(8,128)(2,1)}, u32[]{:S(2)}, u32[]{:S(2)}) collective-permute-start(bf16[512,1024]{1,0:T(8,128)(2,1)} %collective-permute-done.10.refs_17_), channel_id=1, source_target_pairs={{0,1},{1,0},{2,3},{3,2},{4,5},{5,4},{6,7},{7,6},{8,9},{9,8},{10,11... | collective-permute-start | bytes 3145736 | tf_op jit(solution)/shard_map/ppermute | solution.py:37
  196.4 35.4 %collective-permute-start.35 = (bf16[256,1024]{1,0:T(8,128)(2,1)S(1)}, bf16[256,1024]{1,0:T(8,128)(2,1)S(1)}, u32[]{:S(2)}, u32[]{:S(2)}) collective-permute-start(bf16[256,1024]{1,0:T(8,128)(2,1)S(1)} %copy-done.14), channel_id=1, source_target_pairs={{0,2},{1,3},{2,0},{3,1},{4,6},{5,7},{6,4},{7,5},{8,10},{9,11},{10,... | collective-permute-start | bytes 1572872 | tf_op jit(solution)/shard_map/ppermute | solution.py:37
  197.6 34.3 %collective-permute-start.36 = (bf16[256,1024]{1,0:T(8,128)(2,1)}, bf16[256,1024]{1,0:T(8,128)(2,1)S(1)}, u32[]{:S(2)}, u32[]{:S(2)}) collective-permute-start(bf16[256,1024]{1,0:T(8,128)(2,1)} %get-tuple-element.230), channel_id=1, source_target_pairs={{0,3},{1,2},{2,1},{3,0},{4,7},{5,6},{6,5},{7,4},{8,11},{9,10},{10,... | collective-permute-start | bytes 1572872 | tf_op jit(solution)/shard_map/ppermute | solution.py:37
  197.8 34.9 %collective-permute-start.37 = (bf16[256,1024]{1,0:T(8,128)(2,1)S(1)}, bf16[256,1024]{1,0:T(8,128)(2,1)S(1)}, u32[]{:S(2)}, u32[]{:S(2)}) collective-permute-start(bf16[256,1024]{1,0:T(8,128)(2,1)S(1)} %copy-done.31), channel_id=1, source_target_pairs={{0,2},{1,3},{2,0},{3,1},{4,6},{5,7},{6,4},{7,5},{8,10},{9,11},{10,... | collective-permute-start | bytes 1572872 | tf_op jit(solution)/shard_map/ppermute | solution.py:37
  199.0 32.8 %collective-permute-start.32 = (bf16[512,128]{1,0:T(8,128)(2,1)}, bf16[512,128]{1,0:T(8,128)(2,1)S(1)}, u32[]{:S(2)}, u32[]{:S(2)}) collective-permute-start(bf16[512,128]{1,0:T(8,128)(2,1)} %get-tuple-element.220), channel_id=1, source_target_pairs={{0,8},{4,12},{8,0},{12,4},{1,9},{5,13},{9,1},{13,5},{2,10},{6,14},... | collective-permute-start | bytes 393224 | tf_op jit(solution)/shard_map/ppermute | solution.py:37
  201.3 30.5 %collective-permute-start.34 = (bf16[512,128]{1,0:T(8,128)(2,1)}, bf16[512,128]{1,0:T(8,128)(2,1)S(1)}, u32[]{:S(2)}, u32[]{:S(2)}) collective-permute-start(bf16[512,128]{1,0:T(8,128)(2,1)} %get-tuple-element.227), channel_id=1, source_target_pairs={{0,12},{4,8},{8,4},{12,0},{1,13},{5,9},{9,5},{13,1},{2,14},{6,10},... | collective-permute-start | bytes 393224 | tf_op jit(solution)/shard_map/ppermute | solution.py:37
  242.0 37.3 %collective-permute-start.46 = (bf16[1024,512]{1,0:T(8,128)(2,1)}, bf16[1024,512]{1,0:T(8,128)(2,1)S(1)}, u32[]{:S(2)}, u32[]{:S(2)}) collective-permute-start(bf16[1024,512]{1,0:T(8,128)(2,1)} %get-tuple-element.236), channel_id=1, source_target_pairs={{0,16},{16,0},{1,17},{17,1},{2,18},{18,2},{3,19},{19,3},{4,20},{20... | collective-permute-start | bytes 3145736 | tf_op jit(solution)/shard_map/ppermute | solution.py:37
  243.5 33.1 %collective-permute-start.42 = (bf16[272,1024]{1,0:T(8,128)(2,1)S(1)}, bf16[272,1024]{1,0:T(8,128)(2,1)S(1)}, u32[]{:S(2)}, u32[]{:S(2)}) collective-permute-start(bf16[272,1024]{1,0:T(8,128)(2,1)S(1)} %copy-done.23), channel_id=1, source_target_pairs={{0,2},{1,3},{2,0},{3,1},{4,6},{5,7},{6,4},{7,5},{8,10},{9,11},{10,... | collective-permute-start | bytes 1671176 | tf_op jit(solution)/shard_map/ppermute | solution.py:37
  244.7 31.9 %collective-permute-start.43 = (bf16[256,1024]{1,0:T(8,128)(2,1)}, bf16[256,1024]{1,0:T(8,128)(2,1)}, u32[]{:S(2)}, u32[]{:S(2)}) collective-permute-start(bf16[256,1024]{1,0:T(8,128)(2,1)} %get-tuple-element.247), channel_id=1, source_target_pairs={{0,2},{1,3},{2,0},{3,1},{4,6},{5,7},{6,4},{7,5},{8,10},{9,11},{10,... | collective-permute-start | bytes 1572872 | tf_op jit(solution)/shard_map/ppermute | solution.py:37
  245.5 31.1 %collective-permute-start.44 = (bf16[256,1024]{1,0:T(8,128)(2,1)}, bf16[256,1024]{1,0:T(8,128)(2,1)S(1)}, u32[]{:S(2)}, u32[]{:S(2)}) collective-permute-start(bf16[256,1024]{1,0:T(8,128)(2,1)} %get-tuple-element.249), channel_id=1, source_target_pairs={{0,1},{1,0},{2,3},{3,2},{4,5},{5,4},{6,7},{7,6},{8,9},{9,8},{10,11... | collective-permute-start | bytes 1572872 | tf_op jit(solution)/shard_map/ppermute | solution.py:37
  245.5 33.7 %collective-permute-start.45 = (bf16[256,1024]{1,0:T(8,128)(2,1)}, bf16[256,1024]{1,0:T(8,128)(2,1)S(1)}, u32[]{:S(2)}, u32[]{:S(2)}) collective-permute-start(bf16[256,1024]{1,0:T(8,128)(2,1)} %get-tuple-element.251), channel_id=1, source_target_pairs={{0,3},{1,2},{2,1},{3,0},{4,7},{5,6},{6,5},{7,4},{8,11},{9,10},{10,... | collective-permute-start | bytes 1572872 | tf_op jit(solution)/shard_map/ppermute | solution.py:37
  293.7 56.0 %collective-permute-start.55 = (bf16[1344,512]{1,0:T(8,128)(2,1)}, bf16[1344,512]{1,0:T(8,128)(2,1)S(1)}, u32[]{:S(2)}, u32[]{:S(2)}) collective-permute-start(bf16[1344,512]{1,0:T(8,128)(2,1)} %get-tuple-element.259), channel_id=1, source_target_pairs={{0,16},{16,0},{1,17},{17,1},{2,18},{18,2},{3,19},{19,3},{4,20},{20... | collective-permute-start | bytes 4128776 | tf_op jit(solution)/shard_map/ppermute | solution.py:37
  294.1 41.5 %collective-permute-start.47 = (bf16[512,512]{1,0:T(8,128)(2,1)}, bf16[512,512]{1,0:T(8,128)(2,1)S(1)}, u32[]{:S(2)}, u32[]{:S(2)}) collective-permute-start(bf16[512,512]{1,0:T(8,128)(2,1)} %get-tuple-element.255), channel_id=1, source_target_pairs={{0,4},{4,0},{8,12},{12,8},{1,5},{5,1},{9,13},{13,9},{2,6},{6,2},{1... | collective-permute-start | bytes 1572872 | tf_op jit(solution)/shard_map/ppermute | solution.py:37
  295.6 29.7 %collective-permute-start.50 = (bf16[1536,128]{1,0:T(8,128)(2,1)}, bf16[1536,128]{1,0:T(8,128)(2,1)S(1)}, u32[]{:S(2)}, u32[]{:S(2)}) collective-permute-start(bf16[1536,128]{1,0:T(8,128)(2,1)} %get-tuple-element.261), channel_id=1, source_target_pairs={{0,4},{4,0},{8,12},{12,8},{1,5},{5,1},{9,13},{13,9},{2,6},{6,2},{1... | collective-permute-start | bytes 1179656 | tf_op jit(solution)/shard_map/ppermute | solution.py:37
  296.2 29.1 %collective-permute-start.51 = (bf16[1536,128]{1,0:T(8,128)(2,1)}, bf16[1536,128]{1,0:T(8,128)(2,1)S(1)}, u32[]{:S(2)}, u32[]{:S(2)}) collective-permute-start(bf16[1536,128]{1,0:T(8,128)(2,1)} %get-tuple-element.263), channel_id=1, source_target_pairs={{0,8},{4,12},{8,0},{12,4},{1,9},{5,13},{9,1},{13,5},{2,10},{6,14},... | collective-permute-start | bytes 1179656 | tf_op jit(solution)/shard_map/ppermute | solution.py:37
  298.7 37.0 %collective-permute-start.52 = (bf16[1536,128]{1,0:T(8,128)(2,1)}, bf16[1536,128]{1,0:T(8,128)(2,1)S(1)}, u32[]{:S(2)}, u32[]{:S(2)}) collective-permute-start(bf16[1536,128]{1,0:T(8,128)(2,1)} %get-tuple-element.265), channel_id=1, source_target_pairs={{0,12},{4,8},{8,4},{12,0},{1,13},{5,9},{9,5},{13,1},{2,14},{6,10},... | collective-permute-start | bytes 1179656 | tf_op jit(solution)/shard_map/ppermute | solution.py:37
  344.8 17.8 %collective-permute-start.53 = (bf16[512,1024]{1,0:T(8,128)(2,1)}, bf16[512,1024]{1,0:T(8,128)(2,1)}, u32[]{:S(2)}, u32[]{:S(2)}) collective-permute-start(bf16[512,1024]{1,0:T(8,128)(2,1)} %get-tuple-element.271), channel_id=1, source_target_pairs={{0,1},{1,0},{2,3},{3,2},{4,5},{5,4},{6,7},{7,6},{8,9},{9,8},{10,11... | collective-permute-start | bytes 3145736 | tf_op jit(solution)/shard_map/ppermute | solution.py:37
  348.2 34.8 %collective-permute-start.58 = (bf16[512,768]{1,0:T(8,128)(2,1)}, bf16[512,768]{1,0:T(8,128)(2,1)}, u32[]{:S(2)}, u32[]{:S(2)}) collective-permute-start(bf16[512,768]{1,0:T(8,128)(2,1)} %convolution_convert_fusion), channel_id=1, source_target_pairs={{0,16},{16,0},{1,17},{17,1},{2,18},{18,2},{3,19},{19,3},{4,20},{20... | collective-permute-start | bytes 2359304 | tf_op jit(solution)/shard_map/ppermute | solution.py:37
  354.6 24.8 %collective-permute-start.56 = (bf16[672,512]{1,0:T(8,128)(2,1)}, bf16[672,512]{1,0:T(8,128)(2,1)S(1)}, u32[]{:S(2)}, u32[]{:S(2)}) collective-permute-start(bf16[672,512]{1,0:T(8,128)(2,1)} %get-tuple-element.276), channel_id=1, source_target_pairs={{0,4},{4,0},{8,12},{12,8},{1,5},{5,1},{9,13},{13,9},{2,6},{6,2},{1... | collective-permute-start | bytes 2064392 | tf_op jit(solution)/shard_map/ppermute | solution.py:37
  365.8 23.4 %collective-permute-start.60 = (bf16[256,1024]{1,0:T(8,128)(2,1)S(1)}, bf16[256,1024]{1,0:T(8,128)(2,1)}, u32[]{:S(2)}, u32[]{:S(2)}) collective-permute-start(bf16[256,1024]{1,0:T(8,128)(2,1)S(1)} %add_convert_fusion.1), channel_id=1, source_target_pairs={{0,2},{1,3},{2,0},{3,1},{4,6},{5,7},{6,4},{7,5},{8,10},{9,11},{10,... | collective-permute-start | bytes 1572872 | tf_op jit(solution)/shard_map/ppermute | solution.py:37
  366.3 19.7 %collective-permute-start.61 = (bf16[256,512]{1,0:T(8,128)(2,1)S(1)}, bf16[256,512]{1,0:T(8,128)(2,1)}, u32[]{:S(2)}, u32[]{:S(2)}) collective-permute-start(bf16[256,512]{1,0:T(8,128)(2,1)S(1)} %copy-done.20), channel_id=1, source_target_pairs={{0,8},{4,12},{8,0},{12,4},{1,9},{5,13},{9,1},{13,5},{2,10},{6,14},... | collective-permute-start | bytes 786440 | tf_op jit(solution)/shard_map/ppermute | solution.py:37
  379.3 35.8 %collective-permute-start.63 = (bf16[256,1024]{1,0:T(8,128)(2,1)}, bf16[256,1024]{1,0:T(8,128)(2,1)}, u32[]{:S(2)}, u32[]{:S(2)}) collective-permute-start(bf16[256,1024]{1,0:T(8,128)(2,1)} %get-tuple-element.295.refs_0_), channel_id=1, source_target_pairs={{0,1},{1,0},{2,3},{3,2},{4,5},{5,4},{6,7},{7,6},{8,9},{9,8},{10,11... | collective-permute-start | bytes 1572872 | tf_op jit(solution)/shard_map/ppermute | solution.py:37
  379.4 35.8 %collective-permute-start.64 = (bf16[256,1024]{1,0:T(8,128)(2,1)}, bf16[256,1024]{1,0:T(8,128)(2,1)}, u32[]{:S(2)}, u32[]{:S(2)}) collective-permute-start(bf16[256,1024]{1,0:T(8,128)(2,1)} %collective-permute-done.62.refs_1_), channel_id=1, source_target_pairs={{0,1},{1,0},{2,3},{3,2},{4,5},{5,4},{6,7},{7,6},{8,9},{9,8},{10,11... | collective-permute-start | bytes 1572872 | tf_op jit(solution)/shard_map/ppermute | solution.py:37
  390.8 24.5 %collective-permute-start.70 = (bf16[256,1024]{1,0:T(8,128)(2,1)S(1)}, bf16[256,1024]{1,0:T(8,128)(2,1)S(1)}, u32[]{:S(2)}, u32[]{:S(2)}) collective-permute-start(bf16[256,1024]{1,0:T(8,128)(2,1)S(1)} %add_convert_fusion.refs_0_), channel_id=1, source_target_pairs={{0,2},{1,3},{2,0},{3,1},{4,6},{5,7},{6,4},{7,5},{8,10},{9,11},{10,... | collective-permute-start | bytes 1572872 | tf_op jit(solution)/shard_map/ppermute | solution.py:37
  392.5 17.0 %collective-permute-start.57 = (bf16[336,512]{1,0:T(8,128)(2,1)}, bf16[336,512]{1,0:T(8,128)(2,1)S(1)}, u32[]{:S(2)}, u32[]{:S(2)}) collective-permute-start(bf16[336,512]{1,0:T(8,128)(2,1)} %get-tuple-element.284), channel_id=1, source_target_pairs={{0,8},{4,12},{8,0},{12,4},{1,9},{5,13},{9,1},{13,5},{2,10},{6,14},... | collective-permute-start | bytes 1032200 | tf_op jit(solution)/shard_map/ppermute | solution.py:37
  412.2 29.6 %collective-permute-start.66 = (bf16[336,512]{1,0:T(8,128)(2,1)}, bf16[336,512]{1,0:T(8,128)(2,1)S(1)}, u32[]{:S(2)}, u32[]{:S(2)}) collective-permute-start(bf16[336,512]{1,0:T(8,128)(2,1)} %merge.4.refs_0_), channel_id=1, source_target_pairs={{0,8},{4,12},{8,0},{12,4},{1,9},{5,13},{9,1},{13,5},{2,10},{6,14},... | collective-permute-start | bytes 1032200 | tf_op jit(solution)/shard_map/ppermute | solution.py:37
  412.2 23.9 %collective-permute-start.65 = (bf16[128,768]{1,0:T(8,128)(2,1)}, bf16[128,768]{1,0:T(8,128)(2,1)S(1)}, u32[]{:S(2)}, u32[]{:S(2)}) collective-permute-start(bf16[128,768]{1,0:T(8,128)(2,1)} %get-tuple-element.292), channel_id=1, source_target_pairs={{0,8},{4,12},{8,0},{12,4},{1,9},{5,13},{9,1},{13,5},{2,10},{6,14},... | collective-permute-start | bytes 589832 | tf_op jit(solution)/shard_map/ppermute | solution.py:37
  415.2 28.7 %collective-permute-start.67 = (bf16[256,512]{1,0:T(8,128)(2,1)S(1)}, bf16[256,512]{1,0:T(8,128)(2,1)}, u32[]{:S(2)}, u32[]{:S(2)}) collective-permute-start(bf16[256,512]{1,0:T(8,128)(2,1)S(1)} %copy-done.20), channel_id=1, source_target_pairs={{0,4},{4,0},{8,12},{12,8},{1,5},{5,1},{9,13},{13,9},{2,6},{6,2},{1... | collective-permute-start | bytes 786440 | tf_op jit(solution)/shard_map/ppermute | solution.py:37
  415.2 50.5 %collective-permute-start.71 = (bf16[256,1024]{1,0:T(8,128)(2,1)S(1)}, bf16[256,1024]{1,0:T(8,128)(2,1)S(1)}, u32[]{:S(2)}, u32[]{:S(2)}) collective-permute-start(bf16[256,1024]{1,0:T(8,128)(2,1)S(1)} %add_convert_fusion.refs_0_), channel_id=1, source_target_pairs={{0,1},{1,0},{2,3},{3,2},{4,5},{5,4},{6,7},{7,6},{8,9},{9,8},{10,11... | collective-permute-start | bytes 1572872 | tf_op jit(solution)/shard_map/ppermute | solution.py:37
  415.3 50.5 %collective-permute-start.72 = (bf16[256,1024]{1,0:T(8,128)(2,1)S(1)}, bf16[256,1024]{1,0:T(8,128)(2,1)S(1)}, u32[]{:S(2)}, u32[]{:S(2)}) collective-permute-start(bf16[256,1024]{1,0:T(8,128)(2,1)S(1)} %collective-permute-done.70.refs_1_), channel_id=1, source_target_pairs={{0,1},{1,0},{2,3},{3,2},{4,5},{5,4},{6,7},{7,6},{8,9},{9,8},{10,11... | collective-permute-start | bytes 1572872 | tf_op jit(solution)/shard_map/ppermute | solution.py:37
  441.8 29.2 %collective-permute-start.73 = (bf16[336,512]{1,0:T(8,128)(2,1)S(1)}, bf16[336,512]{1,0:T(8,128)(2,1)S(1)}, u32[]{:S(2)}, u32[]{:S(2)}) collective-permute-start(bf16[336,512]{1,0:T(8,128)(2,1)S(1)} %copy-done.16), channel_id=1, source_target_pairs={{0,4},{4,0},{8,12},{12,8},{1,5},{5,1},{9,13},{13,9},{2,6},{6,2},{1... | collective-permute-start | bytes 1032200 | tf_op jit(solution)/shard_map/ppermute | solution.py:37
  443.9 27.2 %collective-permute-start.74 = (bf16[336,512]{1,0:T(8,128)(2,1)S(1)}, bf16[336,512]{1,0:T(8,128)(2,1)S(1)}, u32[]{:S(2)}, u32[]{:S(2)}) collective-permute-start(bf16[336,512]{1,0:T(8,128)(2,1)S(1)} %collective-permute-done.66.refs_1_), channel_id=1, source_target_pairs={{0,4},{4,0},{8,12},{12,8},{1,5},{5,1},{9,13},{13,9},{2,6},{6,2},{1... | collective-permute-start | bytes 1032200 | tf_op jit(solution)/shard_map/ppermute | solution.py:37
  444.7 18.1 %collective-permute-start.69 = (bf16[128,768]{1,0:T(8,128)(2,1)}, bf16[128,768]{1,0:T(8,128)(2,1)S(1)}, u32[]{:S(2)}, u32[]{:S(2)}) collective-permute-start(bf16[128,768]{1,0:T(8,128)(2,1)} %merge.5.refs_0_), channel_id=1, source_target_pairs={{0,8},{4,12},{8,0},{12,4},{1,9},{5,13},{9,1},{13,5},{2,10},{6,14},... | collective-permute-start | bytes 589832 | tf_op jit(solution)/shard_map/ppermute | solution.py:37
  (97 other events, 992.7 us)

commit v5 on v4

--- a/solution.py
+++ b/solution.py
@@ -1062,8 +1062,7 @@
         lane = jnp.arange(LANES)[None, :]
         in_docs = (lane >= HEAD) & (lane < HEAD + DOCS)
         folded = (lane >= HEAD + DOCS) & (lane < HEAD + DOCS + 3)
-        due(w_qkv)
-        wi_far = chips(in_line(w_in))
+        due(w_qkv, all_docs)
         wi = gather(in_line(w_in), "dp")
         kv = call(
             functools.partial(project_body, dp=dp, n=heads),
@@ -1079,6 +1078,7 @@
         )
         kv = exchange(kv)
         marks = step(lambda d: jnp.where(in_docs, lane - HEAD != d[:, None], folded).astype(BF16), all_docs)
+        wi_far = chips(in_line(w_in))
         due(tall, kv, wi_far)
         tall_cores = [[swap(in_line(p), "tp", 1)] for p in tall]
         tall_own = gather(in_line(tall[0]), "dp")
@@ -1210,12 +1210,14 @@
     low = chips(low)
     qkv_sum.halve()
     in_sum.merge()
-    output = place(ids, cores(out_low), tp, dp, length)
+    due(out_low)
+    output = place(ids, out_low + [swap(p, "tp", 1) for p in lined(out_low)], tp, dp, length)
     qkv_sum.merge()
     in_sum.last()
     (w_out_grad,) = out_sum.columns([width // dp])
     qkv_sum.last()
-    input_grad = place(ids, cores(low), tp, dp, length)
+    due(low)
+    input_grad = place(ids, low + [swap(p, "tp", 1) for p in lined(low)], tp, dp, length)
     w_in_grad, w_o_grad, terms = in_sum.rows(hidden, lw)
     w_q_grad, w_k_grad, w_v_grad = qkv_sum.columns([lw] * 3)
     return (

time: 490 us -> 481 us (0.982)
  waiting for transfers between devices: 167 us -> 149 us
  starting transfers between devices: 80.1 us -> 85.8 us
    ppermute x77, waiting for transfers between devices: 167 us -> 149 us  [swap(): return lax.ppermute(value, axis, [(i, i ^ bit) for i in range(n)])]
    ppermute x77, starting transfers between devices: 80.1 us -> 85.8 us  [swap(): return lax.ppermute(value, axis, [(i, i ^ bit) for i in range(n)])]
    unnamed x140 -> x157, local copies, waits for them, and re-layouts: 17.4 us -> 18.4 us
  transfers between devices with their start and end apart: 77 -> 77, of which waited for: 26 -> 25; matrix products, arithmetic and copies ran while one was open for 5% -> 5% of each run, Pallas kernels for 34% -> 35%
where the time goes in v5:
time: 481 us; the launch traced here: 472 us
  Pallas kernels  192 us (40%)
  waiting for transfers between devices  149 us (31%)
  starting transfers between devices  85.8 us (18%)
  local copies, waits for them, and re-layouts  24.1 us (5%)
  other arithmetic  13.1 us (3%)
  matrix products  6.95 us (1%)
    pallas_call x28, Pallas kernels, call(): pl.pallas_call(body, out_shape=out_shape, scratch_shapes=list(scratch), c...  192 us
    ppermute x77, waiting for transfers between devices, swap(): return lax.ppermute(value, axis, [(i, i ^ bit) for i in range(n)])  149 us
    ppermute x77, starting transfers between devices, swap(): return lax.ppermute(value, axis, [(i, i ^ bit) for i in range(n)])  85.8 us
    unnamed x157, local copies, waits for them, and re-layouts  18.4 us
  transfers between devices with their start and end apart: 77, of which 25 were waited for; matrix products, arithmetic and copies ran while one was open for 5% of the time, Pallas kernels for 35%

profile of v5, /device:TPU:0, one launch (start us, length us, event | category | flops | bytes accessed | tf_op | source)
XLA Modules:
  0.0 472.3 jit_solution(17722818869986821410)
XLA Ops:
  3.7 3.1 collective-permute-start
  12.8 3.1 arrange.2.x.refs_5_
  17.8 3.7 collective-permute-start.3
  22.5 2.7 sine_multiply_fusion
  27.7 5.9 %project.1 = (bf16[1536,128]{1,0:T(8,128)(2,1)}, bf16[1536,128]{1,0:T(8,128)(2,1)}, bf16[1536,128]{1,0:T(8,128)(2,1)}, bf16[1536,128]{1,0:T(8,128)(2,1)}) custom-call(s32[3]{0:T(128)} %pad_add_fusion.ids, bf16[1024,1024]{1,0:T(8,128)(2,1)} %arrange.2.x.refs_5_, bf16[512,768]{1,0:T(8,128)(2,1)} %copy-done.8, ...), custom_call_target="tpu_custom_call" | custom-call | flops 1 | bytes 1 | tf_op jit(solution)/shard_map/project/pallas_call | solution.py:113
  33.6 2.7 select_convert_fusion.refs_4_.refs_9_
  38.6 2.9 collective-permute-start.6
  41.5 12.9 %collective-permute-done.5.refs_1_.refs_5_ = bf16[1536,128]{1,0:T(8,128)(2,1)S(1)} collective-permute-done((bf16[1536,128]{1,0:T(8,128)(2,1)}, bf16[1536,128]{1,0:T(8,128)(2,1)S(1)}, u32[]{:S(2)}, u32[]{:S(2)}) %collective-permute-start.5) | collective-permute-done | bytes 393248 | tf_op jit(solution)/shard_map/ppermute | solution.py:37
  54.4 2.5 collective-permute-start.7
  56.9 9.1 %collective-permute-done.6.refs_2_.refs_6_ = bf16[1536,128]{1,0:T(8,128)(2,1)S(1)} collective-permute-done((bf16[1536,128]{1,0:T(8,128)(2,1)}, bf16[1536,128]{1,0:T(8,128)(2,1)S(1)}, u32[]{:S(2)}, u32[]{:S(2)}) %collective-permute-start.6) | collective-permute-done | bytes 393248 | tf_op jit(solution)/shard_map/ppermute | solution.py:37
  71.1 16.2 %attend.2 = (bf16[512,128]{1,0:T(8,128)(2,1)}, bf16[512,128]{1,0:T(8,128)(2,1)}, f32[1024,128]{1,0:T(8,128)}) custom-call(bf16[1536,128]{1,0:T(8,128)(2,1)} %get-tuple-element.185.refs_0_.refs_4_, bf16[1536,128]{1,0:T(8,128)(2,1)} %copy-done.2, bf16[1536,128]{1,0:T(8,128)(2,1)} %copy-done.3, bf16[1536,128]{1,0:T(8,128)(2,1)} %copy-done.4, ...), custom_call_target="tpu_custom_call" | custom-call | flops 1 | bytes 1 | tf_op jit(solution)/shard_map/attend/pallas_call | solution.py:113
  87.3 4.8 %collective-permute-done.10.refs_17_ = bf16[512,1024]{1,0:T(8,128)(2,1)} collective-permute-done((bf16[512,1024]{1,0:T(8,128)(2,1)}, bf16[512,1024]{1,0:T(8,128)(2,1)}, u32[]{:S(2)}, u32[]{:S(2)}) %collective-permute-start.10) | collective-permute-done | bytes 1048608 | tf_op jit(solution)/shard_map/ppermute | solution.py:37
  95.1 16.4 %attend.3 = (bf16[512,128]{1,0:T(8,128)(2,1)}, bf16[512,128]{1,0:T(8,128)(2,1)}, f32[1024,128]{1,0:T(8,128)}) custom-call(bf16[1536,128]{1,0:T(8,128)(2,1)} %get-tuple-element.185.refs_0_.refs_4_, bf16[1536,128]{1,0:T(8,128)(2,1)} %copy-done.2, bf16[1536,128]{1,0:T(8,128)(2,1)} %copy-done.3, bf16[1536,128]{1,0:T(8,128)(2,1)} %copy-done.4, ...), custom_call_target="tpu_custom_call" | custom-call | flops 1 | bytes 1 | tf_op jit(solution)/shard_map/attend/pallas_call | solution.py:113
  112.1 7.5 %collective-permute-start.16 = (bf16[512,128]{1,0:T(8,128)(2,1)S(1)}, bf16[512,128]{1,0:T(8,128)(2,1)S(1)}, u32[]{:S(2)}, u32[]{:S(2)}) collective-permute-start(bf16[512,128]{1,0:T(8,128)(2,1)S(1)} %copy-done.60), channel_id=1, source_target_pairs={{0,4},{4,0},{8,12},{12,8},{1,5},{5,1},{9,13},{13,9},{2,6},{6,2},{1... | collective-permute-start | bytes 393224 | tf_op jit(solution)/shard_map/ppermute | solution.py:37
  120.5 4.4 collective-permute-done.16.refs_1_
  126.5 5.5 %collective-permute-done.17.refs_2_ = bf16[512,128]{1,0:T(8,128)(2,1)S(1)} collective-permute-done((bf16[512,128]{1,0:T(8,128)(2,1)}, bf16[512,128]{1,0:T(8,128)(2,1)S(1)}, u32[]{:S(2)}, u32[]{:S(2)}) %collective-permute-start.17) | collective-permute-done | bytes 131104 | tf_op jit(solution)/shard_map/ppermute | solution.py:37
  138.0 4.4 collective-permute-done.22.refs_1_
  145.7 13.6 %forward.1 = (bf16[256,1024]{1,0:T(8,128)(2,1)}, bf16[256,1024]{1,0:T(8,128)(2,1)}, bf16[256,4096]{1,0:T(8,128)(2,1)}, f32[256,1024]{1,0:T(8,128)}, f32[256,128]...) custom-call(bf16[256,256]{1,0:T(8,128)(2,1)} %get-tuple-element.198., ...), custom_call_target="tpu_custom_call" | custom-call | flops 1 | bytes 1 | tf_op jit(solution)/shard_map/forward/pallas_call | solution.py:113
  161.3 12.5 %backward.1 = (bf16[272,1024]{1,0:T(8,128)(2,1)}, f32[256,1024]{1,0:T(8,128)}, bf16[256,1024]{1,0:T(8,128)(2,1)}, bf16[256,1024]{1,0:T(8,128)(2,1)}, bf16[256,10...) custom-call(bf16[256,1024]{1,0:T(8,128)(2,1)} %get-tuple-element.237, ...), custom_call_target="tpu_custom_call" | custom-call | flops 1 | bytes 1 | tf_op jit(solution)/shard_map/backward/pallas_call | solution.py:113
  176.4 4.2 collective-permute-done.29.refs_1_
  184.6 2.9 collective-permute-start.33
  187.5 4.5 collective-permute-done.33.refs_1_
  194.7 2.7 collective-permute-start.32
  198.9 28.5 %attend_back.2 = (bf16[512,128]{1,0:T(8,128)(2,1)}, bf16[512,128]{1,0:T(8,128)(2,1)}, f32[128,4096]{1,0:T(8,128)}) custom-call(bf16[512,128]{1,0:T(8,128)(2,1)} %get-tuple-element.228.refs_0_, bf16[512,128]{1,0:T(8,128)(2,1)} %copy-done.63, bf16[512,128]{1,0:T(8,128)(2,1)} %get-tuple-element.195.refs_0_.refs_2_, ...), custom_call_target="tpu_custom_call" | custom-call | flops 1 | bytes 1 | tf_op jit(solution)/shard_map/attend_back/pallas_call | solution.py:113
  231.9 5.6 %product.1 = (bf16[1024,512]{1,0:T(8,128)(2,1)}, f32[1024,512]{1,0:T(8,128)}) custom-call(bf16[256,1024]{1,0:T(8,128)(2,1)} %get-tuple-element.239.refs_0_, bf16[256,1024]{1,0:T(8,128)(2,1)} %copy-done.35, bf16[256,1024]{1,0:T(8,128)(2,1)} %copy-done.36, bf16[256,1024]{1,0:T(8,128)(2,1)} %copy-done.40, bf16[256,1024]{1,0:T(8,128)(2,1)} %get-tuple-element.237.refs_0_.refs_4_, ...), custom_call_target="tpu_custom_call" | custom-call | flops 1 | bytes 1 | tf_op jit(solution)/shard_map/product/pallas_call | solution.py:113
  241.4 29.7 %attend_back.3 = (bf16[1536,128]{1,0:T(8,128)(2,1)}, bf16[1536,128]{1,0:T(8,128)(2,1)}, bf16[1536,128]{1,0:T(8,128)(2,1)}, bf16[1536,128]{1,0:T(8,128)(2,1)}) custom-call(bf16[512,128]{1,0:T(8,128)(2,1)} %copy-done.61, bf16[512,128]{1,0:T(8,128)(2,1)} %copy-done.62, bf16[512,128]{1,0:T(8,128)(2,1)} %get-tuple-element.190.refs_2_, ...), custom_call_target="tpu_custom_call" | custom-call | flops 1 | bytes 1 | tf_op jit(solution)/shard_map/attend_back/pallas_call | solution.py:113
  271.2 2.6 collective-permute-done.45.refs_3_
  275.5 3.2 halve.6
  280.4 7.8 %products.1 = (bf16[1344,512]{1,0:T(8,128)(2,1)}, f32[1344,512]{1,0:T(8,128)}) custom-call(bf16[256,1024]{1,0:T(8,128)(2,1)} %get-tuple-element.260.refs_0_, bf16[256,1024]{1,0:T(8,128)(2,1)} %collective-permute-done.43.refs_1_, bf16[256,1024]{1,0:T(8,128)(2,1)} %copy-done.38, bf16[256,1024]{1,0:T(8,128)(2,1)} %copy-done.39, ...), custom_call_target="tpu_custom_call" | custom-call | flops 1 | bytes 1 | tf_op jit(solution)/shard_map/products/pallas_call | solution.py:113
  295.6 25.1 %collective-permute-done.50.refs_1_ = bf16[1536,128]{1,0:T(8,128)(2,1)S(1)} collective-permute-done((bf16[1536,128]{1,0:T(8,128)(2,1)}, bf16[1536,128]{1,0:T(8,128)(2,1)S(1)}, u32[]{:S(2)}, u32[]{:S(2)}) %collective-permute-start.50) | collective-permute-done | bytes 393248 | tf_op jit(solution)/shard_map/ppermute | solution.py:37
  320.7 10.1 %collective-permute-done.52.refs_3_ = bf16[1536,128]{1,0:T(8,128)(2,1)S(1)} collective-permute-done((bf16[1536,128]{1,0:T(8,128)(2,1)S(1)}, bf16[1536,128]{1,0:T(8,128)(2,1)S(1)}, u32[]{:S(2)}, u32[]{:S(2)}) %collective-permute-start.52) | collective-permute-done | bytes 393248 | tf_op jit(solution)/shard_map/ppermute | solution.py:37
  334.0 6.0 %input_grad.1 = (bf16[1024,768]{1,0:T(8,128)(2,1)}, bf16[512,1024]{1,0:T(8,128)(2,1)}, f32[512,1024]{1,0:T(8,128)}) custom-call(s32[3]{0:T(128)} %pad_add_fusion.ids, bf16[1536,128]{1,0:T(8,128)(2,1)} %get-tuple-element.273.refs_0_, bf16[1536,128]{1,0:T(8,128)(2,1)} %copy-done.43, bf16[1536,128]{1,0:T(8,128)(2,1)} %copy-done.44, ...), custom_call_target="tpu_custom_call" | custom-call | flops 1 | bytes 1 | tf_op jit(solution)/shard_map/input_grad/pallas_call | solution.py:113
  340.0 3.4 convolution_convert_fusion
  343.9 3.7 halve.8
  349.7 3.6 fusion.keep
  357.0 2.6 add_convert_fusion.1
  361.6 10.5 %collective-permute-done.56.got = bf16[672,512]{1,0:T(8,128)(2,1)S(1)} collective-permute-done((bf16[672,512]{1,0:T(8,128)(2,1)}, bf16[672,512]{1,0:T(8,128)(2,1)S(1)}, u32[]{:S(2)}, u32[]{:S(2)}) %collective-permute-start.56) | collective-permute-done | bytes 688160 | tf_op jit(solution)/shard_map/ppermute | solution.py:37
  372.9 2.8 halve.9
  375.7 2.8 halve.10
  383.3 14.0 %collective-permute-done.59.got = bf16[256,768]{1,0:T(8,128)(2,1)S(1)} collective-permute-done((bf16[256,768]{1,0:T(8,128)(2,1)}, bf16[256,768]{1,0:T(8,128)(2,1)S(1)}, u32[]{:S(2)}, u32[]{:S(2)}) %collective-permute-start.59) | collective-permute-done | bytes 393248 | tf_op jit(solution)/shard_map/ppermute | solution.py:37
  403.5 4.2 collective-permute-start.70
  412.7 3.8 place.2
  416.5 10.3 %collective-permute-done.65.got = bf16[128,768]{1,0:T(8,128)(2,1)S(1)} collective-permute-done((bf16[128,768]{1,0:T(8,128)(2,1)}, bf16[128,768]{1,0:T(8,128)(2,1)S(1)}, u32[]{:S(2)}, u32[]{:S(2)}) %collective-permute-start.65) | collective-permute-done | bytes 196640 | tf_op jit(solution)/shard_map/ppermute | solution.py:37
  429.3 9.0 %collective-permute-done.66.refs_1_ = bf16[336,512]{1,0:T(8,128)(2,1)S(1)} collective-permute-done((bf16[336,512]{1,0:T(8,128)(2,1)}, bf16[336,512]{1,0:T(8,128)(2,1)S(1)}, u32[]{:S(2)}, u32[]{:S(2)}) %collective-permute-start.66) | collective-permute-done | bytes 344096 | tf_op jit(solution)/shard_map/ppermute | solution.py:37
  439.8 2.7 place_columns.2
  447.9 3.8 place.3
  454.0 7.4 %collective-permute-done.74.refs_3_ = bf16[336,512]{1,0:T(8,128)(2,1)S(1)} collective-permute-done((bf16[336,512]{1,0:T(8,128)(2,1)S(1)}, bf16[336,512]{1,0:T(8,128)(2,1)S(1)}, u32[]{:S(2)}, u32[]{:S(2)}) %collective-permute-start.74) | collective-permute-done | bytes 344096 | tf_op jit(solution)/shard_map/ppermute | solution.py:37
  462.1 3.5 place_rows.1
  (319 shorter events, 115.6 us)
Async XLA Ops:
  3.7 24.1 %collective-permute-start = (bf16[512,768]{1,0:T(8,128)(2,1)S(1)}, bf16[512,768]{1,0:T(8,128)(2,1)}, u32[]{:S(2)}, u32[]{:S(2)}) collective-permute-start(bf16[512,768]{1,0:T(8,128)(2,1)S(1)} %constant_dynamic-update-slice_fusion.refs_0_.refs_4_), channel_id=1, source_target_pairs={{0,16},{16,0},{1,17},{17,1},{2,18},{18,2},{3,19},{19,3},{4,20},{20... | collective-permute-start | bytes 2359304 | tf_op jit(solution)/shard_map/ppermute | solution.py:37
  10.5 55.4 %collective-permute-start.4 = (bf16[1296,512]{1,0:T(8,128)(2,1)S(1)}, bf16[1296,512]{1,0:T(8,128)(2,1)S(1)}, u32[]{:S(2)}, u32[]{:S(2)}) collective-permute-start(bf16[1296,512]{1,0:T(8,128)(2,1)S(1)} %pad_maximum_fusion.refs_6_), channel_id=1, source_target_pairs={{0,2},{1,3},{2,0},{3,1},{4,6},{5,7},{6,4},{7,5},{8,10},{9,11},{10,... | collective-permute-start | bytes 3981320 | tf_op jit(solution)/shard_map/ppermute | solution.py:37
  36.3 29.7 %collective-permute-start.8 = (bf16[512,1024]{1,0:T(8,128)(2,1)}, bf16[512,1024]{1,0:T(8,128)(2,1)S(1)}, u32[]{:S(2)}, u32[]{:S(2)}) collective-permute-start(bf16[512,1024]{1,0:T(8,128)(2,1)} %refs_14_.1), channel_id=1, source_target_pairs={{0,2},{1,3},{2,0},{3,1},{4,6},{5,7},{6,4},{7,5},{8,10},{9,11},{10,... | collective-permute-start | bytes 3145736 | tf_op jit(solution)/shard_map/ppermute | solution.py:37
  36.8 17.5 %collective-permute-start.5 = (bf16[1536,128]{1,0:T(8,128)(2,1)}, bf16[1536,128]{1,0:T(8,128)(2,1)S(1)}, u32[]{:S(2)}, u32[]{:S(2)}) collective-permute-start(bf16[1536,128]{1,0:T(8,128)(2,1)} %get-tuple-element.175), channel_id=1, source_target_pairs={{0,4},{4,0},{8,12},{12,8},{1,5},{5,1},{9,13},{13,9},{2,6},{6,2},{1... | collective-permute-start | bytes 1179656 | tf_op jit(solution)/shard_map/ppermute | solution.py:37
  38.1 28.5 %collective-permute-start.9 = (bf16[512,1024]{1,0:T(8,128)(2,1)}, bf16[512,1024]{1,0:T(8,128)(2,1)}, u32[]{:S(2)}, u32[]{:S(2)}) collective-permute-start(bf16[512,1024]{1,0:T(8,128)(2,1)} %refs_14_.1), channel_id=1, source_target_pairs={{0,16},{16,0},{1,17},{17,1},{2,18},{18,2},{3,19},{19,3},{4,20},{20... | collective-permute-start | bytes 3145736 | tf_op jit(solution)/shard_map/ppermute | solution.py:37
  38.6 27.4 %collective-permute-start.6 = (bf16[1536,128]{1,0:T(8,128)(2,1)}, bf16[1536,128]{1,0:T(8,128)(2,1)S(1)}, u32[]{:S(2)}, u32[]{:S(2)}) collective-permute-start(bf16[1536,128]{1,0:T(8,128)(2,1)} %get-tuple-element.176), channel_id=1, source_target_pairs={{0,8},{4,12},{8,0},{12,4},{1,9},{5,13},{9,1},{13,5},{2,10},{6,14},... | collective-permute-start | bytes 1179656 | tf_op jit(solution)/shard_map/ppermute | solution.py:37
  66.0 26.0 %collective-permute-start.11 = (bf16[1296,512]{1,0:T(8,128)(2,1)S(1)}, bf16[1296,512]{1,0:T(8,128)(2,1)}, u32[]{:S(2)}, u32[]{:S(2)}) collective-permute-start(bf16[1296,512]{1,0:T(8,128)(2,1)S(1)} %pad_maximum_fusion.refs_6_), channel_id=1, source_target_pairs={{0,1},{1,0},{2,3},{3,2},{4,5},{5,4},{6,7},{7,6},{8,9},{9,8},{10,11... | collective-permute-start | bytes 3981320 | tf_op jit(solution)/shard_map/ppermute | solution.py:37
  66.1 26.0 %collective-permute-start.12 = (bf16[1296,512]{1,0:T(8,128)(2,1)S(1)}, bf16[1296,512]{1,0:T(8,128)(2,1)}, u32[]{:S(2)}, u32[]{:S(2)}) collective-permute-start(bf16[1296,512]{1,0:T(8,128)(2,1)S(1)} %collective-permute-done.4.refs_8_), channel_id=1, source_target_pairs={{0,1},{1,0},{2,3},{3,2},{4,5},{5,4},{6,7},{7,6},{8,9},{9,8},{10,11... | collective-permute-start | bytes 3981320 | tf_op jit(solution)/shard_map/ppermute | solution.py:37
  67.1 25.0 %collective-permute-start.10 = (bf16[512,1024]{1,0:T(8,128)(2,1)}, bf16[512,1024]{1,0:T(8,128)(2,1)}, u32[]{:S(2)}, u32[]{:S(2)}) collective-permute-start(bf16[512,1024]{1,0:T(8,128)(2,1)} %collective-permute-done.9.refs_15_), channel_id=1, source_target_pairs={{0,2},{1,3},{2,0},{3,1},{4,6},{5,7},{6,4},{7,5},{8,10},{9,11},{10,... | collective-permute-start | bytes 3145736 | tf_op jit(solution)/shard_map/ppermute | solution.py:37
  68.5 43.0 %collective-permute-start.15 = (bf16[1296,512]{1,0:T(8,128)(2,1)S(1)}, bf16[1296,512]{1,0:T(8,128)(2,1)}, u32[]{:S(2)}, u32[]{:S(2)}) collective-permute-start(bf16[1296,512]{1,0:T(8,128)(2,1)S(1)} %pad_maximum_fusion.refs_6_), channel_id=1, source_target_pairs={{0,16},{16,0},{1,17},{17,1},{2,18},{18,2},{3,19},{19,3},{4,20},{20... | collective-permute-start | bytes 3981320 | tf_op jit(solution)/shard_map/ppermute | solution.py:37
  92.1 19.4 %collective-permute-start.13 = (bf16[512,1024]{1,0:T(8,128)(2,1)}, bf16[512,1024]{1,0:T(8,128)(2,1)}, u32[]{:S(2)}, u32[]{:S(2)}) collective-permute-start(bf16[512,1024]{1,0:T(8,128)(2,1)} %refs_14_.1), channel_id=1, source_target_pairs={{0,1},{1,0},{2,3},{3,2},{4,5},{5,4},{6,7},{7,6},{8,9},{9,8},{10,11... | collective-permute-start | bytes 3145736 | tf_op jit(solution)/shard_map/ppermute | solution.py:37
  92.1 19.4 %collective-permute-start.14 = (bf16[512,1024]{1,0:T(8,128)(2,1)}, bf16[512,1024]{1,0:T(8,128)(2,1)}, u32[]{:S(2)}, u32[]{:S(2)}) collective-permute-start(bf16[512,1024]{1,0:T(8,128)(2,1)} %collective-permute-done.9.refs_15_), channel_id=1, source_target_pairs={{0,1},{1,0},{2,3},{3,2},{4,5},{5,4},{6,7},{7,6},{8,9},{9,8},{10,11... | collective-permute-start | bytes 3145736 | tf_op jit(solution)/shard_map/ppermute | solution.py:37
  92.6 42.7 %collective-permute-start.21 = (bf16[1296,512]{1,0:T(8,128)(2,1)S(1)}, bf16[1296,512]{1,0:T(8,128)(2,1)}, u32[]{:S(2)}, u32[]{:S(2)}) collective-permute-start(bf16[1296,512]{1,0:T(8,128)(2,1)S(1)} %collective-permute-done.4.refs_8_), channel_id=1, source_target_pairs={{0,16},{16,0},{1,17},{17,1},{2,18},{18,2},{3,19},{19,3},{4,20},{20... | collective-permute-start | bytes 3981320 | tf_op jit(solution)/shard_map/ppermute | solution.py:37
  111.5 20.5 %collective-permute-start.19 = (bf16[512,1024]{1,0:T(8,128)(2,1)}, bf16[512,1024]{1,0:T(8,128)(2,1)S(1)}, u32[]{:S(2)}, u32[]{:S(2)}) collective-permute-start(bf16[512,1024]{1,0:T(8,128)(2,1)} %copy-done.9), channel_id=1, source_target_pairs={{0,1},{1,0},{2,3},{3,2},{4,5},{5,4},{6,7},{7,6},{8,9},{9,8},{10,11... | collective-permute-start | bytes 3145736 | tf_op jit(solution)/shard_map/ppermute | solution.py:37
  111.6 20.4 %collective-permute-start.20 = (bf16[512,1024]{1,0:T(8,128)(2,1)}, bf16[512,1024]{1,0:T(8,128)(2,1)S(1)}, u32[]{:S(2)}, u32[]{:S(2)}) collective-permute-start(bf16[512,1024]{1,0:T(8,128)(2,1)} %collective-permute-done.10.refs_17_), channel_id=1, source_target_pairs={{0,1},{1,0},{2,3},{3,2},{4,5},{5,4},{6,7},{7,6},{8,9},{9,8},{10,11... | collective-permute-start | bytes 3145736 | tf_op jit(solution)/shard_map/ppermute | solution.py:37
  159.4 14.8 %collective-permute-start.27 = (bf16[256,1024]{1,0:T(8,128)(2,1)}, bf16[256,1024]{1,0:T(8,128)(2,1)S(1)}, u32[]{:S(2)}, u32[]{:S(2)}) collective-permute-start(bf16[256,1024]{1,0:T(8,128)(2,1)} %get-tuple-element.214), channel_id=1, source_target_pairs={{0,2},{1,3},{2,0},{3,1},{4,6},{5,7},{6,4},{7,5},{8,10},{9,11},{10,... | collective-permute-start | bytes 1572872 | tf_op jit(solution)/shard_map/ppermute | solution.py:37
  192.0 35.4 %collective-permute-start.35 = (bf16[256,1024]{1,0:T(8,128)(2,1)S(1)}, bf16[256,1024]{1,0:T(8,128)(2,1)}, u32[]{:S(2)}, u32[]{:S(2)}) collective-permute-start(bf16[256,1024]{1,0:T(8,128)(2,1)S(1)} %copy-done.14), channel_id=1, source_target_pairs={{0,2},{1,3},{2,0},{3,1},{4,6},{5,7},{6,4},{7,5},{8,10},{9,11},{10,... | collective-permute-start | bytes 1572872 | tf_op jit(solution)/shard_map/ppermute | solution.py:37
  193.2 34.3 %collective-permute-start.36 = (bf16[256,1024]{1,0:T(8,128)(2,1)}, bf16[256,1024]{1,0:T(8,128)(2,1)S(1)}, u32[]{:S(2)}, u32[]{:S(2)}) collective-permute-start(bf16[256,1024]{1,0:T(8,128)(2,1)} %get-tuple-element.234), channel_id=1, source_target_pairs={{0,3},{1,2},{2,1},{3,0},{4,7},{5,6},{6,5},{7,4},{8,11},{9,10},{10,... | collective-permute-start | bytes 1572872 | tf_op jit(solution)/shard_map/ppermute | solution.py:37
  193.4 34.9 %collective-permute-start.37 = (bf16[256,1024]{1,0:T(8,128)(2,1)S(1)}, bf16[256,1024]{1,0:T(8,128)(2,1)S(1)}, u32[]{:S(2)}, u32[]{:S(2)}) collective-permute-start(bf16[256,1024]{1,0:T(8,128)(2,1)S(1)} %copy-done.33), channel_id=1, source_target_pairs={{0,2},{1,3},{2,0},{3,1},{4,6},{5,7},{6,4},{7,5},{8,10},{9,11},{10,... | collective-permute-start | bytes 1572872 | tf_op jit(solution)/shard_map/ppermute | solution.py:37
  194.7 32.7 %collective-permute-start.32 = (bf16[512,128]{1,0:T(8,128)(2,1)}, bf16[512,128]{1,0:T(8,128)(2,1)S(1)}, u32[]{:S(2)}, u32[]{:S(2)}) collective-permute-start(bf16[512,128]{1,0:T(8,128)(2,1)} %get-tuple-element.224), channel_id=1, source_target_pairs={{0,8},{4,12},{8,0},{12,4},{1,9},{5,13},{9,1},{13,5},{2,10},{6,14},... | collective-permute-start | bytes 393224 | tf_op jit(solution)/shard_map/ppermute | solution.py:37
  197.4 30.0 %collective-permute-start.34 = (bf16[512,128]{1,0:T(8,128)(2,1)}, bf16[512,128]{1,0:T(8,128)(2,1)S(1)}, u32[]{:S(2)}, u32[]{:S(2)}) collective-permute-start(bf16[512,128]{1,0:T(8,128)(2,1)} %get-tuple-element.231), channel_id=1, source_target_pairs={{0,12},{4,8},{8,4},{12,0},{1,13},{5,9},{9,5},{13,1},{2,14},{6,10},... | collective-permute-start | bytes 393224 | tf_op jit(solution)/shard_map/ppermute | solution.py:37
  237.5 36.2 %collective-permute-start.46 = (bf16[1024,512]{1,0:T(8,128)(2,1)}, bf16[1024,512]{1,0:T(8,128)(2,1)S(1)}, u32[]{:S(2)}, u32[]{:S(2)}) collective-permute-start(bf16[1024,512]{1,0:T(8,128)(2,1)} %get-tuple-element.240), channel_id=1, source_target_pairs={{0,16},{16,0},{1,17},{17,1},{2,18},{18,2},{3,19},{19,3},{4,20},{20... | collective-permute-start | bytes 3145736 | tf_op jit(solution)/shard_map/ppermute | solution.py:37
  238.1 33.1 %collective-permute-start.42 = (bf16[272,1024]{1,0:T(8,128)(2,1)S(1)}, bf16[272,1024]{1,0:T(8,128)(2,1)S(1)}, u32[]{:S(2)}, u32[]{:S(2)}) collective-permute-start(bf16[272,1024]{1,0:T(8,128)(2,1)S(1)} %copy-done.22), channel_id=1, source_target_pairs={{0,2},{1,3},{2,0},{3,1},{4,6},{5,7},{6,4},{7,5},{8,10},{9,11},{10,... | collective-permute-start | bytes 1671176 | tf_op jit(solution)/shard_map/ppermute | solution.py:37
  239.3 31.9 %collective-permute-start.43 = (bf16[256,1024]{1,0:T(8,128)(2,1)}, bf16[256,1024]{1,0:T(8,128)(2,1)}, u32[]{:S(2)}, u32[]{:S(2)}) collective-permute-start(bf16[256,1024]{1,0:T(8,128)(2,1)} %get-tuple-element.251), channel_id=1, source_target_pairs={{0,2},{1,3},{2,0},{3,1},{4,6},{5,7},{6,4},{7,5},{8,10},{9,11},{10,... | collective-permute-start | bytes 1572872 | tf_op jit(solution)/shard_map/ppermute | solution.py:37
  240.1 31.1 %collective-permute-start.44 = (bf16[256,1024]{1,0:T(8,128)(2,1)}, bf16[256,1024]{1,0:T(8,128)(2,1)S(1)}, u32[]{:S(2)}, u32[]{:S(2)}) collective-permute-start(bf16[256,1024]{1,0:T(8,128)(2,1)} %get-tuple-element.253), channel_id=1, source_target_pairs={{0,1},{1,0},{2,3},{3,2},{4,5},{5,4},{6,7},{7,6},{8,9},{9,8},{10,11... | collective-permute-start | bytes 1572872 | tf_op jit(solution)/shard_map/ppermute | solution.py:37
  240.1 33.7 %collective-permute-start.45 = (bf16[256,1024]{1,0:T(8,128)(2,1)}, bf16[256,1024]{1,0:T(8,128)(2,1)S(1)}, u32[]{:S(2)}, u32[]{:S(2)}) collective-permute-start(bf16[256,1024]{1,0:T(8,128)(2,1)} %get-tuple-element.255), channel_id=1, source_target_pairs={{0,3},{1,2},{2,1},{3,0},{4,7},{5,6},{6,5},{7,4},{8,11},{9,10},{10,... | collective-permute-start | bytes 1572872 | tf_op jit(solution)/shard_map/ppermute | solution.py:37
  288.2 55.7 %collective-permute-start.55 = (bf16[1344,512]{1,0:T(8,128)(2,1)}, bf16[1344,512]{1,0:T(8,128)(2,1)}, u32[]{:S(2)}, u32[]{:S(2)}) collective-permute-start(bf16[1344,512]{1,0:T(8,128)(2,1)} %get-tuple-element.263), channel_id=1, source_target_pairs={{0,16},{16,0},{1,17},{17,1},{2,18},{18,2},{3,19},{19,3},{4,20},{20... | collective-permute-start | bytes 4128776 | tf_op jit(solution)/shard_map/ppermute | solution.py:37
  289.7 41.1 %collective-permute-start.47 = (bf16[512,512]{1,0:T(8,128)(2,1)S(1)}, bf16[512,512]{1,0:T(8,128)(2,1)S(1)}, u32[]{:S(2)}, u32[]{:S(2)}) collective-permute-start(bf16[512,512]{1,0:T(8,128)(2,1)S(1)} %copy-done.72), channel_id=1, source_target_pairs={{0,4},{4,0},{8,12},{12,8},{1,5},{5,1},{9,13},{13,9},{2,6},{6,2},{1... | collective-permute-start | bytes 1572872 | tf_op jit(solution)/shard_map/ppermute | solution.py:37
  291.2 29.4 %collective-permute-start.50 = (bf16[1536,128]{1,0:T(8,128)(2,1)}, bf16[1536,128]{1,0:T(8,128)(2,1)S(1)}, u32[]{:S(2)}, u32[]{:S(2)}) collective-permute-start(bf16[1536,128]{1,0:T(8,128)(2,1)} %get-tuple-element.265), channel_id=1, source_target_pairs={{0,4},{4,0},{8,12},{12,8},{1,5},{5,1},{9,13},{13,9},{2,6},{6,2},{1... | collective-permute-start | bytes 1179656 | tf_op jit(solution)/shard_map/ppermute | solution.py:37
  291.8 28.9 %collective-permute-start.51 = (bf16[1536,128]{1,0:T(8,128)(2,1)}, bf16[1536,128]{1,0:T(8,128)(2,1)S(1)}, u32[]{:S(2)}, u32[]{:S(2)}) collective-permute-start(bf16[1536,128]{1,0:T(8,128)(2,1)} %get-tuple-element.267), channel_id=1, source_target_pairs={{0,8},{4,12},{8,0},{12,4},{1,9},{5,13},{9,1},{13,5},{2,10},{6,14},... | collective-permute-start | bytes 1179656 | tf_op jit(solution)/shard_map/ppermute | solution.py:37
  294.1 36.7 %collective-permute-start.52 = (bf16[1536,128]{1,0:T(8,128)(2,1)S(1)}, bf16[1536,128]{1,0:T(8,128)(2,1)S(1)}, u32[]{:S(2)}, u32[]{:S(2)}) collective-permute-start(bf16[1536,128]{1,0:T(8,128)(2,1)S(1)} %copy-done.73), channel_id=1, source_target_pairs={{0,12},{4,8},{8,4},{12,0},{1,13},{5,9},{9,5},{13,1},{2,14},{6,10},... | collective-permute-start | bytes 1179656 | tf_op jit(solution)/shard_map/ppermute | solution.py:37
  340.0 17.0 %collective-permute-start.53 = (bf16[512,1024]{1,0:T(8,128)(2,1)}, bf16[512,1024]{1,0:T(8,128)(2,1)S(1)}, u32[]{:S(2)}, u32[]{:S(2)}) collective-permute-start(bf16[512,1024]{1,0:T(8,128)(2,1)} %get-tuple-element.275), channel_id=1, source_target_pairs={{0,1},{1,0},{2,3},{3,2},{4,5},{5,4},{6,7},{7,6},{8,9},{9,8},{10,11... | collective-permute-start | bytes 3145736 | tf_op jit(solution)/shard_map/ppermute | solution.py:37
  340.0 14.4 %collective-permute-start.54 = (bf16[256,512]{1,0:T(8,128)(2,1)}, bf16[256,512]{1,0:T(8,128)(2,1)S(1)}, u32[]{:S(2)}, u32[]{:S(2)}) collective-permute-start(bf16[256,512]{1,0:T(8,128)(2,1)} %get-tuple-element.272), channel_id=1, source_target_pairs={{0,8},{4,12},{8,0},{12,4},{1,9},{5,13},{9,1},{13,5},{2,10},{6,14},... | collective-permute-start | bytes 786440 | tf_op jit(solution)/shard_map/ppermute | solution.py:37
  343.4 32.4 %collective-permute-start.58 = (bf16[512,768]{1,0:T(8,128)(2,1)}, bf16[512,768]{1,0:T(8,128)(2,1)}, u32[]{:S(2)}, u32[]{:S(2)}) collective-permute-start(bf16[512,768]{1,0:T(8,128)(2,1)} %convolution_convert_fusion), channel_id=1, source_target_pairs={{0,16},{16,0},{1,17},{17,1},{2,18},{18,2},{3,19},{19,3},{4,20},{20... | collective-permute-start | bytes 2359304 | tf_op jit(solution)/shard_map/ppermute | solution.py:37
  347.6 24.5 %collective-permute-start.56 = (bf16[672,512]{1,0:T(8,128)(2,1)}, bf16[672,512]{1,0:T(8,128)(2,1)S(1)}, u32[]{:S(2)}, u32[]{:S(2)}) collective-permute-start(bf16[672,512]{1,0:T(8,128)(2,1)} %get-tuple-element.280), channel_id=1, source_target_pairs={{0,4},{4,0},{8,12},{12,8},{1,5},{5,1},{9,13},{13,9},{2,6},{6,2},{1... | collective-permute-start | bytes 2064392 | tf_op jit(solution)/shard_map/ppermute | solution.py:37
  359.6 21.0 %collective-permute-start.60 = (bf16[256,1024]{1,0:T(8,128)(2,1)}, bf16[256,1024]{1,0:T(8,128)(2,1)S(1)}, u32[]{:S(2)}, u32[]{:S(2)}) collective-permute-start(bf16[256,1024]{1,0:T(8,128)(2,1)} %add_convert_fusion.1), channel_id=1, source_target_pairs={{0,2},{1,3},{2,0},{3,1},{4,6},{5,7},{6,4},{7,5},{8,10},{9,11},{10,... | collective-permute-start | bytes 1572872 | tf_op jit(solution)/shard_map/ppermute | solution.py:37
  361.2 19.4 %collective-permute-start.61 = (bf16[256,512]{1,0:T(8,128)(2,1)S(1)}, bf16[256,512]{1,0:T(8,128)(2,1)}, u32[]{:S(2)}, u32[]{:S(2)}) collective-permute-start(bf16[256,512]{1,0:T(8,128)(2,1)S(1)} %copy-done.19), channel_id=1, source_target_pairs={{0,8},{4,12},{8,0},{12,4},{1,9},{5,13},{9,1},{13,5},{2,10},{6,14},... | collective-permute-start | bytes 786440 | tf_op jit(solution)/shard_map/ppermute | solution.py:37
  361.2 41.7 %collective-permute-start.62 = (bf16[256,1024]{1,0:T(8,128)(2,1)}, bf16[256,1024]{1,0:T(8,128)(2,1)}, u32[]{:S(2)}, u32[]{:S(2)}) collective-permute-start(bf16[256,1024]{1,0:T(8,128)(2,1)} %get-tuple-element.299.refs_0_), channel_id=1, source_target_pairs={{0,2},{1,3},{2,0},{3,1},{4,6},{5,7},{6,4},{7,5},{8,10},{9,11},{10,... | collective-permute-start | bytes 1572872 | tf_op jit(solution)/shard_map/ppermute | solution.py:37
  378.6 18.8 %collective-permute-start.59 = (bf16[256,768]{1,0:T(8,128)(2,1)}, bf16[256,768]{1,0:T(8,128)(2,1)S(1)}, u32[]{:S(2)}, u32[]{:S(2)}) collective-permute-start(bf16[256,768]{1,0:T(8,128)(2,1)} %get-tuple-element.291), channel_id=1, source_target_pairs={{0,4},{4,0},{8,12},{12,8},{1,5},{5,1},{9,13},{13,9},{2,6},{6,2},{1... | collective-permute-start | bytes 1179656 | tf_op jit(solution)/shard_map/ppermute | solution.py:37
  378.6 21.6 %collective-permute-start.57 = (bf16[336,512]{1,0:T(8,128)(2,1)S(1)}, bf16[336,512]{1,0:T(8,128)(2,1)S(1)}, u32[]{:S(2)}, u32[]{:S(2)}) collective-permute-start(bf16[336,512]{1,0:T(8,128)(2,1)S(1)} %copy-done.74), channel_id=1, source_target_pairs={{0,8},{4,12},{8,0},{12,4},{1,9},{5,13},{9,1},{13,5},{2,10},{6,14},... | collective-permute-start | bytes 1032200 | tf_op jit(solution)/shard_map/ppermute | solution.py:37
  403.5 39.0 %collective-permute-start.70 = (bf16[256,1024]{1,0:T(8,128)(2,1)S(1)}, bf16[256,1024]{1,0:T(8,128)(2,1)S(1)}, u32[]{:S(2)}, u32[]{:S(2)}) collective-permute-start(bf16[256,1024]{1,0:T(8,128)(2,1)S(1)} %add_convert_fusion.refs_0_), channel_id=1, source_target_pairs={{0,2},{1,3},{2,0},{3,1},{4,6},{5,7},{6,4},{7,5},{8,10},{9,11},{10,... | collective-permute-start | bytes 1572872 | tf_op jit(solution)/shard_map/ppermute | solution.py:37
  407.7 19.1 %collective-permute-start.65 = (bf16[128,768]{1,0:T(8,128)(2,1)}, bf16[128,768]{1,0:T(8,128)(2,1)S(1)}, u32[]{:S(2)}, u32[]{:S(2)}) collective-permute-start(bf16[128,768]{1,0:T(8,128)(2,1)} %get-tuple-element.296), channel_id=1, source_target_pairs={{0,8},{4,12},{8,0},{12,4},{1,9},{5,13},{9,1},{13,5},{2,10},{6,14},... | collective-permute-start | bytes 589832 | tf_op jit(solution)/shard_map/ppermute | solution.py:37
  408.2 30.1 %collective-permute-start.66 = (bf16[336,512]{1,0:T(8,128)(2,1)}, bf16[336,512]{1,0:T(8,128)(2,1)S(1)}, u32[]{:S(2)}, u32[]{:S(2)}) collective-permute-start(bf16[336,512]{1,0:T(8,128)(2,1)} %merge.4.refs_0_), channel_id=1, source_target_pairs={{0,8},{4,12},{8,0},{12,4},{1,9},{5,13},{9,1},{13,5},{2,10},{6,14},... | collective-permute-start | bytes 1032200 | tf_op jit(solution)/shard_map/ppermute | solution.py:37
  410.6 27.7 %collective-permute-start.67 = (bf16[256,512]{1,0:T(8,128)(2,1)S(1)}, bf16[256,512]{1,0:T(8,128)(2,1)S(1)}, u32[]{:S(2)}, u32[]{:S(2)}) collective-permute-start(bf16[256,512]{1,0:T(8,128)(2,1)S(1)} %copy-done.19), channel_id=1, source_target_pairs={{0,4},{4,0},{8,12},{12,8},{1,5},{5,1},{9,13},{13,9},{2,6},{6,2},{1... | collective-permute-start | bytes 786440 | tf_op jit(solution)/shard_map/ppermute | solution.py:37
  410.7 27.7 %collective-permute-start.68 = (bf16[256,512]{1,0:T(8,128)(2,1)}, bf16[256,512]{1,0:T(8,128)(2,1)S(1)}, u32[]{:S(2)}, u32[]{:S(2)}) collective-permute-start(bf16[256,512]{1,0:T(8,128)(2,1)} %collective-permute-done.61.refs_1_), channel_id=1, source_target_pairs={{0,4},{4,0},{8,12},{12,8},{1,5},{5,1},{9,13},{13,9},{2,6},{6,2},{1... | collective-permute-start | bytes 786440 | tf_op jit(solution)/shard_map/ppermute | solution.py:37
  443.1 18.3 %collective-permute-start.74 = (bf16[336,512]{1,0:T(8,128)(2,1)S(1)}, bf16[336,512]{1,0:T(8,128)(2,1)S(1)}, u32[]{:S(2)}, u32[]{:S(2)}) collective-permute-start(bf16[336,512]{1,0:T(8,128)(2,1)S(1)} %collective-permute-done.66.refs_1_), channel_id=1, source_target_pairs={{0,4},{4,0},{8,12},{12,8},{1,5},{5,1},{9,13},{13,9},{2,6},{6,2},{1... | collective-permute-start | bytes 1032200 | tf_op jit(solution)/shard_map/ppermute | solution.py:37
  445.1 22.0 %collective-permute-start.75 = (bf16[128,768]{1,0:T(8,128)(2,1)S(1)}, bf16[128,768]{1,0:T(8,128)(2,1)}, u32[]{:S(2)}, u32[]{:S(2)}) collective-permute-start(bf16[128,768]{1,0:T(8,128)(2,1)S(1)} %copy-done.20), channel_id=1, source_target_pairs={{0,4},{4,0},{8,12},{12,8},{1,5},{5,1},{9,13},{13,9},{2,6},{6,2},{1... | collective-permute-start | bytes 589832 | tf_op jit(solution)/shard_map/ppermute | solution.py:37
  445.1 23.8 %collective-permute-start.76 = (bf16[128,768]{1,0:T(8,128)(2,1)S(1)}, bf16[128,768]{1,0:T(8,128)(2,1)S(1)}, u32[]{:S(2)}, u32[]{:S(2)}) collective-permute-start(bf16[128,768]{1,0:T(8,128)(2,1)S(1)} %collective-permute-done.69.refs_1_), channel_id=1, source_target_pairs={{0,4},{4,0},{8,12},{12,8},{1,5},{5,1},{9,13},{13,9},{2,6},{6,2},{1... | collective-permute-start | bytes 589832 | tf_op jit(solution)/shard_map/ppermute | solution.py:37
  (104 other events, 964.0 us)

commit v6 on v5

--- a/solution.py
+++ b/solution.py
@@ -465,7 +465,7 @@
 
 
 BQ = 256
-KC = 1024
+KC = 2048
 
 
 def fill_keys(kv, marks, ka, va):

time: 481 us -> 481 us (level)
  no operation moved by 1% of the time
where the time goes in v6:
time: 481 us; the launch traced here: 472 us
  Pallas kernels  190 us (40%)
  waiting for transfers between devices  150 us (31%)
  starting transfers between devices  85.8 us (18%)
  local copies, waits for them, and re-layouts  24.1 us (5%)
  other arithmetic  13.1 us (3%)
  matrix products  6.95 us (1%)
    pallas_call x28, Pallas kernels, call(): pl.pallas_call(body, out_shape=out_shape, scratch_shapes=list(scratch), c...  190 us
    ppermute x77, waiting for transfers between devices, swap(): return lax.ppermute(value, axis, [(i, i ^ bit) for i in range(n)])  150 us
    ppermute x77, starting transfers between devices, swap(): return lax.ppermute(value, axis, [(i, i ^ bit) for i in range(n)])  85.8 us
    unnamed x157, local copies, waits for them, and re-layouts  18.4 us
  transfers between devices with their start and end apart: 77, of which 25 were waited for; matrix products, arithmetic and copies ran while one was open for 5% of the time, Pallas kernels for 35%

profile of v6, /device:TPU:0, one launch (start us, length us, event | category | flops | bytes accessed | tf_op | source)
XLA Modules:
  0.0 472.3 jit_solution(7314067830776407134)
XLA Ops:
  3.7 3.1 collective-permute-start
  12.8 3.1 arrange.2.x.refs_5_
  17.8 3.7 collective-permute-start.3
  22.5 2.7 sine_multiply_fusion
  27.7 5.9 %project.1 = (bf16[1536,128]{1,0:T(8,128)(2,1)}, bf16[1536,128]{1,0:T(8,128)(2,1)}, bf16[1536,128]{1,0:T(8,128)(2,1)}, bf16[1536,128]{1,0:T(8,128)(2,1)}) custom-call(s32[3]{0:T(128)} %pad_add_fusion.ids, bf16[1024,1024]{1,0:T(8,128)(2,1)} %arrange.2.x.refs_5_, bf16[512,768]{1,0:T(8,128)(2,1)} %copy-done.8, ...), custom_call_target="tpu_custom_call" | custom-call | flops 1 | bytes 1 | tf_op jit(solution)/shard_map/project/pallas_call | solution.py:113
  33.6 2.7 select_convert_fusion.refs_4_.refs_9_
  38.6 2.9 collective-permute-start.6
  41.5 12.9 %collective-permute-done.5.refs_1_.refs_5_ = bf16[1536,128]{1,0:T(8,128)(2,1)S(1)} collective-permute-done((bf16[1536,128]{1,0:T(8,128)(2,1)}, bf16[1536,128]{1,0:T(8,128)(2,1)S(1)}, u32[]{:S(2)}, u32[]{:S(2)}) %collective-permute-start.5) | collective-permute-done | bytes 393248 | tf_op jit(solution)/shard_map/ppermute | solution.py:37
  54.4 2.5 collective-permute-start.7
  56.9 9.1 %collective-permute-done.6.refs_2_.refs_6_ = bf16[1536,128]{1,0:T(8,128)(2,1)S(1)} collective-permute-done((bf16[1536,128]{1,0:T(8,128)(2,1)}, bf16[1536,128]{1,0:T(8,128)(2,1)S(1)}, u32[]{:S(2)}, u32[]{:S(2)}) %collective-permute-start.6) | collective-permute-done | bytes 393248 | tf_op jit(solution)/shard_map/ppermute | solution.py:37
  71.1 16.2 %attend.2 = (bf16[512,128]{1,0:T(8,128)(2,1)}, bf16[512,128]{1,0:T(8,128)(2,1)}, f32[1024,128]{1,0:T(8,128)}) custom-call(bf16[1536,128]{1,0:T(8,128)(2,1)} %get-tuple-element.185.refs_0_.refs_4_, bf16[1536,128]{1,0:T(8,128)(2,1)} %copy-done.2, bf16[1536,128]{1,0:T(8,128)(2,1)} %copy-done.3, bf16[1536,128]{1,0:T(8,128)(2,1)} %copy-done.4, ...), custom_call_target="tpu_custom_call" | custom-call | flops 1 | bytes 1 | tf_op jit(solution)/shard_map/attend/pallas_call | solution.py:113
  87.3 4.8 %collective-permute-done.10.refs_17_ = bf16[512,1024]{1,0:T(8,128)(2,1)} collective-permute-done((bf16[512,1024]{1,0:T(8,128)(2,1)}, bf16[512,1024]{1,0:T(8,128)(2,1)}, u32[]{:S(2)}, u32[]{:S(2)}) %collective-permute-start.10) | collective-permute-done | bytes 1048608 | tf_op jit(solution)/shard_map/ppermute | solution.py:37
  95.1 16.4 %attend.3 = (bf16[512,128]{1,0:T(8,128)(2,1)}, bf16[512,128]{1,0:T(8,128)(2,1)}, f32[1024,128]{1,0:T(8,128)}) custom-call(bf16[1536,128]{1,0:T(8,128)(2,1)} %get-tuple-element.185.refs_0_.refs_4_, bf16[1536,128]{1,0:T(8,128)(2,1)} %copy-done.2, bf16[1536,128]{1,0:T(8,128)(2,1)} %copy-done.3, bf16[1536,128]{1,0:T(8,128)(2,1)} %copy-done.4, ...), custom_call_target="tpu_custom_call" | custom-call | flops 1 | bytes 1 | tf_op jit(solution)/shard_map/attend/pallas_call | solution.py:113
  112.1 7.5 %collective-permute-start.16 = (bf16[512,128]{1,0:T(8,128)(2,1)S(1)}, bf16[512,128]{1,0:T(8,128)(2,1)S(1)}, u32[]{:S(2)}, u32[]{:S(2)}) collective-permute-start(bf16[512,128]{1,0:T(8,128)(2,1)S(1)} %copy-done.60), channel_id=1, source_target_pairs={{0,4},{4,0},{8,12},{12,8},{1,5},{5,1},{9,13},{13,9},{2,6},{6,2},{1... | collective-permute-start | bytes 393224 | tf_op jit(solution)/shard_map/ppermute | solution.py:37
  120.5 4.4 collective-permute-done.16.refs_1_
  126.5 5.5 %collective-permute-done.17.refs_2_ = bf16[512,128]{1,0:T(8,128)(2,1)S(1)} collective-permute-done((bf16[512,128]{1,0:T(8,128)(2,1)}, bf16[512,128]{1,0:T(8,128)(2,1)S(1)}, u32[]{:S(2)}, u32[]{:S(2)}) %collective-permute-start.17) | collective-permute-done | bytes 131104 | tf_op jit(solution)/shard_map/ppermute | solution.py:37
  138.0 4.4 collective-permute-done.22.refs_1_
  145.7 13.6 %forward.1 = (bf16[256,1024]{1,0:T(8,128)(2,1)}, bf16[256,1024]{1,0:T(8,128)(2,1)}, bf16[256,4096]{1,0:T(8,128)(2,1)}, f32[256,1024]{1,0:T(8,128)}, f32[256,128]...) custom-call(bf16[256,256]{1,0:T(8,128)(2,1)} %get-tuple-element.198., ...), custom_call_target="tpu_custom_call" | custom-call | flops 1 | bytes 1 | tf_op jit(solution)/shard_map/forward/pallas_call | solution.py:113
  161.3 12.5 %backward.1 = (bf16[272,1024]{1,0:T(8,128)(2,1)}, f32[256,1024]{1,0:T(8,128)}, bf16[256,1024]{1,0:T(8,128)(2,1)}, bf16[256,1024]{1,0:T(8,128)(2,1)}, bf16[256,10...) custom-call(bf16[256,1024]{1,0:T(8,128)(2,1)} %get-tuple-element.237, ...), custom_call_target="tpu_custom_call" | custom-call | flops 1 | bytes 1 | tf_op jit(solution)/shard_map/backward/pallas_call | solution.py:113
  176.4 4.2 collective-permute-done.29.refs_1_
  184.6 2.9 collective-permute-start.33
  187.5 4.5 collective-permute-done.33.refs_1_
  194.7 2.8 collective-permute-start.32
  198.9 27.8 %attend_back.2 = (bf16[512,128]{1,0:T(8,128)(2,1)}, bf16[512,128]{1,0:T(8,128)(2,1)}, f32[128,4096]{1,0:T(8,128)}) custom-call(bf16[512,128]{1,0:T(8,128)(2,1)} %get-tuple-element.228.refs_0_, bf16[512,128]{1,0:T(8,128)(2,1)} %copy-done.63, bf16[512,128]{1,0:T(8,128)(2,1)} %get-tuple-element.195.refs_0_.refs_2_, ...), custom_call_target="tpu_custom_call" | custom-call | flops 1 | bytes 1 | tf_op jit(solution)/shard_map/attend_back/pallas_call | solution.py:113
  231.9 5.6 %product.1 = (bf16[1024,512]{1,0:T(8,128)(2,1)}, f32[1024,512]{1,0:T(8,128)}) custom-call(bf16[256,1024]{1,0:T(8,128)(2,1)} %get-tuple-element.239.refs_0_, bf16[256,1024]{1,0:T(8,128)(2,1)} %copy-done.35, bf16[256,1024]{1,0:T(8,128)(2,1)} %copy-done.36, bf16[256,1024]{1,0:T(8,128)(2,1)} %copy-done.40, bf16[256,1024]{1,0:T(8,128)(2,1)} %get-tuple-element.237.refs_0_.refs_4_, ...), custom_call_target="tpu_custom_call" | custom-call | flops 1 | bytes 1 | tf_op jit(solution)/shard_map/product/pallas_call | solution.py:113
  241.4 29.1 %attend_back.3 = (bf16[1536,128]{1,0:T(8,128)(2,1)}, bf16[1536,128]{1,0:T(8,128)(2,1)}, bf16[1536,128]{1,0:T(8,128)(2,1)}, bf16[1536,128]{1,0:T(8,128)(2,1)}) custom-call(bf16[512,128]{1,0:T(8,128)(2,1)} %copy-done.61, bf16[512,128]{1,0:T(8,128)(2,1)} %copy-done.62, bf16[512,128]{1,0:T(8,128)(2,1)} %get-tuple-element.190.refs_2_, ...), custom_call_target="tpu_custom_call" | custom-call | flops 1 | bytes 1 | tf_op jit(solution)/shard_map/attend_back/pallas_call | solution.py:113
  270.6 3.3 collective-permute-done.45.refs_3_
  275.6 3.2 halve.6
  280.4 7.8 %products.1 = (bf16[1344,512]{1,0:T(8,128)(2,1)}, f32[1344,512]{1,0:T(8,128)}) custom-call(bf16[256,1024]{1,0:T(8,128)(2,1)} %get-tuple-element.260.refs_0_, bf16[256,1024]{1,0:T(8,128)(2,1)} %collective-permute-done.43.refs_1_, bf16[256,1024]{1,0:T(8,128)(2,1)} %copy-done.38, bf16[256,1024]{1,0:T(8,128)(2,1)} %copy-done.39, ...), custom_call_target="tpu_custom_call" | custom-call | flops 1 | bytes 1 | tf_op jit(solution)/shard_map/products/pallas_call | solution.py:113
  295.6 25.1 %collective-permute-done.50.refs_1_ = bf16[1536,128]{1,0:T(8,128)(2,1)S(1)} collective-permute-done((bf16[1536,128]{1,0:T(8,128)(2,1)}, bf16[1536,128]{1,0:T(8,128)(2,1)S(1)}, u32[]{:S(2)}, u32[]{:S(2)}) %collective-permute-start.50) | collective-permute-done | bytes 393248 | tf_op jit(solution)/shard_map/ppermute | solution.py:37
  320.7 10.2 %collective-permute-done.52.refs_3_ = bf16[1536,128]{1,0:T(8,128)(2,1)S(1)} collective-permute-done((bf16[1536,128]{1,0:T(8,128)(2,1)S(1)}, bf16[1536,128]{1,0:T(8,128)(2,1)S(1)}, u32[]{:S(2)}, u32[]{:S(2)}) %collective-permute-start.52) | collective-permute-done | bytes 393248 | tf_op jit(solution)/shard_map/ppermute | solution.py:37
  334.0 6.0 %input_grad.1 = (bf16[1024,768]{1,0:T(8,128)(2,1)}, bf16[512,1024]{1,0:T(8,128)(2,1)}, f32[512,1024]{1,0:T(8,128)}) custom-call(s32[3]{0:T(128)} %pad_add_fusion.ids, bf16[1536,128]{1,0:T(8,128)(2,1)} %get-tuple-element.273.refs_0_, bf16[1536,128]{1,0:T(8,128)(2,1)} %copy-done.43, bf16[1536,128]{1,0:T(8,128)(2,1)} %copy-done.44, ...), custom_call_target="tpu_custom_call" | custom-call | flops 1 | bytes 1 | tf_op jit(solution)/shard_map/input_grad/pallas_call | solution.py:113
  340.0 3.4 convolution_convert_fusion
  343.9 3.7 halve.8
  349.7 3.6 fusion.keep
  357.0 2.6 add_convert_fusion.1
  361.6 10.5 %collective-permute-done.56.got = bf16[672,512]{1,0:T(8,128)(2,1)S(1)} collective-permute-done((bf16[672,512]{1,0:T(8,128)(2,1)}, bf16[672,512]{1,0:T(8,128)(2,1)S(1)}, u32[]{:S(2)}, u32[]{:S(2)}) %collective-permute-start.56) | collective-permute-done | bytes 688160 | tf_op jit(solution)/shard_map/ppermute | solution.py:37
  372.9 2.8 halve.9
  375.7 2.8 halve.10
  383.3 14.0 %collective-permute-done.59.got = bf16[256,768]{1,0:T(8,128)(2,1)S(1)} collective-permute-done((bf16[256,768]{1,0:T(8,128)(2,1)}, bf16[256,768]{1,0:T(8,128)(2,1)S(1)}, u32[]{:S(2)}, u32[]{:S(2)}) %collective-permute-start.59) | collective-permute-done | bytes 393248 | tf_op jit(solution)/shard_map/ppermute | solution.py:37
  403.5 4.3 collective-permute-start.70
  412.7 3.8 place.2
  416.5 10.3 %collective-permute-done.65.got = bf16[128,768]{1,0:T(8,128)(2,1)S(1)} collective-permute-done((bf16[128,768]{1,0:T(8,128)(2,1)}, bf16[128,768]{1,0:T(8,128)(2,1)S(1)}, u32[]{:S(2)}, u32[]{:S(2)}) %collective-permute-start.65) | collective-permute-done | bytes 196640 | tf_op jit(solution)/shard_map/ppermute | solution.py:37
  429.3 9.0 %collective-permute-done.66.refs_1_ = bf16[336,512]{1,0:T(8,128)(2,1)S(1)} collective-permute-done((bf16[336,512]{1,0:T(8,128)(2,1)}, bf16[336,512]{1,0:T(8,128)(2,1)S(1)}, u32[]{:S(2)}, u32[]{:S(2)}) %collective-permute-start.66) | collective-permute-done | bytes 344096 | tf_op jit(solution)/shard_map/ppermute | solution.py:37
  439.8 2.7 place_columns.2
  448.0 3.8 place.3
  454.0 7.4 %collective-permute-done.74.refs_3_ = bf16[336,512]{1,0:T(8,128)(2,1)S(1)} collective-permute-done((bf16[336,512]{1,0:T(8,128)(2,1)S(1)}, bf16[336,512]{1,0:T(8,128)(2,1)S(1)}, u32[]{:S(2)}, u32[]{:S(2)}) %collective-permute-start.74) | collective-permute-done | bytes 344096 | tf_op jit(solution)/shard_map/ppermute | solution.py:37
  462.1 3.5 place_rows.1
  (319 shorter events, 116.2 us)
Async XLA Ops:
  3.7 24.1 %collective-permute-start = (bf16[512,768]{1,0:T(8,128)(2,1)S(1)}, bf16[512,768]{1,0:T(8,128)(2,1)}, u32[]{:S(2)}, u32[]{:S(2)}) collective-permute-start(bf16[512,768]{1,0:T(8,128)(2,1)S(1)} %constant_dynamic-update-slice_fusion.refs_0_.refs_4_), channel_id=1, source_target_pairs={{0,16},{16,0},{1,17},{17,1},{2,18},{18,2},{3,19},{19,3},{4,20},{20... | collective-permute-start | bytes 2359304 | tf_op jit(solution)/shard_map/ppermute | solution.py:37
  10.5 55.4 %collective-permute-start.4 = (bf16[1296,512]{1,0:T(8,128)(2,1)S(1)}, bf16[1296,512]{1,0:T(8,128)(2,1)S(1)}, u32[]{:S(2)}, u32[]{:S(2)}) collective-permute-start(bf16[1296,512]{1,0:T(8,128)(2,1)S(1)} %pad_maximum_fusion.refs_6_), channel_id=1, source_target_pairs={{0,2},{1,3},{2,0},{3,1},{4,6},{5,7},{6,4},{7,5},{8,10},{9,11},{10,... | collective-permute-start | bytes 3981320 | tf_op jit(solution)/shard_map/ppermute | solution.py:37
  36.3 29.7 %collective-permute-start.8 = (bf16[512,1024]{1,0:T(8,128)(2,1)}, bf16[512,1024]{1,0:T(8,128)(2,1)S(1)}, u32[]{:S(2)}, u32[]{:S(2)}) collective-permute-start(bf16[512,1024]{1,0:T(8,128)(2,1)} %refs_14_.1), channel_id=1, source_target_pairs={{0,2},{1,3},{2,0},{3,1},{4,6},{5,7},{6,4},{7,5},{8,10},{9,11},{10,... | collective-permute-start | bytes 3145736 | tf_op jit(solution)/shard_map/ppermute | solution.py:37
  36.8 17.5 %collective-permute-start.5 = (bf16[1536,128]{1,0:T(8,128)(2,1)}, bf16[1536,128]{1,0:T(8,128)(2,1)S(1)}, u32[]{:S(2)}, u32[]{:S(2)}) collective-permute-start(bf16[1536,128]{1,0:T(8,128)(2,1)} %get-tuple-element.175), channel_id=1, source_target_pairs={{0,4},{4,0},{8,12},{12,8},{1,5},{5,1},{9,13},{13,9},{2,6},{6,2},{1... | collective-permute-start | bytes 1179656 | tf_op jit(solution)/shard_map/ppermute | solution.py:37
  38.1 28.5 %collective-permute-start.9 = (bf16[512,1024]{1,0:T(8,128)(2,1)}, bf16[512,1024]{1,0:T(8,128)(2,1)}, u32[]{:S(2)}, u32[]{:S(2)}) collective-permute-start(bf16[512,1024]{1,0:T(8,128)(2,1)} %refs_14_.1), channel_id=1, source_target_pairs={{0,16},{16,0},{1,17},{17,1},{2,18},{18,2},{3,19},{19,3},{4,20},{20... | collective-permute-start | bytes 3145736 | tf_op jit(solution)/shard_map/ppermute | solution.py:37
  38.6 27.4 %collective-permute-start.6 = (bf16[1536,128]{1,0:T(8,128)(2,1)}, bf16[1536,128]{1,0:T(8,128)(2,1)S(1)}, u32[]{:S(2)}, u32[]{:S(2)}) collective-permute-start(bf16[1536,128]{1,0:T(8,128)(2,1)} %get-tuple-element.176), channel_id=1, source_target_pairs={{0,8},{4,12},{8,0},{12,4},{1,9},{5,13},{9,1},{13,5},{2,10},{6,14},... | collective-permute-start | bytes 1179656 | tf_op jit(solution)/shard_map/ppermute | solution.py:37
  66.0 26.0 %collective-permute-start.11 = (bf16[1296,512]{1,0:T(8,128)(2,1)S(1)}, bf16[1296,512]{1,0:T(8,128)(2,1)}, u32[]{:S(2)}, u32[]{:S(2)}) collective-permute-start(bf16[1296,512]{1,0:T(8,128)(2,1)S(1)} %pad_maximum_fusion.refs_6_), channel_id=1, source_target_pairs={{0,1},{1,0},{2,3},{3,2},{4,5},{5,4},{6,7},{7,6},{8,9},{9,8},{10,11... | collective-permute-start | bytes 3981320 | tf_op jit(solution)/shard_map/ppermute | solution.py:37
  66.1 26.0 %collective-permute-start.12 = (bf16[1296,512]{1,0:T(8,128)(2,1)S(1)}, bf16[1296,512]{1,0:T(8,128)(2,1)}, u32[]{:S(2)}, u32[]{:S(2)}) collective-permute-start(bf16[1296,512]{1,0:T(8,128)(2,1)S(1)} %collective-permute-done.4.refs_8_), channel_id=1, source_target_pairs={{0,1},{1,0},{2,3},{3,2},{4,5},{5,4},{6,7},{7,6},{8,9},{9,8},{10,11... | collective-permute-start | bytes 3981320 | tf_op jit(solution)/shard_map/ppermute | solution.py:37
  67.1 25.0 %collective-permute-start.10 = (bf16[512,1024]{1,0:T(8,128)(2,1)}, bf16[512,1024]{1,0:T(8,128)(2,1)}, u32[]{:S(2)}, u32[]{:S(2)}) collective-permute-start(bf16[512,1024]{1,0:T(8,128)(2,1)} %collective-permute-done.9.refs_15_), channel_id=1, source_target_pairs={{0,2},{1,3},{2,0},{3,1},{4,6},{5,7},{6,4},{7,5},{8,10},{9,11},{10,... | collective-permute-start | bytes 3145736 | tf_op jit(solution)/shard_map/ppermute | solution.py:37
  68.5 43.0 %collective-permute-start.15 = (bf16[1296,512]{1,0:T(8,128)(2,1)S(1)}, bf16[1296,512]{1,0:T(8,128)(2,1)}, u32[]{:S(2)}, u32[]{:S(2)}) collective-permute-start(bf16[1296,512]{1,0:T(8,128)(2,1)S(1)} %pad_maximum_fusion.refs_6_), channel_id=1, source_target_pairs={{0,16},{16,0},{1,17},{17,1},{2,18},{18,2},{3,19},{19,3},{4,20},{20... | collective-permute-start | bytes 3981320 | tf_op jit(solution)/shard_map/ppermute | solution.py:37
  92.1 19.4 %collective-permute-start.13 = (bf16[512,1024]{1,0:T(8,128)(2,1)}, bf16[512,1024]{1,0:T(8,128)(2,1)}, u32[]{:S(2)}, u32[]{:S(2)}) collective-permute-start(bf16[512,1024]{1,0:T(8,128)(2,1)} %refs_14_.1), channel_id=1, source_target_pairs={{0,1},{1,0},{2,3},{3,2},{4,5},{5,4},{6,7},{7,6},{8,9},{9,8},{10,11... | collective-permute-start | bytes 3145736 | tf_op jit(solution)/shard_map/ppermute | solution.py:37
  92.1 19.4 %collective-permute-start.14 = (bf16[512,1024]{1,0:T(8,128)(2,1)}, bf16[512,1024]{1,0:T(8,128)(2,1)}, u32[]{:S(2)}, u32[]{:S(2)}) collective-permute-start(bf16[512,1024]{1,0:T(8,128)(2,1)} %collective-permute-done.9.refs_15_), channel_id=1, source_target_pairs={{0,1},{1,0},{2,3},{3,2},{4,5},{5,4},{6,7},{7,6},{8,9},{9,8},{10,11... | collective-permute-start | bytes 3145736 | tf_op jit(solution)/shard_map/ppermute | solution.py:37
  92.6 42.7 %collective-permute-start.21 = (bf16[1296,512]{1,0:T(8,128)(2,1)S(1)}, bf16[1296,512]{1,0:T(8,128)(2,1)}, u32[]{:S(2)}, u32[]{:S(2)}) collective-permute-start(bf16[1296,512]{1,0:T(8,128)(2,1)S(1)} %collective-permute-done.4.refs_8_), channel_id=1, source_target_pairs={{0,16},{16,0},{1,17},{17,1},{2,18},{18,2},{3,19},{19,3},{4,20},{20... | collective-permute-start | bytes 3981320 | tf_op jit(solution)/shard_map/ppermute | solution.py:37
  111.5 20.5 %collective-permute-start.19 = (bf16[512,1024]{1,0:T(8,128)(2,1)}, bf16[512,1024]{1,0:T(8,128)(2,1)S(1)}, u32[]{:S(2)}, u32[]{:S(2)}) collective-permute-start(bf16[512,1024]{1,0:T(8,128)(2,1)} %copy-done.9), channel_id=1, source_target_pairs={{0,1},{1,0},{2,3},{3,2},{4,5},{5,4},{6,7},{7,6},{8,9},{9,8},{10,11... | collective-permute-start | bytes 3145736 | tf_op jit(solution)/shard_map/ppermute | solution.py:37
  111.6 20.4 %collective-permute-start.20 = (bf16[512,1024]{1,0:T(8,128)(2,1)}, bf16[512,1024]{1,0:T(8,128)(2,1)S(1)}, u32[]{:S(2)}, u32[]{:S(2)}) collective-permute-start(bf16[512,1024]{1,0:T(8,128)(2,1)} %collective-permute-done.10.refs_17_), channel_id=1, source_target_pairs={{0,1},{1,0},{2,3},{3,2},{4,5},{5,4},{6,7},{7,6},{8,9},{9,8},{10,11... | collective-permute-start | bytes 3145736 | tf_op jit(solution)/shard_map/ppermute | solution.py:37
  159.4 14.8 %collective-permute-start.27 = (bf16[256,1024]{1,0:T(8,128)(2,1)}, bf16[256,1024]{1,0:T(8,128)(2,1)S(1)}, u32[]{:S(2)}, u32[]{:S(2)}) collective-permute-start(bf16[256,1024]{1,0:T(8,128)(2,1)} %get-tuple-element.214), channel_id=1, source_target_pairs={{0,2},{1,3},{2,0},{3,1},{4,6},{5,7},{6,4},{7,5},{8,10},{9,11},{10,... | collective-permute-start | bytes 1572872 | tf_op jit(solution)/shard_map/ppermute | solution.py:37
  192.0 34.7 %collective-permute-start.35 = (bf16[256,1024]{1,0:T(8,128)(2,1)S(1)}, bf16[256,1024]{1,0:T(8,128)(2,1)}, u32[]{:S(2)}, u32[]{:S(2)}) collective-permute-start(bf16[256,1024]{1,0:T(8,128)(2,1)S(1)} %copy-done.14), channel_id=1, source_target_pairs={{0,2},{1,3},{2,0},{3,1},{4,6},{5,7},{6,4},{7,5},{8,10},{9,11},{10,... | collective-permute-start | bytes 1572872 | tf_op jit(solution)/shard_map/ppermute | solution.py:37
  193.2 33.6 %collective-permute-start.36 = (bf16[256,1024]{1,0:T(8,128)(2,1)}, bf16[256,1024]{1,0:T(8,128)(2,1)S(1)}, u32[]{:S(2)}, u32[]{:S(2)}) collective-permute-start(bf16[256,1024]{1,0:T(8,128)(2,1)} %get-tuple-element.234), channel_id=1, source_target_pairs={{0,3},{1,2},{2,1},{3,0},{4,7},{5,6},{6,5},{7,4},{8,11},{9,10},{10,... | collective-permute-start | bytes 1572872 | tf_op jit(solution)/shard_map/ppermute | solution.py:37
  193.4 34.9 %collective-permute-start.37 = (bf16[256,1024]{1,0:T(8,128)(2,1)S(1)}, bf16[256,1024]{1,0:T(8,128)(2,1)S(1)}, u32[]{:S(2)}, u32[]{:S(2)}) collective-permute-start(bf16[256,1024]{1,0:T(8,128)(2,1)S(1)} %copy-done.33), channel_id=1, source_target_pairs={{0,2},{1,3},{2,0},{3,1},{4,6},{5,7},{6,4},{7,5},{8,10},{9,11},{10,... | collective-permute-start | bytes 1572872 | tf_op jit(solution)/shard_map/ppermute | solution.py:37
  194.7 32.1 %collective-permute-start.32 = (bf16[512,128]{1,0:T(8,128)(2,1)}, bf16[512,128]{1,0:T(8,128)(2,1)S(1)}, u32[]{:S(2)}, u32[]{:S(2)}) collective-permute-start(bf16[512,128]{1,0:T(8,128)(2,1)} %get-tuple-element.224), channel_id=1, source_target_pairs={{0,8},{4,12},{8,0},{12,4},{1,9},{5,13},{9,1},{13,5},{2,10},{6,14},... | collective-permute-start | bytes 393224 | tf_op jit(solution)/shard_map/ppermute | solution.py:37
  197.4 29.3 %collective-permute-start.34 = (bf16[512,128]{1,0:T(8,128)(2,1)}, bf16[512,128]{1,0:T(8,128)(2,1)S(1)}, u32[]{:S(2)}, u32[]{:S(2)}) collective-permute-start(bf16[512,128]{1,0:T(8,128)(2,1)} %get-tuple-element.231), channel_id=1, source_target_pairs={{0,12},{4,8},{8,4},{12,0},{1,13},{5,9},{9,5},{13,1},{2,14},{6,10},... | collective-permute-start | bytes 393224 | tf_op jit(solution)/shard_map/ppermute | solution.py:37
  237.5 36.3 %collective-permute-start.46 = (bf16[1024,512]{1,0:T(8,128)(2,1)}, bf16[1024,512]{1,0:T(8,128)(2,1)S(1)}, u32[]{:S(2)}, u32[]{:S(2)}) collective-permute-start(bf16[1024,512]{1,0:T(8,128)(2,1)} %get-tuple-element.240), channel_id=1, source_target_pairs={{0,16},{16,0},{1,17},{17,1},{2,18},{18,2},{3,19},{19,3},{4,20},{20... | collective-permute-start | bytes 3145736 | tf_op jit(solution)/shard_map/ppermute | solution.py:37
  238.1 32.4 %collective-permute-start.42 = (bf16[272,1024]{1,0:T(8,128)(2,1)S(1)}, bf16[272,1024]{1,0:T(8,128)(2,1)S(1)}, u32[]{:S(2)}, u32[]{:S(2)}) collective-permute-start(bf16[272,1024]{1,0:T(8,128)(2,1)S(1)} %copy-done.22), channel_id=1, source_target_pairs={{0,2},{1,3},{2,0},{3,1},{4,6},{5,7},{6,4},{7,5},{8,10},{9,11},{10,... | collective-permute-start | bytes 1671176 | tf_op jit(solution)/shard_map/ppermute | solution.py:37
  239.3 31.3 %collective-permute-start.43 = (bf16[256,1024]{1,0:T(8,128)(2,1)}, bf16[256,1024]{1,0:T(8,128)(2,1)}, u32[]{:S(2)}, u32[]{:S(2)}) collective-permute-start(bf16[256,1024]{1,0:T(8,128)(2,1)} %get-tuple-element.251), channel_id=1, source_target_pairs={{0,2},{1,3},{2,0},{3,1},{4,6},{5,7},{6,4},{7,5},{8,10},{9,11},{10,... | collective-permute-start | bytes 1572872 | tf_op jit(solution)/shard_map/ppermute | solution.py:37
  240.1 30.4 %collective-permute-start.44 = (bf16[256,1024]{1,0:T(8,128)(2,1)}, bf16[256,1024]{1,0:T(8,128)(2,1)S(1)}, u32[]{:S(2)}, u32[]{:S(2)}) collective-permute-start(bf16[256,1024]{1,0:T(8,128)(2,1)} %get-tuple-element.253), channel_id=1, source_target_pairs={{0,1},{1,0},{2,3},{3,2},{4,5},{5,4},{6,7},{7,6},{8,9},{9,8},{10,11... | collective-permute-start | bytes 1572872 | tf_op jit(solution)/shard_map/ppermute | solution.py:37
  240.1 33.7 %collective-permute-start.45 = (bf16[256,1024]{1,0:T(8,128)(2,1)}, bf16[256,1024]{1,0:T(8,128)(2,1)S(1)}, u32[]{:S(2)}, u32[]{:S(2)}) collective-permute-start(bf16[256,1024]{1,0:T(8,128)(2,1)} %get-tuple-element.255), channel_id=1, source_target_pairs={{0,3},{1,2},{2,1},{3,0},{4,7},{5,6},{6,5},{7,4},{8,11},{9,10},{10,... | collective-permute-start | bytes 1572872 | tf_op jit(solution)/shard_map/ppermute | solution.py:37
  288.2 55.7 %collective-permute-start.55 = (bf16[1344,512]{1,0:T(8,128)(2,1)}, bf16[1344,512]{1,0:T(8,128)(2,1)}, u32[]{:S(2)}, u32[]{:S(2)}) collective-permute-start(bf16[1344,512]{1,0:T(8,128)(2,1)} %get-tuple-element.263), channel_id=1, source_target_pairs={{0,16},{16,0},{1,17},{17,1},{2,18},{18,2},{3,19},{19,3},{4,20},{20... | collective-permute-start | bytes 4128776 | tf_op jit(solution)/shard_map/ppermute | solution.py:37
  289.7 41.1 %collective-permute-start.47 = (bf16[512,512]{1,0:T(8,128)(2,1)S(1)}, bf16[512,512]{1,0:T(8,128)(2,1)S(1)}, u32[]{:S(2)}, u32[]{:S(2)}) collective-permute-start(bf16[512,512]{1,0:T(8,128)(2,1)S(1)} %copy-done.72), channel_id=1, source_target_pairs={{0,4},{4,0},{8,12},{12,8},{1,5},{5,1},{9,13},{13,9},{2,6},{6,2},{1... | collective-permute-start | bytes 1572872 | tf_op jit(solution)/shard_map/ppermute | solution.py:37
  291.2 29.5 %collective-permute-start.50 = (bf16[1536,128]{1,0:T(8,128)(2,1)}, bf16[1536,128]{1,0:T(8,128)(2,1)S(1)}, u32[]{:S(2)}, u32[]{:S(2)}) collective-permute-start(bf16[1536,128]{1,0:T(8,128)(2,1)} %get-tuple-element.265), channel_id=1, source_target_pairs={{0,4},{4,0},{8,12},{12,8},{1,5},{5,1},{9,13},{13,9},{2,6},{6,2},{1... | collective-permute-start | bytes 1179656 | tf_op jit(solution)/shard_map/ppermute | solution.py:37
  291.8 28.9 %collective-permute-start.51 = (bf16[1536,128]{1,0:T(8,128)(2,1)}, bf16[1536,128]{1,0:T(8,128)(2,1)S(1)}, u32[]{:S(2)}, u32[]{:S(2)}) collective-permute-start(bf16[1536,128]{1,0:T(8,128)(2,1)} %get-tuple-element.267), channel_id=1, source_target_pairs={{0,8},{4,12},{8,0},{12,4},{1,9},{5,13},{9,1},{13,5},{2,10},{6,14},... | collective-permute-start | bytes 1179656 | tf_op jit(solution)/shard_map/ppermute | solution.py:37
  294.1 36.7 %collective-permute-start.52 = (bf16[1536,128]{1,0:T(8,128)(2,1)S(1)}, bf16[1536,128]{1,0:T(8,128)(2,1)S(1)}, u32[]{:S(2)}, u32[]{:S(2)}) collective-permute-start(bf16[1536,128]{1,0:T(8,128)(2,1)S(1)} %copy-done.73), channel_id=1, source_target_pairs={{0,12},{4,8},{8,4},{12,0},{1,13},{5,9},{9,5},{13,1},{2,14},{6,10},... | collective-permute-start | bytes 1179656 | tf_op jit(solution)/shard_map/ppermute | solution.py:37
  340.0 17.0 %collective-permute-start.53 = (bf16[512,1024]{1,0:T(8,128)(2,1)}, bf16[512,1024]{1,0:T(8,128)(2,1)S(1)}, u32[]{:S(2)}, u32[]{:S(2)}) collective-permute-start(bf16[512,1024]{1,0:T(8,128)(2,1)} %get-tuple-element.275), channel_id=1, source_target_pairs={{0,1},{1,0},{2,3},{3,2},{4,5},{5,4},{6,7},{7,6},{8,9},{9,8},{10,11... | collective-permute-start | bytes 3145736 | tf_op jit(solution)/shard_map/ppermute | solution.py:37
  340.0 14.4 %collective-permute-start.54 = (bf16[256,512]{1,0:T(8,128)(2,1)}, bf16[256,512]{1,0:T(8,128)(2,1)S(1)}, u32[]{:S(2)}, u32[]{:S(2)}) collective-permute-start(bf16[256,512]{1,0:T(8,128)(2,1)} %get-tuple-element.272), channel_id=1, source_target_pairs={{0,8},{4,12},{8,0},{12,4},{1,9},{5,13},{9,1},{13,5},{2,10},{6,14},... | collective-permute-start | bytes 786440 | tf_op jit(solution)/shard_map/ppermute | solution.py:37
  343.4 32.3 %collective-permute-start.58 = (bf16[512,768]{1,0:T(8,128)(2,1)}, bf16[512,768]{1,0:T(8,128)(2,1)}, u32[]{:S(2)}, u32[]{:S(2)}) collective-permute-start(bf16[512,768]{1,0:T(8,128)(2,1)} %convolution_convert_fusion), channel_id=1, source_target_pairs={{0,16},{16,0},{1,17},{17,1},{2,18},{18,2},{3,19},{19,3},{4,20},{20... | collective-permute-start | bytes 2359304 | tf_op jit(solution)/shard_map/ppermute | solution.py:37
  347.6 24.5 %collective-permute-start.56 = (bf16[672,512]{1,0:T(8,128)(2,1)}, bf16[672,512]{1,0:T(8,128)(2,1)S(1)}, u32[]{:S(2)}, u32[]{:S(2)}) collective-permute-start(bf16[672,512]{1,0:T(8,128)(2,1)} %get-tuple-element.280), channel_id=1, source_target_pairs={{0,4},{4,0},{8,12},{12,8},{1,5},{5,1},{9,13},{13,9},{2,6},{6,2},{1... | collective-permute-start | bytes 2064392 | tf_op jit(solution)/shard_map/ppermute | solution.py:37
  359.6 21.1 %collective-permute-start.60 = (bf16[256,1024]{1,0:T(8,128)(2,1)}, bf16[256,1024]{1,0:T(8,128)(2,1)S(1)}, u32[]{:S(2)}, u32[]{:S(2)}) collective-permute-start(bf16[256,1024]{1,0:T(8,128)(2,1)} %add_convert_fusion.1), channel_id=1, source_target_pairs={{0,2},{1,3},{2,0},{3,1},{4,6},{5,7},{6,4},{7,5},{8,10},{9,11},{10,... | collective-permute-start | bytes 1572872 | tf_op jit(solution)/shard_map/ppermute | solution.py:37
  361.3 19.4 %collective-permute-start.61 = (bf16[256,512]{1,0:T(8,128)(2,1)S(1)}, bf16[256,512]{1,0:T(8,128)(2,1)}, u32[]{:S(2)}, u32[]{:S(2)}) collective-permute-start(bf16[256,512]{1,0:T(8,128)(2,1)S(1)} %copy-done.19), channel_id=1, source_target_pairs={{0,8},{4,12},{8,0},{12,4},{1,9},{5,13},{9,1},{13,5},{2,10},{6,14},... | collective-permute-start | bytes 786440 | tf_op jit(solution)/shard_map/ppermute | solution.py:37
  361.3 41.7 %collective-permute-start.62 = (bf16[256,1024]{1,0:T(8,128)(2,1)}, bf16[256,1024]{1,0:T(8,128)(2,1)}, u32[]{:S(2)}, u32[]{:S(2)}) collective-permute-start(bf16[256,1024]{1,0:T(8,128)(2,1)} %get-tuple-element.299.refs_0_), channel_id=1, source_target_pairs={{0,2},{1,3},{2,0},{3,1},{4,6},{5,7},{6,4},{7,5},{8,10},{9,11},{10,... | collective-permute-start | bytes 1572872 | tf_op jit(solution)/shard_map/ppermute | solution.py:37
  378.6 18.8 %collective-permute-start.59 = (bf16[256,768]{1,0:T(8,128)(2,1)}, bf16[256,768]{1,0:T(8,128)(2,1)S(1)}, u32[]{:S(2)}, u32[]{:S(2)}) collective-permute-start(bf16[256,768]{1,0:T(8,128)(2,1)} %get-tuple-element.291), channel_id=1, source_target_pairs={{0,4},{4,0},{8,12},{12,8},{1,5},{5,1},{9,13},{13,9},{2,6},{6,2},{1... | collective-permute-start | bytes 1179656 | tf_op jit(solution)/shard_map/ppermute | solution.py:37
  378.6 21.6 %collective-permute-start.57 = (bf16[336,512]{1,0:T(8,128)(2,1)S(1)}, bf16[336,512]{1,0:T(8,128)(2,1)S(1)}, u32[]{:S(2)}, u32[]{:S(2)}) collective-permute-start(bf16[336,512]{1,0:T(8,128)(2,1)S(1)} %copy-done.74), channel_id=1, source_target_pairs={{0,8},{4,12},{8,0},{12,4},{1,9},{5,13},{9,1},{13,5},{2,10},{6,14},... | collective-permute-start | bytes 1032200 | tf_op jit(solution)/shard_map/ppermute | solution.py:37
  403.5 39.0 %collective-permute-start.70 = (bf16[256,1024]{1,0:T(8,128)(2,1)S(1)}, bf16[256,1024]{1,0:T(8,128)(2,1)S(1)}, u32[]{:S(2)}, u32[]{:S(2)}) collective-permute-start(bf16[256,1024]{1,0:T(8,128)(2,1)S(1)} %add_convert_fusion.refs_0_), channel_id=1, source_target_pairs={{0,2},{1,3},{2,0},{3,1},{4,6},{5,7},{6,4},{7,5},{8,10},{9,11},{10,... | collective-permute-start | bytes 1572872 | tf_op jit(solution)/shard_map/ppermute | solution.py:37
  407.7 19.1 %collective-permute-start.65 = (bf16[128,768]{1,0:T(8,128)(2,1)}, bf16[128,768]{1,0:T(8,128)(2,1)S(1)}, u32[]{:S(2)}, u32[]{:S(2)}) collective-permute-start(bf16[128,768]{1,0:T(8,128)(2,1)} %get-tuple-element.296), channel_id=1, source_target_pairs={{0,8},{4,12},{8,0},{12,4},{1,9},{5,13},{9,1},{13,5},{2,10},{6,14},... | collective-permute-start | bytes 589832 | tf_op jit(solution)/shard_map/ppermute | solution.py:37
  408.2 30.1 %collective-permute-start.66 = (bf16[336,512]{1,0:T(8,128)(2,1)}, bf16[336,512]{1,0:T(8,128)(2,1)S(1)}, u32[]{:S(2)}, u32[]{:S(2)}) collective-permute-start(bf16[336,512]{1,0:T(8,128)(2,1)} %merge.4.refs_0_), channel_id=1, source_target_pairs={{0,8},{4,12},{8,0},{12,4},{1,9},{5,13},{9,1},{13,5},{2,10},{6,14},... | collective-permute-start | bytes 1032200 | tf_op jit(solution)/shard_map/ppermute | solution.py:37
  410.7 27.7 %collective-permute-start.67 = (bf16[256,512]{1,0:T(8,128)(2,1)S(1)}, bf16[256,512]{1,0:T(8,128)(2,1)S(1)}, u32[]{:S(2)}, u32[]{:S(2)}) collective-permute-start(bf16[256,512]{1,0:T(8,128)(2,1)S(1)} %copy-done.19), channel_id=1, source_target_pairs={{0,4},{4,0},{8,12},{12,8},{1,5},{5,1},{9,13},{13,9},{2,6},{6,2},{1... | collective-permute-start | bytes 786440 | tf_op jit(solution)/shard_map/ppermute | solution.py:37
  410.7 27.7 %collective-permute-start.68 = (bf16[256,512]{1,0:T(8,128)(2,1)}, bf16[256,512]{1,0:T(8,128)(2,1)S(1)}, u32[]{:S(2)}, u32[]{:S(2)}) collective-permute-start(bf16[256,512]{1,0:T(8,128)(2,1)} %collective-permute-done.61.refs_1_), channel_id=1, source_target_pairs={{0,4},{4,0},{8,12},{12,8},{1,5},{5,1},{9,13},{13,9},{2,6},{6,2},{1... | collective-permute-start | bytes 786440 | tf_op jit(solution)/shard_map/ppermute | solution.py:37
  443.1 18.3 %collective-permute-start.74 = (bf16[336,512]{1,0:T(8,128)(2,1)S(1)}, bf16[336,512]{1,0:T(8,128)(2,1)S(1)}, u32[]{:S(2)}, u32[]{:S(2)}) collective-permute-start(bf16[336,512]{1,0:T(8,128)(2,1)S(1)} %collective-permute-done.66.refs_1_), channel_id=1, source_target_pairs={{0,4},{4,0},{8,12},{12,8},{1,5},{5,1},{9,13},{13,9},{2,6},{6,2},{1... | collective-permute-start | bytes 1032200 | tf_op jit(solution)/shard_map/ppermute | solution.py:37
  445.1 22.0 %collective-permute-start.75 = (bf16[128,768]{1,0:T(8,128)(2,1)S(1)}, bf16[128,768]{1,0:T(8,128)(2,1)}, u32[]{:S(2)}, u32[]{:S(2)}) collective-permute-start(bf16[128,768]{1,0:T(8,128)(2,1)S(1)} %copy-done.20), channel_id=1, source_target_pairs={{0,4},{4,0},{8,12},{12,8},{1,5},{5,1},{9,13},{13,9},{2,6},{6,2},{1... | collective-permute-start | bytes 589832 | tf_op jit(solution)/shard_map/ppermute | solution.py:37
  445.1 23.8 %collective-permute-start.76 = (bf16[128,768]{1,0:T(8,128)(2,1)S(1)}, bf16[128,768]{1,0:T(8,128)(2,1)S(1)}, u32[]{:S(2)}, u32[]{:S(2)}) collective-permute-start(bf16[128,768]{1,0:T(8,128)(2,1)S(1)} %collective-permute-done.69.refs_1_), channel_id=1, source_target_pairs={{0,4},{4,0},{8,12},{12,8},{1,5},{5,1},{9,13},{13,9},{2,6},{6,2},{1... | collective-permute-start | bytes 589832 | tf_op jit(solution)/shard_map/ppermute | solution.py:37
  (104 other events, 965.7 us)
